TPU v7x, 32 devices: a whole 2x2x4 slice. The times are simulated.
32 devices in a mesh: fsdp: 32 (over z, y, x, core).
Axes of the slice: x: 2, y: 2, z: 4, core: 2. Of those that a mesh axis runs over, the one named last changes fastest.
Arguments:
- tokens: bfloat16 [512, 64, 768], P('fsdp'), may hold values from -6 to 6
- lengths: int32 [512], P('fsdp'), may hold values from 3 to 64, as said below
- partners: int32 [256], P('fsdp'), may hold values from 0 to 255, each once
- out_cotangent: bfloat16 [512, 64, 768], P('fsdp'), may hold values from -6 to 6
- w_query: bfloat16 [768, 768], P('fsdp'), may hold values from -0.21875 to 0.21875
- w_key: bfloat16 [768, 768], P('fsdp'), may hold values from -0.21875 to 0.21875
- w_value: bfloat16 [768, 768], P('fsdp'), may hold values from -0.21875 to 0.21875
- w_output: bfloat16 [768, 768], P('fsdp'), may hold values from -0.625 to 0.625
- b_query: bfloat16 [768], P('fsdp'), may hold values from -1.5 to 1.5
- b_value: bfloat16 [768], P('fsdp'), may hold values from -1.5 to 1.5
- b_output: bfloat16 [768], P('fsdp'), may hold values from -1.5 to 1.5
- gain_attn: bfloat16 [768], P('fsdp'), may hold values from 0.5 to 1.5
- shift_attn: bfloat16 [768], P('fsdp'), may hold values from -1.5 to 1.5
- w_inner: bfloat16 [768, 3072], P('fsdp'), may hold values from -0.21875 to 0.21875
- b_inner: bfloat16 [3072], P('fsdp'), may hold values from -1.5 to 1.5
- w_outer: bfloat16 [3072, 768], P('fsdp'), may hold values from -0.15625 to 0.15625
- b_outer: bfloat16 [768], P('fsdp'), may hold values from -1.5 to 1.5
- gain_ffn: bfloat16 [768], P('fsdp'), may hold values from 0.5 to 1.5
- shift_ffn: bfloat16 [768], P('fsdp'), may hold values from -1.5 to 1.5
Outputs:
- loss: float32 [], replicated
- block_out: bfloat16 [512, 64, 768], P('fsdp')
- grad_tokens: float32 [512, 64, 768], P('fsdp')
- grad_w_query: float32 [768, 768], P('fsdp')
- grad_w_key: float32 [768, 768], P('fsdp')
- grad_w_value: float32 [768, 768], P('fsdp')
- grad_w_output: float32 [768, 768], P('fsdp')
- grad_b_query: float32 [768], P('fsdp')
- grad_b_value: float32 [768], P('fsdp')
- grad_b_output: float32 [768], P('fsdp')
- grad_gain_attn: float32 [768], P('fsdp')
- grad_shift_attn: float32 [768], P('fsdp')
- grad_w_inner: float32 [768, 3072], P('fsdp')
- grad_b_inner: float32 [3072], P('fsdp')
- grad_w_outer: float32 [3072, 768], P('fsdp')
- grad_b_outer: float32 [768], P('fsdp')
- grad_gain_ffn: float32 [768], P('fsdp')
- grad_shift_ffn: float32 [768], P('fsdp')
Inputs may be any that keep to these rules, and one draw needn't show every extreme that they name: `lengths`: each sentence slot has 3 to 64 live tokens, heavy toward short ones; at least one slot has 64.
All inputs are finite; a program needn't handle non-finite values.
Results may differ from a plain program's by a relative error of at most 0.013.
Values may be sent and summed in bfloat16 or wider, within the bound.
No kernel may reach another device: no remote copies, remote signals or barrier semaphores. Data moves between devices by JAX's collectives and lax.ppermute only.
A program may use at most 192 MiB of HBM per device.

v0:
```python
import jax
import jax.numpy as jnp
from jax import lax
from jax.sharding import PartitionSpec as P

D = 768
HEADS = 12
HEAD_DIM = 64
LEN = 64


norm_eps = 1e-12
pool_eps = 1e-06
sim_scale = 50.0
sim_margin = 0.3


def project(rows, weight):
    return jnp.dot(rows, weight, preferred_element_type=jnp.float32)


def project_back(grad, weight):
    return lax.dot_general(
        grad, weight, (((1,), (1,)), ((), ())), preferred_element_type=jnp.float32
    )


def weight_grad(rows, grad):
    return lax.dot_general(rows, grad, (((0,), (0,)), ((), ())), preferred_element_type=jnp.float32)


def scaled_norm(field, gain_vec):
    centred = field - jnp.mean(field, axis=-1, keepdims=True)
    variance = jnp.mean(centred * centred, axis=-1, keepdims=True)
    return centred * lax.rsqrt(variance + norm_eps) * gain_vec


def exact_gelu(field):
    return jax.nn.gelu(field, approximate=False)


def normalize(field):
    return field * lax.rsqrt(jnp.sum(field * field, axis=-1, keepdims=True) + pool_eps)


def scores_of(queries, key_rows, visible):
    raw = jnp.einsum(
        "bqhd,bkhd->bhqk", queries, key_rows, preferred_element_type=jnp.float32
    ) * HEAD_DIM ** (-0.5)
    return jnp.where(visible, raw, -1e30)


def column_sum(field):
    return jnp.sum(field.astype(jnp.float32), axis=0)


def local(
    tokens,
    lengths,
    partners,
    out_cotangent,
    w_query,
    w_key,
    w_value,
    w_output,
    b_query,
    b_value,
    b_output,
    gain_attn,
    shift_attn,
    w_inner,
    b_inner,
    w_outer,
    b_outer,
    gain_ffn,
    shift_ffn,
):
    count = tokens.shape[0]
    half = count // 2
    shape_four = (count, LEN, HEADS, HEAD_DIM)
    token_rows = tokens.reshape(count * LEN, D)
    positions = jnp.arange(LEN, dtype=jnp.int32)
    visible = (positions[None, :] < lengths[:, None])[:, None, None, :]
    attn_full = (
        lax.all_gather(w_query, "fsdp", axis=0, tiled=True),
        lax.all_gather(w_key, "fsdp", axis=0, tiled=True),
        lax.all_gather(w_value, "fsdp", axis=0, tiled=True),
        lax.all_gather(w_output, "fsdp", axis=0, tiled=True),
        lax.all_gather(b_query, "fsdp", axis=0, tiled=True),
        lax.all_gather(b_value, "fsdp", axis=0, tiled=True),
        lax.all_gather(b_output, "fsdp", axis=0, tiled=True),
        lax.all_gather(gain_attn, "fsdp", axis=0, tiled=True),
        lax.all_gather(shift_attn, "fsdp", axis=0, tiled=True),
    )
    (
        query_mat,
        key_mat,
        value_mat,
        output_mat,
        query_bias,
        value_bias,
        output_bias,
        attn_gain,
        attn_shift,
    ) = attn_full
    queries = (project(token_rows, query_mat) + query_bias).astype(jnp.bfloat16).reshape(shape_four)
    key_rows = project(token_rows, key_mat).astype(jnp.bfloat16).reshape(shape_four)
    value_rows = (
        (project(token_rows, value_mat) + value_bias).astype(jnp.bfloat16).reshape(shape_four)
    )
    scores = scores_of(queries, key_rows, visible)
    row_top = jnp.max(scores, axis=-1, keepdims=True)
    expd = jnp.exp(scores - row_top)
    row_total = jnp.sum(expd, axis=-1, keepdims=True)
    probs = expd / row_total
    score_lse = row_top + jnp.log(row_total)
    context = jnp.einsum(
        "bhqk,bkhd->bqhd",
        probs.astype(jnp.bfloat16),
        value_rows,
        preferred_element_type=jnp.float32,
    )
    context = context.astype(jnp.bfloat16).reshape(count * LEN, D)
    resid_attn = token_rows.astype(jnp.float32) + (project(context, output_mat) + output_bias)
    normed_attn = scaled_norm(resid_attn, attn_gain.astype(jnp.float32)) + attn_shift
    ffn_full = (
        lax.all_gather(w_inner, "fsdp", axis=0, tiled=True),
        lax.all_gather(b_inner, "fsdp", axis=0, tiled=True),
        lax.all_gather(w_outer, "fsdp", axis=0, tiled=True),
        lax.all_gather(b_outer, "fsdp", axis=0, tiled=True),
        lax.all_gather(gain_ffn, "fsdp", axis=0, tiled=True),
        lax.all_gather(shift_ffn, "fsdp", axis=0, tiled=True),
    )
    inner_mat, inner_bias, outer_mat, outer_bias, ffn_gain, ffn_shift = ffn_full
    normed_low = normed_attn.astype(jnp.bfloat16)
    hidden_pre = project(normed_low, inner_mat) + inner_bias
    hidden_act = exact_gelu(hidden_pre).astype(jnp.bfloat16)
    resid_ffn = normed_attn + (project(hidden_act, outer_mat) + outer_bias)
    block_rows = scaled_norm(resid_ffn, ffn_gain.astype(jnp.float32)) + ffn_shift
    block_out = block_rows.astype(jnp.bfloat16).reshape(count, LEN, D)
    cls_rows = block_rows.reshape(count, LEN, D)[:, 0, :]
    unit, pool_back = jax.vjp(normalize, cls_rows)
    unit_low = unit.astype(jnp.bfloat16)
    every_unit = lax.all_gather(unit_low, "fsdp", axis=0, tiled=True)
    every_pair = every_unit.reshape(every_unit.shape[0] // 2, 2, D)
    all_targets = every_pair[:, 1, :]
    own_pair = unit_low.reshape(half, 2, D)
    own_sources = own_pair[:, 0, :]
    npairs = all_targets.shape[0]
    sims = project_back(own_sources, all_targets) * sim_scale
    matched = partners[:, None] == jnp.arange(npairs, dtype=jnp.int32)[None, :]
    sims = sims - jnp.where(matched, sim_scale * sim_margin, 0.0)
    sim_top = jnp.max(sims, axis=1, keepdims=True)
    row_lse = sim_top + jnp.log(jnp.sum(jnp.exp(sims - sim_top), axis=1, keepdims=True))
    col_part = jnp.sum(jnp.exp(sims - sim_scale), axis=0)
    positive = jnp.sum(jnp.where(matched, sims, 0.0))
    local_loss = jnp.sum(row_lse) - 2.0 * positive
    col_total, loss_total = lax.psum((col_part, local_loss), "fsdp")
    col_lse = sim_scale + jnp.log(col_total)
    loss = (loss_total + jnp.sum(col_lse)) / (2.0 * npairs)
    d_sims = 0.5 * (jnp.exp(sims - row_lse) + jnp.exp(sims - col_lse[None, :])) - jnp.where(
        matched, 1.0, 0.0
    )
    d_sims_low = (d_sims * sim_scale).astype(jnp.bfloat16)
    d_source = project(d_sims_low, all_targets)
    target_part = weight_grad(d_sims_low, own_sources)
    d_target = lax.psum_scatter(target_part, "fsdp", scatter_dimension=0, tiled=True)
    d_unit = jnp.stack([d_source, d_target], axis=1).reshape(count, D)
    (d_cls,) = pool_back(d_unit)
    d_block = out_cotangent.astype(jnp.float32).at[:, 0, :].add(d_cls).reshape(count * LEN, D)
    inner_back, outer_back, ffn_gain_back = (
        lax.all_gather(w_inner, "fsdp", axis=0, tiled=True),
        lax.all_gather(w_outer, "fsdp", axis=0, tiled=True),
        lax.all_gather(gain_ffn, "fsdp", axis=0, tiled=True),
    )
    _, ffn_norm_back = jax.vjp(scaled_norm, resid_ffn, ffn_gain_back.astype(jnp.float32))
    d_resid_ffn, d_ffn_gain = ffn_norm_back(d_block)
    d_ffn_shift = jnp.sum(d_block, axis=0)
    d_branch = d_resid_ffn.astype(jnp.bfloat16)
    d_outer_bias = column_sum(d_branch)
    d_outer_mat = weight_grad(hidden_act, d_branch)
    d_act = project_back(d_branch, outer_back)
    _, gelu_back = jax.vjp(exact_gelu, hidden_pre)
    (d_pre,) = gelu_back(d_act)
    d_hidden = d_pre.astype(jnp.bfloat16)
    d_inner_mat = weight_grad(normed_low, d_hidden)
    d_inner_bias = column_sum(d_hidden)
    d_normed = d_resid_ffn + project_back(d_hidden, inner_back)
    grad_w_inner, grad_b_inner, grad_w_outer, grad_b_outer, grad_gain_ffn, grad_shift_ffn = (
        lax.psum_scatter(d_inner_mat, "fsdp", scatter_dimension=0, tiled=True),
        lax.psum_scatter(d_inner_bias, "fsdp", scatter_dimension=0, tiled=True),
        lax.psum_scatter(d_outer_mat, "fsdp", scatter_dimension=0, tiled=True),
        lax.psum_scatter(d_outer_bias, "fsdp", scatter_dimension=0, tiled=True),
        lax.psum_scatter(d_ffn_gain, "fsdp", scatter_dimension=0, tiled=True),
        lax.psum_scatter(d_ffn_shift, "fsdp", scatter_dimension=0, tiled=True),
    )
    query_back, key_back, value_back, output_back, attn_gain_back = (
        lax.all_gather(w_query, "fsdp", axis=0, tiled=True),
        lax.all_gather(w_key, "fsdp", axis=0, tiled=True),
        lax.all_gather(w_value, "fsdp", axis=0, tiled=True),
        lax.all_gather(w_output, "fsdp", axis=0, tiled=True),
        lax.all_gather(gain_attn, "fsdp", axis=0, tiled=True),
    )
    _, attn_norm_back = jax.vjp(scaled_norm, resid_attn, attn_gain_back.astype(jnp.float32))
    d_resid_attn, d_attn_gain = attn_norm_back(d_normed)
    d_attn_shift = jnp.sum(d_normed, axis=0)
    d_attn_out = d_resid_attn.astype(jnp.bfloat16)
    d_output_bias = column_sum(d_attn_out)
    d_output_mat = weight_grad(context, d_attn_out)
    d_context = project_back(d_attn_out, output_back).astype(jnp.bfloat16).reshape(shape_four)
    probs_again = jnp.exp(scores_of(queries, key_rows, visible) - score_lse)
    d_probs = jnp.einsum(
        "bqhd,bkhd->bhqk", d_context, value_rows, preferred_element_type=jnp.float32
    )
    d_values = jnp.einsum(
        "bhqk,bqhd->bkhd",
        probs_again.astype(jnp.bfloat16),
        d_context,
        preferred_element_type=jnp.float32,
    )
    d_values = d_values.astype(jnp.bfloat16).reshape(count * LEN, D)
    d_scores = (
        probs_again * (d_probs - jnp.sum(probs_again * d_probs, axis=-1, keepdims=True))
    ).astype(jnp.bfloat16)
    d_queries = jnp.einsum(
        "bhqk,bkhd->bqhd", d_scores, key_rows, preferred_element_type=jnp.float32
    ) * HEAD_DIM ** (-0.5)
    d_queries = d_queries.astype(jnp.bfloat16).reshape(count * LEN, D)
    d_keys = jnp.einsum(
        "bhqk,bqhd->bkhd", d_scores, queries, preferred_element_type=jnp.float32
    ) * HEAD_DIM ** (-0.5)
    d_keys = d_keys.astype(jnp.bfloat16).reshape(count * LEN, D)
    d_query_mat = weight_grad(token_rows, d_queries)
    d_key_mat = weight_grad(token_rows, d_keys)
    d_value_mat = weight_grad(token_rows, d_values)
    d_query_bias = column_sum(d_queries)
    d_value_bias = column_sum(d_values)
    grad_rows = (
        d_resid_attn
        + project_back(d_queries, query_back)
        + project_back(d_keys, key_back)
        + project_back(d_values, value_back)
    )
    (
        grad_w_query,
        grad_w_key,
        grad_w_value,
        grad_w_output,
        grad_b_query,
        grad_b_value,
        grad_b_output,
        grad_gain_attn,
        grad_shift_attn,
    ) = (
        lax.psum_scatter(d_query_mat, "fsdp", scatter_dimension=0, tiled=True),
        lax.psum_scatter(d_key_mat, "fsdp", scatter_dimension=0, tiled=True),
        lax.psum_scatter(d_value_mat, "fsdp", scatter_dimension=0, tiled=True),
        lax.psum_scatter(d_output_mat, "fsdp", scatter_dimension=0, tiled=True),
        lax.psum_scatter(d_query_bias, "fsdp", scatter_dimension=0, tiled=True),
        lax.psum_scatter(d_value_bias, "fsdp", scatter_dimension=0, tiled=True),
        lax.psum_scatter(d_output_bias, "fsdp", scatter_dimension=0, tiled=True),
        lax.psum_scatter(d_attn_gain, "fsdp", scatter_dimension=0, tiled=True),
        lax.psum_scatter(d_attn_shift, "fsdp", scatter_dimension=0, tiled=True),
    )
    return (
        loss,
        block_out,
        grad_rows.reshape(count, LEN, D),
        grad_w_query,
        grad_w_key,
        grad_w_value,
        grad_w_output,
        grad_b_query,
        grad_b_value,
        grad_b_output,
        grad_gain_attn,
        grad_shift_attn,
        grad_w_inner,
        grad_b_inner,
        grad_w_outer,
        grad_b_outer,
        grad_gain_ffn,
        grad_shift_ffn,
    )


def solution(mesh):
    in_specs = (
        P("fsdp", None, None),
        P("fsdp"),
        P("fsdp"),
        P("fsdp", None, None),
        P("fsdp", None),
        P("fsdp", None),
        P("fsdp", None),
        P("fsdp", None),
        P("fsdp"),
        P("fsdp"),
        P("fsdp"),
        P("fsdp"),
        P("fsdp"),
        P("fsdp", None),
        P("fsdp"),
        P("fsdp", None),
        P("fsdp"),
        P("fsdp"),
        P("fsdp"),
    )
    out_specs = (
        P(),
        P("fsdp", None, None),
        P("fsdp", None, None),
        P("fsdp", None),
        P("fsdp", None),
        P("fsdp", None),
        P("fsdp", None),
        P("fsdp"),
        P("fsdp"),
        P("fsdp"),
        P("fsdp"),
        P("fsdp"),
        P("fsdp", None),
        P("fsdp"),
        P("fsdp", None),
        P("fsdp"),
        P("fsdp"),
        P("fsdp"),
    )
    return jax.shard_map(local, mesh=mesh, in_specs=in_specs, out_specs=out_specs, check_vma=False)
```

profile of v0, /device:TPU:0, one launch (start us, length us, event | category | flops | bytes accessed | tf_op | source)
XLA Modules:
  0.0 1316.7 jit_solution(8292508203558177508)
XLA Ops:
  19.5 42.6 %all-reduce.19 = (bf16[768]{0:T(1024)(128)(2,1)S(1)}, bf16[768]{0:T(1024)(128)(2,1)S(1)}, bf16[768]{0:T(1024)(128)(2,1)S(1)}, bf16[768]{0:T(1024)(128)(2,1)S(1)}...) all-reduce(bf16[768]{0:T(1024)(128)(2,1)S(1)} %dynamic-update-slice, ...), channel_id=1, replica_groups=mesh['fsdp'=32] {'fsdp'}, use_global_device_ids=true, to_apply=%add.1 | all-reduce | flops 9216 | bytes 36864
  62.2 5.6 all-gather.11.cloned.1.call-done
  67.8 3.1 convolution_convert_fusion.1
  70.9 3.9 reshape.305
  74.8 48.9 %all-gather.7.cloned.1.call-done = bf16[768,768]{1,0:T(8,128)(2,1)} async-done(((bf16[24,768]{1,0:T(8,128)(2,1)}), bf16[768,768]{1,0:T(8,128)(2,1)}) %all-gather.7.cloned.1.call-update) | async-done | bytes 1179664 | tf_op jit(solution)/shard_map/all_gather | solution.py:87
  123.7 2.7 add_convert_fusion.2
  126.4 3.9 reshape.307
  130.2 49.4 %all-gather.9.cloned.1.call-done = bf16[768,768]{1,0:T(8,128)(2,1)} async-done(((bf16[24,768]{1,0:T(8,128)(2,1)}), bf16[768,768]{1,0:T(8,128)(2,1)}) %all-gather.9.cloned.1.call-update) | async-done | bytes 1179664 | tf_op jit(solution)/shard_map/all_gather | solution.py:85
  179.6 2.7 add_convert_fusion.1
  182.3 3.9 reshape.308
  186.2 6.4 copy.101
  192.6 4.7 fusion.50
  197.4 1.9 fusion.6
  201.9 2.1 convert_bitcast_fusion.1
  204.0 2.4 copy.88
  206.5 3.2 reshape.269
  209.7 25.7 %all-gather.13.cloned.1.call-done = bf16[768,768]{1,0:T(8,128)(2,1)} async-done(((bf16[24,768]{1,0:T(8,128)(2,1)}), bf16[768,768]{1,0:T(8,128)(2,1)}) %all-gather.13.cloned.1.call-update) | async-done | bytes 1179664 | tf_op jit(solution)/shard_map/all_gather | solution.py:88
  235.4 3.8 fusion.51
  239.8 61.0 %all-gather.15.cloned.1.call-done = bf16[768,3072]{1,0:T(8,128)(2,1)} async-done(((bf16[24,3072]{1,0:T(8,128)(2,1)}), bf16[768,3072]{1,0:T(8,128)(2,1)}) %all-gather.15.cloned.1.call-update) | async-done | bytes 4718608 | tf_op jit(solution)/shard_map/all_gather | solution.py:127
  300.8 35.8 %multiply_convert_fusion = (bf16[1024,3072]{1,0:T(8,128)(2,1)}, f32[1024,3072]{1,0:T(8,128)}, f32[1024,3072]{1,0:T(8,128)}) fusion(f32[3072]{0:T(1024)S(1)} %convert_element_type.137, bf16[768,3072]{1,0:T(8,128)(2,1)} %all-gather.15.cloned.1.call-done, f32[1024,768]{1,0:T(8,128)S(1)} %get-tuple-element.132, f32[768]{0:T(1024)S(1)} %convert_element_type.135, ...), kind=kOutput, calls=%fused_computation.4 | convolution fusion | flops 5043388416 | bytes 39348224 | tf_op jit(solution)/shard_map/dot_general | solution.py:19
  336.6 29.4 %all-gather.17.cloned.1.call-done = bf16[3072,768]{1,0:T(8,128)(2,1)} async-done(((bf16[96,768]{1,0:T(8,128)(2,1)}), bf16[3072,768]{1,0:T(8,128)(2,1)}) %all-gather.17.cloned.1.call-update) | async-done | bytes 4718608 | tf_op jit(solution)/shard_map/all_gather | solution.py:129
  366.0 9.5 fusion.52
  376.0 2.8 fusion.44
  379.3 1.8 fusion.48
  381.4 44.2 %all_gather.71 = bf16[512,768]{1,0:T(8,128)(2,1)} all-gather(bf16[16,768]{1,0:T(8,128)(2,1)S(1)} %fusion.29), channel_id=1, replica_groups=mesh['fsdp'=32] {'fsdp'}, dimensions={0}, use_global_device_ids=true | all-gather | bytes 811008 | tf_op jit(solution)/shard_map/all_gather | solution.py:144
  425.6 2.8 reshape.271
  428.5 2.0 slice.38
  432.5 36.8 %psum.15 = f32[256]{0:T(256)S(1)} all-reduce(f32[256]{0:T(256)S(1)} %get-tuple-element.89), channel_id=1, replica_groups=mesh['fsdp'=32] {'fsdp'}, use_global_device_ids=true, to_apply=%region_13.14 | all-reduce | flops 256 | bytes 2048 | tf_op jit(solution)/shard_map/psum | solution.py:158
  471.9 4.1 copy_convert_fusion
  476.1 91.7 %reduce-scatter.14.cloned.1.call-done = f32[8,768]{1,0:T(8,128)} async-done(((f32[256,768]{1,0:T(8,128)}), f32[8,768]{1,0:T(8,128)}) %reduce-scatter.14.cloned.1.call-update) | async-done | bytes 24592 | tf_op jit(solution)/shard_map/reduce_scatter | solution.py:167
  570.4 3.7 copy.94
  575.0 2.0 fusion.46
  579.2 18.3 %convert_reduce_fusion = (f32[3072]{0:T(1024)S(1)}, bf16[1024,3072]{1,0:T(8,128)(2,1)}) fusion(f32[1024,3072]{1,0:T(8,128)} %get-tuple-element.126, bf16[1024,768]{1,0:T(8,128)(2,1)} %get-tuple-element.114, bf16[3072,768]{1,0:T(8,128)(2,1)} %all-gather.17.cloned.1.call-done, f32[1024,3072]{1,0:T(8,128)} %get-tuple-element.133, ...), kind=kOutput, calls=%fused_computation.2 | convolution fusion | flops 4885312512 | bytes 37773312 | tf_op jit(solution)/shard_map/dot_general | solution.py:23
  597.5 9.6 multiply_reduce_fusion.1
  611.2 2.8 fusion.56
  614.2 2.6 convolution_convert_fusion
  616.7 6.2 reshape.306
  622.9 10.5 multiply_reduce_fusion
  633.5 4.9 multiply_convert_fusion.3
  640.0 3.5 fusion.11
  643.5 4.2 copy.104
  647.8 3.2 reshape.278
  650.9 4.7 convolution_bitcast_fusion.1
  655.6 3.2 copy.116
  658.9 5.7 convert_reduce_fusion.2
  664.6 4.4 copy.100
  669.0 3.2 reshape.277
  672.2 3.3 convolution_bitcast_fusion.2
  675.5 2.0 copy.114
  677.6 7.7 convert_reduce_fusion.1
  685.2 4.2 copy.106
  689.5 3.2 reshape.279
  692.7 4.7 convolution_bitcast_fusion
  697.3 3.2 copy.118
  700.7 10.7 fusion.40
  712.7 10.4 fusion.57
  725.4 40.8 %all-reduce.18 = (f32[]{:T(128)}, f32[768]{0:T(1024)S(1)}, f32[768]{0:T(1024)S(1)}, f32[768]{0:T(1024)S(1)}, f32[768]{0:T(1024)S(1)}, /*index=5*/f32[768]{0:T(10...) all-reduce(f32[]{:T(128)S(6)} %sub.93, ...), channel_id=1, replica_groups=mesh['fsdp'=32] {'fsdp'}, use_global_device_ids=true, to_apply=%region_11.12 | all-reduce | flops 9217 | bytes 73736 | tf_op jit(solution)/shard_map/psum | solution.py:158
  772.8 3.4 fusion.55
  779.0 3.6 add_add_fusion.2
  782.5 34.5 %reduce-scatter.24.cloned.1.call-done = f32[24,768]{1,0:T(8,128)} async-done(((f32[768,768]{1,0:T(8,128)}), f32[24,768]{1,0:T(8,128)}) %reduce-scatter.24.cloned.1.call-update) | async-done | bytes 73744
  817.1 103.8 %reduce-scatter.22.cloned.1.call-done = f32[24,768]{1,0:T(8,128)} async-done(((f32[768,768]{1,0:T(8,128)}), f32[24,768]{1,0:T(8,128)}) %reduce-scatter.22.cloned.1.call-update) | async-done | bytes 73744
  920.8 104.8 %reduce-scatter.26.cloned.1.call-done = f32[24,768]{1,0:T(8,128)} async-done(((f32[768,768]{1,0:T(8,128)}), f32[24,768]{1,0:T(8,128)}) %reduce-scatter.26.cloned.1.call-update) | async-done | bytes 73744
  1025.6 140.9 %reduce-scatter.18.cloned.1.call-done = f32[24,3072]{1,0:T(8,128)} async-done(((f32[768,3072]{1,0:T(8,128)}), f32[24,3072]{1,0:T(8,128)}) %reduce-scatter.18.cloned.1.call-update) | async-done | bytes 294928 | tf_op jit(solution)/shard_map/reduce_scatter | solution.py:190
  1166.5 142.1 %reduce-scatter.20.cloned.1.call-done = f32[96,768]{1,0:T(8,128)} async-done(((f32[3072,768]{1,0:T(8,128)}), f32[96,768]{1,0:T(8,128)}) %reduce-scatter.20.cloned.1.call-update) | async-done | bytes 294928 | tf_op jit(solution)/shard_map/reduce_scatter | solution.py:192
  (170 shorter events, 43.0 us)
Async XLA Ops:
  7.2 60.6 %all-gather.11.cloned.1.call-start = ((), (), s32[]{:S(2)}) async-start(), calls=%async_computation.9 | async-start | bytes 1216512 | tf_op jit(solution)/shard_map/all_gather | solution.py:86
  7.9 115.8 %all-gather.7.cloned.1.call-start = ((), (), s32[]{:S(2)}) async-start(), calls=%async_computation.7 | async-start | bytes 1216512 | tf_op jit(solution)/shard_map/all_gather | solution.py:87
  8.7 171.0 %all-gather.9.cloned.1.call-start = ((), (), s32[]{:S(2)}) async-start(), calls=%async_computation.8 | async-start | bytes 1216512 | tf_op jit(solution)/shard_map/all_gather | solution.py:85
  9.4 226.0 %all-gather.13.cloned.1.call-start = ((), (), s32[]{:S(2)}) async-start(), calls=%async_computation.10 | async-start | bytes 1216512 | tf_op jit(solution)/shard_map/all_gather | solution.py:88
  10.0 290.8 %all-gather.15.cloned.1.call-start = ((), (), s32[]{:S(2)}) async-start(), calls=%async_computation.11 | async-start | bytes 4866048 | tf_op jit(solution)/shard_map/all_gather | solution.py:127
  10.6 355.4 %all-gather.17.cloned.1.call-start = ((), (), s32[]{:S(2)}) async-start(), calls=%async_computation.12 | async-start | bytes 4866048 | tf_op jit(solution)/shard_map/all_gather | solution.py:129
  11.1 556.7 %reduce-scatter.14.cloned.1.call-start = ((), (), s32[]{:S(2)}) async-start(), calls=%async_computation.13 | async-start | bytes 811008 | tf_op jit(solution)/shard_map/reduce_scatter | solution.py:167
  70.9 52.8 %copy-start.28 = (bf16[16,64,768]{2,1,0:T(8,128)(2,1)S(1)}, bf16[16,64,768]{2,1,0:T(8,128)(2,1)}, u32[]{:S(2)}) copy-start(bf16[16,64,768]{2,1,0:T(8,128)(2,1)} %param.21) | copy-start | bytes 4718596
  192.6 4.7 copy-start.5
  197.3 3.2 copy-start
  197.3 3.2 copy-start.18
  197.4 4.5 copy-start.9
  201.9 2.1 copy-start.23
  239.2 97.3 %copy-start.1 = (f32[1024,768]{1,0:T(8,128)}, f32[1024,768]{1,0:T(8,128)S(1)}, u32[]{:S(2)}) copy-start(f32[1024,768]{1,0:T(8,128)S(1)} %get-tuple-element.132) | copy-start | bytes 9437188
  239.8 96.8 %copy-start.25 = (f32[1024]{0:T(1024)}, f32[1024]{0:T(1024)S(1)}, u32[]{:S(2)}) copy-start(f32[1024]{0:T(1024)S(1)} %multiply_reduce_fusion.5) | copy-start | bytes 12292
  378.8 52.6 %copy-start.27 = (s32[8]{0:T(128)S(1)}, s32[8]{0:T(128)}, u32[]{:S(2)}) copy-start(s32[8]{0:T(128)} %param.23) | copy-start | bytes 100
  430.5 0.9 copy-start.21
  471.8 310.7 %reduce-scatter.16.cloned.1.call-start = ((), (), s32[]{:S(2)}) async-start(), calls=%async_computation.14 | async-start | bytes 2433024 | tf_op jit(solution)/shard_map/reduce_scatter | solution.py:258
  471.9 4.1 copy-start.22
  577.0 2.1 copy-start.10
  579.2 18.3 %copy-start.2 = (f32[1024,768]{1,0:T(8,128)S(1)}, f32[1024,768]{1,0:T(8,128)}, u32[]{:S(2)}) copy-start(f32[1024,768]{1,0:T(8,128)} %copy-done.1) | copy-start | bytes 9437188
  579.2 18.3 %copy-start.11 = (f32[1024,768]{1,0:T(8,128)S(1)}, f32[1024,768]{1,0:T(8,128)}, u32[]{:S(2)}) copy-start(f32[1024,768]{1,0:T(8,128)} %copy-done.10) | copy-start | bytes 9437188
  597.5 9.6 copy-start.26
  608.7 1.6 copy-start.7
  608.7 2.5 copy-start.15
  611.2 2.9 copy-start.19
  611.2 2.9 copy-start.24
  611.2 2.9 copy-start.30
  614.1 203.0 %reduce-scatter.24.cloned.1.call-start = ((), (), s32[]{:S(2)}) async-start(), calls=%async_computation.18 | async-start | bytes 2433024
  616.7 16.7 %slice-start = ((s8[6291456]{0:T(1024)(128)(4,1)}), s8[2097152]{0:T(1024)(128)(4,1)S(1)}, s32[]{:S(2)}) async-start(s8[6291456]{0:T(1024)(128)(4,1)} %bitcast.113), calls=%async_computation.20 | async-start | bytes 4194304
  622.9 10.5 slice-start.1
  633.5 6.6 copy-start.6
  638.3 1.7 copy-start.12
  655.6 3.3 copy-start.13
  658.8 262.0 %reduce-scatter.22.cloned.1.call-start = ((), (), s32[]{:S(2)}) async-start(), calls=%async_computation.17 | async-start | bytes 2433024
  677.5 348.1 %reduce-scatter.26.cloned.1.call-start = ((), (), s32[]{:S(2)}) async-start(), calls=%async_computation.19 | async-start | bytes 2433024
  697.3 3.3 copy-start.3
  700.6 465.9 %reduce-scatter.18.cloned.1.call-start = ((), (), s32[]{:S(2)}) async-start(), calls=%async_computation.15 | async-start | bytes 9732096 | tf_op jit(solution)/shard_map/reduce_scatter | solution.py:190
  711.3 1.4 copy-start.17
  711.3 597.3 %reduce-scatter.20.cloned.1.call-start = ((), (), s32[]{:S(2)}) async-start(), calls=%async_computation.16 | async-start | bytes 9732096 | tf_op jit(solution)/shard_map/reduce_scatter | solution.py:192
  723.1 1.9 copy-start.4
  772.8 3.4 copy-start.16
  772.8 3.4 copy-start.29
  776.2 1.9 copy-start.8
  776.2 2.4 copy-start.14
  776.2 2.8 copy-start.20
Sparse Core Ops, SparseCore 0:
  10.9 56.8 all-gather.10
  70.7 53.0 all-gather.6
  126.6 52.9 all-gather.8
  182.4 52.9 all-gather.12
  238.1 62.5 all-gather.14
  303.5 62.4 all-gather.16
  471.9 95.8 reduce-scatter.13
  614.2 98.0 reduce-scatter.15
  719.0 98.0 reduce-scatter.23
  822.8 97.9 reduce-scatter.21
  927.5 98.0 reduce-scatter.25
  1031.9 134.4 reduce-scatter.17
  1174.0 134.5 reduce-scatter.19
where the time goes:
time: 1330 us; the launch traced here: 1320 us
  waiting for transfers between devices  842 us (63%)
  matrix products  169 us (13%)
  blocking collectives  164 us (12%)
  local copies, waits for them, and re-layouts  95.3 us (7%)
  other arithmetic  26.8 us (2%)
  between operations  19 us (1%)
    unnamed x16, waiting for transfers between devices  247 us
    reduce_scatter x1, waiting for transfers between devices, local(): lax.psum_scatter(d_outer_mat, 'fsdp', scatter_dimension=0, tiled=True)  142 us
    reduce_scatter x1, waiting for transfers between devices, local(): lax.psum_scatter(d_inner_mat, 'fsdp', scatter_dimension=0, tiled=True)  141 us
    reduce_scatter x1, waiting for transfers between devices, local(): lax.psum_scatter(target_part, 'fsdp', scatter_dimension=0, tiled=True)  91.7 us
    psum x2, blocking collectives, local(): col_total, loss_total = lax.psum((col_part, local_loss), 'fsdp')  77.6 us
    all_gather x1, waiting for transfers between devices, local(): lax.all_gather(w_inner, 'fsdp', axis=0, tiled=True)  61 us
    dot_general x7, matrix products, project(): return jnp.dot(rows, weight, preferred_element_type=jnp.float32)  57.8 us
    all_gather x1, waiting for transfers between devices, local(): lax.all_gather(w_query, 'fsdp', axis=0, tiled=True)  49.4 us
  transfers between devices with their start and end apart: 13, of which 12 were waited for; matrix products, arithmetic and copies ran while one was open for 16% of the time, Pallas kernels for 0%

commit v1 on v0

v1 whole, which is shorter than its diff:
```python
import jax
import jax.numpy as jnp
from jax import lax
from jax.sharding import PartitionSpec as P

D = 768
HEADS = 12
HEAD_DIM = 64
LEN = 64
HALF = D // 2

norm_eps = 1e-12
pool_eps = 1e-06
sim_scale = 50.0
sim_margin = 0.3

AXIS = "fsdp"
CUBE = 32
CORE = [(i, i ^ 1) for i in range(CUBE)]
FAR_Z = [(i, i ^ 16) for i in range(CUBE)]
NEAR_Z = [(i, i ^ 8) for i in range(CUBE)]
FIRST = [(i, i ^ (4 if i & 1 else 2)) for i in range(CUBE)]
SECOND = [(i, i ^ (2 if i & 1 else 4)) for i in range(CUBE)]


def project(rows, weight):
    return jnp.dot(rows, weight, preferred_element_type=jnp.float32)


def project_back(grad, weight):
    return lax.dot_general(
        grad, weight, (((1,), (1,)), ((), ())), preferred_element_type=jnp.float32
    )


def weight_grad(rows, grad):
    return lax.dot_general(rows, grad, (((0,), (0,)), ((), ())), preferred_element_type=jnp.float32)


def scaled_norm(field, gain_vec):
    centred = field - jnp.mean(field, axis=-1, keepdims=True)
    variance = jnp.mean(centred * centred, axis=-1, keepdims=True)
    return centred * lax.rsqrt(variance + norm_eps) * gain_vec


def exact_gelu(field):
    return jax.nn.gelu(field, approximate=False)


def normalize(field):
    return field * lax.rsqrt(jnp.sum(field * field, axis=-1, keepdims=True) + pool_eps)


def scores_of(queries, key_rows, visible):
    raw = jnp.einsum(
        "bqhd,bkhd->bhqk", queries, key_rows, preferred_element_type=jnp.float32
    ) * HEAD_DIM ** (-0.5)
    return jnp.where(visible, raw, -1e30)


def column_sum(field):
    return jnp.sum(field.astype(jnp.float32), axis=0)


class Place:
    def __init__(self):
        me = lax.axis_index(AXIS)
        self.core = me & 1
        x, y = (me >> 1) & 1, (me >> 2) & 1
        self.near_z, self.far_z = (me >> 3) & 1, (me >> 4) & 1
        self.first = jnp.where(self.core == 0, x, y)
        self.second = jnp.where(self.core == 0, y, x)


def join(own, other, axis, bit):
    shape = own.shape[:axis] + (2,) + own.shape[axis:]
    where = lax.broadcasted_iota(jnp.int32, shape, axis)
    return jnp.where(where == bit, jnp.expand_dims(own, axis), jnp.expand_dims(other, axis))


def pick(field, axis, bit):
    return lax.dynamic_index_in_dim(field, bit, axis, keepdims=False)


def send(field, route):
    return lax.ppermute(field, AXIS, route)


def spread(block, place):
    block = join(block, send(block, FAR_Z), 0, place.far_z)
    block = join(block, send(block, NEAR_Z), 1, place.near_z)
    block = join(block, send(block, FIRST), 2, place.first)
    return join(block, send(block, SECOND), 3, place.second)


def cores(block, place):
    other = send(block, CORE)
    zero = jnp.where(place.core == 0, block, other)
    one = jnp.where(place.core == 0, other, block)
    return jnp.swapaxes(zero, 2, 3), one


def gather_rows(pieces, place):
    joined = []
    for piece in pieces:
        halves = piece.reshape(piece.shape[0], piece.shape[1], 2, HALF)
        joined.append((pick(halves, 2, place.core), pick(halves, 2, 1 - place.core)))
    away = jnp.concatenate([b.reshape(-1, HALF) for _, b in joined], axis=0)
    came = send(away, CORE)
    rows, at = [], 0
    for own, _ in joined:
        count = own.shape[0] * own.shape[1]
        other = came[at : at + count].reshape(own.shape)
        rows.append(join(own, other, 1, place.core).reshape(-1, HALF))
        at += count
    zero, one = cores(spread(jnp.concatenate(rows, axis=0), place), place)
    out, at = [], 0
    chips = CUBE // 2
    for piece in pieces:
        m, r, _ = piece.shape
        count = 2 * m * r
        both = jnp.concatenate(
            [part[..., at : at + count, :].reshape(chips, m, 2 * r, HALF) for part in (zero, one)],
            axis=-1,
        )
        out.append(jnp.swapaxes(both, 0, 1))
        at += count
    return out


def scatter_rows(pieces, place):
    chips = CUBE // 2
    whole = jnp.concatenate(
        [jnp.swapaxes(p, 0, 1).reshape(chips, -1, D) for p in pieces], axis=1
    )
    whole = whole.reshape(2, 2, 2, 2, whole.shape[1], D)
    zero = jnp.swapaxes(whole[..., :HALF], 2, 3)
    one = whole[..., HALF:]
    keep = jnp.where(place.core == 0, zero, one)
    away = jnp.where(place.core == 0, one, zero).astype(jnp.bfloat16)
    total = keep + send(away, CORE).astype(jnp.float32)
    for axis, bit, route in (
        (2, place.first, FIRST),
        (2, place.second, SECOND),
        (1, place.near_z, NEAR_Z),
        (0, place.far_z, FAR_Z),
    ):
        away = pick(total, axis, 1 - bit).astype(jnp.bfloat16)
        total = pick(total, axis, bit) + send(away, route).astype(jnp.float32)
    own, other, at = [], [], 0
    for p in pieces:
        m, _, r2, _ = p.shape
        part = total[at : at + m * r2].reshape(m, 2, r2 // 2, HALF)
        own.append(pick(part, 1, place.core).reshape(-1, HALF))
        other.append(pick(part, 1, 1 - place.core).reshape(-1, HALF))
        at += m * r2
    own = jnp.concatenate(own, axis=0)
    came = send(jnp.concatenate(other, axis=0), CORE)
    both = jnp.swapaxes(join(own, came, 0, place.core), 0, 1).reshape(-1, D)
    out, at = [], 0
    for p in pieces:
        m, _, r2, _ = p.shape
        count = m * (r2 // 2)
        out.append(both[at : at + count].reshape(m, r2 // 2, D))
        at += count
    return out


def gather_units(unit_low, place):
    zero, one = cores(spread(unit_low, place), place)
    return jnp.stack([zero, one], axis=4).reshape(-1, D)


def pad_row(parts):
    row = jnp.concatenate(parts)
    return jnp.pad(row, (0, 8 * D - row.shape[0])).reshape(1, 8, D)


def cube_gather(weights, vectors, partners, place):
    w_query, w_key, w_value, w_output, w_inner, w_outer = weights
    r = w_query.shape[0]
    low = jnp.bfloat16
    codes = [(partners % 64).astype(low), (partners // 64).astype(low)]
    row = pad_row(list(vectors) + codes)
    attn, rows = gather_rows([jnp.stack([w_query, w_key, w_value, w_output]), row], place)
    (inner,) = gather_rows([jnp.swapaxes(w_inner.reshape(r, 4, D), 0, 1)], place)
    (outer,) = gather_rows([w_outer[None]], place)
    attn = attn.reshape(4, D, D)
    inner = jnp.swapaxes(inner.reshape(4, D, D), 0, 1).reshape(D, 4 * D)
    outer = outer.reshape(4 * D, D)
    rows = rows.reshape(CUBE, 8 * D)
    full, at = [], 0
    for v in list(vectors):
        full.append(rows[:, at : at + v.shape[0]].reshape(-1))
        at += v.shape[0]
    count = partners.shape[0]
    low_code = rows[:, at : at + count].astype(jnp.int32).reshape(-1)
    high_code = rows[:, at + count : at + 2 * count].astype(jnp.int32).reshape(-1)
    return (attn[0], attn[1], attn[2], attn[3], inner, outer), full, low_code + 64 * high_code


def cut_rows(full):
    return full.reshape(1, CUBE // 2, -1, D)


def vector_rows(vectors):
    rows = jnp.concatenate([v.reshape(CUBE, -1) for v in vectors], axis=1)
    rows = jnp.pad(rows, ((0, 0), (0, 8 * D - rows.shape[1])))
    return rows.reshape(1, CUBE // 2, 16, D)


def own_vectors(row, vectors):
    row, out, at = row.reshape(-1), [], 0
    for v in vectors:
        count = v.shape[0] // CUBE
        out.append(row[at : at + count])
        at += count
    return out


def local(
    tokens,
    lengths,
    partners,
    out_cotangent,
    w_query,
    w_key,
    w_value,
    w_output,
    b_query,
    b_value,
    b_output,
    gain_attn,
    shift_attn,
    w_inner,
    b_inner,
    w_outer,
    b_outer,
    gain_ffn,
    shift_ffn,
):
    devices = lax.axis_size(AXIS)
    cube = devices == CUBE
    place = Place() if cube else None
    count = tokens.shape[0]
    half = count // 2
    shape_four = (count, LEN, HEADS, HEAD_DIM)
    token_rows = tokens.reshape(count * LEN, D)
    positions = jnp.arange(LEN, dtype=jnp.int32)
    visible = (positions[None, :] < lengths[:, None])[:, None, None, :]
    weights = (w_query, w_key, w_value, w_output, w_inner, w_outer)
    vectors = (b_query, b_value, b_output, gain_attn, shift_attn, b_inner, b_outer, gain_ffn, shift_ffn)
    if cube:
        full, vec, all_partners = cube_gather(weights, vectors, partners, place)
    else:
        full, vec, all_partners = jax.tree.map(
            lambda v: lax.all_gather(v, AXIS, axis=0, tiled=True), (weights, vectors, partners)
        )
    query_mat, key_mat, value_mat, output_mat, inner_mat, outer_mat = full
    (
        query_bias,
        value_bias,
        output_bias,
        attn_gain,
        attn_shift,
        inner_bias,
        outer_bias,
        ffn_gain,
        ffn_shift,
    ) = vec
    queries = (project(token_rows, query_mat) + query_bias).astype(jnp.bfloat16).reshape(shape_four)
    key_rows = project(token_rows, key_mat).astype(jnp.bfloat16).reshape(shape_four)
    value_rows = (
        (project(token_rows, value_mat) + value_bias).astype(jnp.bfloat16).reshape(shape_four)
    )
    scores = scores_of(queries, key_rows, visible)
    row_top = jnp.max(scores, axis=-1, keepdims=True)
    expd = jnp.exp(scores - row_top)
    row_total = jnp.sum(expd, axis=-1, keepdims=True)
    probs = expd / row_total
    score_lse = row_top + jnp.log(row_total)
    context = jnp.einsum(
        "bhqk,bkhd->bqhd",
        probs.astype(jnp.bfloat16),
        value_rows,
        preferred_element_type=jnp.float32,
    )
    context = context.astype(jnp.bfloat16).reshape(count * LEN, D)
    resid_attn = token_rows.astype(jnp.float32) + (project(context, output_mat) + output_bias)
    normed_attn = scaled_norm(resid_attn, attn_gain.astype(jnp.float32)) + attn_shift
    normed_low = normed_attn.astype(jnp.bfloat16)
    hidden_pre = project(normed_low, inner_mat) + inner_bias
    hidden_act = exact_gelu(hidden_pre).astype(jnp.bfloat16)
    resid_ffn = normed_attn + (project(hidden_act, outer_mat) + outer_bias)
    block_rows = scaled_norm(resid_ffn, ffn_gain.astype(jnp.float32)) + ffn_shift
    block_out = block_rows.astype(jnp.bfloat16).reshape(count, LEN, D)
    cls_rows = block_rows.reshape(count, LEN, D)[:, 0, :]
    unit, pool_back = jax.vjp(normalize, cls_rows)
    unit_low = unit.astype(jnp.bfloat16)
    if cube:
        every_unit = gather_units(unit_low, place)
    else:
        every_unit = lax.all_gather(unit_low, AXIS, axis=0, tiled=True)
    every_pair = every_unit.reshape(every_unit.shape[0] // 2, 2, D)
    all_sources = every_pair[:, 0, :]
    all_targets = every_pair[:, 1, :]
    npairs = all_targets.shape[0]
    sims = project_back(all_sources, all_targets) * sim_scale
    matched = all_partners[:, None] == jnp.arange(npairs, dtype=jnp.int32)[None, :]
    sims = sims - jnp.where(matched, sim_scale * sim_margin, 0.0)
    row_top = jnp.max(sims, axis=1, keepdims=True)
    row_lse = row_top + jnp.log(jnp.sum(jnp.exp(sims - row_top), axis=1, keepdims=True))
    col_top = jnp.max(sims, axis=0, keepdims=True)
    col_lse = col_top + jnp.log(jnp.sum(jnp.exp(sims - col_top), axis=0, keepdims=True))
    positive = jnp.sum(jnp.where(matched, sims, 0.0))
    loss = (jnp.sum(row_lse) + jnp.sum(col_lse) - 2.0 * positive) / (2.0 * npairs)
    d_sims = 0.5 * (jnp.exp(sims - row_lse) + jnp.exp(sims - col_lse)) - jnp.where(
        matched, 1.0, 0.0
    )
    d_sims_low = (d_sims * sim_scale).astype(jnp.bfloat16)
    first = lax.axis_index(AXIS) * half
    d_source = project(lax.dynamic_slice_in_dim(d_sims_low, first, half, 0), all_targets)
    d_target = weight_grad(lax.dynamic_slice_in_dim(d_sims_low, first, half, 1), all_sources)
    d_unit = jnp.stack([d_source, d_target], axis=1).reshape(count, D)
    (d_cls,) = pool_back(d_unit)
    d_block = out_cotangent.astype(jnp.float32).at[:, 0, :].add(d_cls).reshape(count * LEN, D)
    _, ffn_norm_back = jax.vjp(scaled_norm, resid_ffn, ffn_gain.astype(jnp.float32))
    d_resid_ffn, d_ffn_gain = ffn_norm_back(d_block)
    d_ffn_shift = jnp.sum(d_block, axis=0)
    d_branch = d_resid_ffn.astype(jnp.bfloat16)
    d_outer_bias = column_sum(d_branch)
    d_outer_mat = weight_grad(hidden_act, d_branch)
    d_act = project_back(d_branch, outer_mat)
    _, gelu_back = jax.vjp(exact_gelu, hidden_pre)
    (d_pre,) = gelu_back(d_act)
    d_hidden = d_pre.astype(jnp.bfloat16)
    d_inner_mat = weight_grad(normed_low, d_hidden)
    d_inner_bias = column_sum(d_hidden)
    d_normed = d_resid_ffn + project_back(d_hidden, inner_mat)
    if cube:
        ((g_outer,),) = (scatter_rows([cut_rows(d_outer_mat)], place),)
        (g_inner,) = scatter_rows(
            [jnp.swapaxes(d_inner_mat.reshape(D, 4, D), 0, 1).reshape(4, CUBE // 2, -1, D)], place
        )
        grad_w_outer = g_outer[0]
        grad_w_inner = jnp.swapaxes(g_inner, 0, 1).reshape(-1, 4 * D)
    _, attn_norm_back = jax.vjp(scaled_norm, resid_attn, attn_gain.astype(jnp.float32))
    d_resid_attn, d_attn_gain = attn_norm_back(d_normed)
    d_attn_shift = jnp.sum(d_normed, axis=0)
    d_attn_out = d_resid_attn.astype(jnp.bfloat16)
    d_output_bias = column_sum(d_attn_out)
    d_output_mat = weight_grad(context, d_attn_out)
    d_context = project_back(d_attn_out, output_mat).astype(jnp.bfloat16).reshape(shape_four)
    probs_again = jnp.exp(scores_of(queries, key_rows, visible) - score_lse)
    d_probs = jnp.einsum(
        "bqhd,bkhd->bhqk", d_context, value_rows, preferred_element_type=jnp.float32
    )
    d_values = jnp.einsum(
        "bhqk,bqhd->bkhd",
        probs_again.astype(jnp.bfloat16),
        d_context,
        preferred_element_type=jnp.float32,
    )
    d_values = d_values.astype(jnp.bfloat16).reshape(count * LEN, D)
    d_scores = (
        probs_again * (d_probs - jnp.sum(probs_again * d_probs, axis=-1, keepdims=True))
    ).astype(jnp.bfloat16)
    d_queries = jnp.einsum(
        "bhqk,bkhd->bqhd", d_scores, key_rows, preferred_element_type=jnp.float32
    ) * HEAD_DIM ** (-0.5)
    d_queries = d_queries.astype(jnp.bfloat16).reshape(count * LEN, D)
    d_keys = jnp.einsum(
        "bhqk,bqhd->bkhd", d_scores, queries, preferred_element_type=jnp.float32
    ) * HEAD_DIM ** (-0.5)
    d_keys = d_keys.astype(jnp.bfloat16).reshape(count * LEN, D)
    d_query_mat = weight_grad(token_rows, d_queries)
    d_key_mat = weight_grad(token_rows, d_keys)
    d_value_mat = weight_grad(token_rows, d_values)
    d_query_bias = column_sum(d_queries)
    d_value_bias = column_sum(d_values)
    grad_rows = (
        d_resid_attn
        + project_back(d_queries, query_mat)
        + project_back(d_keys, key_mat)
        + project_back(d_values, value_mat)
    )
    d_vectors = (
        d_query_bias,
        d_value_bias,
        d_output_bias,
        d_attn_gain,
        d_attn_shift,
        d_inner_bias,
        d_outer_bias,
        d_ffn_gain,
        d_ffn_shift,
    )
    if cube:
        mats = jnp.stack([d_query_mat, d_key_mat, d_value_mat, d_output_mat])
        g_attn, g_row = scatter_rows(
            [mats.reshape(4, CUBE // 2, -1, D), vector_rows(d_vectors)], place
        )
        grad_w_query, grad_w_key, grad_w_value, grad_w_output = (g_attn[i] for i in range(4))
        grads = own_vectors(g_row, d_vectors)
    else:

        def scatter(v):
            return lax.psum_scatter(v, AXIS, scatter_dimension=0, tiled=True)

        grad_w_query, grad_w_key, grad_w_value, grad_w_output, grad_w_inner, grad_w_outer = (
            scatter(v)
            for v in (d_query_mat, d_key_mat, d_value_mat, d_output_mat, d_inner_mat, d_outer_mat)
        )
        grads = [scatter(v) for v in d_vectors]
    (
        grad_b_query,
        grad_b_value,
        grad_b_output,
        grad_gain_attn,
        grad_shift_attn,
        grad_b_inner,
        grad_b_outer,
        grad_gain_ffn,
        grad_shift_ffn,
    ) = grads
    return (
        loss,
        block_out,
        grad_rows.reshape(count, LEN, D),
        grad_w_query,
        grad_w_key,
        grad_w_value,
        grad_w_output,
        grad_b_query,
        grad_b_value,
        grad_b_output,
        grad_gain_attn,
        grad_shift_attn,
        grad_w_inner,
        grad_b_inner,
        grad_w_outer,
        grad_b_outer,
        grad_gain_ffn,
        grad_shift_ffn,
    )


def solution(mesh):
    rows, cols = P(AXIS), P(AXIS, None)
    cube = P(AXIS, None, None)
    in_specs = (cube, rows, rows, cube) + (cols,) * 4 + (rows,) * 5 + (cols, rows, cols) + (rows,) * 3
    out_specs = (P(), cube, cube) + (cols,) * 4 + (rows,) * 5 + (cols, rows, cols) + (rows,) * 3
    return jax.shard_map(local, mesh=mesh, in_specs=in_specs, out_specs=out_specs, check_vma=False)
```

time: 1330 us -> 570 us (0.43)
  waiting for transfers between devices: 842 us -> 145 us
  blocking collectives: 164 us -> 0 us
  other arithmetic: 26.8 us -> 72.4 us
  starting transfers between devices: 0.52 us -> 45.6 us
  local copies, waits for them, and re-layouts: 95.3 us -> 136 us
    reduce_scatter x4 -> x0, waiting for transfers between devices: 375 us -> none  [the longest x1 142 us: local(): lax.psum_scatter(d_outer_mat, 'fsdp', scatter_dimension=0, tiled=True)]
    unnamed x16 -> x0, waiting for transfers between devices: 247 us -> none
    all_gather x6 -> x0, waiting for transfers between devices: 220 us -> none  [the longest x1 61 us: local(): lax.all_gather(w_inner, 'fsdp', axis=0, tiled=True)]
    ppermute x0 -> x41, waiting for transfers between devices: none -> 145 us  [send(): return lax.ppermute(field, AXIS, route)]
    psum x2 -> x0, blocking collectives: 77.6 us -> none  [local(): col_total, loss_total = lax.psum((col_part, local_loss), 'fsdp')]
    ppermute x0 -> x41, starting transfers between devices: none -> 45.6 us  [send(): return lax.ppermute(field, AXIS, route)]
    all_gather x1 -> x0, blocking collectives: 44.2 us -> none  [local(): every_unit = lax.all_gather(unit_low, 'fsdp', axis=0, tiled=True)]
    unnamed x1 -> x0, blocking collectives: 42.6 us -> none
  transfers between devices with their start and end apart: 13 -> 41, of which waited for: 12 -> 23; matrix products, arithmetic and copies ran while one was open for 16% -> 20% of each run, Pallas kernels for 0% -> 0%
where the time goes in v1:
time: 570 us; the launch traced here: 563 us
  matrix products  158 us (28%)
  waiting for transfers between devices  145 us (25%)
  local copies, waits for them, and re-layouts  136 us (24%)
  other arithmetic  72.4 us (13%)
  starting transfers between devices  45.6 us (8%)
  between operations  5.93 us (1%)
    ppermute x41, waiting for transfers between devices, send(): return lax.ppermute(field, AXIS, route)  145 us
    dot_general x7, matrix products, project(): return jnp.dot(rows, weight, preferred_element_type=jnp.float32)  61.3 us
    ppermute x41, starting transfers between devices, send(): return lax.ppermute(field, AXIS, route)  45.6 us
    dot_general x7, matrix products, project_back(): lax.dot_general(grad, weight, (((1,), (1,)), ((), ())), preferred_element...  37 us
    dot_general x7, matrix products, weight_grad(): lax.dot_general(rows, grad, (((0,), (0,)), ((), ())), preferred_element_t...  35 us
    unnamed x175, local copies, waits for them, and re-layouts  18 us
    add x3, other arithmetic, scatter_rows(): total = keep + send(away, CORE).astype(jnp.float32)  13.1 us
  transfers between devices with their start and end apart: 41, of which 23 were waited for; matrix products, arithmetic and copies ran while one was open for 20% of the time, Pallas kernels for 0%

profile of v1, /device:TPU:0, one launch (start us, length us, event | category | flops | bytes accessed | tf_op | source)
XLA Modules:
  0.0 562.7 jit_solution(13625191876247089967)
XLA Ops:
  4.6 6.1 %concatenate.47 = bf16[304]{0:T(512)(128)(2,1)S(1)} concatenate(bf16[24]{0:T(256)(128)(2,1)} %param.29, bf16[24]{0:T(256)(128)(2,1)} %param.30, bf16[24]{0:T(256)(128)(2,1)} %param.31, bf16[24]{0:T(256)(128)(2,1)} %param.32, bf16[24]{0:T(256)(128)(2,1)} %param.33, bf16[96]{0:T(256)(128)(2,1)} %param.35, bf16[24]{0:T(256)(128)(2,1)} %param.37, bf16[24]{0:T(256)(128)(2,1)} %param.38, ...), dimensions={0} | concatenate | bytes 1216 | tf_op jit(solution)/shard_map/concatenate | solution.py:175
  15.5 3.7 collective-permute-start.13
  20.0 10.1 %collective-permute-done.13 = bf16[192,384]{1,0:T(8,128)(2,1)S(1)} collective-permute-done((bf16[192,384]{1,0:T(8,128)(2,1)S(1)}, bf16[192,384]{1,0:T(8,128)(2,1)S(1)}, u32[]{:S(2)}, u32[]{:S(2)}) %collective-permute-start.13) | collective-permute-done | bytes 147488 | tf_op jit(solution)/shard_map/ppermute | solution.py:86
  30.2 3.0 collective-permute-done.7
  35.6 7.7 %collective-permute-done.14 = bf16[2,192,384]{2,1,0:T(8,128)(2,1)S(1)} collective-permute-done((bf16[2,192,384]{2,1,0:T(8,128)(2,1)S(1)}, bf16[2,192,384]{2,1,0:T(8,128)(2,1)S(1)}, u32[]{:S(2)}, u32[]{:S(2)}) %collective-permute-start.14) | collective-permute-done | bytes 294944 | tf_op jit(solution)/shard_map/ppermute | solution.py:86
  43.2 5.2 collective-permute-done.8
  53.5 6.7 %collective-permute-done.1 = bf16[208,384]{1,0:T(8,128)(2,1)S(1)} collective-permute-done((bf16[208,384]{1,0:T(8,128)(2,1)S(1)}, bf16[208,384]{1,0:T(8,128)(2,1)S(1)}, u32[]{:S(2)}, u32[]{:S(2)}) %collective-permute-start.1) | collective-permute-done | bytes 159776 | tf_op jit(solution)/shard_map/ppermute | solution.py:86
  61.0 3.9 collective-permute-done.9
  70.6 15.8 %collective-permute-done.3 = bf16[2,2,208,384]{3,2,1,0:T(8,128)(2,1)S(1)} collective-permute-done((bf16[2,2,208,384]{3,2,1,0:T(8,128)(2,1)S(1)}, bf16[2,2,208,384]{3,2,1,0:T(8,128)(2,1)S(1)}, u32[]{:S(2)}, u32[]{:S(2)}) %collective-permute-start.3) | collective-permute-done | bytes 639008 | tf_op jit(solution)/shard_map/ppermute | solution.py:86
  89.5 12.6 %collective-permute-done.10 = bf16[2,2,2,192,384]{4,3,2,1,0:T(8,128)(2,1)} collective-permute-done((bf16[2,2,2,192,384]{4,3,2,1,0:T(8,128)(2,1)}, bf16[2,2,2,192,384]{4,3,2,1,0:T(8,128)(2,1)}, u32[]{:S(2)}, u32[]{:S(2)}) %collective-permute-start.10) | collective-permute-done | bytes 1179680 | tf_op jit(solution)/shard_map/ppermute | solution.py:86
  102.1 2.9 broadcast_select_fusion.2
  105.6 10.1 %collective-permute-done.4 = bf16[2,2,2,208,384]{4,3,2,1,0:T(8,128)(2,1)S(1)} collective-permute-done((bf16[2,2,2,208,384]{4,3,2,1,0:T(8,128)(2,1)S(1)}, bf16[2,2,2,208,384]{4,3,2,1,0:T(8,128)(2,1)S(1)}, u32[]{:S(2)}, u32[]{:S(2)}) %collective-permute-start.4) | collective-permute-done | bytes 1277984 | tf_op jit(solution)/shard_map/ppermute | solution.py:86
  124.8 6.8 %copy.141 = bf16[768,4,768]{0,2,1:T(8,128)(2,1)} copy(bf16[768,4,768]{2,0,1:T(8,128)(2,1)} %bitcast.348) | data formatting | bytes 9437184 | tf_op jit(solution)/shard_map/transpose | solution.py:189
  142.6 4.1 fusion.35
  146.7 4.1 reshape.675
  150.8 5.5 fusion.34
  156.3 5.2 reshape.674
  161.6 5.0 copy.151
  166.6 4.3 fusion.33
  171.0 5.2 reshape.676
  176.2 5.0 copy.134
  181.2 4.2 fusion.85
  193.8 3.2 reshape.677
  197.0 4.1 fusion.86
  201.7 37.6 %multiply_convert_fusion = (bf16[1024,3072]{1,0:T(8,128)(2,1)S(1)}, f32[1024,3072]{1,0:T(8,128)}, f32[1024,3072]{1,0:T(8,128)}) fusion(f32[3072]{0:T(1024)S(1)} %reshape.724, bf16[768,3072]{0,1:T(8,128)(2,1)S(1)} %bitcast.362, f32[1024,768]{1,0:T(8,128)S(1)} %get-tuple-element.121, f32[768]{0:T(1024)S(1)} %reshape.723, f32[768]{0:T(1024)S(1)} %reshape.722, ...), kind=kOutput, calls=%fused_computation.4 | convolution fusion | flops 5043388416 | bytes 39348224 | tf_op jit(solution)/shard_map/dot_general | solution.py:27
  239.3 5.5 fusion.87
  248.5 3.1 collective-permute-start.18
  259.3 3.2 collective-permute-done.20
  265.1 3.9 copy_convert_fusion
  276.2 3.1 reshape_reshape.14
  279.3 2.8 fusion.82
  286.3 3.7 copy.148
  294.3 16.8 %convert_reduce_fusion = (f32[3072]{0:T(1024)S(1)}, bf16[1024,3072]{1,0:T(8,128)(2,1)}) fusion(f32[1024,3072]{1,0:T(8,128)} %get-tuple-element.55, bf16[1024,768]{1,0:T(8,128)(2,1)S(1)} %get-tuple-element.41, bf16[3072,384]{1,0:T(8,128)(2,1)} %bitcast.368, bf16[3072,384]{1,0:T(8,128)(2,1)} %bitcast.370, f32[1024,3072]{1,0:T(8,128)} %get-tuple-element.122, ...), kind=kOutput, calls=%fused_computation.2 | convolution fusion | flops 4894749696 | bytes 37773312 | tf_op jit(solution)/shard_map/dot_general | solution.py:31
  311.1 10.4 %multiply_reduce_fusion.1 = (f32[768]{0:T(1024)S(1)}, f32[1024]{0:T(1024)S(1)}, f32[768]{0:T(1024)S(1)}, f32[1024,768]{1,0:T(8,128)S(1)}) fusion(f32[1024,768]{1,0:T(8,128)S(1)} %copy-done.4, f32[1024]{0:T(1024)S(1)} %fusion.64, f32[1024]{0:T(1024)S(1)} %broadcast_multiply_fusion.1, f32[768]{0:T(1024)S(1)} %reshape.722, ...), kind=kOutput, calls=%fused_computation.57 | convolution fusion | flops 4839699456 | bytes 20472832 | tf_op jit(solution)/shard_map/dot_general | solution.py:31
  321.6 8.4 %fusion.70 = f32[768,3072]{1,0:T(8,128)} fusion(bf16[1024,3072]{1,0:T(8,128)(2,1)S(1)} %copy-done.18, f32[1024,768]{1,0:T(8,128)S(1)} %copy-done.4, f32[768]{0:T(1024)S(1)} %reshape.723, f32[768]{0:T(1024)S(1)} %reshape.722, f32[1024]{0:T(1024)S(1)} %fusion.64, f32[1024]{0:T(1024)S(1)} %broadcast_multiply_fusion.1), kind=kOutput, calls=%fused_computation.265 | convolution fusion | flops 4835770368 | bytes 18888704 | tf_op jit(solution)/shard_map/dot_general | solution.py:37
  330.0 10.3 %fusion.93 = f32[3072,768]{1,0:T(8,128)} fusion(bf16[1024,3072]{1,0:T(8,128)(2,1)} %copy-done.59, bf16[1024,768]{1,0:T(8,128)(2,1)S(1)} %get-tuple-element.41), kind=kOutput, calls=%fused_computation.285 | convolution fusion | flops 4831838208 | bytes 17301504 | tf_op jit(solution)/shard_map/dot_general | solution.py:37
  346.6 6.2 %reshape.729 = bf16[16,64,12,64]{3,2,1,0:T(8,128)(2,1)} reshape(bf16[1024,768]{1,0:T(8,128)(2,1)} %convolution_convert_fusion) | data formatting | bytes 3145728 | tf_op jit(solution)/shard_map/reshape | solution.py:353
  352.8 7.6 %convert_reduce_fusion.1 = (f32[12,64]{1,0:T(8,128)S(1)}, bf16[16,64,12,64]{3,1,2,0:T(8,128)(2,1)}) fusion(bf16[16,64,12,64]{3,2,1,0:T(8,128)(2,1)} %reshape.729, f32[16,12,64,64]{2,3,1,0:T(8,128)} %copy-done, f32[16,12,64]{2,1,0:T(8,128)S(1)} %log_add_fusion), kind=kOutput, calls=%fused_computation.22 | convolution fusion | flops 104594688 | bytes 6343680 | tf_op jit(solution)/shard_map/bhqk,bqhd->bkhd/dot_general | solution.py:358
  360.9 4.7 multiply_reduce_fusion
  365.6 4.8 multiply_convert_fusion.3
  370.4 3.6 fusion.13
  374.0 3.2 convert_reduce_fusion.2
  377.7 4.6 copy.262
  382.3 4.5 copy.167
  387.2 3.1 convolution_bitcast_fusion
  390.3 6.0 %select_convert_fusion.2 = bf16[2,2,2,2,192,384]{5,4,2,3,1,0:T(8,128)(2,1)} fusion(f32[2,2,2,2,192,768]{5,4,3,2,1,0:T(8,128)} %bitcast.336, pred[]{:T(512)S(6)} %eq.47), kind=kLoop, calls=%fused_computation.49 | loop fusion | flops 1179648 | bytes 9437185 | tf_op jit(solution)/shard_map/convert_element_type | solution.py:140
  398.7 4.2 copy.158
  402.9 3.2 reshape.693
  407.5 4.7 fusion.91
  412.2 4.2 copy.160
  416.4 3.2 reshape.694
  419.6 4.7 fusion.92
  424.3 4.2 copy.154
  428.6 3.2 reshape.692
  431.7 3.5 fusion.90
  444.7 5.3 convert_add_fusion.2
  455.1 5.4 convert_add_fusion.1
  473.9 15.1 %collective-permute-done.36 = bf16[2,2,2,192,384]{4,3,2,1,0:T(8,128)(2,1)S(1)} collective-permute-done((bf16[2,2,2,192,384]{4,3,2,1,0:T(8,128)(2,1)S(1)}, bf16[2,2,2,192,384]{4,3,2,1,0:T(8,128)(2,1)S(1)}, u32[]{:S(2)}, u32[]{:S(2)}) %collective-permute-start.36) | collective-permute-done | bytes 1179680 | tf_op jit(solution)/shard_map/ppermute | solution.py:86
  490.9 18.0 %collective-permute-done.24 = bf16[2,2,2,208,384]{4,3,2,1,0:T(8,128)(2,1)S(1)} collective-permute-done((bf16[2,2,2,208,384]{4,3,2,1,0:T(8,128)(2,1)S(1)}, bf16[2,2,2,208,384]{4,3,2,1,0:T(8,128)(2,1)S(1)}, u32[]{:S(2)}, u32[]{:S(2)}) %collective-permute-start.24) | collective-permute-done | bytes 1277984 | tf_op jit(solution)/shard_map/ppermute | solution.py:86
  513.4 9.2 %collective-permute-done.32 = bf16[2,192,384]{2,1,0:T(8,128)(2,1)S(1)} collective-permute-done((bf16[2,192,384]{2,1,0:T(8,128)(2,1)S(1)}, bf16[2,192,384]{2,1,0:T(8,128)(2,1)S(1)}, u32[]{:S(2)}, u32[]{:S(2)}) %collective-permute-start.32) | collective-permute-done | bytes 294944 | tf_op jit(solution)/shard_map/ppermute | solution.py:86
  526.9 3.0 collective-permute-start.39
  534.7 2.7 collective-permute-done.39
  537.6 3.8 add_add_fusion.2
  544.7 10.5 %collective-permute-done.27 = bf16[208,384]{1,0:T(8,128)(2,1)S(1)} collective-permute-done((bf16[208,384]{1,0:T(8,128)(2,1)S(1)}, bf16[208,384]{1,0:T(8,128)(2,1)S(1)}, u32[]{:S(2)}, u32[]{:S(2)}) %collective-permute-start.27) | collective-permute-done | bytes 159776 | tf_op jit(solution)/shard_map/ppermute | solution.py:86
  (432 shorter events, 146.8 us)
Async XLA Ops:
  2.0 13.4 %collective-permute-start.12 = (bf16[96,384]{1,0:T(8,128)(2,1)S(1)}, bf16[96,384]{1,0:T(8,128)(2,1)S(1)}, u32[]{:S(2)}, u32[]{:S(2)}) collective-permute-start(bf16[96,384]{1,0:T(8,128)(2,1)S(1)} %bitcast.406), channel_id=1, source_target_pairs={{0,1},{1,0},{2,3},{3,2},{4,5},{5,4},{6,7},{7,6},{8,9},{9,8},{10,11... | collective-permute-start | bytes 221192 | tf_op jit(solution)/shard_map/ppermute | solution.py:86
  3.8 15.4 %collective-permute-start.6 = (bf16[96,384]{1,0:T(8,128)(2,1)S(1)}, bf16[96,384]{1,0:T(8,128)(2,1)S(1)}, u32[]{:S(2)}, u32[]{:S(2)}) collective-permute-start(bf16[96,384]{1,0:T(8,128)(2,1)S(1)} %bitcast.405), channel_id=1, source_target_pairs={{0,1},{1,0},{2,3},{3,2},{4,5},{5,4},{6,7},{7,6},{8,9},{9,8},{10,11... | collective-permute-start | bytes 221192 | tf_op jit(solution)/shard_map/ppermute | solution.py:86
  14.4 4.7 collective-permute-start
  14.9 35.1 %copy-start.51 = (pred[2]{0:T(512)(128)(4,1)}, pred[2]{0:T(512)(128)(4,1)S(1)}, u32[]{:S(2)}) copy-start(pred[2]{0:T(512)(128)(4,1)S(1)} %iota_compare_fusion.2) | copy-start | bytes 10
  15.5 14.7 %collective-permute-start.13 = (bf16[192,384]{1,0:T(8,128)(2,1)S(1)}, bf16[192,384]{1,0:T(8,128)(2,1)S(1)}, u32[]{:S(2)}, u32[]{:S(2)}) collective-permute-start(bf16[192,384]{1,0:T(8,128)(2,1)S(1)} %bitcast_select_fusion), channel_id=1, source_target_pairs={{0,16},{1,17},{2,18},{3,19},{4,20},{5,21},{6,22},{7,23},{8,24},{9,... | collective-permute-start | bytes 442376 | tf_op jit(solution)/shard_map/ppermute | solution.py:86
  19.3 13.8 %collective-permute-start.7 = (bf16[192,384]{1,0:T(8,128)(2,1)S(1)}, bf16[192,384]{1,0:T(8,128)(2,1)S(1)}, u32[]{:S(2)}, u32[]{:S(2)}) collective-permute-start(bf16[192,384]{1,0:T(8,128)(2,1)S(1)} %get-tuple-element.114), channel_id=1, source_target_pairs={{0,16},{1,17},{2,18},{3,19},{4,20},{5,21},{6,22},{7,23},{8,24},{9,... | collective-permute-start | bytes 442376 | tf_op jit(solution)/shard_map/ppermute | solution.py:86
  20.0 46.7 %copy-start.49 = (pred[2]{0:T(512)(128)(4,1)}, pred[2]{0:T(512)(128)(4,1)S(1)}, u32[]{:S(2)}) copy-start(pred[2]{0:T(512)(128)(4,1)S(1)} %iota_compare_fusion.3) | copy-start | bytes 10
  33.3 9.9 %collective-permute-start.14 = (bf16[2,192,384]{2,1,0:T(8,128)(2,1)S(1)}, bf16[2,192,384]{2,1,0:T(8,128)(2,1)S(1)}, u32[]{:S(2)}, u32[]{:S(2)}) collective-permute-start(bf16[2,192,384]{2,1,0:T(8,128)(2,1)S(1)} %get-tuple-element.112), channel_id=1, source_target_pairs={{0,8},{1,9},{2,10},{3,11},{4,12},{5,13},{6,14},{7,15},{8,0},{9,1},... | collective-permute-start | bytes 884744 | tf_op jit(solution)/shard_map/ppermute | solution.py:86
  34.1 14.4 %collective-permute-start.8 = (bf16[2,192,384]{2,1,0:T(8,128)(2,1)S(1)}, bf16[2,192,384]{2,1,0:T(8,128)(2,1)S(1)}, u32[]{:S(2)}, u32[]{:S(2)}) collective-permute-start(bf16[2,192,384]{2,1,0:T(8,128)(2,1)S(1)} %get-tuple-element.113), channel_id=1, source_target_pairs={{0,8},{1,9},{2,10},{3,11},{4,12},{5,13},{6,14},{7,15},{8,0},{9,1},... | collective-permute-start | bytes 884744 | tf_op jit(solution)/shard_map/ppermute | solution.py:86
  35.5 33.3 %copy-start.47 = (pred[2]{0:T(512)(128)(4,1)}, pred[2]{0:T(512)(128)(4,1)S(1)}, u32[]{:S(2)}) copy-start(pred[2]{0:T(512)(128)(4,1)S(1)} %iota_compare_fusion.4) | copy-start | bytes 10
  48.7 12.3 %collective-permute-start.15 = (bf16[2,2,192,384]{3,2,1,0:T(8,128)(2,1)S(1)}, bf16[2,2,192,384]{3,2,1,0:T(8,128)(2,1)S(1)}, u32[]{:S(2)}, u32[]{:S(2)}) collective-permute-start(bf16[2,2,192,384]{3,2,1,0:T(8,128)(2,1)S(1)} %get-tuple-element.110), channel_id=1, source_target_pairs={{0,2},{1,5},{2,0},{3,7},{4,6},{5,1},{6,4},{7,3},{8,10},{9,13},{10,... | collective-permute-start | bytes 1769480 | tf_op jit(solution)/shard_map/ppermute | solution.py:86
  50.1 14.9 %collective-permute-start.9 = (bf16[2,2,192,384]{3,2,1,0:T(8,128)(2,1)S(1)}, bf16[2,2,192,384]{3,2,1,0:T(8,128)(2,1)S(1)}, u32[]{:S(2)}, u32[]{:S(2)}) collective-permute-start(bf16[2,2,192,384]{3,2,1,0:T(8,128)(2,1)S(1)} %get-tuple-element.111), channel_id=1, source_target_pairs={{0,2},{1,5},{2,0},{3,7},{4,6},{5,1},{6,4},{7,3},{8,10},{9,13},{10,... | collective-permute-start | bytes 1769480 | tf_op jit(solution)/shard_map/ppermute | solution.py:86
  50.9 9.3 %collective-permute-start.1 = (bf16[208,384]{1,0:T(8,128)(2,1)S(1)}, bf16[208,384]{1,0:T(8,128)(2,1)S(1)}, u32[]{:S(2)}, u32[]{:S(2)}) collective-permute-start(bf16[208,384]{1,0:T(8,128)(2,1)S(1)} %pad_maximum_fusion.8), channel_id=1, source_target_pairs={{0,16},{1,17},{2,18},{3,19},{4,20},{5,21},{6,22},{7,23},{8,24},{9,... | collective-permute-start | bytes 479240 | tf_op jit(solution)/shard_map/ppermute | solution.py:86
  53.5 32.9 %copy-start.53 = (pred[2]{0:T(512)(128)(4,1)}, pred[2]{0:T(512)(128)(4,1)S(1)}, u32[]{:S(2)}) copy-start(pred[2]{0:T(512)(128)(4,1)S(1)} %iota_compare_fusion.5) | copy-start | bytes 10
  60.3 8.6 %collective-permute-start.2 = (bf16[2,208,384]{2,1,0:T(8,128)(2,1)S(1)}, bf16[2,208,384]{2,1,0:T(8,128)(2,1)S(1)}, u32[]{:S(2)}, u32[]{:S(2)}) collective-permute-start(bf16[2,208,384]{2,1,0:T(8,128)(2,1)S(1)} %broadcast_select_fusion.16), channel_id=1, source_target_pairs={{0,8},{1,9},{2,10},{3,11},{4,12},{5,13},{6,14},{7,15},{8,0},{9,1},... | collective-permute-start | bytes 958472 | tf_op jit(solution)/shard_map/ppermute | solution.py:86
  66.7 22.8 %collective-permute-start.16 = (bf16[2,2,2,192,384]{4,3,2,1,0:T(8,128)(2,1)}, bf16[2,2,2,192,384]{4,3,2,1,0:T(8,128)(2,1)}, u32[]{:S(2)}, u32[]{:S(2)}) collective-permute-start(bf16[2,2,2,192,384]{4,3,2,1,0:T(8,128)(2,1)} %get-tuple-element.108), channel_id=1, source_target_pairs={{0,4},{1,3},{2,6},{3,1},{4,0},{5,7},{6,2},{7,5},{8,12},{9,11},{10,... | collective-permute-start | bytes 3538952 | tf_op jit(solution)/shard_map/ppermute | solution.py:86
  68.0 34.1 %collective-permute-start.10 = (bf16[2,2,2,192,384]{4,3,2,1,0:T(8,128)(2,1)}, bf16[2,2,2,192,384]{4,3,2,1,0:T(8,128)(2,1)}, u32[]{:S(2)}, u32[]{:S(2)}) collective-permute-start(bf16[2,2,2,192,384]{4,3,2,1,0:T(8,128)(2,1)} %get-tuple-element.109), channel_id=1, source_target_pairs={{0,4},{1,3},{2,6},{3,1},{4,0},{5,7},{6,2},{7,5},{8,12},{9,11},{10,... | collective-permute-start | bytes 3538952 | tf_op jit(solution)/shard_map/ppermute | solution.py:86
  69.0 17.4 %collective-permute-start.3 = (bf16[2,2,208,384]{3,2,1,0:T(8,128)(2,1)S(1)}, bf16[2,2,208,384]{3,2,1,0:T(8,128)(2,1)S(1)}, u32[]{:S(2)}, u32[]{:S(2)}) collective-permute-start(bf16[2,2,208,384]{3,2,1,0:T(8,128)(2,1)S(1)} %broadcast_select_fusion.11), channel_id=1, source_target_pairs={{0,2},{1,5},{2,0},{3,7},{4,6},{5,1},{6,4},{7,3},{8,10},{9,13},{10,... | collective-permute-start | bytes 1916936 | tf_op jit(solution)/shard_map/ppermute | solution.py:86
  86.7 29.0 %collective-permute-start.4 = (bf16[2,2,2,208,384]{4,3,2,1,0:T(8,128)(2,1)S(1)}, bf16[2,2,2,208,384]{4,3,2,1,0:T(8,128)(2,1)S(1)}, u32[]{:S(2)}, u32[]{:S(2)}) collective-permute-start(bf16[2,2,2,208,384]{4,3,2,1,0:T(8,128)(2,1)S(1)} %broadcast_select_fusion.8), channel_id=1, source_target_pairs={{0,4},{1,3},{2,6},{3,1},{4,0},{5,7},{6,2},{7,5},{8,12},{9,11},{10,... | collective-permute-start | bytes 3833864 | tf_op jit(solution)/shard_map/ppermute | solution.py:86
  88.2 43.4 %copy-start.43 = (pred[2]{0:T(512)(128)(4,1)}, pred[2]{0:T(512)(128)(4,1)S(1)}, u32[]{:S(2)}) copy-start(pred[2]{0:T(512)(128)(4,1)S(1)} %iota_compare_fusion.6) | copy-start | bytes 10
  105.0 12.5 %copy-start.58 = (s32[16]{0:T(128)S(1)}, s32[16]{0:T(128)}, u32[]{:S(2)}) copy-start(s32[16]{0:T(128)} %param.22) | copy-start | bytes 196
  105.0 12.5 %collective-permute-start.17 = (bf16[2,2,2,2,192,384]{5,4,2,3,1,0:T(8,128)(2,1)S(1)}, bf16[2,2,2,2,192,384]{5,4,2,3,1,0:T(8,128)(2,1)S(1)}, u32[]{:S(2)}, u32[]{:S(2)}) collective-permute-start(bf16[2,2,2,2,192,384]{5,4,2,3,1,0:T(8,128)(2,1)S(1)} %get-tuple-element.106), channel_id=1, source_target_pairs={{0,1},{1,0},{2,3},{3,2},{4,5},{5,4},{6,7},{7,6},{8,9},{9,8},{10,11... | collective-permute-start | bytes 7077896 | tf_op jit(solution)/shard_map/ppermute | solution.py:86
  105.1 16.0 %collective-permute-start.11 = (bf16[2,2,2,2,192,384]{5,4,2,3,1,0:T(8,128)(2,1)S(1)}, bf16[2,2,2,2,192,384]{5,4,2,3,1,0:T(8,128)(2,1)S(1)}, u32[]{:S(2)}, u32[]{:S(2)}) collective-permute-start(bf16[2,2,2,2,192,384]{5,4,2,3,1,0:T(8,128)(2,1)S(1)} %get-tuple-element.107), channel_id=1, source_target_pairs={{0,1},{1,0},{2,3},{3,2},{4,5},{5,4},{6,7},{7,6},{8,9},{9,8},{10,11... | collective-permute-start | bytes 7077896 | tf_op jit(solution)/shard_map/ppermute | solution.py:86
  117.5 14.1 %collective-permute-start.5 = (bf16[2,2,2,2,208,384]{5,4,2,3,1,0:T(8,128)(2,1)}, bf16[2,2,2,2,208,384]{5,4,2,3,1,0:T(8,128)(2,1)}, u32[]{:S(2)}, u32[]{:S(2)}) collective-permute-start(bf16[2,2,2,2,208,384]{5,4,2,3,1,0:T(8,128)(2,1)} %broadcast_select_fusion), channel_id=1, source_target_pairs={{0,1},{1,0},{2,3},{3,2},{4,5},{5,4},{6,7},{7,6},{8,9},{9,8},{10,11... | collective-permute-start | bytes 7667720 | tf_op jit(solution)/shard_map/ppermute | solution.py:86
  140.7 61.0 %copy-start.44 = (f32[3072]{0:T(1024)}, f32[3072]{0:T(1024)S(1)}, u32[]{:S(2)}) copy-start(f32[3072]{0:T(1024)S(1)} %reshape.724) | copy-start | bytes 36868
  150.8 30.4 %copy-start.8 = (bf16[16,64,12,64]{1,0,3,2:T(8,128)(2,1)}, bf16[16,64,12,64]{1,0,3,2:T(8,128)(2,1)S(1)}, u32[]{:S(2)}) copy-start(bf16[16,64,12,64]{1,0,3,2:T(8,128)(2,1)S(1)} %reshape.675) | copy-start | bytes 4718596
  201.1 38.2 %copy-start.3 = (f32[1024,768]{1,0:T(8,128)}, f32[1024,768]{1,0:T(8,128)S(1)}, u32[]{:S(2)}) copy-start(f32[1024,768]{1,0:T(8,128)S(1)} %get-tuple-element.121) | copy-start | bytes 9437188
  201.6 37.7 %copy-start.40 = (f32[1024]{0:T(1024)}, f32[1024]{0:T(1024)S(1)}, u32[]{:S(2)}) copy-start(f32[1024]{0:T(1024)S(1)} %multiply_reduce_fusion.5) | copy-start | bytes 12292
  201.7 37.6 %copy-start.24 = (bf16[2,2,2,2,192,384]{5,4,3,2,1,0:T(8,128)(2,1)S(1)}, bf16[2,2,2,2,192,384]{5,4,3,2,1,0:T(8,128)(2,1)}, u32[]{:S(2)}) copy-start(bf16[2,2,2,2,192,384]{5,4,3,2,1,0:T(8,128)(2,1)} %copy.142) | copy-start | bytes 7077892
  201.7 37.6 %copy-start.25 = (bf16[2,2,2,2,192,384]{5,4,2,3,1,0:T(8,128)(2,1)S(1)}, bf16[2,2,2,2,192,384]{5,4,2,3,1,0:T(8,128)(2,1)}, u32[]{:S(2)}) copy-start(bf16[2,2,2,2,192,384]{5,4,2,3,1,0:T(8,128)(2,1)} %get-tuple-element.58) | copy-start | bytes 7077892
  245.5 12.2 %copy-start.48 = (pred[2]{0:T(512)(128)(4,1)S(1)}, pred[2]{0:T(512)(128)(4,1)}, u32[]{:S(2)}) copy-start(pred[2]{0:T(512)(128)(4,1)} %copy-done.47) | copy-start | bytes 10
  248.5 5.0 collective-permute-start.18
  253.6 4.1 collective-permute-start.19
  257.8 4.8 collective-permute-start.20
  263.6 5.7 %collective-permute-start.21 = (bf16[2,2,2,16,768]{4,3,2,1,0:T(8,128)(2,1)S(1)}, bf16[2,2,2,16,768]{4,3,2,1,0:T(8,128)(2,1)S(1)}, u32[]{:S(2)}, u32[]{:S(2)}) collective-permute-start(bf16[2,2,2,16,768]{4,3,2,1,0:T(8,128)(2,1)S(1)} %broadcast_select_fusion.19), channel_id=1, source_target_pairs={{0,4},{1,3},{2,6},{3,1},{4,0},{5,7},{6,2},{7,5},{8,12},{9,11},{10,... | collective-permute-start | bytes 589832 | tf_op jit(solution)/shard_map/ppermute | solution.py:86
  271.5 2.5 collective-permute-start.22
  294.3 16.8 %copy-start.4 = (f32[1024,768]{1,0:T(8,128)S(1)}, f32[1024,768]{1,0:T(8,128)}, u32[]{:S(2)}) copy-start(f32[1024,768]{1,0:T(8,128)} %copy-done.3) | copy-start | bytes 9437188
  346.6 13.8 %slice-start = ((s8[6291456]{0:T(1024)(128)(4,1)}), s8[2097152]{0:T(1024)(128)(4,1)S(1)}, s32[]{:S(2)}) async-start(s8[6291456]{0:T(1024)(128)(4,1)} %bitcast.329), calls=%async_computation | async-start | bytes 4194304
  396.2 48.4 %collective-permute-start.29 = (bf16[2,2,2,2,192,384]{5,4,2,3,1,0:T(8,128)(2,1)}, bf16[2,2,2,2,192,384]{5,4,2,3,1,0:T(8,128)(2,1)}, u32[]{:S(2)}, u32[]{:S(2)}) collective-permute-start(bf16[2,2,2,2,192,384]{5,4,2,3,1,0:T(8,128)(2,1)} %select_convert_fusion.2), channel_id=1, source_target_pairs={{0,1},{1,0},{2,3},{3,2},{4,5},{5,4},{6,7},{7,6},{8,9},{9,8},{10,11... | collective-permute-start | bytes 7077896 | tf_op jit(solution)/shard_map/ppermute | solution.py:86
  398.7 56.4 %collective-permute-start.35 = (bf16[2,2,2,2,192,384]{5,4,2,3,1,0:T(8,128)(2,1)}, bf16[2,2,2,2,192,384]{5,4,2,3,1,0:T(8,128)(2,1)}, u32[]{:S(2)}, u32[]{:S(2)}) collective-permute-start(bf16[2,2,2,2,192,384]{5,4,2,3,1,0:T(8,128)(2,1)} %select_convert_fusion.1), channel_id=1, source_target_pairs={{0,1},{1,0},{2,3},{3,2},{4,5},{5,4},{6,7},{7,6},{8,9},{9,8},{10,11... | collective-permute-start | bytes 7077896 | tf_op jit(solution)/shard_map/ppermute | solution.py:86
  444.0 18.9 %collective-permute-start.23 = (bf16[2,2,2,2,208,384]{5,4,2,3,1,0:T(8,128)(2,1)}, bf16[2,2,2,2,208,384]{5,4,2,3,1,0:T(8,128)(2,1)}, u32[]{:S(2)}, u32[]{:S(2)}) collective-permute-start(bf16[2,2,2,2,208,384]{5,4,2,3,1,0:T(8,128)(2,1)} %select_convert_fusion), channel_id=1, source_target_pairs={{0,1},{1,0},{2,3},{3,2},{4,5},{5,4},{6,7},{7,6},{8,9},{9,8},{10,11... | collective-permute-start | bytes 7667720 | tf_op jit(solution)/shard_map/ppermute | solution.py:86
  444.6 10.5 %slice-start.11 = ((s8[9437184]{0:T(1024)(128)(4,1)}), s8[4194304]{0:T(1024)(128)(4,1)S(1)}, s32[]{:S(2)}) async-start(s8[9437184]{0:T(1024)(128)(4,1)} %bitcast.345), calls=%async_computation.11 | async-start | bytes 8388608
  452.4 10.6 %slice-start.2 = ((s8[9437184]{0:T(1024)(128)(4,1)}), s8[4194304]{0:T(1024)(128)(4,1)S(1)}, s32[]{:S(2)}) async-start(s8[9437184]{0:T(1024)(128)(4,1)} %bitcast.333), calls=%async_computation.2 | async-start | bytes 8388608
  452.4 10.6 %slice-start.5 = ((s8[5111808]{0:T(1024)(128)(4,1)}), s8[4194304]{0:T(1024)(128)(4,1)S(1)}, s32[]{:S(2)}) async-start(s8[5111808]{0:T(1024)(128)(4,1)} %bitcast.338), calls=%async_computation.5 | async-start | bytes 8388608
  453.6 16.5 %collective-permute-start.30 = (bf16[2,2,2,192,384]{4,3,2,1,0:T(8,128)(2,1)}, bf16[2,2,2,192,384]{4,3,2,1,0:T(8,128)(2,1)}, u32[]{:S(2)}, u32[]{:S(2)}) collective-permute-start(bf16[2,2,2,192,384]{4,3,2,1,0:T(8,128)(2,1)} %fusion.37), channel_id=1, source_target_pairs={{0,2},{1,5},{2,0},{3,7},{4,6},{5,1},{6,4},{7,3},{8,10},{9,13},{10,... | collective-permute-start | bytes 3538952 | tf_op jit(solution)/shard_map/ppermute | solution.py:86
  462.4 26.6 %collective-permute-start.36 = (bf16[2,2,2,192,384]{4,3,2,1,0:T(8,128)(2,1)S(1)}, bf16[2,2,2,192,384]{4,3,2,1,0:T(8,128)(2,1)S(1)}, u32[]{:S(2)}, u32[]{:S(2)}) collective-permute-start(bf16[2,2,2,192,384]{4,3,2,1,0:T(8,128)(2,1)S(1)} %fusion.38), channel_id=1, source_target_pairs={{0,2},{1,5},{2,0},{3,7},{4,6},{5,1},{6,4},{7,3},{8,10},{9,13},{10,... | collective-permute-start | bytes 3538952 | tf_op jit(solution)/shard_map/ppermute | solution.py:86
  465.6 43.4 %collective-permute-start.24 = (bf16[2,2,2,208,384]{4,3,2,1,0:T(8,128)(2,1)S(1)}, bf16[2,2,2,208,384]{4,3,2,1,0:T(8,128)(2,1)S(1)}, u32[]{:S(2)}, u32[]{:S(2)}) collective-permute-start(bf16[2,2,2,208,384]{4,3,2,1,0:T(8,128)(2,1)S(1)} %fusion.36), channel_id=1, source_target_pairs={{0,2},{1,5},{2,0},{3,7},{4,6},{5,1},{6,4},{7,3},{8,10},{9,13},{10,... | collective-permute-start | bytes 3833864 | tf_op jit(solution)/shard_map/ppermute | solution.py:86
  467.0 22.0 %slice-start.15 = ((s8[4718592]{0:T(1024)(128)(4,1)}), s8[4194304]{0:T(1024)(128)(4,1)S(1)}, s32[]{:S(2)}) async-start(s8[4718592]{0:T(1024)(128)(4,1)} %bitcast.351), calls=%async_computation.15 | async-start | bytes 8388608
  468.5 20.5 %slice-start.16 = ((s8[4718592]{0:T(1024)(128)(4,1)}), s8[524288]{0:T(1024)(128)(4,1)S(1)}, s32[]{:S(2)}) async-start(s8[4718592]{0:T(1024)(128)(4,1)} %bitcast.351), calls=%async_computation.16 | async-start | bytes 1048576
  472.3 38.6 %collective-permute-start.31 = (bf16[2,2,192,384]{3,2,1,0:T(8,128)(2,1)S(1)}, bf16[2,2,192,384]{3,2,1,0:T(8,128)(2,1)S(1)}, u32[]{:S(2)}, u32[]{:S(2)}) collective-permute-start(bf16[2,2,192,384]{3,2,1,0:T(8,128)(2,1)S(1)} %fusion.41), channel_id=1, source_target_pairs={{0,4},{1,3},{2,6},{3,1},{4,0},{5,7},{6,2},{7,5},{8,12},{9,11},{10,... | collective-permute-start | bytes 1769480 | tf_op jit(solution)/shard_map/ppermute | solution.py:86
  489.4 23.5 %collective-permute-start.37 = (bf16[2,2,192,384]{3,2,1,0:T(8,128)(2,1)S(1)}, bf16[2,2,192,384]{3,2,1,0:T(8,128)(2,1)S(1)}, u32[]{:S(2)}, u32[]{:S(2)}) collective-permute-start(bf16[2,2,192,384]{3,2,1,0:T(8,128)(2,1)S(1)} %fusion.42), channel_id=1, source_target_pairs={{0,4},{1,3},{2,6},{3,1},{4,0},{5,7},{6,2},{7,5},{8,12},{9,11},{10,... | collective-permute-start | bytes 1769480 | tf_op jit(solution)/shard_map/ppermute | solution.py:86
  509.3 20.6 %collective-permute-start.25 = (bf16[2,2,208,384]{3,2,1,0:T(8,128)(2,1)S(1)}, bf16[2,2,208,384]{3,2,1,0:T(8,128)(2,1)S(1)}, u32[]{:S(2)}, u32[]{:S(2)}) collective-permute-start(bf16[2,2,208,384]{3,2,1,0:T(8,128)(2,1)S(1)} %fusion.40), channel_id=1, source_target_pairs={{0,4},{1,3},{2,6},{3,1},{4,0},{5,7},{6,2},{7,5},{8,12},{9,11},{10,... | collective-permute-start | bytes 1916936 | tf_op jit(solution)/shard_map/ppermute | solution.py:86
  511.1 11.6 %collective-permute-start.32 = (bf16[2,192,384]{2,1,0:T(8,128)(2,1)S(1)}, bf16[2,192,384]{2,1,0:T(8,128)(2,1)S(1)}, u32[]{:S(2)}, u32[]{:S(2)}) collective-permute-start(bf16[2,192,384]{2,1,0:T(8,128)(2,1)S(1)} %fusion.48), channel_id=1, source_target_pairs={{0,8},{1,9},{2,10},{3,11},{4,12},{5,13},{6,14},{7,15},{8,0},{9,1},... | collective-permute-start | bytes 884744 | tf_op jit(solution)/shard_map/ppermute | solution.py:86
  513.1 13.7 %collective-permute-start.38 = (bf16[2,192,384]{2,1,0:T(8,128)(2,1)S(1)}, bf16[2,192,384]{2,1,0:T(8,128)(2,1)S(1)}, u32[]{:S(2)}, u32[]{:S(2)}) collective-permute-start(bf16[2,192,384]{2,1,0:T(8,128)(2,1)S(1)} %fusion.49), channel_id=1, source_target_pairs={{0,8},{1,9},{2,10},{3,11},{4,12},{5,13},{6,14},{7,15},{8,0},{9,1},... | collective-permute-start | bytes 884744 | tf_op jit(solution)/shard_map/ppermute | solution.py:86
  522.7 11.9 %collective-permute-start.33 = (bf16[192,384]{1,0:T(8,128)(2,1)S(1)}, bf16[192,384]{1,0:T(8,128)(2,1)S(1)}, u32[]{:S(2)}, u32[]{:S(2)}) collective-permute-start(bf16[192,384]{1,0:T(8,128)(2,1)S(1)} %fusion.55), channel_id=1, source_target_pairs={{0,16},{1,17},{2,18},{3,19},{4,20},{5,21},{6,22},{7,23},{8,24},{9,... | collective-permute-start | bytes 442376 | tf_op jit(solution)/shard_map/ppermute | solution.py:86
  526.9 10.7 %copy-start.7 = (f32[1024,768]{1,0:T(8,128)S(1)}, f32[1024,768]{1,0:T(8,128)}, u32[]{:S(2)}) copy-start(f32[1024,768]{1,0:T(8,128)} %copy-done.6) | copy-start | bytes 9437188
  526.9 10.7 %copy-start.19 = (bf16[1024,768]{0,1:T(8,128)(2,1)S(1)}, bf16[1024,768]{0,1:T(8,128)(2,1)}, u32[]{:S(2)}) copy-start(bf16[1024,768]{0,1:T(8,128)(2,1)} %reshape.694) | copy-start | bytes 4718596
  526.9 10.7 %copy-start.20 = (bf16[1,16,48,768]{3,2,0,1:T(8,128)(2,1)S(1)}, bf16[1,16,48,768]{3,2,0,1:T(8,128)(2,1)}, u32[]{:S(2)}) copy-start(bf16[1,16,48,768]{3,2,0,1:T(8,128)(2,1)} %get-tuple-element.65) | copy-start | bytes 3538948
  526.9 10.5 %collective-permute-start.39 = (bf16[192,384]{1,0:T(8,128)(2,1)S(1)}, bf16[192,384]{1,0:T(8,128)(2,1)S(1)}, u32[]{:S(2)}, u32[]{:S(2)}) collective-permute-start(bf16[192,384]{1,0:T(8,128)(2,1)S(1)} %fusion.56), channel_id=1, source_target_pairs={{0,16},{1,17},{2,18},{3,19},{4,20},{5,21},{6,22},{7,23},{8,24},{9,... | collective-permute-start | bytes 442376 | tf_op jit(solution)/shard_map/ppermute | solution.py:86
  530.1 14.3 %collective-permute-start.26 = (bf16[2,208,384]{2,1,0:T(8,128)(2,1)S(1)}, bf16[2,208,384]{2,1,0:T(8,128)(2,1)S(1)}, u32[]{:S(2)}, u32[]{:S(2)}) collective-permute-start(bf16[2,208,384]{2,1,0:T(8,128)(2,1)S(1)} %fusion.47), channel_id=1, source_target_pairs={{0,8},{1,9},{2,10},{3,11},{4,12},{5,13},{6,14},{7,15},{8,0},{9,1},... | collective-permute-start | bytes 958472 | tf_op jit(solution)/shard_map/ppermute | solution.py:86
  534.7 9.2 %collective-permute-start.34 = (f32[96,384]{1,0:T(8,128)S(1)}, f32[96,384]{1,0:T(8,128)S(1)}, u32[]{:S(2)}, u32[]{:S(2)}) collective-permute-start(f32[96,384]{1,0:T(8,128)S(1)} %bitcast.404), channel_id=1, source_target_pairs={{0,1},{1,0},{2,3},{3,2},{4,5},{5,4},{6,7},{7,6},{8,9},{9,8},{10,11... | collective-permute-start | bytes 442376 | tf_op jit(solution)/shard_map/ppermute | solution.py:86
  537.5 6.7 %collective-permute-start.40 = (f32[96,384]{1,0:T(8,128)S(1)}, f32[96,384]{1,0:T(8,128)S(1)}, u32[]{:S(2)}, u32[]{:S(2)}) collective-permute-start(f32[96,384]{1,0:T(8,128)S(1)} %get-tuple-element.82), channel_id=1, source_target_pairs={{0,1},{1,0},{2,3},{3,2},{4,5},{5,4},{6,7},{7,6},{8,9},{9,8},{10,11... | collective-permute-start | bytes 442376 | tf_op jit(solution)/shard_map/ppermute | solution.py:86
  544.5 10.7 %collective-permute-start.27 = (bf16[208,384]{1,0:T(8,128)(2,1)S(1)}, bf16[208,384]{1,0:T(8,128)(2,1)S(1)}, u32[]{:S(2)}, u32[]{:S(2)}) collective-permute-start(bf16[208,384]{1,0:T(8,128)(2,1)S(1)} %fusion.50), channel_id=1, source_target_pairs={{0,16},{1,17},{2,18},{3,19},{4,20},{5,21},{6,22},{7,23},{8,24},{9,... | collective-permute-start | bytes 479240 | tf_op jit(solution)/shard_map/ppermute | solution.py:86
  555.3 1.6 collective-permute-start.28
  (56 other events, 259.5 us)

commit v2 on v0

v2 whole, which is shorter than its diff:
```python
import jax
import jax.numpy as jnp
from jax import lax
from jax.experimental import pallas as pl
from jax.experimental.pallas import tpu as pltpu
from jax.sharding import PartitionSpec as P

D = 768
HEADS = 12
HEAD_DIM = 64
LEN = 64
FF = 3072
QUAD = 4
WIDE = QUAD * HEAD_DIM
GROUPS = HEADS // QUAD
ROWS = 256
BLOCK = 768
AXIS = "fsdp"
norm_eps = 1e-12
pool_eps = 1e-06
sim_scale = 50.0
sim_margin = 0.3
f32, low = jnp.float32, jnp.bfloat16
S = jax.ShapeDtypeStruct

B_QUERY, B_VALUE, B_OUTPUT, G_ATTN, S_ATTN, B_OUTER, G_FFN, S_FFN, B_INNER = range(9)
CODES = B_INNER + FF // D


def nn(a, b):
    return lax.dot_general(a, b, (((1,), (0,)), ((), ())), preferred_element_type=f32)


def nt(a, b):
    return lax.dot_general(a, b, (((1,), (1,)), ((), ())), preferred_element_type=f32)


def tn(a, b):
    return lax.dot_general(a, b, (((0,), (0,)), ((), ())), preferred_element_type=f32)


def whole(shape):
    return pl.BlockSpec(shape, lambda *_: (0,) * len(shape), pipeline_mode=pl.Buffered(1))


def row_block(width, rows=ROWS):
    return pl.BlockSpec((rows, width), lambda i, *_: (i, 0))


def params(flops, nbytes, exps=0):
    return dict(
        compiler_params=pltpu.CompilerParams(vmem_limit_bytes=60 << 20),
        cost_estimate=pl.CostEstimate(flops=int(flops), bytes_accessed=int(nbytes), transcendentals=int(exps)),
    )


ANY = pl.BlockSpec(memory_space=pl.ANY)


def part_copies(parts, target, sems, cut):
    me = lax.axis_index(AXIS)
    core, x, y = me & 1, (me >> 1) & 1, (me >> 2) & 1

    def start(zero, one):
        for i in range(2):
            pltpu.make_async_copy(cut(zero[i]), target.at[:, (y + i) & 1, :, 0], sems.at[2 * i]).start()
            pltpu.make_async_copy(cut(one[i]), target.at[:, :, (x + i) & 1, 1], sems.at[2 * i + 1]).start()

    @pl.when(core == 0)
    def _():
        start(parts[:2], parts[2:])

    @pl.when(core == 1)
    def _():
        start(parts[2:], parts[:2])


def part_waits(parts, target, sems, cut):
    for i in range(2):
        pltpu.make_async_copy(cut(parts[i]), target.at[:, i, :, 0], sems.at[2 * i]).wait()
        pltpu.make_async_copy(cut(parts[i]), target.at[:, :, i, 1], sems.at[2 * i + 1]).wait()


def everything(ref):
    return ref


def project_body(cube, x_ref, vec_ref, *refs):
    parts, (q_ref, k_ref, v_ref, full_ref, w_ref, sems, out_sem) = refs[:-7], refs[-7:]
    step = pl.program_id(0)
    full_copy = pltpu.make_async_copy(w_ref, full_ref, out_sem)

    @pl.when(step == 0)
    def _():
        if cube:
            def cut(m):
                return lambda ref: ref.at[:, :, pl.ds(m * 24, 24), :]

            for m in range(4):
                part_copies(parts, w_ref.at[m], sems.at[m], cut(m))
            for m in range(4):
                part_waits(parts, w_ref.at[m], sems.at[m], cut(m))
        else:
            copy = pltpu.make_async_copy(parts[0], w_ref, sems.at[0, 0])
            copy.start()
            copy.wait()
        full_copy.start()

    x = x_ref[...]

    def mat(m):
        return w_ref.at[m].reshape(D, D)[...] if cube else w_ref[m]

    q_ref[...] = (nn(x, mat(0)) + vec_ref[B_QUERY : B_QUERY + 1].astype(f32)).astype(low)
    k_ref[...] = nn(x, mat(1)).astype(low)
    v_ref[...] = (nn(x, mat(2)) + vec_ref[B_VALUE : B_VALUE + 1].astype(f32)).astype(low)

    @pl.when(step == pl.num_programs(0) - 1)
    def _():
        full_copy.wait()


def project(x, vec, parts, cube):
    t = x.shape[0]
    shape = (4, 4, 2, 2, 2, 24, D) if cube else (4, D, D)
    q, k, v, full = pl.pallas_call(
        lambda *refs: project_body(cube, *refs),
        grid=(t // ROWS,),
        in_specs=[row_block(D), whole(vec.shape)] + [ANY] * len(parts),
        out_specs=[row_block(D)] * 3 + [ANY],
        out_shape=[S((t, D), low)] * 3 + [S(shape, low)],
        scratch_shapes=[pltpu.VMEM(shape, low), pltpu.SemaphoreType.DMA((4, 4)), pltpu.SemaphoreType.DMA],
        name="project",
        **params(6 * t * D * D, 8 * t * D + 16 * D * D),
    )(x, vec, *parts)
    return q, k, v, full.reshape(4, D, D)


def head_masks(dtype):
    lane = lax.broadcasted_iota(jnp.int32, (1, WIDE), 1) // HEAD_DIM
    return [jnp.where(lane == h, 1.0, 0.0).astype(dtype) for h in range(QUAD)]


def stacked(rows, masks):
    return jnp.concatenate([rows * m for m in masks], axis=0)


def unstacked(full, masks):
    return sum(full[LEN * h : LEN * (h + 1)] * m for h, m in enumerate(masks))


def table_rows(s, g):
    return pl.ds(pl.multiple_of((s * GROUPS + g) * LEN, LEN), LEN)


def layer_norm(resid):
    centred = resid - jnp.mean(resid, axis=-1, keepdims=True)
    inv = lax.rsqrt(jnp.mean(centred * centred, axis=-1, keepdims=True) + norm_eps)
    return centred * inv, inv


def layer_norm_back(grad, gain, hat, inv):
    grad = grad * gain
    mean = jnp.mean(grad, axis=-1, keepdims=True)
    along = jnp.mean(grad * hat, axis=-1, keepdims=True)
    return (grad - mean - hat * along) * inv


def attend_body(start, len_ref, x_ref, q_ref, k_ref, v_ref, wo_ref, vec_ref, *refs):
    p_ref, c_ref, hat_ref, inv_ref, n_ref = refs[-5:]
    masks, masks32 = head_masks(low), head_masks(f32)
    per = ROWS // LEN
    first = (start + pl.program_id(0)) * per
    key_at = lax.broadcasted_iota(jnp.int32, (LEN, WIDE), 0)

    def sentence(s):
        rows = pl.ds(pl.multiple_of(s * LEN, LEN), LEN)
        seen = key_at < len_ref[first + s]
        for g in range(GROUPS):
            cols = pl.ds(g * WIDE, WIDE)
            q, k, v = q_ref[rows, cols], k_ref[rows, cols], v_ref[rows, cols]
            scores = nt(k, stacked(q, masks)) * HEAD_DIM ** (-0.5)
            scores = jnp.where(seen, scores, -1e30)
            expd = jnp.exp(scores - jnp.max(scores, axis=0, keepdims=True))
            probs = expd * (1.0 / jnp.sum(expd, axis=0, keepdims=True))
            p_ref[table_rows(s, g), :] = probs
            c_ref[rows, cols] = unstacked(tn(probs.astype(low), v), masks32).astype(low)

    pl.loop(0, per, unroll=UNROLL)(sentence)
    branch = nn(c_ref[...], wo_ref[0]) + vec_ref[B_OUTPUT : B_OUTPUT + 1].astype(f32)
    hat, inv = layer_norm(x_ref[...].astype(f32) + branch)
    hat_ref[...] = hat
    inv_ref[...] = inv
    n_ref[...] = (hat * vec_ref[G_ATTN : G_ATTN + 1].astype(f32) + vec_ref[S_ATTN : S_ATTN + 1].astype(f32)).astype(low)


UNROLL = 2


def some_rows(start):
    return lambda width, rows=ROWS: pl.BlockSpec((rows, width), lambda i, *_: (start + i, 0))


def mat_of(m):
    return pl.BlockSpec((1, D, D), lambda *_: (m, 0, 0), pipeline_mode=pl.Buffered(1))


def attend(lengths, x, q, k, v, full, vec, start, count, before=()):
    t = x.shape[0]
    rows = some_rows(start)
    return pl.pallas_call(
        lambda *refs: attend_body(start, *refs),
        grid_spec=pltpu.PrefetchScalarGridSpec(
            num_scalar_prefetch=1,
            grid=(count,),
            in_specs=[rows(D)] * 4 + [mat_of(3), whole(vec.shape)] + [ANY] * len(before),
            out_specs=[rows(WIDE, GROUPS * ROWS), rows(D), rows(D), rows(1), rows(D)],
        ),
        out_shape=[S((GROUPS * t, WIDE), f32), S((t, D), low), S((t, D), f32), S((t, 1), f32), S((t, D), low)],
        input_output_aliases={7 + i: i for i in range(len(before))},
        name="attend",
        **params(12 * count * ROWS * D * D, 26 * count * ROWS * D, count * ROWS * D),
    )(lengths, x, q, k, v, full, vec, *before)


def attend_back_body(
    dres_ref, dh_ref, wi_ref, hat_ref, inv_ref, wo_ref, q_ref, k_ref, v_ref, p_ref, vec_ref, *refs
):
    dr_ref, dq_ref, dk_ref, dv_ref, sums_ref, dc_ref = refs[-6:]
    hat = hat_ref[...]
    dn = dres_ref[...] + nt(dh_ref[...], wi_ref[...])
    dres = layer_norm_back(dn, vec_ref[G_ATTN : G_ATTN + 1].astype(f32), hat, inv_ref[...])
    dr_ref[...] = dres
    dao = dres.astype(low)
    dc_ref[...] = nt(dao, wo_ref[0]).astype(low)

    @pl.when(pl.program_id(0) == 0)
    def _():
        sums_ref[...] = jnp.zeros_like(sums_ref)

    sums_ref[B_OUTPUT : B_OUTPUT + 1] += jnp.sum(dao.astype(f32), axis=0, keepdims=True)
    sums_ref[G_ATTN : G_ATTN + 1] += jnp.sum(dn * hat, axis=0, keepdims=True)
    sums_ref[S_ATTN : S_ATTN + 1] += jnp.sum(dn, axis=0, keepdims=True)
    masks, masks32 = head_masks(low), head_masks(f32)

    def sentence(s):
        rows = pl.ds(pl.multiple_of(s * LEN, LEN), LEN)
        for g in range(GROUPS):
            cols = pl.ds(g * WIDE, WIDE)
            q, k, v, dc = q_ref[rows, cols], k_ref[rows, cols], v_ref[rows, cols], dc_ref[rows, cols]
            p = p_ref[table_rows(s, g), :]
            dcs = stacked(dc, masks)
            dp = nt(v, dcs)
            dv_ref[rows, cols] = nn(p.astype(low), dcs).astype(low)
            ds = (p * (dp - jnp.sum(p * dp, axis=0, keepdims=True))).astype(low)
            dk_ref[rows, cols] = (nn(ds, stacked(q, masks)) * HEAD_DIM ** (-0.5)).astype(low)
            dq_ref[rows, cols] = (unstacked(tn(ds, k), masks32) * HEAD_DIM ** (-0.5)).astype(low)

    pl.loop(0, ROWS // LEN, unroll=UNROLL)(sentence)
    sums_ref[B_QUERY : B_QUERY + 1] += jnp.sum(dq_ref[...].astype(f32), axis=0, keepdims=True)
    sums_ref[B_VALUE : B_VALUE + 1] += jnp.sum(dv_ref[...].astype(f32), axis=0, keepdims=True)


def attend_back(dres, dh, wi, hat, inv, full, q, k, v, p, vec, start, count, before=()):
    t = dres.shape[0]
    rows = some_rows(start)
    return pl.pallas_call(
        attend_back_body,
        grid=(count,),
        in_specs=[rows(D), rows(FF), whole((D, FF)), rows(D), rows(1), mat_of(3), rows(D), rows(D), rows(D),
                  rows(WIDE, GROUPS * ROWS), whole(vec.shape)] + [ANY] * len(before),
        out_specs=[rows(D)] * 4 + [whole((8, D))],
        out_shape=[S((t, D), f32)] + [S((t, D), low)] * 3 + [S((8, D), f32)],
        input_output_aliases={11 + i: i for i in range(len(before))},
        scratch_shapes=[pltpu.VMEM((ROWS, D), low)],
        name="attend_back",
        **params(24 * count * ROWS * D * D, 40 * count * ROWS * D),
    )(dres, dh, wi, hat, inv, full, q, k, v, p, vec, *before)


def gelu_parts(h):
    d = 1.0 + (0.3275911 * 0.7071067811865476) * jnp.abs(h)
    t = pl.reciprocal(d, approx=True)
    t = t * (2.0 - d * t)
    poly = t * (0.127414796 + t * (-0.142248368 + t * (0.7107068705 + t * (-0.7265760135 + t * 0.5307027145))))
    bell = jnp.exp(-0.5 * (h * h))
    tail = poly * bell
    cdf = jnp.where(h >= 0, 1.0 - tail, tail)
    return h * cdf, cdf + h * (bell * 0.3989422804014327)


def assemble(cube, parts, w_ref, full_ref, sems, out_sem):
    onward = pltpu.make_async_copy(w_ref, full_ref, out_sem)

    @pl.when(pl.program_id(0) == 0)
    def _():
        if cube:
            part_copies(parts, w_ref, sems, everything)
            part_waits(parts, w_ref, sems, everything)
        else:
            copy = pltpu.make_async_copy(parts[0], w_ref, sems.at[0])
            copy.start()
            copy.wait()
        onward.start()

    return onward


def inner_body(cube, n_ref, vec_ref, *refs):
    parts, (a_ref, gp_ref, full_ref, w_ref, sems, out_sem) = refs[:-6], refs[-6:]
    onward = assemble(cube, parts, w_ref, full_ref, sems, out_sem)
    n = n_ref[...]
    w = w_ref.reshape(D, FF) if cube else w_ref
    for j in range(FF // BLOCK):
        cols = pl.ds(j * BLOCK, BLOCK)
        h = nn(n, w[:, cols]) + vec_ref[B_INNER + j : B_INNER + j + 1].astype(f32)
        act, slope = gelu_parts(h)
        a_ref[:, cols] = act.astype(low)
        gp_ref[:, cols] = slope.astype(low)

    @pl.when(pl.program_id(0) == pl.num_programs(0) - 1)
    def _():
        onward.wait()


def inner(n, vec, parts, cube):
    t = n.shape[0]
    shape = (4, 2, 2, 2, 24, FF) if cube else (D, FF)
    act, slope, full = pl.pallas_call(
        lambda *refs: inner_body(cube, *refs),
        grid=(t // ROWS,),
        in_specs=[row_block(D), whole(vec.shape)] + [ANY] * len(parts),
        out_specs=[row_block(FF), row_block(FF), ANY],
        out_shape=[S((t, FF), low), S((t, FF), low), S(shape, low)],
        scratch_shapes=[pltpu.VMEM(shape, low), pltpu.SemaphoreType.DMA((4,)), pltpu.SemaphoreType.DMA],
        name="inner",
        **params(6 * t * D * FF, 2 * t * D + 4 * t * FF + 4 * D * FF, 2 * t * FF),
    )(n, vec, *parts)
    return act, slope, full.reshape(D, FF)


def outer_body(cube, a_ref, hat_ref, vec_ref, *refs):
    parts = refs[:-9]
    out_ref, hat2_ref, inv_ref, cls_ref, unit_ref, full_ref, w_ref, sems, out_sem = refs[-9:]
    onward = assemble(cube, parts, w_ref, full_ref, sems, out_sem)
    step = pl.program_id(0)
    w = w_ref.reshape(FF, D) if cube else w_ref
    branch = nn(a_ref[...], w[...]) + vec_ref[B_OUTER : B_OUTER + 1].astype(f32)
    normed = hat_ref[...] * vec_ref[G_ATTN : G_ATTN + 1].astype(f32) + vec_ref[S_ATTN : S_ATTN + 1].astype(f32)
    hat, inv = layer_norm(normed + branch)
    hat2_ref[...] = hat
    inv_ref[...] = inv
    rows = hat * vec_ref[G_FFN : G_FFN + 1].astype(f32) + vec_ref[S_FFN : S_FFN + 1].astype(f32)
    out_ref[...] = rows.astype(low)
    pairs = rows.shape[0] // LEN // 2
    for s in range(pairs):
        at = pl.ds(step * pairs + s, 1)
        for side in range(2):
            cols = pl.ds(side * D, D)
            cls = rows[LEN * (2 * s + side) : LEN * (2 * s + side) + 1]
            cls_ref[at, cols] = cls
            unit_ref[at, cols] = cls * lax.rsqrt(jnp.sum(cls * cls, axis=-1, keepdims=True) + pool_eps)

    @pl.when(step == pl.num_programs(0) - 1)
    def _():
        onward.wait()


def outer(act, hat, vec, parts, cube):
    t = hat.shape[0]
    shape = (4, 2, 2, 2, 96, D) if cube else (FF, D)
    pairs = t // LEN // 2
    once = pl.BlockSpec((pairs, 2 * D), lambda i: (0, 0))
    *outs, full = pl.pallas_call(
        lambda *refs: outer_body(cube, *refs),
        grid=(t // ROWS,),
        in_specs=[row_block(FF), row_block(D), whole(vec.shape)] + [ANY] * len(parts),
        out_specs=[row_block(D), row_block(D), row_block(1), once, once, ANY],
        out_shape=[S((t, D), low), S((t, D), f32), S((t, 1), f32), S((pairs, 2 * D), f32), S((pairs, 2 * D), f32), S(shape, low)],
        scratch_shapes=[pltpu.VMEM(shape, low), pltpu.SemaphoreType.DMA((4,)), pltpu.SemaphoreType.DMA],
        name="outer",
        **params(2 * t * D * FF, 10 * t * D + 2 * t * FF + 4 * D * FF),
    )(act, hat, vec, *parts)
    return *outs, full.reshape(FF, D)


def write_shares(full, keep_ref, away_ref, put):
    core = lax.axis_index(AXIS) & 1

    def write(zero, one):
        for y in range(2):
            for x in range(2):
                put(zero, x, y, full(y, x, 0))
                put(one, y, x, full(y, x, 1))

    @pl.when(core == 0)
    def _():
        write(keep_ref, away_ref)

    @pl.when(core == 1)
    def _():
        write(away_ref, keep_ref)


def outer_back_body(cube, cot_ref, dc_ref, hat2_ref, inv2_ref, a_ref, vec_ref, dres_ref, dbr_ref, sums_ref, *refs):
    j = pl.program_id(0)

    @pl.when(j == 0)
    def _():
        dgain = jnp.zeros((1, D), f32)
        dshift = jnp.zeros((1, D), f32)
        dbias = jnp.zeros((1, D), f32)
        at = lax.broadcasted_iota(jnp.int32, (ROWS, D), 0)
        for b in range(cot_ref.shape[0] // ROWS):
            rows = pl.ds(b * ROWS, ROWS)
            d = cot_ref[rows, :].astype(f32)
            hat = hat2_ref[rows, :]
            for s in range(ROWS // LEN):
                whose = b * (ROWS // LEN) + s
                extra = dc_ref[whose // 2 : whose // 2 + 1, (whose % 2) * D : (whose % 2 + 1) * D]
                d += jnp.where(at == LEN * s, extra, 0.0)
            dgain += jnp.sum(d * hat, axis=0, keepdims=True)
            dshift += jnp.sum(d, axis=0, keepdims=True)
            dres = layer_norm_back(d, vec_ref[G_FFN : G_FFN + 1].astype(f32), hat, inv2_ref[rows, :])
            dres_ref[rows, :] = dres
            dbr = dres.astype(low)
            dbr_ref[rows, :] = dbr
            dbias += jnp.sum(dbr.astype(f32), axis=0, keepdims=True)
        sums_ref[...] = jnp.zeros_like(sums_ref)
        sums_ref[0:1] = dbias
        sums_ref[1:2] = dgain
        sums_ref[2:3] = dshift

    dw = tn(a_ref[...], dbr_ref[...])
    if cube:
        dw = dw.reshape(2, 2, 2, 96, D)

        def put(ref, p, q, value):
            ref[0, p, q] = value.astype(ref.dtype)

        write_shares(lambda y, x, c: dw[y, x, c], *refs, put)
    else:
        refs[0][...] = dw


def outer_back(cot, dc, hat2, inv2, a, vec, cube):
    t = cot.shape[0]
    if cube:
        spec = pl.BlockSpec((1, 2, 2, 96, D), lambda j: (j, 0, 0, 0, 0))
        specs, shapes = [spec] * 2, [S((4, 2, 2, 96, D), KEEP), S((4, 2, 2, 96, D), low)]
    else:
        specs, shapes = [pl.BlockSpec((BLOCK, D), lambda j: (j, 0))], [S((FF, D), f32)]
    return pl.pallas_call(
        lambda *refs: outer_back_body(cube, *refs),
        grid=(FF // BLOCK,),
        in_specs=[whole((t, D)), whole(dc.shape), whole((t, D)), whole((t, 1)), pl.BlockSpec((t, BLOCK), lambda j: (0, j)),
                  whole(vec.shape)],
        out_specs=[whole((t, D)), whole((t, D)), whole((8, D))] + specs,
        out_shape=[S((t, D), f32), S((t, D), low), S((8, D), f32)] + shapes,
        name="outer_back",
        **params(4 * t * D * FF, 14 * t * D + 2 * t * FF + 8 * D * FF),
    )(cot, dc, hat2, inv2, a, vec)


def inner_back_body(cube, dbr_ref, n_ref, gp_ref, wo_ref, dh_ref, sums_ref, *refs):
    dh = (gp_ref[...].astype(f32) * nt(dbr_ref[...], wo_ref[...])).astype(low)
    dh_ref[...] = dh
    sums_ref[pl.ds(pl.program_id(0), 1), :] = jnp.sum(dh.astype(f32), axis=0, keepdims=True)
    dw = tn(n_ref[...], dh)
    if cube:
        dw = dw.reshape(4, 2, 2, 2, 24, BLOCK)

        def put(ref, p, q, value):
            ref[:, p, q] = value.astype(ref.dtype)

        write_shares(lambda y, x, c: dw[:, y, x, c], *refs, put)
    else:
        refs[0][...] = dw


def inner_back(dbr, n, gp, wo, cube):
    t = n.shape[0]
    fblk = pl.BlockSpec((t, BLOCK), lambda j: (0, j))
    if cube:
        spec = pl.BlockSpec((4, 2, 2, 24, BLOCK), lambda j: (0, 0, 0, 0, j))
        specs, shapes = [spec] * 2, [S((4, 2, 2, 24, FF), KEEP), S((4, 2, 2, 24, FF), low)]
    else:
        specs, shapes = [pl.BlockSpec((D, BLOCK), lambda j: (0, j))], [S((D, FF), f32)]
    return pl.pallas_call(
        lambda *refs: inner_back_body(cube, *refs),
        grid=(FF // BLOCK,),
        in_specs=[whole((t, D)), whole((t, D)), fblk, pl.BlockSpec((BLOCK, D), lambda j: (j, 0))],
        out_specs=[fblk, whole((4, D))] + specs,
        out_shape=[S((t, FF), low), S((4, D), f32)] + shapes,
        name="inner_back",
        **params(4 * t * D * FF, 4 * t * D + 4 * t * FF + 8 * D * FF),
    )(dbr, n, gp, wo)


KEEP = f32


def mats_body(cube, x_ref, c_ref, dq_ref, dk_ref, dv_ref, dr_ref, *refs):
    x = x_ref[...]
    for m, (rows, grad) in enumerate(((x_ref, dq_ref), (x_ref, dk_ref), (x_ref, dv_ref), (c_ref, dr_ref))):
        full = tn(rows[...], grad[...].astype(low))
        if cube:
            full = full.reshape(4, 2, 2, 2, 24, full.shape[-1])

            def put(ref, p, q, value, m=m):
                ref[:, p, q, m] = value.astype(ref.dtype)

            write_shares(lambda y, x, c: full[:, y, x, c], *refs, put)
        else:
            refs[0][m] = full


def mats(x, c, dq, dk, dv, dr, cube):
    t = x.shape[0]
    wide = 256
    col = pl.BlockSpec((t, wide), lambda j: (0, j))
    if cube:
        spec = pl.BlockSpec((4, 2, 2, 4, 24, wide), lambda j: (0, 0, 0, 0, 0, j))
        specs, shapes = [spec] * 2, [S((4, 2, 2, 4, 24, D), KEEP), S((4, 2, 2, 4, 24, D), low)]
    else:
        specs, shapes = [pl.BlockSpec((4, D, wide), lambda j: (0, 0, j))], [S((4, D, D), f32)]
    return pl.pallas_call(
        lambda *refs: mats_body(cube, *refs),
        grid=(D // wide,),
        in_specs=[whole((t, D)), whole((t, D)), col, col, col, col],
        out_specs=specs,
        out_shape=shapes,
        name="mats",
        **params(8 * t * D * D, 14 * t * D + 16 * D * D),
    )(x, c, dq, dk, dv, dr)


def token_grad_body(dr_ref, dq_ref, dk_ref, dv_ref, wq_ref, wk_ref, wv_ref, o_ref):
    o_ref[...] = (
        dr_ref[...] + nt(dq_ref[...], wq_ref[0]) + nt(dk_ref[...], wk_ref[0]) + nt(dv_ref[...], wv_ref[0])
    )


def token_grad(dr, dq, dk, dv, full):
    t = dr.shape[0]

    return pl.pallas_call(
        token_grad_body,
        grid=(t // ROWS,),
        in_specs=[row_block(D)] * 4 + [mat_of(0), mat_of(1), mat_of(2)],
        out_specs=row_block(D),
        out_shape=S((t, D), f32),
        name="token_grad",
        **params(6 * t * D * D, 14 * t * D + 6 * D * D),
    )(dr, dq, dk, dv, full, full, full)


def loss_body(units_ref, codes_ref, cls_ref, loss_ref, dc_ref, table_ref, ds_ref):
    sources, targets = units_ref[:, :D], units_ref[:, D:]
    pairs, own = units_ref.shape[0], cls_ref.shape[0]
    codes = codes_ref[CODES : CODES + 2, :pairs].astype(f32)
    partner = (codes[0:1] + 64.0 * codes[1:2]).astype(jnp.int32)
    matched = lax.broadcasted_iota(jnp.int32, (pairs, pairs), 0) == partner
    sims = nt(targets, sources) * sim_scale - jnp.where(matched, sim_scale * sim_margin, 0.0)
    row_top = jnp.max(sims, axis=0, keepdims=True)
    row_lse = row_top + jnp.log(jnp.sum(jnp.exp(sims - row_top), axis=0, keepdims=True))
    col_top = jnp.max(sims, axis=1, keepdims=True)
    col_lse = col_top + jnp.log(jnp.sum(jnp.exp(sims - col_top), axis=1, keepdims=True))
    total = (
        jnp.sum(row_lse, axis=1, keepdims=True)
        + jnp.sum(col_lse, axis=0, keepdims=True)
        - 2.0 * jnp.sum(jnp.sum(jnp.where(matched, sims, 0.0), axis=1, keepdims=True), axis=0, keepdims=True)
    )
    loss_ref[...] = jnp.broadcast_to(total * (0.5 / pairs), loss_ref.shape)
    d_sims = 0.5 * (jnp.exp(sims - row_lse) + jnp.exp(sims - col_lse)) - jnp.where(matched, 1.0, 0.0)
    d_low = (d_sims * sim_scale).astype(low)
    table_ref[...] = nn(d_low, sources)
    ds_ref[...] = tn(d_low, targets)
    mine = pl.ds(pl.multiple_of(lax.axis_index(AXIS) * own, own), own)
    for side, ref in enumerate((ds_ref, table_ref)):
        cols = pl.ds(side * D, D)
        cls, du = cls_ref[:, cols], ref[mine, :]
        inv = lax.rsqrt(jnp.sum(cls * cls, axis=-1, keepdims=True) + pool_eps)
        dc_ref[:, cols] = inv * du - cls * (inv * inv * inv * jnp.sum(du * cls, axis=-1, keepdims=True))


def pair_loss(units, vec, cls):
    pairs, own = units.shape[0], cls.shape[0]
    loss, dc = pl.pallas_call(
        loss_body,
        in_specs=[whole(units.shape), whole(vec.shape), whole(cls.shape)],
        out_specs=[whole((8, 128)), whole(cls.shape)],
        out_shape=[S((8, 128), f32), S(cls.shape, f32)],
        scratch_shapes=[pltpu.VMEM((pairs, D), f32), pltpu.VMEM((pairs, D), f32)],
        grid=(1,),
        name="pair_loss",
        **params(6 * pairs * pairs * D, 4 * pairs * D, 4 * pairs * pairs),
    )(units, vec, cls)
    return loss[0, 0], dc


CUBE = 32
CORE = [(i, i ^ 1) for i in range(CUBE)]
FAR_Z = [(i, i ^ 16) for i in range(CUBE)]
NEAR_Z = [(i, i ^ 8) for i in range(CUBE)]
FIRST = [(i, i ^ (4 if i & 1 else 2)) for i in range(CUBE)]
SECOND = [(i, i ^ (2 if i & 1 else 4)) for i in range(CUBE)]
ROUTES = (CORE, FIRST, SECOND, NEAR_Z, FAR_Z)


class Place:
    def __init__(self):
        self.me = lax.axis_index(AXIS)
        self.core = self.me & 1
        x, y = (self.me >> 1) & 1, (self.me >> 2) & 1
        self.near_z, self.far_z = (self.me >> 3) & 1, (self.me >> 4) & 1
        self.first = jnp.where(self.core == 0, x, y)
        self.second = jnp.where(self.core == 0, y, x)


def join(own, other, axis, bit):
    shape = own.shape[:axis] + (2,) + own.shape[axis:]
    where = lax.broadcasted_iota(jnp.int32, shape, axis)
    return jnp.where(where == bit, jnp.expand_dims(own, axis), jnp.expand_dims(other, axis))


def pick(field, axis, bit):
    return lax.dynamic_index_in_dim(field, bit, axis, keepdims=False)


def send(field, route):
    return lax.ppermute(field, AXIS, route)


def spread(block, place):
    block = join(block, send(block, FAR_Z), 0, place.far_z)
    block = join(block, send(block, NEAR_Z), 1, place.near_z)
    return join(block, send(block, FIRST), 2, place.first)


def gather_blocks(block, place):
    near = spread(block, place)
    block = join(near, send(near, SECOND), 3, place.second)
    other = send(block, CORE)
    zero = jnp.where(place.core == 0, block, other)
    one = jnp.where(place.core == 0, other, block)
    return jnp.stack([jnp.swapaxes(zero, 2, 3), one], axis=4).reshape(-1, block.shape[-1])


def together(*values):
    return lax.optimization_barrier(values)


class Reduction:
    def __init__(self, keep, came, place):
        self.stages = ((2, place.first), (2, place.second), (1, place.near_z), (0, place.far_z))
        shape = (2, 2, *keep.shape[1:])
        self.total = keep.reshape(shape).astype(f32) + came.reshape(shape).astype(f32)

    def split(self, stage):
        axis, bit = self.stages[stage]
        return pick(self.total, axis, bit), pick(self.total, axis, 1 - bit).astype(low)

    def meet(self, kept, came):
        self.total = kept + came.astype(f32)
        return self


def spread_rows(rows, at, count):
    r = rows.shape[1]
    lane = lax.broadcasted_iota(jnp.int32, (r, D), 1)
    copies = nn(rows, jnp.where(lane % r == lax.broadcasted_iota(jnp.int32, (r, D), 0), 1.0, 0.0).astype(low))
    lane = lax.broadcasted_iota(jnp.int32, (count, D), 1)
    row = lax.broadcasted_iota(jnp.int32, (count, D), 0)
    return copies, lane // r, row


def vector_table(vectors, partners, place):
    *small, inner = vectors
    copies, lane, _ = spread_rows(jnp.stack(small), place.me, len(small))
    table = [jnp.where(lane == place.me, copies, 0.0)]
    fold = D // inner.shape[0]
    copies, lane, row = spread_rows(inner[None], place.me, FF // D)
    table.append(jnp.where((row == place.me // fold) & (lane == place.me % fold), copies, 0.0))
    codes = jnp.stack([partners % 64, partners // 64]).astype(low)
    copies, lane, _ = spread_rows(codes, place.me, 2)
    table.append(jnp.where(lane == place.me, copies, 0.0))
    table.append(jnp.zeros((2, D), f32))
    table = jnp.concatenate(table, axis=0).astype(low)
    for route in (FAR_Z, NEAR_Z, FIRST, SECOND, CORE):
        table = table + send(table, route)
    return table


def own_vectors(sums_attn, sums_ffn, place):
    total = jnp.concatenate([sums_attn, sums_ffn], axis=0)
    for route in ROUTES:
        total = total + send(total.astype(low), route).astype(f32)
    r, fold = D // CUBE, FF // CUBE
    mine = lax.dynamic_slice(total, (0, place.me * r), (16, r))
    inner = lax.dynamic_slice(total, (11 + place.me // (D // fold), (place.me % (D // fold)) * fold), (1, fold))
    return [mine[i] for i in (0, 1, 2, 3, 4, 8, 9, 10)] + [inner[0]]


def pack_body(*refs):
    *mats, out, sems = refs
    r = mats[0].shape[0]
    copies = [pltpu.make_async_copy(m, out.at[pl.ds(i * r, r), :], sems.at[i]) for i, m in enumerate(mats)]
    for copy in copies:
        copy.start()
    for copy in copies:
        copy.wait()


def pack(*mats):
    r, n = mats[0].shape
    return pl.pallas_call(
        pack_body,
        in_specs=[ANY] * len(mats),
        out_specs=ANY,
        out_shape=S((len(mats) * r, n), low),
        scratch_shapes=[pltpu.SemaphoreType.DMA((len(mats),))],
        name="pack",
    )(*mats)


def plain_loss(units, partners, cls):
    sources, targets = units[:, :D], units[:, D:]
    npairs, own = units.shape[0], cls.shape[0]
    sims = nt(sources, targets) * sim_scale
    matched = partners[:, None] == jnp.arange(npairs, dtype=jnp.int32)[None, :]
    sims = sims - jnp.where(matched, sim_scale * sim_margin, 0.0)
    row_top = jnp.max(sims, axis=1, keepdims=True)
    row_lse = row_top + jnp.log(jnp.sum(jnp.exp(sims - row_top), axis=1, keepdims=True))
    col_top = jnp.max(sims, axis=0, keepdims=True)
    col_lse = col_top + jnp.log(jnp.sum(jnp.exp(sims - col_top), axis=0, keepdims=True))
    positive = jnp.sum(jnp.where(matched, sims, 0.0))
    loss = (jnp.sum(row_lse) + jnp.sum(col_lse) - 2.0 * positive) / (2.0 * npairs)
    d_sims = 0.5 * (jnp.exp(sims - row_lse) + jnp.exp(sims - col_lse)) - jnp.where(matched, 1.0, 0.0)
    d_low = (d_sims * sim_scale).astype(low)
    first = lax.axis_index(AXIS) * own
    du = [
        nn(lax.dynamic_slice_in_dim(d_low, first, own, 0), targets),
        tn(lax.dynamic_slice_in_dim(d_low, first, own, 1), sources),
    ]
    dc = []
    for side in range(2):
        c = cls[:, side * D : (side + 1) * D]
        inv = lax.rsqrt(jnp.sum(c * c, axis=-1, keepdims=True) + pool_eps)
        dc.append(inv * du[side] - c * (inv * inv * inv * jnp.sum(du[side] * c, axis=-1, keepdims=True)))
    return loss, jnp.concatenate(dc, axis=1)


def every(v):
    return lax.all_gather(v, AXIS, axis=0, tiled=True)


def scatter(v):
    return lax.psum_scatter(v, AXIS, scatter_dimension=0, tiled=True)


def local(
    tokens,
    lengths,
    partners,
    out_cotangent,
    w_query,
    w_key,
    w_value,
    w_output,
    b_query,
    b_value,
    b_output,
    gain_attn,
    shift_attn,
    w_inner,
    b_inner,
    w_outer,
    b_outer,
    gain_ffn,
    shift_ffn,
):
    cube = lax.axis_size(AXIS) == CUBE
    count = tokens.shape[0]
    x = tokens.reshape(count * LEN, D)
    vectors = (b_query, b_value, b_output, gain_attn, shift_attn, b_outer, gain_ffn, shift_ffn, b_inner)
    if cube:
        place = Place()
        attn = pack(w_query, w_key, w_value, w_output)
        attn = join(attn, send(attn, FAR_Z), 0, place.far_z)
        attn = join(attn, send(attn, NEAR_Z), 1, place.near_z)
        w_inner, attn = together(w_inner, attn)
        inn = join(w_inner, send(w_inner, FAR_Z), 0, place.far_z)
        attn = join(attn, send(attn, FIRST), 2, place.first)
        w_outer, inn, attn = together(w_outer, inn, attn)
        out = join(w_outer, send(w_outer, FAR_Z), 0, place.far_z)
        inn = join(inn, send(inn, NEAR_Z), 1, place.near_z)
        vec = vector_table(vectors, partners, place)
        attn_near = attn.reshape(4, 2, 96, D)
        attn_far = send(attn_near, SECOND)
        inn, attn_far = together(inn, attn_far)
        out = join(out, send(out, NEAR_Z), 1, place.near_z)
        attn_parts = (attn_near, attn_far, send(attn_near, CORE), send(attn_far, CORE))
        attn_parts, inn = together(attn_parts, inn)
        inn = join(inn, send(inn, FIRST), 2, place.first).reshape(4, 2, 24, FF)
        queries, keys, values, full = project(x, vec, attn_parts, cube)
        queries, inn, out = together(queries, inn, out)
        blocks = count * LEN // ROWS
        inn_far = send(inn, SECOND)
        out = join(out, send(out, FIRST), 2, place.first).reshape(4, 2, 96, D)
        upper = attend(lengths, x, queries, keys, values, full, vec, 0, blocks // 2)
        upper, inn, inn_far, out = together(upper, inn, inn_far, out)
        inn_parts = (inn, inn_far, send(inn, CORE), send(inn_far, CORE))
        out_far = send(out, SECOND)
        probs, context, hat1, inv1, normed = attend(
            lengths, x, queries, keys, values, full, vec, blocks // 2, blocks - blocks // 2, upper
        )
        normed, inn_parts = together(normed, inn_parts)
        act, slope, inner_mat = inner(normed, vec, inn_parts, cube)
        out_parts = (out, out_far, send(out, CORE), send(out_far, CORE))
        block_out, hat2, inv2, cls, unit, outer_mat = outer(act, hat1, vec, out_parts, cube)
        loss, d_cls = pair_loss(gather_blocks(unit.astype(low), place), vec, cls)
        dres, dbr, sums_outer, keep_o, away_o = outer_back(
            out_cotangent.reshape(count * LEN, D), d_cls, hat2, inv2, act, vec, cube
        )
        dbr, away_o = together(dbr, away_o)
        came_o = send(away_o, CORE)
        dh, sums_inner, keep_i, away_i = inner_back(dbr, normed, slope, outer_mat, cube)
        out, inn = Reduction(keep_o, came_o, place), None
        kept_o, away_o = out.split(0)
        dh, kept_o, away_o, away_i = together(dh, kept_o, away_o, away_i)
        came_i, came_o = send(away_i, CORE), send(away_o, FIRST)
        upper = attend_back(dres, dh, inner_mat, hat1, inv1, full, queries, keys, values, probs, vec, 0, blocks // 2)
        inn = Reduction(keep_i, came_i, place)
        kept_i, away_i = inn.split(0)
        kept_o, away_o = out.meet(kept_o, came_o).split(1)
        upper, kept_i, away_i, kept_o, away_o = together(upper, kept_i, away_i, kept_o, away_o)
        came_i, came_o = send(away_i, FIRST), send(away_o, SECOND)
        d_resid, d_queries, d_keys, d_values, sums_lower = attend_back(
            dres, dh, inner_mat, hat1, inv1, full, queries, keys, values, probs, vec,
            blocks // 2, blocks - blocks // 2, upper[:4],
        )
        kept_i, away_i = inn.meet(kept_i, came_i).split(1)
        kept_o, away_o = out.meet(kept_o, came_o).split(2)
        d_resid, kept_i, away_i, kept_o, away_o = together(d_resid, kept_i, away_i, kept_o, away_o)
        came_i, came_o = send(away_i, SECOND), send(away_o, NEAR_Z)
        keep_a, away_a = mats(x, context, d_queries, d_keys, d_values, d_resid, cube)
        kept_i, away_i = inn.meet(kept_i, came_i).split(2)
        kept_o, away_o = out.meet(kept_o, came_o).split(3)
        keep_a, away_a, kept_i, away_i, kept_o, away_o, d_resid = together(
            keep_a, away_a, kept_i, away_i, kept_o, away_o, d_resid
        )
        came_a, came_i, came_o = send(away_a, CORE), send(away_i, NEAR_Z), send(away_o, FAR_Z)
        grad_rows = token_grad(d_resid, d_queries, d_keys, d_values, full)
        grad_w_outer = out.meet(kept_o, came_o).total
        kept_i, away_i = inn.meet(kept_i, came_i).split(3)
        att = Reduction(keep_a, came_a, place)
        kept_a, away_a = att.split(0)
        kept_i, away_i, kept_a, away_a, grad_rows = together(kept_i, away_i, kept_a, away_a, grad_rows)
        grad_w_inner = inn.meet(kept_i, send(away_i, FAR_Z)).total
        for stage in range(3):
            kept_a, away_a = att.meet(kept_a, send(away_a, ROUTES[1 + stage])).split(stage + 1)
        g_mats = att.meet(kept_a, send(away_a, FAR_Z)).total
        sums_ffn = jnp.concatenate([sums_outer[:3], sums_inner, sums_outer[3:4]], axis=0)
        grads = own_vectors(upper[4] + sums_lower, sums_ffn, place)
    else:
        rows = [every(v).reshape(-1, D) for v in vectors]
        vec = jnp.concatenate(rows + [jnp.zeros((4, D), low)], axis=0)
        mats_in = (jnp.stack([every(w) for w in (w_query, w_key, w_value, w_output)]),)
        blocks = count * LEN // ROWS
        queries, keys, values, full = project(x, vec, mats_in, cube)
        probs, context, hat1, inv1, normed = attend(lengths, x, queries, keys, values, full, vec, 0, blocks)
        act, slope, inner_mat = inner(normed, vec, (every(w_inner),), cube)
        block_out, hat2, inv2, cls, unit, outer_mat = outer(act, hat1, vec, (every(w_outer),), cube)
        loss, d_cls = plain_loss(every(unit.astype(low)), every(partners), cls)
        dres, dbr, sums_outer, d_outer = outer_back(
            out_cotangent.reshape(count * LEN, D), d_cls, hat2, inv2, act, vec, cube
        )
        dh, sums_inner, d_inner = inner_back(dbr, normed, slope, outer_mat, cube)
        d_resid, d_queries, d_keys, d_values, sums_attn = attend_back(
            dres, dh, inner_mat, hat1, inv1, full, queries, keys, values, probs, vec, 0, blocks
        )
        (d_mats,) = mats(x, context, d_queries, d_keys, d_values, d_resid, cube)
        grad_rows = token_grad(d_resid, d_queries, d_keys, d_values, full)
        grad_w_outer, grad_w_inner = scatter(d_outer), scatter(d_inner)
        g_mats = [scatter(d_mats[m]) for m in range(4)]
        grads = [scatter(sums_attn[i]) for i in range(5)] + [scatter(sums_outer[i]) for i in range(3)]
        grads.append(scatter(sums_inner.reshape(-1)))
    (
        grad_b_query,
        grad_b_value,
        grad_b_output,
        grad_gain_attn,
        grad_shift_attn,
        grad_b_outer,
        grad_gain_ffn,
        grad_shift_ffn,
        grad_b_inner,
    ) = grads
    return (
        loss,
        block_out.reshape(count, LEN, D),
        grad_rows.reshape(count, LEN, D),
        g_mats[0],
        g_mats[1],
        g_mats[2],
        g_mats[3],
        grad_b_query,
        grad_b_value,
        grad_b_output,
        grad_gain_attn,
        grad_shift_attn,
        grad_w_inner,
        grad_b_inner,
        grad_w_outer,
        grad_b_outer,
        grad_gain_ffn,
        grad_shift_ffn,
    )


def solution(mesh):
    rows, cols = P(AXIS), P(AXIS, None)
    cube = P(AXIS, None, None)
    in_specs = (cube, rows, rows, cube) + (cols,) * 4 + (rows,) * 5 + (cols, rows, cols) + (rows,) * 3
    out_specs = (P(), cube, cube) + (cols,) * 4 + (rows,) * 5 + (cols, rows, cols) + (rows,) * 3
    return jax.shard_map(local, mesh=mesh, in_specs=in_specs, out_specs=out_specs, check_vma=False)
```

time: 1330 us -> 378 us (0.28)
  waiting for transfers between devices: 842 us -> 128 us
  Pallas kernels: 0 us -> 169 us
  matrix products: 169 us -> 0.42 us
  blocking collectives: 164 us -> 0 us
  local copies, waits for them, and re-layouts: 95.3 us -> 10.4 us
  starting transfers between devices: 0.52 us -> 41.6 us
  between operations: 19 us -> 1.96 us
    reduce_scatter x4 -> x0, waiting for transfers between devices: 375 us -> none  [the longest x1 142 us: local(): lax.psum_scatter(d_outer_mat, 'fsdp', scatter_dimension=0, tiled=True)]
    unnamed x16 -> x0, waiting for transfers between devices: 247 us -> none
    all_gather x6 -> x0, waiting for transfers between devices: 220 us -> none  [the longest x1 61 us: local(): lax.all_gather(w_inner, 'fsdp', axis=0, tiled=True)]
    pallas_call x0 -> x13, Pallas kernels: none -> 169 us  [the longest x2 37.7 us: attend_back(): pl.pallas_call(attend_back_body, grid=(count,), in_specs=[rows(D), rows(F...]
    dot_general x27 -> x3, matrix products: 169 us -> 0.42 us  [nn(): lax.dot_general(a, b, (((1,), (0,)), ((), ())), preferred_element_type=f32)]
    ppermute x0 -> x48, waiting for transfers between devices: none -> 128 us  [send(): return lax.ppermute(field, AXIS, route)]
    psum x2 -> x0, blocking collectives: 77.6 us -> none  [local(): col_total, loss_total = lax.psum((col_part, local_loss), 'fsdp')]
    all_gather x1 -> x0, blocking collectives: 44.2 us -> none  [local(): every_unit = lax.all_gather(unit_low, 'fsdp', axis=0, tiled=True)]
  transfers between devices with their start and end apart: 13 -> 48, of which waited for: 12 -> 30; matrix products, arithmetic and copies ran while one was open for 16% -> 4% of each run, Pallas kernels for 0% -> 36%
where the time goes in v2:
time: 378 us; the launch traced here: 375 us
  Pallas kernels  169 us (45%)
  waiting for transfers between devices  128 us (34%)
  starting transfers between devices  41.6 us (11%)
  other arithmetic  23.4 us (6%)
  local copies, waits for them, and re-layouts  10.4 us (3%)
    ppermute x48, waiting for transfers between devices, send(): return lax.ppermute(field, AXIS, route)  128 us
    ppermute x48, starting transfers between devices, send(): return lax.ppermute(field, AXIS, route)  41.6 us
    pallas_call x2, Pallas kernels, attend_back(): pl.pallas_call(attend_back_body, grid=(count,), in_specs=[rows(D), rows(F...  37.7 us
    pallas_call x1, Pallas kernels, inner(): pl.pallas_call(lambda *refs: inner_body(cube, *refs), grid=(t // ROWS,),...  22.4 us
    pallas_call x2, Pallas kernels, attend(): pl.pallas_call(lambda *refs: attend_body(start, *refs), grid_spec=pltpu.P...  22.2 us
    pallas_call x1, Pallas kernels, mats(): pl.pallas_call(lambda *refs: mats_body(cube, *refs), grid=(D // wide,), i...  16.8 us
    pallas_call x1, Pallas kernels, inner_back(): pl.pallas_call(lambda *refs: inner_back_body(cube, *refs), grid=(FF // BL...  15.8 us
    pallas_call x1, Pallas kernels, outer_back(): pl.pallas_call(lambda *refs: outer_back_body(cube, *refs), grid=(FF // BL...  14.8 us
  transfers between devices with their start and end apart: 48, of which 30 were waited for; matrix products, arithmetic and copies ran while one was open for 4% of the time, Pallas kernels for 36%

profile of v2, /device:TPU:0, one launch (start us, length us, event | category | flops | bytes accessed | tf_op | source)
XLA Modules:
  0.0 374.6 jit_solution(4761559319141590804)
XLA Ops:
  0.7 5.6 %pack.1 = bf16[96,768]{1,0:T(8,128)(2,1)} custom-call(bf16[24,768]{1,0:T(8,128)(2,1)} %refs_0_.3, bf16[24,768]{1,0:T(8,128)(2,1)} %refs_1_.1, bf16[24,768]{1,0:T(8,128)(2,1)} %refs_2_.1, bf16[24,768]{1,0:T(8,128)(2,1)} %refs_3_.1), custom_call_target="tpu_custom_call" | custom-call | tf_op jit(solution)/shard_map/pack/pallas_call | solution.py:717
  6.3 4.1 %collective-permute-start.5 = (bf16[96,768]{1,0:T(8,128)(2,1)}, bf16[96,768]{1,0:T(8,128)(2,1)S(1)}, u32[]{:S(2)}, u32[]{:S(2)}) collective-permute-start(bf16[96,768]{1,0:T(8,128)(2,1)} %pack.1), channel_id=1, source_target_pairs={{0,16},{1,17},{2,18},{3,19},{4,20},{5,21},{6,22},{7,23},{8,24},{9,... | collective-permute-start | bytes 442376 | tf_op jit(solution)/shard_map/ppermute | solution.py:632
  11.3 6.3 %collective-permute-done.5 = bf16[96,768]{1,0:T(8,128)(2,1)S(1)} collective-permute-done((bf16[96,768]{1,0:T(8,128)(2,1)}, bf16[96,768]{1,0:T(8,128)(2,1)S(1)}, u32[]{:S(2)}, u32[]{:S(2)}) %collective-permute-start.5) | collective-permute-done | bytes 147488 | tf_op jit(solution)/shard_map/ppermute | solution.py:632
  19.6 7.3 %collective-permute-done.6 = bf16[2,96,768]{2,1,0:T(8,128)(2,1)S(1)} collective-permute-done((bf16[2,96,768]{2,1,0:T(8,128)(2,1)S(1)}, bf16[2,96,768]{2,1,0:T(8,128)(2,1)S(1)}, u32[]{:S(2)}, u32[]{:S(2)}) %collective-permute-start.6) | collective-permute-done | bytes 294944 | tf_op jit(solution)/shard_map/ppermute | solution.py:632
  27.1 3.2 collective-permute-start.7
  30.3 1.5 collective-permute-start.8
  31.8 5.2 %collective-permute-done.7 = bf16[24,3072]{1,0:T(8,128)(2,1)S(1)} collective-permute-done((bf16[24,3072]{1,0:T(8,128)(2,1)S(1)}, bf16[24,3072]{1,0:T(8,128)(2,1)S(1)}, u32[]{:S(2)}, u32[]{:S(2)}) %collective-permute-start.7) | collective-permute-done | bytes 147488 | tf_op jit(solution)/shard_map/ppermute | solution.py:632
  37.1 3.1 collective-permute-done.8
  40.4 1.6 collective-permute-start.10
  42.0 1.7 collective-permute-start.9
  43.8 5.1 %collective-permute-done.9 = bf16[2,24,3072]{2,1,0:T(8,128)(2,1)S(1)} collective-permute-done((bf16[2,24,3072]{2,1,0:T(8,128)(2,1)S(1)}, bf16[2,24,3072]{2,1,0:T(8,128)(2,1)S(1)}, u32[]{:S(2)}, u32[]{:S(2)}) %collective-permute-start.9) | collective-permute-done | bytes 294944 | tf_op jit(solution)/shard_map/ppermute | solution.py:632
  49.1 7.7 %collective-permute-done.10.refs_3_ = bf16[4,2,96,768]{3,2,1,0:T(8,128)(2,1)} collective-permute-done((bf16[4,2,96,768]{3,2,1,0:T(8,128)(2,1)S(1)}, bf16[4,2,96,768]{3,2,1,0:T(8,128)(2,1)}, u32[]{:S(2)}, u32[]{:S(2)}) %collective-permute-start.10) | collective-permute-done | bytes 1179680 | tf_op jit(solution)/shard_map/ppermute | solution.py:632
  57.3 2.8 collective-permute-start
  60.1 8.1 %collective-permute-done.14 = bf16[96,768]{1,0:T(8,128)(2,1)S(1)} collective-permute-done((bf16[96,768]{1,0:T(8,128)(2,1)S(1)}, bf16[96,768]{1,0:T(8,128)(2,1)S(1)}, u32[]{:S(2)}, u32[]{:S(2)}) %collective-permute-start.14) | collective-permute-done | bytes 147488 | tf_op jit(solution)/shard_map/ppermute | solution.py:632
  68.5 1.9 collective-permute-start.1
  70.5 6.8 %collective-permute-done.1 = bf16[16,768]{1,0:T(8,128)(2,1)S(1)} collective-permute-done((bf16[16,768]{1,0:T(8,128)(2,1)S(1)}, bf16[16,768]{1,0:T(8,128)(2,1)S(1)}, u32[]{:S(2)}, u32[]{:S(2)}) %collective-permute-start.1) | collective-permute-done | bytes 24608 | tf_op jit(solution)/shard_map/ppermute | solution.py:632
  77.3 1.6 collective-permute-start.2
  78.8 2.3 collective-permute-done.2
  81.2 1.6 collective-permute-start.3
  82.8 2.3 collective-permute-done.3
  87.0 1.5 collective-permute-start.13
  88.6 9.4 %project.1 = (bf16[1024,768]{1,0:T(8,128)(2,1)}, bf16[1024,768]{1,0:T(8,128)(2,1)}, bf16[1024,768]{1,0:T(8,128)(2,1)}, bf16[4,4,2,2,2,24,768]{6,5,4,3,2,1,0:T(8,128)(2,1)}) custom-call(bf16[1024,768]{1,0:T(8,128)(2,1)} %bitcast.131, bf16[16,768]{1,0:T(8,128)(2,1)} %add.203.refs_1_.refs_6_.refs_2_.codes_ref.refs_5_.vec_ref, ...), custom_call_target="tpu_custom_call" | custom-call | flops 3623878656 | bytes 15728640 | tf_op jit(solution)/shard_map/project/pallas_call | solution.py:126
  98.2 1.6 collective-permute-start.16
  100.3 11.1 %attend.2 = (f32[3072,256]{1,0:T(8,128)}, bf16[1024,768]{1,0:T(8,128)(2,1)}, f32[1024,768]{1,0:T(8,128)}, f32[1024,1]{1,0:T(8,128)}, bf16[1024,768]{1,0:T(8,128)(2,1)}) custom-call(s32[16]{0:T(128)} %refs_0_.5, bf16[1024,768]{1,0:T(8,128)(2,1)} %bitcast.132, bf16[1024,768]{1,0:T(8,128)(2,1)} %get-tuple-element.137.refs_2_.q_ref, ...), custom_call_target="tpu_custom_call" | custom-call | flops 3623878656 | bytes 10223616 | tf_op jit(solution)/shard_map/attend/pallas_call | solution.py:211
  111.4 4.7 %collective-permute-done.17 = bf16[2,2,96,768]{3,2,1,0:T(8,128)(2,1)S(1)} collective-permute-done((bf16[2,2,96,768]{3,2,1,0:T(8,128)(2,1)S(1)}, bf16[2,2,96,768]{3,2,1,0:T(8,128)(2,1)S(1)}, u32[]{:S(2)}, u32[]{:S(2)}) %collective-permute-start.17) | collective-permute-done | bytes 589856 | tf_op jit(solution)/shard_map/ppermute | solution.py:632
  116.2 4.7 %collective-permute-done.16.refs_3_ = bf16[4,2,24,3072]{3,2,1,0:T(8,128)(2,1)} collective-permute-done((bf16[4,2,24,3072]{3,2,1,0:T(8,128)(2,1)S(1)}, bf16[4,2,24,3072]{3,2,1,0:T(8,128)(2,1)}, u32[]{:S(2)}, u32[]{:S(2)}) %collective-permute-start.16) | collective-permute-done | bytes 1179680 | tf_op jit(solution)/shard_map/ppermute | solution.py:632
  122.1 11.1 %attend.3 = (f32[3072,256]{1,0:T(8,128)}, bf16[1024,768]{1,0:T(8,128)(2,1)}, f32[1024,768]{1,0:T(8,128)}, f32[1024,1]{1,0:T(8,128)}, bf16[1024,768]{1,0:T(8,128)(2,1)}) custom-call(s32[16]{0:T(128)} %refs_0_.5, bf16[1024,768]{1,0:T(8,128)(2,1)} %bitcast.133, ...), custom_call_target="tpu_custom_call", output_to_operand_aliasing={{0}: (7, {}), {1}: (8, {}), {2}: (9, {}), {3}: (10, {}), {4... | custom-call | flops 3623878656 | bytes 10223616 | tf_op jit(solution)/shard_map/attend/pallas_call | solution.py:211
  133.2 4.4 %collective-permute-done.20.refs_4_ = bf16[4,2,96,768]{3,2,1,0:T(8,128)(2,1)S(1)} collective-permute-done((bf16[4,2,96,768]{3,2,1,0:T(8,128)(2,1)S(1)}, bf16[4,2,96,768]{3,2,1,0:T(8,128)(2,1)S(1)}, u32[]{:S(2)}, u32[]{:S(2)}) %collective-permute-start.20) | collective-permute-done | bytes 1179680 | tf_op jit(solution)/shard_map/ppermute | solution.py:632
  137.6 22.4 %inner.1 = (bf16[1024,3072]{1,0:T(8,128)(2,1)}, bf16[1024,3072]{1,0:T(8,128)(2,1)}, bf16[4,2,2,2,24,3072]{5,4,3,2,1,0:T(8,128)(2,1)}) custom-call(bf16[1024,768]{1,0:T(8,128)(2,1)} %get-tuple-element.156.refs_0_.refs_1_, bf16[16,768]{1,0:T(8,128)(2,1)} %add.203.refs_1_.refs_6_.refs_2_.codes_ref.refs_5_.vec_ref, bf16[4,2,24,3072]{3,2,1,0:T(8,128)(2,1)} %copy-done.4, ...), custom_call_target="tpu_custom_call" | custom-call | flops 14495514624 | bytes 23592960 | tf_op jit(solution)/shard_map/inner/pallas_call | solution.py:329
  161.1 12.6 %outer.1 = (bf16[1024,768]{1,0:T(8,128)(2,1)}, f32[1024,768]{1,0:T(8,128)}, f32[1024,1]{1,0:T(8,128)}, f32[8,1536]{1,0:T(8,128)}, f32[8,1536]{1,0:T(8,128)}, /*index=5*/bf16[4,2,2,2,96,768]{5,4,3,2,1,0:T(8,128)(2,1)}) custom-call(bf16[1024,3072]{1,0:T(8,128)(2,1)} %get-tuple-element.161.refs_0_.refs_4_, f32[1024,768]{1,0:T(8,128)} %get-tuple-element.162.refs_1_.hat_ref, ...), custom_call_target="tpu_custom_call" | custom-call | flops 4831838208 | bytes 23592960 | tf_op jit(solution)/shard_map/outer/pallas_call | solution.py:374
  174.9 4.3 %collective-permute-done.23 = bf16[8,1536]{1,0:T(8,128)(2,1)S(1)} collective-permute-done((bf16[8,1536]{1,0:T(8,128)(2,1)S(1)}, bf16[8,1536]{1,0:T(8,128)(2,1)S(1)}, u32[]{:S(2)}, u32[]{:S(2)}) %collective-permute-start.23) | collective-permute-done | bytes 24608 | tf_op jit(solution)/shard_map/ppermute | solution.py:632
  179.6 3.8 %collective-permute-done.24 = bf16[2,8,1536]{2,1,0:T(8,128)(2,1)S(1)} collective-permute-done((bf16[2,8,1536]{2,1,0:T(8,128)(2,1)S(1)}, bf16[2,8,1536]{2,1,0:T(8,128)(2,1)S(1)}, u32[]{:S(2)}, u32[]{:S(2)}) %collective-permute-start.24) | collective-permute-done | bytes 49184 | tf_op jit(solution)/shard_map/ppermute | solution.py:632
  184.1 4.7 %collective-permute-done.25 = bf16[2,2,8,1536]{3,2,1,0:T(8,128)(2,1)S(1)} collective-permute-done((bf16[2,2,8,1536]{3,2,1,0:T(8,128)(2,1)S(1)}, bf16[2,2,8,1536]{3,2,1,0:T(8,128)(2,1)S(1)}, u32[]{:S(2)}, u32[]{:S(2)}) %collective-permute-start.25) | collective-permute-done | bytes 98336 | tf_op jit(solution)/shard_map/ppermute | solution.py:632
  189.6 5.0 %collective-permute-done.26 = bf16[2,2,2,8,1536]{4,3,2,1,0:T(8,128)(2,1)S(1)} collective-permute-done((bf16[2,2,2,8,1536]{4,3,2,1,0:T(8,128)(2,1)S(1)}, bf16[2,2,2,8,1536]{4,3,2,1,0:T(8,128)(2,1)S(1)}, u32[]{:S(2)}, u32[]{:S(2)}) %collective-permute-start.26) | collective-permute-done | bytes 196640 | tf_op jit(solution)/shard_map/ppermute | solution.py:632
  194.7 1.7 collective-permute-done.27
  197.6 2.9 pair_loss.1
  200.5 14.8 %outer_back.1 = (f32[1024,768]{1,0:T(8,128)}, bf16[1024,768]{1,0:T(8,128)(2,1)}, f32[8,768]{1,0:T(8,128)}, f32[4,2,2,96,768]{4,3,2,1,0:T(8,128)}, bf16[4,2,2,96,768]{4,3,2,1,0:T(8,128)(2,1)}) custom-call(bf16[1024,768]{1,0:T(8,128)(2,1)} %bitcast.149, f32[8,1536]{1,0:T(8,128)} %get-tuple-element.169.refs_1_, f32[1024,768]{1,0:T(8,128)} %get-tuple-element.170.refs_2_, ...), custom_call_target="tpu_custom_call" | custom-call | flops 9663676416 | bytes 36175872 | tf_op jit(solution)/shard_map/outer_back/pallas_call | solution.py:453
  215.5 15.8 %inner_back.1 = (bf16[1024,3072]{1,0:T(8,128)(2,1)}, f32[4,768]{1,0:T(4,128)}, f32[4,2,2,24,3072]{4,3,2,1,0:T(8,128)}, bf16[4,2,2,24,3072]{4,3,2,1,0:T(8,128)(2,1)}) custom-call(bf16[1024,768]{1,0:T(8,128)(2,1)} %get-tuple-element.175.refs_0_, bf16[1024,768]{1,0:T(8,128)(2,1)} %get-tuple-element.156.refs_0_.refs_1_, ...), custom_call_target="tpu_custom_call" | custom-call | flops 9663676416 | bytes 34603008 | tf_op jit(solution)/shard_map/inner_back/pallas_call | solution.py:489
  231.3 3.0 convert_add_fusion.2
  235.6 18.7 %attend_back.2 = (f32[1024,768]{1,0:T(8,128)}, bf16[1024,768]{1,0:T(8,128)(2,1)}, bf16[1024,768]{1,0:T(8,128)(2,1)}, bf16[1024,768]{1,0:T(8,128)(2,1)}, f32[8,768]{1,0:T(8,128)}) custom-call(f32[1024,768]{1,0:T(8,128)} %get-tuple-element.172.dres_ref, bf16[1024,3072]{1,0:T(8,128)(2,1)} %get-tuple-element.182.dh_ref, bf16[768,3072]{1,0:T(8,128)(2,1)} %bitcast.120, ...), custom_call_target="tpu_custom_call" | custom-call | flops 7247757312 | bytes 15728640 | tf_op jit(solution)/shard_map/attend_back/pallas_call | solution.py:267
  254.3 1.6 convert_add_fusion.5
  256.9 3.7 convert_add_fusion.1
  260.8 1.2 fusion.1
  262.8 1.5 collective-permute-start.31
  264.2 19.0 %attend_back.3 = (f32[1024,768]{1,0:T(8,128)}, bf16[1024,768]{1,0:T(8,128)(2,1)}, bf16[1024,768]{1,0:T(8,128)(2,1)}, bf16[1024,768]{1,0:T(8,128)(2,1)}, f32[8,768]{1,0:T(8,128)}) custom-call(f32[1024,768]{1,0:T(8,128)} %get-tuple-element.172.dres_ref, ...), custom_call_target="tpu_custom_call", output_to_operand_aliasing={{0}: (11, {}), {1}: (12, {}), {2}: (13, {}), {3}: (14, {})} | custom-call | flops 7247757312 | bytes 15728640 | tf_op jit(solution)/shard_map/attend_back/pallas_call | solution.py:267
  283.3 1.2 convert_add_fusion.7
  285.4 1.6 convert_add_fusion.4
  287.5 1.4 collective-permute-start.33
  288.9 16.8 %mats.1 = (f32[4,2,2,4,24,768]{5,4,3,2,1,0:T(8,128)}, bf16[4,2,2,4,24,768]{5,4,3,2,1,0:T(8,128)(2,1)}) custom-call(bf16[1024,768]{1,0:T(8,128)(2,1)} %bitcast.134, bf16[1024,768]{1,0:T(8,128)(2,1)} %get-tuple-element.168.refs_1_, bf16[1024,768]{1,0:T(8,128)(2,1)} %get-tuple-element.199.refs_2_.dq_ref, bf16[1024,768]{1,0:T(8,128)(2,1)} %get-tuple-element.200.refs_3_.dk_ref, ...), custom_call_target="tpu_custom_call" | custom-call | flops 4831838208 | bytes 20447232 | tf_op jit(solution)/shard_map/mats/pallas_call | solution.py:527
  306.7 1.8 collective-permute-start.35
  308.5 8.9 %token_grad.1 = f32[1024,768]{1,0:T(8,128)} custom-call(f32[1024,768]{1,0:T(8,128)} %get-tuple-element.218.refs_5_.dr_ref, bf16[1024,768]{1,0:T(8,128)(2,1)} %get-tuple-element.199.refs_2_.dq_ref, bf16[1024,768]{1,0:T(8,128)(2,1)} %get-tuple-element.200.refs_3_.dk_ref, bf16[1024,768]{1,0:T(8,128)(2,1)} %get-tuple-element.201.refs_4_.dv_ref, ...), custom_call_target="tpu_custom_call" | custom-call | flops 3623878656 | bytes 14548992 | tf_op jit(solution)/shard_map/token_grad/pallas_call | solution.py:547
  317.6 3.0 convert_add_fusion
  322.9 1.6 collective-permute-start.42
  324.5 13.0 %collective-permute-done.42 = bf16[16,768]{1,0:T(8,128)(2,1)S(1)} collective-permute-done((bf16[16,768]{1,0:T(8,128)(2,1)S(1)}, bf16[16,768]{1,0:T(8,128)(2,1)S(1)}, u32[]{:S(2)}, u32[]{:S(2)}) %collective-permute-start.42) | collective-permute-done | bytes 24608 | tf_op jit(solution)/shard_map/ppermute | solution.py:632
  338.3 3.2 collective-permute-done.43
  343.8 1.5 collective-permute-done.44
  346.0 1.2 slice.45
  347.2 4.9 %collective-permute-done.45 = bf16[16,768]{1,0:T(8,128)(2,1)S(1)} collective-permute-done((bf16[16,768]{1,0:T(8,128)(2,1)S(1)}, bf16[16,768]{1,0:T(8,128)(2,1)S(1)}, u32[]{:S(2)}, u32[]{:S(2)}) %collective-permute-start.45) | collective-permute-done | bytes 24608 | tf_op jit(solution)/shard_map/ppermute | solution.py:632
  353.4 1.2 bitcast_add_fusion
  354.6 1.6 collective-permute-start.39
  356.8 4.9 %collective-permute-done.47 = bf16[96,768]{1,0:T(8,128)(2,1)S(1)} collective-permute-done((bf16[96,768]{1,0:T(8,128)(2,1)S(1)}, bf16[96,768]{1,0:T(8,128)(2,1)S(1)}, u32[]{:S(2)}, u32[]{:S(2)}) %collective-permute-start.47) | collective-permute-done | bytes 147488 | tf_op jit(solution)/shard_map/ppermute | solution.py:632
  362.4 3.2 collective-permute-done.39
  365.9 3.7 collective-permute-done.46
  370.4 3.1 collective-permute-done.40
  (184 shorter events, 30.1 us)
Async XLA Ops:
  0.7 26.3 %copy-start.7 = (bf16[24,3072]{1,0:T(8,128)(2,1)S(1)}, bf16[24,3072]{1,0:T(8,128)(2,1)}, u32[]{:S(2)}) copy-start(bf16[24,3072]{1,0:T(8,128)(2,1)} %param.32) | copy-start | bytes 442372
  6.3 11.3 %collective-permute-start.5 = (bf16[96,768]{1,0:T(8,128)(2,1)}, bf16[96,768]{1,0:T(8,128)(2,1)S(1)}, u32[]{:S(2)}, u32[]{:S(2)}) collective-permute-start(bf16[96,768]{1,0:T(8,128)(2,1)} %pack.1), channel_id=1, source_target_pairs={{0,16},{1,17},{2,18},{3,19},{4,20},{5,21},{6,22},{7,23},{8,24},{9,... | collective-permute-start | bytes 442376 | tf_op jit(solution)/shard_map/ppermute | solution.py:632
  18.6 8.3 %collective-permute-start.6 = (bf16[2,96,768]{2,1,0:T(8,128)(2,1)S(1)}, bf16[2,96,768]{2,1,0:T(8,128)(2,1)S(1)}, u32[]{:S(2)}, u32[]{:S(2)}) collective-permute-start(bf16[2,96,768]{2,1,0:T(8,128)(2,1)S(1)} %broadcast_select_fusion.8), channel_id=1, source_target_pairs={{0,8},{1,9},{2,10},{3,11},{4,12},{5,13},{6,14},{7,15},{8,0},{9,1},... | collective-permute-start | bytes 884744 | tf_op jit(solution)/shard_map/ppermute | solution.py:632
  27.0 29.8 %copy-start.13 = (bf16[24]{0:T(256)(128)(2,1)S(1)}, bf16[24]{0:T(256)(128)(2,1)}, u32[]{:S(2)}) copy-start(bf16[24]{0:T(256)(128)(2,1)} %param.27) | copy-start | bytes 148
  27.0 29.8 %copy-start.14 = (bf16[24]{0:T(256)(128)(2,1)S(1)}, bf16[24]{0:T(256)(128)(2,1)}, u32[]{:S(2)}) copy-start(bf16[24]{0:T(256)(128)(2,1)} %param.28) | copy-start | bytes 148
  27.0 29.8 %copy-start.15 = (bf16[24]{0:T(256)(128)(2,1)S(1)}, bf16[24]{0:T(256)(128)(2,1)}, u32[]{:S(2)}) copy-start(bf16[24]{0:T(256)(128)(2,1)} %param.29) | copy-start | bytes 148
  27.1 29.8 %copy-start.16 = (bf16[24]{0:T(256)(128)(2,1)S(1)}, bf16[24]{0:T(256)(128)(2,1)}, u32[]{:S(2)}) copy-start(bf16[24]{0:T(256)(128)(2,1)} %param.30) | copy-start | bytes 148
  27.1 29.8 %copy-start.17 = (bf16[24]{0:T(256)(128)(2,1)S(1)}, bf16[24]{0:T(256)(128)(2,1)}, u32[]{:S(2)}) copy-start(bf16[24]{0:T(256)(128)(2,1)} %param.31) | copy-start | bytes 148
  27.1 29.8 %copy-start.18 = (bf16[24]{0:T(256)(128)(2,1)S(1)}, bf16[24]{0:T(256)(128)(2,1)}, u32[]{:S(2)}) copy-start(bf16[24]{0:T(256)(128)(2,1)} %param.35) | copy-start | bytes 148
  27.1 29.8 %copy-start.19 = (bf16[24]{0:T(256)(128)(2,1)S(1)}, bf16[24]{0:T(256)(128)(2,1)}, u32[]{:S(2)}) copy-start(bf16[24]{0:T(256)(128)(2,1)} %param.36) | copy-start | bytes 148
  27.1 29.8 %copy-start.20 = (bf16[24]{0:T(256)(128)(2,1)S(1)}, bf16[24]{0:T(256)(128)(2,1)}, u32[]{:S(2)}) copy-start(bf16[24]{0:T(256)(128)(2,1)} %param.37) | copy-start | bytes 148
  27.1 30.0 %copy-start.8 = (bf16[96,768]{1,0:T(8,128)(2,1)S(1)}, bf16[96,768]{1,0:T(8,128)(2,1)}, u32[]{:S(2)}) copy-start(bf16[96,768]{1,0:T(8,128)(2,1)} %param.34) | copy-start | bytes 442372
  27.1 9.8 %collective-permute-start.7 = (bf16[24,3072]{1,0:T(8,128)(2,1)S(1)}, bf16[24,3072]{1,0:T(8,128)(2,1)S(1)}, u32[]{:S(2)}, u32[]{:S(2)}) collective-permute-start(bf16[24,3072]{1,0:T(8,128)(2,1)S(1)} %copy-done.7), channel_id=1, source_target_pairs={{0,16},{1,17},{2,18},{3,19},{4,20},{5,21},{6,22},{7,23},{8,24},{9,... | collective-permute-start | bytes 442376 | tf_op jit(solution)/shard_map/ppermute | solution.py:632
  30.3 9.9 %collective-permute-start.8 = (bf16[2,2,96,768]{3,2,1,0:T(8,128)(2,1)S(1)}, bf16[2,2,96,768]{3,2,1,0:T(8,128)(2,1)S(1)}, u32[]{:S(2)}, u32[]{:S(2)}) collective-permute-start(bf16[2,2,96,768]{3,2,1,0:T(8,128)(2,1)S(1)} %broadcast_select_fusion.5), channel_id=1, source_target_pairs={{0,2},{1,5},{2,0},{3,7},{4,6},{5,1},{6,4},{7,3},{8,10},{9,13},{10,... | collective-permute-start | bytes 1769480 | tf_op jit(solution)/shard_map/ppermute | solution.py:632
  40.4 48.2 %copy-start.3 = (bf16[2,2,2,96,768]{4,3,2,1,0:T(8,128)(2,1)}, bf16[2,2,2,96,768]{4,3,2,1,0:T(8,128)(2,1)S(1)}, u32[]{:S(2)}) copy-start(bf16[2,2,2,96,768]{4,3,2,1,0:T(8,128)(2,1)S(1)} %broadcast_select_fusion.2) | copy-start | bytes 3538948
  40.4 16.4 %collective-permute-start.10 = (bf16[4,2,96,768]{3,2,1,0:T(8,128)(2,1)S(1)}, bf16[4,2,96,768]{3,2,1,0:T(8,128)(2,1)}, u32[]{:S(2)}, u32[]{:S(2)}) collective-permute-start(bf16[4,2,96,768]{3,2,1,0:T(8,128)(2,1)S(1)} %bitcast.135), channel_id=1, source_target_pairs={{0,4},{1,3},{2,6},{3,1},{4,0},{5,7},{6,2},{7,5},{8,12},{9,11},{10,... | collective-permute-start | bytes 3538952 | tf_op jit(solution)/shard_map/ppermute | solution.py:632
  42.0 7.0 %collective-permute-start.9 = (bf16[2,24,3072]{2,1,0:T(8,128)(2,1)S(1)}, bf16[2,24,3072]{2,1,0:T(8,128)(2,1)S(1)}, u32[]{:S(2)}, u32[]{:S(2)}) collective-permute-start(bf16[2,24,3072]{2,1,0:T(8,128)(2,1)S(1)} %broadcast_select_fusion.9), channel_id=1, source_target_pairs={{0,8},{1,9},{2,10},{3,11},{4,12},{5,13},{6,14},{7,15},{8,0},{9,1},... | collective-permute-start | bytes 884744 | tf_op jit(solution)/shard_map/ppermute | solution.py:632
  43.8 43.1 %collective-permute-start.11 = (bf16[4,2,96,768]{3,2,1,0:T(8,128)(2,1)S(1)}, bf16[4,2,96,768]{3,2,1,0:T(8,128)(2,1)}, u32[]{:S(2)}, u32[]{:S(2)}) collective-permute-start(bf16[4,2,96,768]{3,2,1,0:T(8,128)(2,1)S(1)} %bitcast.136), channel_id=1, source_target_pairs={{0,1},{1,0},{2,3},{3,2},{4,5},{5,4},{6,7},{7,6},{8,9},{9,8},{10,11... | collective-permute-start | bytes 3538952 | tf_op jit(solution)/shard_map/ppermute | solution.py:632
  56.7 30.2 %collective-permute-start.12 = (bf16[4,2,96,768]{3,2,1,0:T(8,128)(2,1)}, bf16[4,2,96,768]{3,2,1,0:T(8,128)(2,1)}, u32[]{:S(2)}, u32[]{:S(2)}) collective-permute-start(bf16[4,2,96,768]{3,2,1,0:T(8,128)(2,1)} %collective-permute-done.10.refs_3_), channel_id=1, source_target_pairs={{0,1},{1,0},{2,3},{3,2},{4,5},{5,4},{6,7},{7,6},{8,9},{9,8},{10,11... | collective-permute-start | bytes 3538952 | tf_op jit(solution)/shard_map/ppermute | solution.py:632
  57.1 11.1 %collective-permute-start.14 = (bf16[96,768]{1,0:T(8,128)(2,1)S(1)}, bf16[96,768]{1,0:T(8,128)(2,1)S(1)}, u32[]{:S(2)}, u32[]{:S(2)}) collective-permute-start(bf16[96,768]{1,0:T(8,128)(2,1)S(1)} %copy-done.8), channel_id=1, source_target_pairs={{0,16},{1,17},{2,18},{3,19},{4,20},{5,21},{6,22},{7,23},{8,24},{9,... | collective-permute-start | bytes 442376 | tf_op jit(solution)/shard_map/ppermute | solution.py:632
  57.3 11.2 %collective-permute-start = (bf16[16,768]{1,0:T(8,128)(2,1)S(1)}, bf16[16,768]{1,0:T(8,128)(2,1)S(1)}, u32[]{:S(2)}, u32[]{:S(2)}) collective-permute-start(bf16[16,768]{1,0:T(8,128)(2,1)S(1)} %maximum_maximum_fusion), channel_id=1, source_target_pairs={{0,16},{1,17},{2,18},{3,19},{4,20},{5,21},{6,22},{7,23},{8,24},{9,... | collective-permute-start | bytes 73736 | tf_op jit(solution)/shard_map/ppermute | solution.py:632
  68.3 20.2 %collective-permute-start.15 = (bf16[2,96,768]{2,1,0:T(8,128)(2,1)S(1)}, bf16[2,96,768]{2,1,0:T(8,128)(2,1)S(1)}, u32[]{:S(2)}, u32[]{:S(2)}) collective-permute-start(bf16[2,96,768]{2,1,0:T(8,128)(2,1)S(1)} %broadcast_select_fusion.7), channel_id=1, source_target_pairs={{0,8},{1,9},{2,10},{3,11},{4,12},{5,13},{6,14},{7,15},{8,0},{9,1},... | collective-permute-start | bytes 884744 | tf_op jit(solution)/shard_map/ppermute | solution.py:632
  68.5 8.7 %collective-permute-start.1 = (bf16[16,768]{1,0:T(8,128)(2,1)S(1)}, bf16[16,768]{1,0:T(8,128)(2,1)S(1)}, u32[]{:S(2)}, u32[]{:S(2)}) collective-permute-start(bf16[16,768]{1,0:T(8,128)(2,1)S(1)} %fusion.64), channel_id=1, source_target_pairs={{0,8},{1,9},{2,10},{3,11},{4,12},{5,13},{6,14},{7,15},{8,0},{9,1},... | collective-permute-start | bytes 73736 | tf_op jit(solution)/shard_map/ppermute | solution.py:632
  77.3 3.9 %collective-permute-start.2 = (bf16[16,768]{1,0:T(8,128)(2,1)S(1)}, bf16[16,768]{1,0:T(8,128)(2,1)S(1)}, u32[]{:S(2)}, u32[]{:S(2)}) collective-permute-start(bf16[16,768]{1,0:T(8,128)(2,1)S(1)} %add.200), channel_id=1, source_target_pairs={{0,2},{1,5},{2,0},{3,7},{4,6},{5,1},{6,4},{7,3},{8,10},{9,13},{10,... | collective-permute-start | bytes 73736 | tf_op jit(solution)/shard_map/ppermute | solution.py:632
  81.2 3.9 %collective-permute-start.3 = (bf16[16,768]{1,0:T(8,128)(2,1)S(1)}, bf16[16,768]{1,0:T(8,128)(2,1)S(1)}, u32[]{:S(2)}, u32[]{:S(2)}) collective-permute-start(bf16[16,768]{1,0:T(8,128)(2,1)S(1)} %add.201), channel_id=1, source_target_pairs={{0,4},{1,3},{2,6},{3,1},{4,0},{5,7},{6,2},{7,5},{8,12},{9,11},{10,... | collective-permute-start | bytes 73736 | tf_op jit(solution)/shard_map/ppermute | solution.py:632
  85.1 1.3 collective-permute-start.4
  87.0 11.1 %collective-permute-start.13 = (bf16[2,2,24,3072]{3,2,1,0:T(8,128)(2,1)S(1)}, bf16[2,2,24,3072]{3,2,1,0:T(8,128)(2,1)S(1)}, u32[]{:S(2)}, u32[]{:S(2)}) collective-permute-start(bf16[2,2,24,3072]{3,2,1,0:T(8,128)(2,1)S(1)} %broadcast_select_fusion.3), channel_id=1, source_target_pairs={{0,2},{1,5},{2,0},{3,7},{4,6},{5,1},{6,4},{7,3},{8,10},{9,13},{10,... | collective-permute-start | bytes 1769480 | tf_op jit(solution)/shard_map/ppermute | solution.py:632
  98.2 22.7 %copy-start.4 = (bf16[4,2,24,3072]{3,2,1,0:T(8,128)(2,1)}, bf16[4,2,24,3072]{3,2,1,0:T(8,128)(2,1)S(1)}, u32[]{:S(2)}) copy-start(bf16[4,2,24,3072]{3,2,1,0:T(8,128)(2,1)S(1)} %broadcast_select_fusion.1.refs_2_) | copy-start | bytes 3538948
  98.2 22.7 %collective-permute-start.16 = (bf16[4,2,24,3072]{3,2,1,0:T(8,128)(2,1)S(1)}, bf16[4,2,24,3072]{3,2,1,0:T(8,128)(2,1)}, u32[]{:S(2)}, u32[]{:S(2)}) collective-permute-start(bf16[4,2,24,3072]{3,2,1,0:T(8,128)(2,1)S(1)} %broadcast_select_fusion.1.refs_2_), channel_id=1, source_target_pairs={{0,4},{1,3},{2,6},{3,1},{4,0},{5,7},{6,2},{7,5},{8,12},{9,11},{10,... | collective-permute-start | bytes 3538952 | tf_op jit(solution)/shard_map/ppermute | solution.py:632
  99.8 16.3 %collective-permute-start.17 = (bf16[2,2,96,768]{3,2,1,0:T(8,128)(2,1)S(1)}, bf16[2,2,96,768]{3,2,1,0:T(8,128)(2,1)S(1)}, u32[]{:S(2)}, u32[]{:S(2)}) collective-permute-start(bf16[2,2,96,768]{3,2,1,0:T(8,128)(2,1)S(1)} %broadcast_select_fusion.4), channel_id=1, source_target_pairs={{0,2},{1,5},{2,0},{3,7},{4,6},{5,1},{6,4},{7,3},{8,10},{9,13},{10,... | collective-permute-start | bytes 1769480 | tf_op jit(solution)/shard_map/ppermute | solution.py:632
  116.2 17.0 %copy-start.5 = (bf16[4,2,96,768]{3,2,1,0:T(8,128)(2,1)}, bf16[4,2,96,768]{3,2,1,0:T(8,128)(2,1)S(1)}, u32[]{:S(2)}) copy-start(bf16[4,2,96,768]{3,2,1,0:T(8,128)(2,1)S(1)} %broadcast_select_fusion.refs_3_) | copy-start | bytes 3538948
  120.9 12.3 %collective-permute-start.18 = (bf16[4,2,24,3072]{3,2,1,0:T(8,128)(2,1)S(1)}, bf16[4,2,24,3072]{3,2,1,0:T(8,128)(2,1)}, u32[]{:S(2)}, u32[]{:S(2)}) collective-permute-start(bf16[4,2,24,3072]{3,2,1,0:T(8,128)(2,1)S(1)} %broadcast_select_fusion.1.refs_2_), channel_id=1, source_target_pairs={{0,1},{1,0},{2,3},{3,2},{4,5},{5,4},{6,7},{7,6},{8,9},{9,8},{10,11... | collective-permute-start | bytes 3538952 | tf_op jit(solution)/shard_map/ppermute | solution.py:632
  120.9 12.3 %collective-permute-start.19 = (bf16[4,2,24,3072]{3,2,1,0:T(8,128)(2,1)}, bf16[4,2,24,3072]{3,2,1,0:T(8,128)(2,1)}, u32[]{:S(2)}, u32[]{:S(2)}) collective-permute-start(bf16[4,2,24,3072]{3,2,1,0:T(8,128)(2,1)} %collective-permute-done.16.refs_3_), channel_id=1, source_target_pairs={{0,1},{1,0},{2,3},{3,2},{4,5},{5,4},{6,7},{7,6},{8,9},{9,8},{10,11... | collective-permute-start | bytes 3538952 | tf_op jit(solution)/shard_map/ppermute | solution.py:632
  121.4 16.2 %collective-permute-start.20 = (bf16[4,2,96,768]{3,2,1,0:T(8,128)(2,1)S(1)}, bf16[4,2,96,768]{3,2,1,0:T(8,128)(2,1)S(1)}, u32[]{:S(2)}, u32[]{:S(2)}) collective-permute-start(bf16[4,2,96,768]{3,2,1,0:T(8,128)(2,1)S(1)} %broadcast_select_fusion.refs_3_), channel_id=1, source_target_pairs={{0,4},{1,3},{2,6},{3,1},{4,0},{5,7},{6,2},{7,5},{8,12},{9,11},{10,... | collective-permute-start | bytes 3538952 | tf_op jit(solution)/shard_map/ppermute | solution.py:632
  122.1 37.9 %collective-permute-start.21 = (bf16[4,2,96,768]{3,2,1,0:T(8,128)(2,1)S(1)}, bf16[4,2,96,768]{3,2,1,0:T(8,128)(2,1)}, u32[]{:S(2)}, u32[]{:S(2)}) collective-permute-start(bf16[4,2,96,768]{3,2,1,0:T(8,128)(2,1)S(1)} %broadcast_select_fusion.refs_3_), channel_id=1, source_target_pairs={{0,1},{1,0},{2,3},{3,2},{4,5},{5,4},{6,7},{7,6},{8,9},{9,8},{10,11... | collective-permute-start | bytes 3538952 | tf_op jit(solution)/shard_map/ppermute | solution.py:632
  137.6 22.4 %copy-start.21 = (bf16[4,2,96,768]{3,2,1,0:T(8,128)(2,1)}, bf16[4,2,96,768]{3,2,1,0:T(8,128)(2,1)S(1)}, u32[]{:S(2)}) copy-start(bf16[4,2,96,768]{3,2,1,0:T(8,128)(2,1)S(1)} %collective-permute-done.20.refs_4_) | copy-start | bytes 3538948
  137.6 22.4 %collective-permute-start.22 = (bf16[4,2,96,768]{3,2,1,0:T(8,128)(2,1)S(1)}, bf16[4,2,96,768]{3,2,1,0:T(8,128)(2,1)S(1)}, u32[]{:S(2)}, u32[]{:S(2)}) collective-permute-start(bf16[4,2,96,768]{3,2,1,0:T(8,128)(2,1)S(1)} %collective-permute-done.20.refs_4_), channel_id=1, source_target_pairs={{0,1},{1,0},{2,3},{3,2},{4,5},{5,4},{6,7},{7,6},{8,9},{9,8},{10,11... | collective-permute-start | bytes 3538952 | tf_op jit(solution)/shard_map/ppermute | solution.py:632
  174.5 4.7 %collective-permute-start.23 = (bf16[8,1536]{1,0:T(8,128)(2,1)S(1)}, bf16[8,1536]{1,0:T(8,128)(2,1)S(1)}, u32[]{:S(2)}, u32[]{:S(2)}) collective-permute-start(bf16[8,1536]{1,0:T(8,128)(2,1)S(1)} %convert_element_type.167), channel_id=1, source_target_pairs={{0,16},{1,17},{2,18},{3,19},{4,20},{5,21},{6,22},{7,23},{8,24},{9,... | collective-permute-start | bytes 73736 | tf_op jit(solution)/shard_map/ppermute | solution.py:632
  179.3 4.1 %collective-permute-start.24 = (bf16[2,8,1536]{2,1,0:T(8,128)(2,1)S(1)}, bf16[2,8,1536]{2,1,0:T(8,128)(2,1)S(1)}, u32[]{:S(2)}, u32[]{:S(2)}) collective-permute-start(bf16[2,8,1536]{2,1,0:T(8,128)(2,1)S(1)} %broadcast_select_fusion.12), channel_id=1, source_target_pairs={{0,8},{1,9},{2,10},{3,11},{4,12},{5,13},{6,14},{7,15},{8,0},{9,1},... | collective-permute-start | bytes 147464 | tf_op jit(solution)/shard_map/ppermute | solution.py:632
  183.5 5.2 %collective-permute-start.25 = (bf16[2,2,8,1536]{3,2,1,0:T(8,128)(2,1)S(1)}, bf16[2,2,8,1536]{3,2,1,0:T(8,128)(2,1)S(1)}, u32[]{:S(2)}, u32[]{:S(2)}) collective-permute-start(bf16[2,2,8,1536]{3,2,1,0:T(8,128)(2,1)S(1)} %broadcast_select_fusion.11), channel_id=1, source_target_pairs={{0,2},{1,5},{2,0},{3,7},{4,6},{5,1},{6,4},{7,3},{8,10},{9,13},{10,... | collective-permute-start | bytes 294920 | tf_op jit(solution)/shard_map/ppermute | solution.py:632
  188.8 5.7 %collective-permute-start.26 = (bf16[2,2,2,8,1536]{4,3,2,1,0:T(8,128)(2,1)S(1)}, bf16[2,2,2,8,1536]{4,3,2,1,0:T(8,128)(2,1)S(1)}, u32[]{:S(2)}, u32[]{:S(2)}) collective-permute-start(bf16[2,2,2,8,1536]{4,3,2,1,0:T(8,128)(2,1)S(1)} %broadcast_select_fusion.10), channel_id=1, source_target_pairs={{0,4},{1,3},{2,6},{3,1},{4,0},{5,7},{6,2},{7,5},{8,12},{9,11},{10,... | collective-permute-start | bytes 589832 | tf_op jit(solution)/shard_map/ppermute | solution.py:632
  194.7 1.8 collective-permute-start.27
  215.3 16.0 %collective-permute-start.28 = (bf16[4,2,2,96,768]{4,3,2,1,0:T(8,128)(2,1)}, bf16[4,2,2,96,768]{4,3,2,1,0:T(8,128)(2,1)S(1)}, u32[]{:S(2)}, u32[]{:S(2)}) collective-permute-start(bf16[4,2,2,96,768]{4,3,2,1,0:T(8,128)(2,1)} %get-tuple-element.180), channel_id=1, source_target_pairs={{0,1},{1,0},{2,3},{3,2},{4,5},{5,4},{6,7},{7,6},{8,9},{9,8},{10,11... | collective-permute-start | bytes 7077896 | tf_op jit(solution)/shard_map/ppermute | solution.py:632
  234.7 22.3 %collective-permute-start.29 = (bf16[4,2,2,24,3072]{4,3,2,1,0:T(8,128)(2,1)}, bf16[4,2,2,24,3072]{4,3,2,1,0:T(8,128)(2,1)}, u32[]{:S(2)}, u32[]{:S(2)}) collective-permute-start(bf16[4,2,2,24,3072]{4,3,2,1,0:T(8,128)(2,1)} %get-tuple-element.192), channel_id=1, source_target_pairs={{0,1},{1,0},{2,3},{3,2},{4,5},{5,4},{6,7},{7,6},{8,9},{9,8},{10,11... | collective-permute-start | bytes 7077896 | tf_op jit(solution)/shard_map/ppermute | solution.py:632
  235.1 19.2 %collective-permute-start.30 = (bf16[2,2,2,96,768]{4,3,0,1,2:T(8,128)(2,1)S(1)}, bf16[2,2,2,96,768]{4,3,0,1,2:T(8,128)(2,1)}, u32[]{:S(2)}, u32[]{:S(2)}) collective-permute-start(bf16[2,2,2,96,768]{4,3,0,1,2:T(8,128)(2,1)S(1)} %fusion), channel_id=1, source_target_pairs={{0,2},{1,5},{2,0},{3,7},{4,6},{5,1},{6,4},{7,3},{8,10},{9,13},{10,... | collective-permute-start | bytes 3538952 | tf_op jit(solution)/shard_map/ppermute | solution.py:632
  262.1 21.2 %collective-permute-start.32 = (bf16[2,2,96,768]{3,2,0,1:T(8,128)(2,1)}, bf16[2,2,96,768]{3,2,0,1:T(8,128)(2,1)}, u32[]{:S(2)}, u32[]{:S(2)}) collective-permute-start(bf16[2,2,96,768]{3,2,0,1:T(8,128)(2,1)} %fusion.5), channel_id=1, source_target_pairs={{0,4},{1,3},{2,6},{3,1},{4,0},{5,7},{6,2},{7,5},{8,12},{9,11},{10,... | collective-permute-start | bytes 1769480 | tf_op jit(solution)/shard_map/ppermute | solution.py:632
  262.8 22.6 %collective-permute-start.31 = (bf16[2,2,2,24,3072]{4,3,0,1,2:T(8,128)(2,1)}, bf16[2,2,2,24,3072]{4,3,0,1,2:T(8,128)(2,1)}, u32[]{:S(2)}, u32[]{:S(2)}) collective-permute-start(bf16[2,2,2,24,3072]{4,3,0,1,2:T(8,128)(2,1)} %fusion.1), channel_id=1, source_target_pairs={{0,2},{1,5},{2,0},{3,7},{4,6},{5,1},{6,4},{7,3},{8,10},{9,13},{10,... | collective-permute-start | bytes 3538952 | tf_op jit(solution)/shard_map/ppermute | solution.py:632
  287.1 18.5 %collective-permute-start.34 = (bf16[2,96,768]{2,1,0:T(8,128)(2,1)S(1)}, bf16[2,96,768]{2,1,0:T(8,128)(2,1)S(1)}, u32[]{:S(2)}, u32[]{:S(2)}) collective-permute-start(bf16[2,96,768]{2,1,0:T(8,128)(2,1)S(1)} %fusion.8), channel_id=1, source_target_pairs={{0,8},{1,9},{2,10},{3,11},{4,12},{5,13},{6,14},{7,15},{8,0},{9,1},... | collective-permute-start | bytes 884744 | tf_op jit(solution)/shard_map/ppermute | solution.py:632
  287.5 19.0 %collective-permute-start.33 = (bf16[2,2,24,3072]{3,2,0,1:T(8,128)(2,1)S(1)}, bf16[2,2,24,3072]{3,2,0,1:T(8,128)(2,1)S(1)}, u32[]{:S(2)}, u32[]{:S(2)}) collective-permute-start(bf16[2,2,24,3072]{3,2,0,1:T(8,128)(2,1)S(1)} %fusion.6), channel_id=1, source_target_pairs={{0,4},{1,3},{2,6},{3,1},{4,0},{5,7},{6,2},{7,5},{8,12},{9,11},{10,... | collective-permute-start | bytes 1769480 | tf_op jit(solution)/shard_map/ppermute | solution.py:632
  288.9 16.8 %copy-start.2 = (f32[2,96,768]{2,1,0:T(8,128)S(1)}, f32[2,96,768]{2,1,0:T(8,128)}, u32[]{:S(2)}) copy-start(f32[2,96,768]{2,1,0:T(8,128)} %dynamic-slice_bitcast_fusion.3) | copy-start | bytes 1769476
  306.6 10.9 %collective-permute-start.36 = (bf16[4,2,2,4,24,768]{5,4,3,2,1,0:T(8,128)(2,1)}, bf16[4,2,2,4,24,768]{5,4,3,2,1,0:T(8,128)(2,1)S(1)}, u32[]{:S(2)}, u32[]{:S(2)}) collective-permute-start(bf16[4,2,2,4,24,768]{5,4,3,2,1,0:T(8,128)(2,1)} %get-tuple-element.217), channel_id=1, source_target_pairs={{0,1},{1,0},{2,3},{3,2},{4,5},{5,4},{6,7},{7,6},{8,9},{9,8},{10,11... | collective-permute-start | bytes 7077896 | tf_op jit(solution)/shard_map/ppermute | solution.py:632
  306.7 10.7 %collective-permute-start.35 = (bf16[2,24,3072]{2,1,0:T(8,128)(2,1)S(1)}, bf16[2,24,3072]{2,1,0:T(8,128)(2,1)S(1)}, u32[]{:S(2)}, u32[]{:S(2)}) collective-permute-start(bf16[2,24,3072]{2,1,0:T(8,128)(2,1)S(1)} %fusion.9), channel_id=1, source_target_pairs={{0,8},{1,9},{2,10},{3,11},{4,12},{5,13},{6,14},{7,15},{8,0},{9,1},... | collective-permute-start | bytes 884744 | tf_op jit(solution)/shard_map/ppermute | solution.py:632
  321.0 21.0 %collective-permute-start.37 = (bf16[2,2,2,4,24,768]{5,4,3,0,1,2:T(8,128)(2,1)S(1)}, bf16[2,2,2,4,24,768]{5,4,3,0,1,2:T(8,128)(2,1)S(1)}, u32[]{:S(2)}, u32[]{:S(2)}) collective-permute-start(bf16[2,2,2,4,24,768]{5,4,3,0,1,2:T(8,128)(2,1)S(1)} %fusion.2), channel_id=1, source_target_pairs={{0,2},{1,5},{2,0},{3,7},{4,6},{5,1},{6,4},{7,3},{8,10},{9,13},{10,... | collective-permute-start | bytes 3538952 | tf_op jit(solution)/shard_map/ppermute | solution.py:632
  321.6 1.3 collective-permute-start.41
  322.9 14.6 %collective-permute-start.42 = (bf16[16,768]{1,0:T(8,128)(2,1)S(1)}, bf16[16,768]{1,0:T(8,128)(2,1)S(1)}, u32[]{:S(2)}, u32[]{:S(2)}) collective-permute-start(bf16[16,768]{1,0:T(8,128)(2,1)S(1)} %fusion.24), channel_id=1, source_target_pairs={{0,2},{1,5},{2,0},{3,7},{4,6},{5,1},{6,4},{7,3},{8,10},{9,13},{10,... | collective-permute-start | bytes 73736 | tf_op jit(solution)/shard_map/ppermute | solution.py:632
  337.5 3.9 %collective-permute-start.43 = (bf16[16,768]{1,0:T(8,128)(2,1)S(1)}, bf16[16,768]{1,0:T(8,128)(2,1)S(1)}, u32[]{:S(2)}, u32[]{:S(2)}) collective-permute-start(bf16[16,768]{1,0:T(8,128)(2,1)S(1)} %get-tuple-element.230), channel_id=1, source_target_pairs={{0,4},{1,3},{2,6},{3,1},{4,0},{5,7},{6,2},{7,5},{8,12},{9,11},{10,... | collective-permute-start | bytes 73736 | tf_op jit(solution)/shard_map/ppermute | solution.py:632
  341.5 3.9 %collective-permute-start.44 = (bf16[16,768]{1,0:T(8,128)(2,1)S(1)}, bf16[16,768]{1,0:T(8,128)(2,1)S(1)}, u32[]{:S(2)}, u32[]{:S(2)}) collective-permute-start(bf16[16,768]{1,0:T(8,128)(2,1)S(1)} %fusion.25), channel_id=1, source_target_pairs={{0,8},{1,9},{2,10},{3,11},{4,12},{5,13},{6,14},{7,15},{8,0},{9,1},... | collective-permute-start | bytes 73736 | tf_op jit(solution)/shard_map/ppermute | solution.py:632
  343.2 10.2 %collective-permute-start.38 = (bf16[2,2,4,24,768]{4,3,2,0,1:T(8,128)(2,1)}, bf16[2,2,4,24,768]{4,3,2,0,1:T(8,128)(2,1)}, u32[]{:S(2)}, u32[]{:S(2)}) collective-permute-start(bf16[2,2,4,24,768]{4,3,2,0,1:T(8,128)(2,1)} %fusion.7), channel_id=1, source_target_pairs={{0,4},{1,3},{2,6},{3,1},{4,0},{5,7},{6,2},{7,5},{8,12},{9,11},{10,... | collective-permute-start | bytes 1769480 | tf_op jit(solution)/shard_map/ppermute | solution.py:632
  345.4 6.7 %collective-permute-start.45 = (bf16[16,768]{1,0:T(8,128)(2,1)S(1)}, bf16[16,768]{1,0:T(8,128)(2,1)S(1)}, u32[]{:S(2)}, u32[]{:S(2)}) collective-permute-start(bf16[16,768]{1,0:T(8,128)(2,1)S(1)} %fusion.26), channel_id=1, source_target_pairs={{0,16},{1,17},{2,18},{3,19},{4,20},{5,21},{6,22},{7,23},{8,24},{9,... | collective-permute-start | bytes 73736 | tf_op jit(solution)/shard_map/ppermute | solution.py:632
  352.7 9.0 %collective-permute-start.47 = (bf16[96,768]{1,0:T(8,128)(2,1)S(1)}, bf16[96,768]{1,0:T(8,128)(2,1)S(1)}, u32[]{:S(2)}, u32[]{:S(2)}) collective-permute-start(bf16[96,768]{1,0:T(8,128)(2,1)S(1)} %copy-done.6), channel_id=1, source_target_pairs={{0,16},{1,17},{2,18},{3,19},{4,20},{5,21},{6,22},{7,23},{8,24},{9,... | collective-permute-start | bytes 442376 | tf_op jit(solution)/shard_map/ppermute | solution.py:632
  354.6 19.6 %copy-start.1 = (bf16[96]{0:T(256)(128)(2,1)S(1)}, bf16[96]{0:T(256)(128)(2,1)}, u32[]{:S(2)}) copy-start(bf16[96]{0:T(256)(128)(2,1)} %param.33) | copy-start | bytes 580
  354.6 11.0 %collective-permute-start.39 = (bf16[2,4,24,768]{3,2,1,0:T(8,128)(2,1)S(1)}, bf16[2,4,24,768]{3,2,1,0:T(8,128)(2,1)S(1)}, u32[]{:S(2)}, u32[]{:S(2)}) collective-permute-start(bf16[2,4,24,768]{3,2,1,0:T(8,128)(2,1)S(1)} %fusion.10), channel_id=1, source_target_pairs={{0,8},{1,9},{2,10},{3,11},{4,12},{5,13},{6,14},{7,15},{8,0},{9,1},... | collective-permute-start | bytes 884744 | tf_op jit(solution)/shard_map/ppermute | solution.py:632
  362.4 7.2 %collective-permute-start.46 = (bf16[24,3072]{1,0:T(8,128)(2,1)S(1)}, bf16[24,3072]{1,0:T(8,128)(2,1)S(1)}, u32[]{:S(2)}, u32[]{:S(2)}) collective-permute-start(bf16[24,3072]{1,0:T(8,128)(2,1)S(1)} %fusion.12), channel_id=1, source_target_pairs={{0,16},{1,17},{2,18},{3,19},{4,20},{5,21},{6,22},{7,23},{8,24},{9,... | collective-permute-start | bytes 442376 | tf_op jit(solution)/shard_map/ppermute | solution.py:632
  365.7 7.7 %collective-permute-start.40 = (bf16[4,24,768]{2,1,0:T(8,128)(2,1)S(1)}, bf16[4,24,768]{2,1,0:T(8,128)(2,1)S(1)}, u32[]{:S(2)}, u32[]{:S(2)}) collective-permute-start(bf16[4,24,768]{2,1,0:T(8,128)(2,1)S(1)} %fusion.13), channel_id=1, source_target_pairs={{0,16},{1,17},{2,18},{3,19},{4,20},{5,21},{6,22},{7,23},{8,24},{9,... | collective-permute-start | bytes 442376 | tf_op jit(solution)/shard_map/ppermute | solution.py:632
  (7 other events, 25.9 us)

commit v3 on v2

--- a/solution.py
+++ b/solution.py
@@ -47,9 +47,9 @@
     return pl.BlockSpec((rows, width), lambda i, *_: (i, 0))
 
 
-def params(flops, nbytes, exps=0):
+def params(flops, nbytes, exps=0, room=60):
     return dict(
-        compiler_params=pltpu.CompilerParams(vmem_limit_bytes=60 << 20),
+        compiler_params=pltpu.CompilerParams(vmem_limit_bytes=room << 20),
         cost_estimate=pl.CostEstimate(flops=int(flops), bytes_accessed=int(nbytes), transcendentals=int(exps)),
     )
 
@@ -88,23 +88,24 @@
 def project_body(cube, x_ref, vec_ref, *refs):
     parts, (q_ref, k_ref, v_ref, full_ref, w_ref, sems, out_sem) = refs[:-7], refs[-7:]
     step = pl.program_id(0)
-    full_copy = pltpu.make_async_copy(w_ref, full_ref, out_sem)
+    onward = pltpu.make_async_copy(w_ref, full_ref, out_sem)
 
     @pl.when(step == 0)
     def _():
         if cube:
+
             def cut(m):
                 return lambda ref: ref.at[:, :, pl.ds(m * 24, 24), :]
 
-            for m in range(4):
+            for m in range(3):
                 part_copies(parts, w_ref.at[m], sems.at[m], cut(m))
-            for m in range(4):
+            for m in range(3):
                 part_waits(parts, w_ref.at[m], sems.at[m], cut(m))
         else:
             copy = pltpu.make_async_copy(parts[0], w_ref, sems.at[0, 0])
             copy.start()
             copy.wait()
-        full_copy.start()
+        onward.start()
 
     x = x_ref[...]
 
@@ -117,23 +118,44 @@
 
     @pl.when(step == pl.num_programs(0) - 1)
     def _():
-        full_copy.wait()
+        onward.wait()
 
 
 def project(x, vec, parts, cube):
     t = x.shape[0]
-    shape = (4, 4, 2, 2, 2, 24, D) if cube else (4, D, D)
+    shape = (3, 4, 2, 2, 2, 24, D) if cube else (3, D, D)
     q, k, v, full = pl.pallas_call(
         lambda *refs: project_body(cube, *refs),
         grid=(t // ROWS,),
         in_specs=[row_block(D), whole(vec.shape)] + [ANY] * len(parts),
         out_specs=[row_block(D)] * 3 + [ANY],
         out_shape=[S((t, D), low)] * 3 + [S(shape, low)],
-        scratch_shapes=[pltpu.VMEM(shape, low), pltpu.SemaphoreType.DMA((4, 4)), pltpu.SemaphoreType.DMA],
+        scratch_shapes=[pltpu.VMEM(shape, low), pltpu.SemaphoreType.DMA((3, 4)), pltpu.SemaphoreType.DMA],
         name="project",
-        **params(6 * t * D * D, 8 * t * D + 16 * D * D),
+        **params(6 * t * D * D, 8 * t * D + 12 * D * D, room=60),
     )(x, vec, *parts)
-    return q, k, v, full.reshape(4, D, D)
+    return q, k, v, full.reshape(3, D, D)
+
+
+def assemble(cube, parts, w_ref, full_ref, sems, out_sem):
+    onward = pltpu.make_async_copy(w_ref, full_ref, out_sem)
+
+    @pl.when(pl.program_id(0) == 0)
+    def _():
+        if cube:
+            part_copies(parts, w_ref, sems, everything)
+            part_waits(parts, w_ref, sems, everything)
+        else:
+            copy = pltpu.make_async_copy(parts[0], w_ref, sems.at[0])
+            copy.start()
+            copy.wait()
+        onward.start()
+
+    return onward
+
+
+def scratch_for(shape):
+    return [pltpu.VMEM(shape, low), pltpu.SemaphoreType.DMA((4,)), pltpu.SemaphoreType.DMA]
 
 
 def head_masks(dtype):
@@ -147,10 +169,6 @@
 
 def unstacked(full, masks):
     return sum(full[LEN * h : LEN * (h + 1)] * m for h, m in enumerate(masks))
-
-
-def table_rows(s, g):
-    return pl.ds(pl.multiple_of((s * GROUPS + g) * LEN, LEN), LEN)
 
 
 def layer_norm(resid):
@@ -166,8 +184,8 @@
     return (grad - mean - hat * along) * inv
 
 
-def attend_body(start, len_ref, x_ref, q_ref, k_ref, v_ref, wo_ref, vec_ref, *refs):
-    p_ref, c_ref, hat_ref, inv_ref, n_ref = refs[-5:]
+def attend_body(start, len_ref, q_ref, k_ref, v_ref, *refs):
+    p_ref, c_ref = refs[-2:]
     masks, masks32 = head_masks(low), head_masks(f32)
     per = ROWS // LEN
     first = (start + pl.program_id(0)) * per
@@ -183,18 +201,13 @@
             scores = jnp.where(seen, scores, -1e30)
             expd = jnp.exp(scores - jnp.max(scores, axis=0, keepdims=True))
             probs = expd * (1.0 / jnp.sum(expd, axis=0, keepdims=True))
-            p_ref[table_rows(s, g), :] = probs
+            p_ref[g, rows, :] = probs
             c_ref[rows, cols] = unstacked(tn(probs.astype(low), v), masks32).astype(low)
 
     pl.loop(0, per, unroll=UNROLL)(sentence)
-    branch = nn(c_ref[...], wo_ref[0]) + vec_ref[B_OUTPUT : B_OUTPUT + 1].astype(f32)
-    hat, inv = layer_norm(x_ref[...].astype(f32) + branch)
-    hat_ref[...] = hat
-    inv_ref[...] = inv
-    n_ref[...] = (hat * vec_ref[G_ATTN : G_ATTN + 1].astype(f32) + vec_ref[S_ATTN : S_ATTN + 1].astype(f32)).astype(low)
-
-
-UNROLL = 2
+
+
+UNROLL = 4
 
 
 def some_rows(start):
@@ -205,77 +218,162 @@
     return pl.BlockSpec((1, D, D), lambda *_: (m, 0, 0), pipeline_mode=pl.Buffered(1))
 
 
-def attend(lengths, x, q, k, v, full, vec, start, count, before=()):
-    t = x.shape[0]
+def attend(lengths, q, k, v, start, count, before=()):
+    t = q.shape[0]
     rows = some_rows(start)
     return pl.pallas_call(
         lambda *refs: attend_body(start, *refs),
         grid_spec=pltpu.PrefetchScalarGridSpec(
             num_scalar_prefetch=1,
             grid=(count,),
-            in_specs=[rows(D)] * 4 + [mat_of(3), whole(vec.shape)] + [ANY] * len(before),
-            out_specs=[rows(WIDE, GROUPS * ROWS), rows(D), rows(D), rows(1), rows(D)],
+            in_specs=[rows(D)] * 3 + [ANY] * len(before),
+            out_specs=[pl.BlockSpec((GROUPS, ROWS, WIDE), lambda i, *_: (0, start + i, 0)), rows(D)],
         ),
-        out_shape=[S((GROUPS * t, WIDE), f32), S((t, D), low), S((t, D), f32), S((t, 1), f32), S((t, D), low)],
-        input_output_aliases={7 + i: i for i in range(len(before))},
+        out_shape=[S((GROUPS, t, WIDE), f32), S((t, D), low)],
+        input_output_aliases={4 + i: i for i in range(len(before))},
         name="attend",
-        **params(12 * count * ROWS * D * D, 26 * count * ROWS * D, count * ROWS * D),
-    )(lengths, x, q, k, v, full, vec, *before)
-
-
-def attend_back_body(
-    dres_ref, dh_ref, wi_ref, hat_ref, inv_ref, wo_ref, q_ref, k_ref, v_ref, p_ref, vec_ref, *refs
-):
-    dr_ref, dq_ref, dk_ref, dv_ref, sums_ref, dc_ref = refs[-6:]
+        **params(10 * count * ROWS * D * D, 20 * count * ROWS * D, count * ROWS * D, room=60),
+    )(lengths, q, k, v, *before)
+
+
+def close_body(cube, x_ref, c_ref, vec_ref, *refs):
+    parts, (hat_ref, inv_ref, n_ref, full_ref, w_ref, sems, out_sem) = refs[:-7], refs[-7:]
+    onward = assemble(cube, parts, w_ref, full_ref, sems, out_sem)
+    w = w_ref.reshape(D, D) if cube else w_ref
+    branch = nn(c_ref[...], w[...]) + vec_ref[B_OUTPUT : B_OUTPUT + 1].astype(f32)
+    hat, inv = layer_norm(x_ref[...].astype(f32) + branch)
+    hat_ref[...] = hat
+    inv_ref[...] = inv
+    n_ref[...] = (hat * vec_ref[G_ATTN : G_ATTN + 1].astype(f32) + vec_ref[S_ATTN : S_ATTN + 1].astype(f32)).astype(low)
+
+    @pl.when(pl.program_id(0) == pl.num_programs(0) - 1)
+    def _():
+        onward.wait()
+
+
+def close(x, c, vec, parts, cube):
+    t = x.shape[0]
+    shape = (4, 2, 2, 2, 24, D) if cube else (D, D)
+    hat, inv, n, full = pl.pallas_call(
+        lambda *refs: close_body(cube, *refs),
+        grid=(t // ROWS,),
+        in_specs=[row_block(D), row_block(D), whole(vec.shape)] + [ANY] * len(parts),
+        out_specs=[row_block(D), row_block(1), row_block(D), ANY],
+        out_shape=[S((t, D), f32), S((t, 1), f32), S((t, D), low), S(shape, low)],
+        scratch_shapes=scratch_for(shape),
+        name="close",
+        **params(2 * t * D * D, 10 * t * D + 4 * D * D, room=60),
+    )(x, c, vec, *parts)
+    return hat, inv, n, full.reshape(1, D, D)
+
+
+def open_back_body(dres_ref, dh_ref, wi_ref, hat_ref, inv_ref, wo_ref, vec_ref, before_ref, dr_ref, da_ref, dc_ref, sums_ref):
     hat = hat_ref[...]
     dn = dres_ref[...] + nt(dh_ref[...], wi_ref[...])
     dres = layer_norm_back(dn, vec_ref[G_ATTN : G_ATTN + 1].astype(f32), hat, inv_ref[...])
     dr_ref[...] = dres
     dao = dres.astype(low)
+    da_ref[...] = dao
     dc_ref[...] = nt(dao, wo_ref[0]).astype(low)
 
     @pl.when(pl.program_id(0) == 0)
     def _():
-        sums_ref[...] = jnp.zeros_like(sums_ref)
+        sums_ref[...] = before_ref[...]
 
     sums_ref[B_OUTPUT : B_OUTPUT + 1] += jnp.sum(dao.astype(f32), axis=0, keepdims=True)
     sums_ref[G_ATTN : G_ATTN + 1] += jnp.sum(dn * hat, axis=0, keepdims=True)
     sums_ref[S_ATTN : S_ATTN + 1] += jnp.sum(dn, axis=0, keepdims=True)
+
+
+def open_back(dres, dh, wi, hat, inv, full, vec, sums):
+    t = dres.shape[0]
+    return pl.pallas_call(
+        open_back_body,
+        grid=(t // ROWS,),
+        in_specs=[row_block(D), row_block(FF), whole(wi.shape), row_block(D), row_block(1), mat_of(0), whole(vec.shape), whole((16, D))],
+        out_specs=[row_block(D)] * 3 + [whole((16, D))],
+        out_shape=[S((t, D), f32), S((t, D), low), S((t, D), low), S((16, D), f32)],
+        name="open_back",
+        **params(10 * t * D * D, 20 * t * D + 10 * D * D, room=60),
+    )(dres, dh, wi, hat, inv, full, vec, sums)
+
+
+def heads_back_body(cube, q_ref, k_ref, v_ref, dc_ref, p_ref, x_ref, before_ref, c_hbm, da_hbm, *refs):
+    dq_ref, dk_ref, dv_ref, sums_ref = refs[:4]
+    shares, (c_ref, da_ref, sems) = refs[4:-3], refs[-3:]
+    step = pl.program_id(0)
+    copies = [pltpu.make_async_copy(c_hbm, c_ref, sems.at[0]), pltpu.make_async_copy(da_hbm, da_ref, sems.at[1])]
     masks, masks32 = head_masks(low), head_masks(f32)
+
+    @pl.when(step == 0)
+    def _():
+        for copy in copies:
+            copy.start()
 
     def sentence(s):
         rows = pl.ds(pl.multiple_of(s * LEN, LEN), LEN)
-        for g in range(GROUPS):
-            cols = pl.ds(g * WIDE, WIDE)
-            q, k, v, dc = q_ref[rows, cols], k_ref[rows, cols], v_ref[rows, cols], dc_ref[rows, cols]
-            p = p_ref[table_rows(s, g), :]
-            dcs = stacked(dc, masks)
-            dp = nt(v, dcs)
-            dv_ref[rows, cols] = nn(p.astype(low), dcs).astype(low)
-            ds = (p * (dp - jnp.sum(p * dp, axis=0, keepdims=True))).astype(low)
-            dk_ref[rows, cols] = (nn(ds, stacked(q, masks)) * HEAD_DIM ** (-0.5)).astype(low)
-            dq_ref[rows, cols] = (unstacked(tn(ds, k), masks32) * HEAD_DIM ** (-0.5)).astype(low)
-
-    pl.loop(0, ROWS // LEN, unroll=UNROLL)(sentence)
-    sums_ref[B_QUERY : B_QUERY + 1] += jnp.sum(dq_ref[...].astype(f32), axis=0, keepdims=True)
-    sums_ref[B_VALUE : B_VALUE + 1] += jnp.sum(dv_ref[...].astype(f32), axis=0, keepdims=True)
-
-
-def attend_back(dres, dh, wi, hat, inv, full, q, k, v, p, vec, start, count, before=()):
-    t = dres.shape[0]
-    rows = some_rows(start)
+        q, k, v, dc, p = q_ref[rows, :], k_ref[rows, :], v_ref[rows, :], dc_ref[rows, :], p_ref[0, rows, :]
+        dcs = stacked(dc, masks)
+        dp = nt(v, dcs)
+        dv_ref[rows, :] = nn(p.astype(low), dcs).astype(low)
+        ds = (p * (dp - jnp.sum(p * dp, axis=0, keepdims=True))).astype(low)
+        dk_ref[rows, :] = (nn(ds, stacked(q, masks)) * HEAD_DIM ** (-0.5)).astype(low)
+        dq_ref[rows, :] = (unstacked(tn(ds, k), masks32) * HEAD_DIM ** (-0.5)).astype(low)
+
+    @pl.when(step < GROUPS)
+    def _():
+        pl.loop(0, q_ref.shape[0] // LEN, unroll=BACK_UNROLL)(sentence)
+        sums_ref[...] = jnp.zeros_like(sums_ref)
+        sums_ref[0, :16, :] = before_ref[...]
+        sums_ref[0, B_QUERY : B_QUERY + 1] = jnp.sum(dq_ref[...].astype(f32), axis=0, keepdims=True)
+        sums_ref[0, B_VALUE : B_VALUE + 1] = jnp.sum(dv_ref[...].astype(f32), axis=0, keepdims=True)
+        for m, grad in enumerate((dq_ref, dk_ref, dv_ref)):
+            put_shares(cube, tn(x_ref[...], grad[...]), shares, m)
+
+    @pl.when(step == GROUPS)
+    def _():
+        for copy in copies:
+            copy.wait()
+        for m in range(GROUPS):
+            put_shares(cube, tn(c_ref[...], da_ref[:, m * WIDE : (m + 1) * WIDE]), shares, m)
+
+
+BACK_UNROLL = 16
+
+
+def put_shares(cube, full, refs, m):
+    if cube:
+        full = full.reshape(4, 2, 2, 2, 24, WIDE)
+
+        def put(ref, p, q, value):
+            ref[:, p, q, m] = value.astype(ref.dtype)
+
+        write_shares(lambda y, x, c: full[:, y, x, c], *refs, put)
+    else:
+        refs[0][m] = full
+
+
+def heads_back(q, k, v, dc, p, x, sums, c, da, cube):
+    t = q.shape[0]
+    col = pl.BlockSpec((t, WIDE), lambda i: (0, jnp.minimum(i, GROUPS - 1)))
+    if cube:
+        spec = pl.BlockSpec((4, 2, 2, 3, 24, WIDE), lambda i: (0, 0, 0, i, 0, 0))
+        shape = (4, 2, 2, 3 * GROUPS + 3, 24, WIDE)
+        specs, shapes = [spec] * 2, [S(shape, KEEP), S(shape, low)]
+    else:
+        specs, shapes = [pl.BlockSpec((3, D, WIDE), lambda i: (i, 0, 0))], [S((3 * GROUPS + 3, D, WIDE), f32)]
     return pl.pallas_call(
-        attend_back_body,
-        grid=(count,),
-        in_specs=[rows(D), rows(FF), whole((D, FF)), rows(D), rows(1), mat_of(3), rows(D), rows(D), rows(D),
-                  rows(WIDE, GROUPS * ROWS), whole(vec.shape)] + [ANY] * len(before),
-        out_specs=[rows(D)] * 4 + [whole((8, D))],
-        out_shape=[S((t, D), f32)] + [S((t, D), low)] * 3 + [S((8, D), f32)],
-        input_output_aliases={11 + i: i for i in range(len(before))},
-        scratch_shapes=[pltpu.VMEM((ROWS, D), low)],
-        name="attend_back",
-        **params(24 * count * ROWS * D * D, 40 * count * ROWS * D),
-    )(dres, dh, wi, hat, inv, full, q, k, v, p, vec, *before)
+        lambda *refs: heads_back_body(cube, *refs),
+        grid=(GROUPS + 1,),
+        in_specs=[col] * 4
+        + [pl.BlockSpec((1, t, WIDE), lambda i: (jnp.minimum(i, GROUPS - 1), 0, 0)), whole((t, D))]
+        + [pl.BlockSpec((16, WIDE), lambda i: (0, jnp.minimum(i, GROUPS - 1))), ANY, ANY],
+        out_specs=[col] * 3 + [pl.BlockSpec((1, 24, WIDE), lambda i: (jnp.minimum(i, GROUPS - 1), 0, 0))] + specs,
+        out_shape=[S((t, D), low)] * 3 + [S((GROUPS, 24, WIDE), f32)] + shapes,
+        scratch_shapes=[pltpu.VMEM((t, D), low), pltpu.VMEM((t, D), low), pltpu.SemaphoreType.DMA((2,))],
+        name="heads_back",
+        **params(t * D * 24000, t * D * 20, room=60),
+    )(q, k, v, dc, p, x, sums, c, da)
 
 
 def gelu_parts(h):
@@ -287,23 +385,6 @@
     tail = poly * bell
     cdf = jnp.where(h >= 0, 1.0 - tail, tail)
     return h * cdf, cdf + h * (bell * 0.3989422804014327)
-
-
-def assemble(cube, parts, w_ref, full_ref, sems, out_sem):
-    onward = pltpu.make_async_copy(w_ref, full_ref, out_sem)
-
-    @pl.when(pl.program_id(0) == 0)
-    def _():
-        if cube:
-            part_copies(parts, w_ref, sems, everything)
-            part_waits(parts, w_ref, sems, everything)
-        else:
-            copy = pltpu.make_async_copy(parts[0], w_ref, sems.at[0])
-            copy.start()
-            copy.wait()
-        onward.start()
-
-    return onward
 
 
 def inner_body(cube, n_ref, vec_ref, *refs):
@@ -334,7 +415,7 @@
         out_shape=[S((t, FF), low), S((t, FF), low), S(shape, low)],
         scratch_shapes=[pltpu.VMEM(shape, low), pltpu.SemaphoreType.DMA((4,)), pltpu.SemaphoreType.DMA],
         name="inner",
-        **params(6 * t * D * FF, 2 * t * D + 4 * t * FF + 4 * D * FF, 2 * t * FF),
+        **params(6 * t * D * FF, 2 * t * D + 4 * t * FF + 4 * D * FF, 2 * t * FF, room=60),
     )(n, vec, *parts)
     return act, slope, full.reshape(D, FF)
 
@@ -379,7 +460,7 @@
         out_shape=[S((t, D), low), S((t, D), f32), S((t, 1), f32), S((pairs, 2 * D), f32), S((pairs, 2 * D), f32), S(shape, low)],
         scratch_shapes=[pltpu.VMEM(shape, low), pltpu.SemaphoreType.DMA((4,)), pltpu.SemaphoreType.DMA],
         name="outer",
-        **params(2 * t * D * FF, 10 * t * D + 2 * t * FF + 4 * D * FF),
+        **params(2 * t * D * FF, 10 * t * D + 2 * t * FF + 4 * D * FF, room=60),
     )(act, hat, vec, *parts)
     return *outs, full.reshape(FF, D)
 
@@ -427,9 +508,9 @@
             dbr_ref[rows, :] = dbr
             dbias += jnp.sum(dbr.astype(f32), axis=0, keepdims=True)
         sums_ref[...] = jnp.zeros_like(sums_ref)
-        sums_ref[0:1] = dbias
-        sums_ref[1:2] = dgain
-        sums_ref[2:3] = dshift
+        sums_ref[B_OUTER : B_OUTER + 1] = dbias
+        sums_ref[G_FFN : G_FFN + 1] = dgain
+        sums_ref[S_FFN : S_FFN + 1] = dshift
 
     dw = tn(a_ref[...], dbr_ref[...])
     if cube:
@@ -455,17 +536,21 @@
         grid=(FF // BLOCK,),
         in_specs=[whole((t, D)), whole(dc.shape), whole((t, D)), whole((t, 1)), pl.BlockSpec((t, BLOCK), lambda j: (0, j)),
                   whole(vec.shape)],
-        out_specs=[whole((t, D)), whole((t, D)), whole((8, D))] + specs,
-        out_shape=[S((t, D), f32), S((t, D), low), S((8, D), f32)] + shapes,
+        out_specs=[whole((t, D)), whole((t, D)), whole((16, D))] + specs,
+        out_shape=[S((t, D), f32), S((t, D), low), S((16, D), f32)] + shapes,
         name="outer_back",
-        **params(4 * t * D * FF, 14 * t * D + 2 * t * FF + 8 * D * FF),
+        **params(4 * t * D * FF, 14 * t * D + 2 * t * FF + 8 * D * FF, room=60),
     )(cot, dc, hat2, inv2, a, vec)
 
 
-def inner_back_body(cube, dbr_ref, n_ref, gp_ref, wo_ref, dh_ref, sums_ref, *refs):
+def inner_back_body(cube, dbr_ref, n_ref, gp_ref, wo_ref, before_ref, dh_ref, sums_ref, *refs):
+    @pl.when(pl.program_id(0) == 0)
+    def _():
+        sums_ref[...] = before_ref[...]
+
     dh = (gp_ref[...].astype(f32) * nt(dbr_ref[...], wo_ref[...])).astype(low)
     dh_ref[...] = dh
-    sums_ref[pl.ds(pl.program_id(0), 1), :] = jnp.sum(dh.astype(f32), axis=0, keepdims=True)
+    sums_ref[pl.ds(B_INNER + pl.program_id(0), 1), :] = jnp.sum(dh.astype(f32), axis=0, keepdims=True)
     dw = tn(n_ref[...], dh)
     if cube:
         dw = dw.reshape(4, 2, 2, 2, 24, BLOCK)
@@ -478,7 +563,7 @@
         refs[0][...] = dw
 
 
-def inner_back(dbr, n, gp, wo, cube):
+def inner_back(dbr, n, gp, wo, sums, cube):
     t = n.shape[0]
     fblk = pl.BlockSpec((t, BLOCK), lambda j: (0, j))
     if cube:
@@ -489,50 +574,15 @@
     return pl.pallas_call(
         lambda *refs: inner_back_body(cube, *refs),
         grid=(FF // BLOCK,),
-        in_specs=[whole((t, D)), whole((t, D)), fblk, pl.BlockSpec((BLOCK, D), lambda j: (j, 0))],
-        out_specs=[fblk, whole((4, D))] + specs,
-        out_shape=[S((t, FF), low), S((4, D), f32)] + shapes,
+        in_specs=[whole((t, D)), whole((t, D)), fblk, pl.BlockSpec((BLOCK, D), lambda j: (j, 0)), whole((16, D))],
+        out_specs=[fblk, whole((16, D))] + specs,
+        out_shape=[S((t, FF), low), S((16, D), f32)] + shapes,
         name="inner_back",
-        **params(4 * t * D * FF, 4 * t * D + 4 * t * FF + 8 * D * FF),
-    )(dbr, n, gp, wo)
-
-
-KEEP = f32
-
-
-def mats_body(cube, x_ref, c_ref, dq_ref, dk_ref, dv_ref, dr_ref, *refs):
-    x = x_ref[...]
-    for m, (rows, grad) in enumerate(((x_ref, dq_ref), (x_ref, dk_ref), (x_ref, dv_ref), (c_ref, dr_ref))):
-        full = tn(rows[...], grad[...].astype(low))
-        if cube:
-            full = full.reshape(4, 2, 2, 2, 24, full.shape[-1])
-
-            def put(ref, p, q, value, m=m):
-                ref[:, p, q, m] = value.astype(ref.dtype)
-
-            write_shares(lambda y, x, c: full[:, y, x, c], *refs, put)
-        else:
-            refs[0][m] = full
-
-
-def mats(x, c, dq, dk, dv, dr, cube):
-    t = x.shape[0]
-    wide = 256
-    col = pl.BlockSpec((t, wide), lambda j: (0, j))
-    if cube:
-        spec = pl.BlockSpec((4, 2, 2, 4, 24, wide), lambda j: (0, 0, 0, 0, 0, j))
-        specs, shapes = [spec] * 2, [S((4, 2, 2, 4, 24, D), KEEP), S((4, 2, 2, 4, 24, D), low)]
-    else:
-        specs, shapes = [pl.BlockSpec((4, D, wide), lambda j: (0, 0, j))], [S((4, D, D), f32)]
-    return pl.pallas_call(
-        lambda *refs: mats_body(cube, *refs),
-        grid=(D // wide,),
-        in_specs=[whole((t, D)), whole((t, D)), col, col, col, col],
-        out_specs=specs,
-        out_shape=shapes,
-        name="mats",
-        **params(8 * t * D * D, 14 * t * D + 16 * D * D),
-    )(x, c, dq, dk, dv, dr)
+        **params(4 * t * D * FF, 4 * t * D + 4 * t * FF + 8 * D * FF, room=60),
+    )(dbr, n, gp, wo, sums)
+
+
+KEEP = low
 
 
 def token_grad_body(dr_ref, dq_ref, dk_ref, dv_ref, wq_ref, wk_ref, wv_ref, o_ref):
@@ -551,7 +601,7 @@
         out_specs=row_block(D),
         out_shape=S((t, D), f32),
         name="token_grad",
-        **params(6 * t * D * D, 14 * t * D + 6 * D * D),
+        **params(6 * t * D * D, 14 * t * D + 6 * D * D, room=60),
     )(dr, dq, dk, dv, full, full, full)
 
 
@@ -594,7 +644,7 @@
         scratch_shapes=[pltpu.VMEM((pairs, D), f32), pltpu.VMEM((pairs, D), f32)],
         grid=(1,),
         name="pair_loss",
-        **params(6 * pairs * pairs * D, 4 * pairs * D, 4 * pairs * pairs),
+        **params(6 * pairs * pairs * D, 4 * pairs * D, 4 * pairs * pairs, room=60),
     )(units, vec, cls)
     return loss[0, 0], dc
 
@@ -652,18 +702,51 @@
 
 
 class Reduction:
-    def __init__(self, keep, came, place):
-        self.stages = ((2, place.first), (2, place.second), (1, place.near_z), (0, place.far_z))
-        shape = (2, 2, *keep.shape[1:])
-        self.total = keep.reshape(shape).astype(f32) + came.reshape(shape).astype(f32)
-
-    def split(self, stage):
-        axis, bit = self.stages[stage]
-        return pick(self.total, axis, bit), pick(self.total, axis, 1 - bit).astype(low)
-
-    def meet(self, kept, came):
-        self.total = kept + came.astype(f32)
-        return self
+    def __init__(self, shares, place, early_z=False):
+        keep, self.away = shares
+        self.terms = [keep.reshape(2, 2, *keep.shape[1:])]
+        self.left = [(2, place.first), (2, place.second), (1, place.near_z), (0, place.far_z)]
+        if early_z:
+            self.left = [(1, place.near_z), (1, place.first), (1, place.second), (0, place.far_z)]
+        self.came = self.along = None
+
+    def total(self):
+        self.settle()
+        return sum(term.astype(f32) for term in self.terms)
+
+    def take_along(self, along):
+        self.along = along
+
+    def start(self, route):
+        away = self.away
+        if self.along is not None:
+            away = jnp.concatenate([away.reshape(-1, *self.along.shape[1:]), self.along.astype(low)], axis=0)
+        self.came, self.away = send(away, route), None
+
+    def settle(self):
+        if self.came is not None:
+            came, self.came = self.came, None
+            if self.along is not None:
+                count = self.along.shape[0]
+                self.along = self.along + came[-count:].astype(f32)
+                came = came[:-count]
+            self.terms.append(came.reshape(self.terms[0].shape))
+            if self.left:
+                axis, bit = self.left.pop(0)
+                self.away = sum(pick(term, axis, 1 - bit).astype(f32) for term in self.terms).astype(low)
+                self.terms = [pick(term, axis, bit) for term in self.terms]
+
+
+def windows(sums, *values):
+    for s in sums:
+        s.settle()
+    aways = [s.away for s in sums if s.away is not None]
+    done = together(*values, *aways)
+    values, aways = done[: len(values)], list(done[len(values) :])
+    for s in sums:
+        if s.away is not None:
+            s.away = aways.pop(0)
+    return values
 
 
 def spread_rows(rows, at, count):
@@ -686,42 +769,26 @@
     copies, lane, _ = spread_rows(codes, place.me, 2)
     table.append(jnp.where(lane == place.me, copies, 0.0))
     table.append(jnp.zeros((2, D), f32))
-    table = jnp.concatenate(table, axis=0).astype(low)
-    for route in (FAR_Z, NEAR_Z, FIRST, SECOND, CORE):
-        table = table + send(table, route)
-    return table
-
-
-def own_vectors(sums_attn, sums_ffn, place):
-    total = jnp.concatenate([sums_attn, sums_ffn], axis=0)
-    for route in ROUTES:
-        total = total + send(total.astype(low), route).astype(f32)
+    return jnp.concatenate(table, axis=0).astype(low)
+
+
+def own_vectors(total, place):
     r, fold = D // CUBE, FF // CUBE
-    mine = lax.dynamic_slice(total, (0, place.me * r), (16, r))
-    inner = lax.dynamic_slice(total, (11 + place.me // (D // fold), (place.me % (D // fold)) * fold), (1, fold))
-    return [mine[i] for i in (0, 1, 2, 3, 4, 8, 9, 10)] + [inner[0]]
+    mine = lax.dynamic_slice(total, (0, place.me * r), (B_INNER, r))
+    inner = lax.dynamic_slice(total, (B_INNER + place.me // (D // fold), (place.me % (D // fold)) * fold), (1, fold))
+    return [mine[i] for i in range(B_INNER)] + [inner[0]]
 
 
 def pack_body(*refs):
-    *mats, out, sems = refs
+    *mats, out = refs
     r = mats[0].shape[0]
-    copies = [pltpu.make_async_copy(m, out.at[pl.ds(i * r, r), :], sems.at[i]) for i, m in enumerate(mats)]
-    for copy in copies:
-        copy.start()
-    for copy in copies:
-        copy.wait()
+    for i, mat in enumerate(mats):
+        out[i * r : (i + 1) * r, :] = mat[...]
 
 
 def pack(*mats):
     r, n = mats[0].shape
-    return pl.pallas_call(
-        pack_body,
-        in_specs=[ANY] * len(mats),
-        out_specs=ANY,
-        out_shape=S((len(mats) * r, n), low),
-        scratch_shapes=[pltpu.SemaphoreType.DMA((len(mats),))],
-        name="pack",
-    )(*mats)
+    return pl.pallas_call(pack_body, out_shape=S((len(mats) * r, n), low), name="pack")(*mats)
 
 
 def plain_loss(units, partners, cls):
@@ -784,108 +851,123 @@
     count = tokens.shape[0]
     x = tokens.reshape(count * LEN, D)
     vectors = (b_query, b_value, b_output, gain_attn, shift_attn, b_outer, gain_ffn, shift_ffn, b_inner)
+    blocks = count * LEN // ROWS
+    lower, higher = blocks // 2, blocks - blocks // 2
     if cube:
         place = Place()
-        attn = pack(w_query, w_key, w_value, w_output)
-        attn = join(attn, send(attn, FAR_Z), 0, place.far_z)
-        attn = join(attn, send(attn, NEAR_Z), 1, place.near_z)
-        w_inner, attn = together(w_inner, attn)
+        qkv = pack(w_query, w_key, w_value)
+        vec = vector_table(vectors, partners, place)
+        qkv = join(qkv, send(qkv, FAR_Z), 0, place.far_z)
+        vec = vec + send(vec, FAR_Z)
+        qkv, vec, w_output = together(qkv, vec, w_output)
+        qkv = join(qkv, send(qkv, NEAR_Z), 1, place.near_z)
+        vec = vec + send(vec, NEAR_Z)
+        prj = join(w_output, send(w_output, FAR_Z), 0, place.far_z)
+        qkv, vec, prj, w_inner = together(qkv, vec, prj, w_inner)
+        qkv = join(qkv, send(qkv, FIRST), 2, place.first).reshape(4, 2, 72, D)
+        vec = vec + send(vec, FIRST)
+        prj = join(prj, send(prj, NEAR_Z), 1, place.near_z)
         inn = join(w_inner, send(w_inner, FAR_Z), 0, place.far_z)
-        attn = join(attn, send(attn, FIRST), 2, place.first)
-        w_outer, inn, attn = together(w_outer, inn, attn)
+        qkv, vec, prj, inn = together(qkv, vec, prj, inn)
+        far = send(qkv, SECOND)
+        other = send(qkv, CORE)
+        vec = vec + send(vec, SECOND)
+        prj = join(prj, send(prj, FIRST), 2, place.first).reshape(4, 2, 24, D)
+        inn = join(inn, send(inn, NEAR_Z), 1, place.near_z)
+        far, other, vec, prj, inn = together(far, other, vec, prj, inn)
+        qkv_parts = (qkv, far, other, send(far, CORE))
+        vec = vec + send(vec, CORE)
+        qkv_parts, vec, prj, inn, w_outer = together(qkv_parts, vec, prj, inn, w_outer)
+        inn = join(inn, send(inn, FIRST), 2, place.first).reshape(4, 2, 24, FF)
+        prj_far = send(prj, SECOND)
         out = join(w_outer, send(w_outer, FAR_Z), 0, place.far_z)
-        inn = join(inn, send(inn, NEAR_Z), 1, place.near_z)
-        vec = vector_table(vectors, partners, place)
-        attn_near = attn.reshape(4, 2, 96, D)
-        attn_far = send(attn_near, SECOND)
-        inn, attn_far = together(inn, attn_far)
+        queries, keys, values, full = project(x, vec, qkv_parts, cube)
+        queries, prj_far, inn, out = together(queries, prj_far, inn, out)
+        inn_far = send(inn, SECOND)
         out = join(out, send(out, NEAR_Z), 1, place.near_z)
-        attn_parts = (attn_near, attn_far, send(attn_near, CORE), send(attn_far, CORE))
-        attn_parts, inn = together(attn_parts, inn)
-        inn = join(inn, send(inn, FIRST), 2, place.first).reshape(4, 2, 24, FF)
-        queries, keys, values, full = project(x, vec, attn_parts, cube)
-        queries, inn, out = together(queries, inn, out)
-        blocks = count * LEN // ROWS
-        inn_far = send(inn, SECOND)
+        prj_parts = (prj, prj_far, send(prj, CORE), send(prj_far, CORE))
+        probs, context = attend(lengths, queries, keys, values, 0, blocks)
+        context, inn, inn_far, out, prj_parts = together(context, inn, inn_far, out, prj_parts)
+        inn_parts = (inn, inn_far, send(inn, CORE), send(inn_far, CORE))
         out = join(out, send(out, FIRST), 2, place.first).reshape(4, 2, 96, D)
-        upper = attend(lengths, x, queries, keys, values, full, vec, 0, blocks // 2)
-        upper, inn, inn_far, out = together(upper, inn, inn_far, out)
-        inn_parts = (inn, inn_far, send(inn, CORE), send(inn_far, CORE))
+        hat1, inv1, normed, output_mat = close(x, context, vec, prj_parts, cube)
+        normed, inn_parts, out = together(normed, inn_parts, out)
         out_far = send(out, SECOND)
-        probs, context, hat1, inv1, normed = attend(
-            lengths, x, queries, keys, values, full, vec, blocks // 2, blocks - blocks // 2, upper
-        )
-        normed, inn_parts = together(normed, inn_parts)
+        other = send(out, CORE)
         act, slope, inner_mat = inner(normed, vec, inn_parts, cube)
-        out_parts = (out, out_far, send(out, CORE), send(out_far, CORE))
+        act, out_far, other = together(act, out_far, other)
+        out_parts = (out, out_far, other, send(out_far, CORE))
         block_out, hat2, inv2, cls, unit, outer_mat = outer(act, hat1, vec, out_parts, cube)
         loss, d_cls = pair_loss(gather_blocks(unit.astype(low), place), vec, cls)
-        dres, dbr, sums_outer, keep_o, away_o = outer_back(
+        dres, dbr, sums, *shares = outer_back(
             out_cotangent.reshape(count * LEN, D), d_cls, hat2, inv2, act, vec, cube
         )
-        dbr, away_o = together(dbr, away_o)
-        came_o = send(away_o, CORE)
-        dh, sums_inner, keep_i, away_i = inner_back(dbr, normed, slope, outer_mat, cube)
-        out, inn = Reduction(keep_o, came_o, place), None
-        kept_o, away_o = out.split(0)
-        dh, kept_o, away_o, away_i = together(dh, kept_o, away_o, away_i)
-        came_i, came_o = send(away_i, CORE), send(away_o, FIRST)
-        upper = attend_back(dres, dh, inner_mat, hat1, inv1, full, queries, keys, values, probs, vec, 0, blocks // 2)
-        inn = Reduction(keep_i, came_i, place)
-        kept_i, away_i = inn.split(0)
-        kept_o, away_o = out.meet(kept_o, came_o).split(1)
-        upper, kept_i, away_i, kept_o, away_o = together(upper, kept_i, away_i, kept_o, away_o)
-        came_i, came_o = send(away_i, FIRST), send(away_o, SECOND)
-        d_resid, d_queries, d_keys, d_values, sums_lower = attend_back(
-            dres, dh, inner_mat, hat1, inv1, full, queries, keys, values, probs, vec,
-            blocks // 2, blocks - blocks // 2, upper[:4],
+        o = Reduction(shares, place)
+        (dbr,) = windows([o], dbr)
+        o.start(CORE)
+        dh, sums, *shares = inner_back(dbr, normed, slope, outer_mat, sums, cube)
+        i = Reduction(shares, place, early_z=True)
+        (dh,) = windows([o, i], dh)
+        o.start(FIRST)
+        i.start(CORE)
+        d_resid, d_attn, d_context, sums = open_back(dres, dh, inner_mat, hat1, inv1, output_mat, vec, sums)
+        (d_context,) = windows([o, i], d_context)
+        o.start(SECOND)
+        i.start(NEAR_Z)
+        d_queries, d_keys, d_values, sums, *shares = heads_back(
+            queries, keys, values, d_context, probs, x, sums, context, d_attn, cube
         )
-        kept_i, away_i = inn.meet(kept_i, came_i).split(1)
-        kept_o, away_o = out.meet(kept_o, came_o).split(2)
-        d_resid, kept_i, away_i, kept_o, away_o = together(d_resid, kept_i, away_i, kept_o, away_o)
-        came_i, came_o = send(away_i, SECOND), send(away_o, NEAR_Z)
-        keep_a, away_a = mats(x, context, d_queries, d_keys, d_values, d_resid, cube)
-        kept_i, away_i = inn.meet(kept_i, came_i).split(2)
-        kept_o, away_o = out.meet(kept_o, came_o).split(3)
-        keep_a, away_a, kept_i, away_i, kept_o, away_o, d_resid = together(
-            keep_a, away_a, kept_i, away_i, kept_o, away_o, d_resid
-        )
-        came_a, came_i, came_o = send(away_a, CORE), send(away_i, NEAR_Z), send(away_o, FAR_Z)
+        a = Reduction(shares, place)
+        d_queries, sums, *came = together(d_queries, sums, a.away, o.came, i.came)
+        a.away, o.came, i.came = came
+        a.start(CORE)
+        sums = sums + send(sums.astype(low), CORE).astype(f32)
+        a.settle()
+        a.take_along(sums)
+        windows([o, i, a])
+        a.start(FIRST)
+        o.start(NEAR_Z)
+        i.start(FIRST)
         grad_rows = token_grad(d_resid, d_queries, d_keys, d_values, full)
-        grad_w_outer = out.meet(kept_o, came_o).total
-        kept_i, away_i = inn.meet(kept_i, came_i).split(3)
-        att = Reduction(keep_a, came_a, place)
-        kept_a, away_a = att.split(0)
-        kept_i, away_i, kept_a, away_a, grad_rows = together(kept_i, away_i, kept_a, away_a, grad_rows)
-        grad_w_inner = inn.meet(kept_i, send(away_i, FAR_Z)).total
-        for stage in range(3):
-            kept_a, away_a = att.meet(kept_a, send(away_a, ROUTES[1 + stage])).split(stage + 1)
-        g_mats = att.meet(kept_a, send(away_a, FAR_Z)).total
-        sums_ffn = jnp.concatenate([sums_outer[:3], sums_inner, sums_outer[3:4]], axis=0)
-        grads = own_vectors(upper[4] + sums_lower, sums_ffn, place)
+        (grad_rows,) = windows([o, i, a], grad_rows)
+        a.start(SECOND)
+        i.start(SECOND)
+        o.start(FAR_Z)
+        windows([i, a])
+        a.start(NEAR_Z)
+        i.start(FAR_Z)
+        windows([a])
+        a.start(FAR_Z)
+        grad_w_outer, grad_w_inner, g_a = o.total(), i.total(), a.total()
+        g_mats = [jnp.concatenate([g_a[n], g_a[3 + n], g_a[6 + n]], axis=1) for n in range(3)]
+        g_mats.append(jnp.concatenate([g_a[9], g_a[10], g_a[11]], axis=1))
+        sums = jnp.concatenate([a.along[g] for g in range(GROUPS)], axis=1)
+        grads = own_vectors(sums, place)
     else:
         rows = [every(v).reshape(-1, D) for v in vectors]
         vec = jnp.concatenate(rows + [jnp.zeros((4, D), low)], axis=0)
-        mats_in = (jnp.stack([every(w) for w in (w_query, w_key, w_value, w_output)]),)
-        blocks = count * LEN // ROWS
-        queries, keys, values, full = project(x, vec, mats_in, cube)
-        probs, context, hat1, inv1, normed = attend(lengths, x, queries, keys, values, full, vec, 0, blocks)
+        qkv_parts = (jnp.stack([every(w) for w in (w_query, w_key, w_value)]),)
+        queries, keys, values, full = project(x, vec, qkv_parts, cube)
+        probs, context = attend(lengths, queries, keys, values, 0, blocks)
+        hat1, inv1, normed, output_mat = close(x, context, vec, (every(w_output),), cube)
         act, slope, inner_mat = inner(normed, vec, (every(w_inner),), cube)
         block_out, hat2, inv2, cls, unit, outer_mat = outer(act, hat1, vec, (every(w_outer),), cube)
         loss, d_cls = plain_loss(every(unit.astype(low)), every(partners), cls)
-        dres, dbr, sums_outer, d_outer = outer_back(
+        dres, dbr, sums, d_outer = outer_back(
             out_cotangent.reshape(count * LEN, D), d_cls, hat2, inv2, act, vec, cube
         )
-        dh, sums_inner, d_inner = inner_back(dbr, normed, slope, outer_mat, cube)
-        d_resid, d_queries, d_keys, d_values, sums_attn = attend_back(
-            dres, dh, inner_mat, hat1, inv1, full, queries, keys, values, probs, vec, 0, blocks
+        dh, sums, d_inner = inner_back(dbr, normed, slope, outer_mat, sums, cube)
+        d_resid, d_attn, d_context, sums = open_back(dres, dh, inner_mat, hat1, inv1, output_mat, vec, sums)
+        d_queries, d_keys, d_values, sums, d_a = heads_back(
+            queries, keys, values, d_context, probs, x, sums, context, d_attn, cube
         )
-        (d_mats,) = mats(x, context, d_queries, d_keys, d_values, d_resid, cube)
+        sums = jnp.concatenate([sums[g] for g in range(GROUPS)], axis=1)
         grad_rows = token_grad(d_resid, d_queries, d_keys, d_values, full)
         grad_w_outer, grad_w_inner = scatter(d_outer), scatter(d_inner)
-        g_mats = [scatter(d_mats[m]) for m in range(4)]
-        grads = [scatter(sums_attn[i]) for i in range(5)] + [scatter(sums_outer[i]) for i in range(3)]
-        grads.append(scatter(sums_inner.reshape(-1)))
+        d_mats = [jnp.concatenate([d_a[n], d_a[3 + n], d_a[6 + n]], axis=1) for n in range(3)]
+        d_mats.append(jnp.concatenate([d_a[9], d_a[10], d_a[11]], axis=1))
+        g_mats = [scatter(d) for d in d_mats]
+        grads = [scatter(sums[n]) for n in range(B_INNER)] + [scatter(sums[B_INNER:CODES].reshape(-1))]
     (
         grad_b_query,
         grad_b_value,

time: 378 us -> 324 us (0.86)
  waiting for transfers between devices: 128 us -> 79 us
  Pallas kernels: 169 us -> 148 us
  other arithmetic: 23.4 us -> 40.7 us
  starting transfers between devices: 41.6 us -> 46.2 us
  local copies, waits for them, and re-layouts: 10.4 us -> 6.61 us
    ppermute x48 -> x50, waiting for transfers between devices: 128 us -> 79 us  [send(): return lax.ppermute(field, AXIS, route)]
    convert_element_type x5 -> x17, other arithmetic: 0.08 us -> 24.8 us  [the longest x12 22.2 us: settle(): sum((pick(term, axis, 1 - bit).astype(f32) for term in self.terms))]
    pallas_call x2 -> x1, Pallas kernels: 22.2 us -> 10.7 us  [attend(): pl.pallas_call(lambda *refs: attend_body(start, *refs), grid_spec=pltpu.P...]
    add x22 -> x9, other arithmetic: 18 us -> 6.65 us  [the longest x3 5.13 us: total(): return sum((term.astype(f32) for term in self.terms))]
    pallas_call x4, Pallas kernels: 60.1 us -> 52.3 us  [the longest x1 27.1 us: heads_back(): pl.pallas_call(lambda *refs: heads_back_body(cube, *refs), grid=(GROUPS +...]
    ppermute x48 -> x50, starting transfers between devices: 41.6 us -> 46.2 us  [send(): return lax.ppermute(field, AXIS, route)]
    convert_element_type x12 -> x0, local copies, waits for them, and re-layouts: 4.23 us -> none  [split(): pick(self.total, axis, 1 - bit).astype(low)]
    concatenate x1 -> x10, other arithmetic: 0.08 us -> 3.93 us  [the longest x3 1.91 us: local(): jnp.concatenate([g_a[n], g_a[3 + n], g_a[6 + n]], axis=1)]
  transfers between devices with their start and end apart: 48 -> 50, of which waited for: 30 -> 26; matrix products, arithmetic and copies ran while one was open for 4% -> 9% of each run, Pallas kernels for 36% -> 36%
where the time goes in v3:
time: 324 us; the launch traced here: 323 us
  Pallas kernels  148 us (46%)
  waiting for transfers between devices  79 us (24%)
  starting transfers between devices  46.2 us (14%)
  other arithmetic  40.7 us (13%)
  local copies, waits for them, and re-layouts  6.61 us (2%)
    ppermute x50, waiting for transfers between devices, send(): return lax.ppermute(field, AXIS, route)  79 us
    ppermute x50, starting transfers between devices, send(): return lax.ppermute(field, AXIS, route)  46.2 us
    pallas_call x1, Pallas kernels, heads_back(): pl.pallas_call(lambda *refs: heads_back_body(cube, *refs), grid=(GROUPS +...  27.1 us
    convert_element_type x12, other arithmetic, settle(): sum((pick(term, axis, 1 - bit).astype(f32) for term in self.terms))  22.2 us
    pallas_call x1, Pallas kernels, inner(): pl.pallas_call(lambda *refs: inner_body(cube, *refs), grid=(t // ROWS,),...  22 us
    pallas_call x1, Pallas kernels, open_back(): pl.pallas_call(open_back_body, grid=(t // ROWS,), in_specs=[row_block(D),...  16.4 us
    pallas_call x1, Pallas kernels, inner_back(): pl.pallas_call(lambda *refs: inner_back_body(cube, *refs), grid=(FF // BL...  15.7 us
    pallas_call x1, Pallas kernels, outer_back(): pl.pallas_call(lambda *refs: outer_back_body(cube, *refs), grid=(FF // BL...  14.3 us
  transfers between devices with their start and end apart: 50, of which 26 were waited for; matrix products, arithmetic and copies ran while one was open for 9% of the time, Pallas kernels for 36%

profile of v3, /device:TPU:0, one launch (start us, length us, event | category | flops | bytes accessed | tf_op | source)
XLA Modules:
  0.0 322.7 jit_solution(7390448493778908354)
XLA Ops:
  0.7 1.5 pack.1
  2.2 4.0 %collective-permute-start = (bf16[72,768]{1,0:T(8,128)(2,1)}, bf16[72,768]{1,0:T(8,128)(2,1)S(1)}, u32[]{:S(2)}, u32[]{:S(2)}) collective-permute-start(bf16[72,768]{1,0:T(8,128)(2,1)} %pack.1), channel_id=1, source_target_pairs={{0,16},{1,17},{2,18},{3,19},{4,20},{5,21},{6,22},{7,23},{8,24},{9,... | collective-permute-start | bytes 331784 | tf_op jit(solution)/shard_map/ppermute | solution.py:682
  8.5 4.7 %collective-permute-done.1 = bf16[16,768]{1,0:T(8,128)(2,1)S(1)} collective-permute-done((bf16[16,768]{1,0:T(8,128)(2,1)S(1)}, bf16[16,768]{1,0:T(8,128)(2,1)S(1)}, u32[]{:S(2)}, u32[]{:S(2)}) %collective-permute-start.1) | collective-permute-done | bytes 24608 | tf_op jit(solution)/shard_map/ppermute | solution.py:682
  14.3 1.6 collective-permute-start.3
  15.9 2.2 collective-permute-start.4
  18.3 3.1 collective-permute-done.4
  21.5 3.9 %collective-permute-done.2 = bf16[2,72,768]{2,1,0:T(8,128)(2,1)S(1)} collective-permute-done((bf16[2,72,768]{2,1,0:T(8,128)(2,1)S(1)}, bf16[2,72,768]{2,1,0:T(8,128)(2,1)S(1)}, u32[]{:S(2)}, u32[]{:S(2)}) %collective-permute-start.2) | collective-permute-done | bytes 221216 | tf_op jit(solution)/shard_map/ppermute | solution.py:682
  25.5 1.6 collective-permute-start.6
  29.4 2.7 collective-permute-done.7
  32.1 4.1 %collective-permute-done.8 = bf16[24,3072]{1,0:T(8,128)(2,1)S(1)} collective-permute-done((bf16[24,3072]{1,0:T(8,128)(2,1)S(1)}, bf16[24,3072]{1,0:T(8,128)(2,1)S(1)}, u32[]{:S(2)}, u32[]{:S(2)}) %collective-permute-start.8) | collective-permute-done | bytes 147488 | tf_op jit(solution)/shard_map/ppermute | solution.py:682
  36.5 1.6 collective-permute-start.12
  38.1 1.5 collective-permute-start.11
  40.1 1.8 collective-permute-done.11
  41.9 1.4 collective-permute-done.12
  43.5 1.3 collective-permute-done.13
  44.9 7.7 %collective-permute-done.9.refs_3_ = bf16[4,2,72,768]{3,2,1,0:T(8,128)(2,1)S(1)} collective-permute-done((bf16[4,2,72,768]{3,2,1,0:T(8,128)(2,1)S(1)}, bf16[4,2,72,768]{3,2,1,0:T(8,128)(2,1)S(1)}, u32[]{:S(2)}, u32[]{:S(2)}) %collective-permute-start.9) | collective-permute-done | bytes 884768 | tf_op jit(solution)/shard_map/ppermute | solution.py:682
  53.2 1.9 collective-permute-done.15
  55.8 1.5 collective-permute-start.17
  58.4 9.0 %project.1 = (bf16[1024,768]{1,0:T(8,128)(2,1)}, bf16[1024,768]{1,0:T(8,128)(2,1)}, bf16[1024,768]{1,0:T(8,128)(2,1)}, bf16[3,4,2,2,2,24,768]{6,5,4,3,2,1,0:T(8,128)(2,1)}) custom-call(bf16[1024,768]{1,0:T(8,128)(2,1)} %bitcast.274, bf16[16,768]{1,0:T(8,128)(2,1)} %add.701.refs_1_.refs_2_.codes_ref.refs_5_.vec_ref, bf16[4,2,72,768]{3,2,1,0:T(8,128)(2,1)} %copy-done.10, ...), custom_call_target="tpu_custom_call" | custom-call | flops 3623878656 | bytes 13369344 | tf_op jit(solution)/shard_map/project/pallas_call | solution.py:127
  69.6 2.0 collective-permute-start.20
  71.9 10.7 %attend.1 = (f32[3,1024,256]{2,1,0:T(8,128)}, bf16[1024,768]{1,0:T(8,128)(2,1)}) custom-call(s32[16]{0:T(128)} %refs_0_.3, bf16[1024,768]{1,0:T(8,128)(2,1)} %get-tuple-element.150.refs_1_.refs_0_, bf16[1024,768]{1,0:T(8,128)(2,1)} %get-tuple-element.151.refs_2_.refs_1_, bf16[1024,768]{1,0:T(8,128)(2,1)} %get-tuple-element.152.refs_3_.refs_2_), custom_call_target="tpu_custom_call" | custom-call | flops 6039797760 | bytes 15728640 | tf_op jit(solution)/shard_map/attend/pallas_call | solution.py:224
  82.7 2.1 collective-permute-done.19.refs_3_
  85.4 1.5 collective-permute-start.25
  86.8 7.4 %close.1 = (f32[1024,768]{1,0:T(8,128)}, f32[1024,1]{1,0:T(8,128)}, bf16[1024,768]{1,0:T(8,128)(2,1)}, bf16[4,2,2,2,24,768]{5,4,3,2,1,0:T(8,128)(2,1)}) custom-call(bf16[1024,768]{1,0:T(8,128)(2,1)} %bitcast.275, bf16[1024,768]{1,0:T(8,128)(2,1)} %get-tuple-element.157.refs_1_.refs_7_, bf16[16,768]{1,0:T(8,128)(2,1)} %add.701.refs_1_.refs_2_.codes_ref.refs_5_.vec_ref, ...), custom_call_target="tpu_custom_call" | custom-call | flops 1207959552 | bytes 10223616 | tf_op jit(solution)/shard_map/close/pallas_call | solution.py:257
  96.6 22.0 %inner.1 = (bf16[1024,3072]{1,0:T(8,128)(2,1)}, bf16[1024,3072]{1,0:T(8,128)(2,1)}, bf16[4,2,2,2,24,3072]{5,4,3,2,1,0:T(8,128)(2,1)}) custom-call(bf16[1024,768]{1,0:T(8,128)(2,1)} %get-tuple-element.166.refs_0_.refs_1_, bf16[16,768]{1,0:T(8,128)(2,1)} %add.701.refs_1_.refs_2_.codes_ref.refs_5_.vec_ref, bf16[4,2,24,3072]{3,2,1,0:T(8,128)(2,1)} %copy-done.5, ...), custom_call_target="tpu_custom_call" | custom-call | flops 14495514624 | bytes 23592960 | tf_op jit(solution)/shard_map/inner/pallas_call | solution.py:410
  119.2 2.5 collective-permute-done.28.refs_6_
  122.8 12.6 %outer.1 = (bf16[1024,768]{1,0:T(8,128)(2,1)}, f32[1024,768]{1,0:T(8,128)}, f32[1024,1]{1,0:T(8,128)}, f32[8,1536]{1,0:T(8,128)}, f32[8,1536]{1,0:T(8,128)}, /*index=5*/bf16[4,2,2,2,96,768]{5,4,3,2,1,0:T(8,128)(2,1)}) custom-call(bf16[1024,3072]{1,0:T(8,128)(2,1)} %get-tuple-element.173.refs_0_.refs_4_, f32[1024,768]{1,0:T(8,128)} %get-tuple-element.174.refs_1_.hat_ref, ...), custom_call_target="tpu_custom_call" | custom-call | flops 4831838208 | bytes 23592960 | tf_op jit(solution)/shard_map/outer/pallas_call | solution.py:455
  136.2 2.0 collective-permute-start.29
  138.3 2.7 collective-permute-done.29
  141.0 2.0 collective-permute-start.30
  143.1 2.1 collective-permute-done.30
  145.2 1.7 collective-permute-start.31
  146.9 3.1 collective-permute-done.31
  151.0 4.8 %collective-permute-done.32 = bf16[2,2,2,8,1536]{4,3,2,1,0:T(8,128)(2,1)S(1)} collective-permute-done((bf16[2,2,2,8,1536]{4,3,2,1,0:T(8,128)(2,1)S(1)}, bf16[2,2,2,8,1536]{4,3,2,1,0:T(8,128)(2,1)S(1)}, u32[]{:S(2)}, u32[]{:S(2)}) %collective-permute-start.32) | collective-permute-done | bytes 196640 | tf_op jit(solution)/shard_map/ppermute | solution.py:682
  156.0 1.7 collective-permute-done.33
  158.8 2.9 pair_loss.1
  161.7 14.3 %outer_back.1 = (f32[1024,768]{1,0:T(8,128)}, bf16[1024,768]{1,0:T(8,128)(2,1)}, f32[16,768]{1,0:T(8,128)}, bf16[4,2,2,96,768]{4,3,2,1,0:T(8,128)(2,1)}, bf16[4,2,2,96,768]{4,3,2,1,0:T(8,128)(2,1)}) custom-call(bf16[1024,768]{1,0:T(8,128)(2,1)} %bitcast.273, f32[8,1536]{1,0:T(8,128)} %get-tuple-element.181.refs_1_, f32[1024,768]{1,0:T(8,128)} %get-tuple-element.182.refs_2_, ...), custom_call_target="tpu_custom_call" | custom-call | flops 9663676416 | bytes 36175872 | tf_op jit(solution)/shard_map/outer_back/pallas_call | solution.py:534
  176.1 15.7 %inner_back.1 = (bf16[1024,3072]{1,0:T(8,128)(2,1)}, f32[16,768]{1,0:T(8,128)}, bf16[4,2,2,24,3072]{4,3,2,1,0:T(8,128)(2,1)}, bf16[4,2,2,24,3072]{4,3,2,1,0:T(8,128)(2,1)}) custom-call(bf16[1024,768]{1,0:T(8,128)(2,1)} %get-tuple-element.187.refs_0_, bf16[1024,768]{1,0:T(8,128)(2,1)} %get-tuple-element.166.refs_0_.refs_1_, ...), custom_call_target="tpu_custom_call" | custom-call | flops 9663676416 | bytes 34603008 | tf_op jit(solution)/shard_map/inner_back/pallas_call | solution.py:574
  191.8 1.6 fusion
  194.0 2.2 collective-permute-start.35
  196.1 16.4 %open_back.1 = (f32[1024,768]{1,0:T(8,128)}, bf16[1024,768]{1,0:T(8,128)(2,1)}, bf16[1024,768]{1,0:T(8,128)(2,1)}, f32[16,768]{1,0:T(8,128)}) custom-call(f32[1024,768]{1,0:T(8,128)} %get-tuple-element.184.dres_ref, bf16[1024,3072]{1,0:T(8,128)(2,1)} %get-tuple-element.195.dh_ref, bf16[768,3072]{1,0:T(8,128)(2,1)} %bitcast.277, ...), custom_call_target="tpu_custom_call" | custom-call | flops 6039797760 | bytes 21626880 | tf_op jit(solution)/shard_map/open_back/pallas_call | solution.py:290
  212.5 2.6 fusion.5
  215.2 2.8 fusion.1
  219.6 27.1 %heads_back.1 = (bf16[1024,768]{1,0:T(8,128)(2,1)}, bf16[1024,768]{1,0:T(8,128)(2,1)}, bf16[1024,768]{1,0:T(8,128)(2,1)}, f32[3,24,256]{2,1,0:T(8,128)}, bf16[4,...) custom-call(bf16[1024,768]{1,0:T(8,128)(2,1)} %get-tuple-element.150.refs_1_.refs_0_, ...), custom_call_target="tpu_custom_call" | custom-call | flops 18874368000 | bytes 15728640 | tf_op jit(solution)/shard_map/heads_back/pallas_call | solution.py:365
  248.3 2.4 fusion.4
  250.7 2.1 fusion.10
  253.4 1.6 fusion.2
  255.0 1.6 collective-permute-start.41
  259.5 8.9 %token_grad.1 = f32[1024,768]{1,0:T(8,128)} custom-call(f32[1024,768]{1,0:T(8,128)} %get-tuple-element.200.dr_ref, bf16[1024,768]{1,0:T(8,128)(2,1)} %get-tuple-element.214.dq_ref, bf16[1024,768]{1,0:T(8,128)(2,1)} %get-tuple-element.215.dk_ref, bf16[1024,768]{1,0:T(8,128)(2,1)} %get-tuple-element.216.dv_ref, bf16[3,768,768]{2,1,0:T(8,128)(2,1)} %bitcast.225, ...), custom_call_target="tpu_custom_call" | custom-call | flops 3623878656 | bytes 14548992 | tf_op jit(solution)/shard_map/token_grad/pallas_call | solution.py:597
  268.4 2.0 fusion.16
  271.7 6.6 %collective-permute-done.43 = bf16[99,24,256]{2,1,0:T(8,128)(2,1)} collective-permute-done((bf16[99,24,256]{2,1,0:T(8,128)(2,1)}, bf16[99,24,256]{2,1,0:T(8,128)(2,1)}, u32[]{:S(2)}, u32[]{:S(2)}) %collective-permute-start.43) | collective-permute-done | bytes 1216544 | tf_op jit(solution)/shard_map/ppermute | solution.py:682
  278.3 1.3 slice.128
  279.6 1.5 fusion.3
  284.2 1.3 collective-permute-start.49
  285.5 2.5 collective-permute-done.45
  287.9 1.9 fusion.15
  289.9 4.8 %collective-permute-done.44 = bf16[51,24,256]{2,1,0:T(8,128)(2,1)S(1)} collective-permute-done((bf16[51,24,256]{2,1,0:T(8,128)(2,1)S(1)}, bf16[51,24,256]{2,1,0:T(8,128)(2,1)S(1)}, u32[]{:S(2)}, u32[]{:S(2)}) %collective-permute-start.44) | collective-permute-done | bytes 626720 | tf_op jit(solution)/shard_map/ppermute | solution.py:682
  294.7 1.4 fusion.8
  296.2 1.3 collective-permute-start.46
  298.7 2.1 fusion.11
  301.3 5.5 %collective-permute-done.46 = bf16[27,24,256]{2,1,0:T(8,128)(2,1)S(1)} collective-permute-done((bf16[27,24,256]{2,1,0:T(8,128)(2,1)S(1)}, bf16[27,24,256]{2,1,0:T(8,128)(2,1)S(1)}, u32[]{:S(2)}, u32[]{:S(2)}) %collective-permute-start.46) | collective-permute-done | bytes 331808 | tf_op jit(solution)/shard_map/ppermute | solution.py:682
  309.2 2.3 collective-permute-done.48
  311.5 2.0 fusion.12
  313.4 3.6 %collective-permute-done.47 = bf16[15,24,256]{2,1,0:T(8,128)(2,1)S(1)} collective-permute-done((bf16[15,24,256]{2,1,0:T(8,128)(2,1)S(1)}, bf16[15,24,256]{2,1,0:T(8,128)(2,1)S(1)}, u32[]{:S(2)}, u32[]{:S(2)}) %collective-permute-start.47) | collective-permute-done | bytes 184352 | tf_op jit(solution)/shard_map/ppermute | solution.py:682
  (199 shorter events, 41.2 us)
Async XLA Ops:
  0.7 20.7 %copy-start.23 = (bf16[24,768]{1,0:T(8,128)(2,1)S(1)}, bf16[24,768]{1,0:T(8,128)(2,1)}, u32[]{:S(2)}) copy-start(bf16[24,768]{1,0:T(8,128)(2,1)} %param.26) | copy-start | bytes 110596
  0.7 27.8 %copy-start.19 = (bf16[24,3072]{1,0:T(8,128)(2,1)S(1)}, bf16[24,3072]{1,0:T(8,128)(2,1)}, u32[]{:S(2)}) copy-start(bf16[24,3072]{1,0:T(8,128)(2,1)} %param.32) | copy-start | bytes 442372
  2.2 11.1 %collective-permute-start = (bf16[72,768]{1,0:T(8,128)(2,1)}, bf16[72,768]{1,0:T(8,128)(2,1)S(1)}, u32[]{:S(2)}, u32[]{:S(2)}) collective-permute-start(bf16[72,768]{1,0:T(8,128)(2,1)} %pack.1), channel_id=1, source_target_pairs={{0,16},{1,17},{2,18},{3,19},{4,20},{5,21},{6,22},{7,23},{8,24},{9,... | collective-permute-start | bytes 331784 | tf_op jit(solution)/shard_map/ppermute | solution.py:682
  8.5 4.7 %collective-permute-start.1 = (bf16[16,768]{1,0:T(8,128)(2,1)S(1)}, bf16[16,768]{1,0:T(8,128)(2,1)S(1)}, u32[]{:S(2)}, u32[]{:S(2)}) collective-permute-start(bf16[16,768]{1,0:T(8,128)(2,1)S(1)} %maximum_maximum_fusion), channel_id=1, source_target_pairs={{0,16},{1,17},{2,18},{3,19},{4,20},{5,21},{6,22},{7,23},{8,24},{9,... | collective-permute-start | bytes 73736 | tf_op jit(solution)/shard_map/ppermute | solution.py:682
  14.3 4.0 %collective-permute-start.3 = (bf16[16,768]{1,0:T(8,128)(2,1)S(1)}, bf16[16,768]{1,0:T(8,128)(2,1)S(1)}, u32[]{:S(2)}, u32[]{:S(2)}) collective-permute-start(bf16[16,768]{1,0:T(8,128)(2,1)S(1)} %fusion.65), channel_id=1, source_target_pairs={{0,8},{1,9},{2,10},{3,11},{4,12},{5,13},{6,14},{7,15},{8,0},{9,1},... | collective-permute-start | bytes 73736 | tf_op jit(solution)/shard_map/ppermute | solution.py:682
  15.9 5.5 %collective-permute-start.4 = (bf16[24,768]{1,0:T(8,128)(2,1)}, bf16[24,768]{1,0:T(8,128)(2,1)S(1)}, u32[]{:S(2)}, u32[]{:S(2)}) collective-permute-start(bf16[24,768]{1,0:T(8,128)(2,1)} %param.26), channel_id=1, source_target_pairs={{0,16},{1,17},{2,18},{3,19},{4,20},{5,21},{6,22},{7,23},{8,24},{9,... | collective-permute-start | bytes 110600 | tf_op jit(solution)/shard_map/ppermute | solution.py:682
  18.2 7.2 %collective-permute-start.2 = (bf16[2,72,768]{2,1,0:T(8,128)(2,1)S(1)}, bf16[2,72,768]{2,1,0:T(8,128)(2,1)S(1)}, u32[]{:S(2)}, u32[]{:S(2)}) collective-permute-start(bf16[2,72,768]{2,1,0:T(8,128)(2,1)S(1)} %broadcast_select_fusion.10), channel_id=1, source_target_pairs={{0,8},{1,9},{2,10},{3,11},{4,12},{5,13},{6,14},{7,15},{8,0},{9,1},... | collective-permute-start | bytes 663560 | tf_op jit(solution)/shard_map/ppermute | solution.py:682
  25.5 3.9 %collective-permute-start.6 = (bf16[16,768]{1,0:T(8,128)(2,1)S(1)}, bf16[16,768]{1,0:T(8,128)(2,1)S(1)}, u32[]{:S(2)}, u32[]{:S(2)}) collective-permute-start(bf16[16,768]{1,0:T(8,128)(2,1)S(1)} %add.698), channel_id=1, source_target_pairs={{0,2},{1,5},{2,0},{3,7},{4,6},{5,1},{6,4},{7,3},{8,10},{9,13},{10,... | collective-permute-start | bytes 73736 | tf_op jit(solution)/shard_map/ppermute | solution.py:682
  27.0 5.0 %collective-permute-start.7 = (bf16[2,24,768]{2,1,0:T(8,128)(2,1)S(1)}, bf16[2,24,768]{2,1,0:T(8,128)(2,1)S(1)}, u32[]{:S(2)}, u32[]{:S(2)}) collective-permute-start(bf16[2,24,768]{2,1,0:T(8,128)(2,1)S(1)} %broadcast_select_fusion.14), channel_id=1, source_target_pairs={{0,8},{1,9},{2,10},{3,11},{4,12},{5,13},{6,14},{7,15},{8,0},{9,1},... | collective-permute-start | bytes 221192 | tf_op jit(solution)/shard_map/ppermute | solution.py:682
  27.9 8.5 %collective-permute-start.5 = (bf16[2,2,72,768]{3,2,1,0:T(8,128)(2,1)S(1)}, bf16[2,2,72,768]{3,2,1,0:T(8,128)(2,1)S(1)}, u32[]{:S(2)}, u32[]{:S(2)}) collective-permute-start(bf16[2,2,72,768]{3,2,1,0:T(8,128)(2,1)S(1)} %broadcast_select_fusion.5), channel_id=1, source_target_pairs={{0,2},{1,5},{2,0},{3,7},{4,6},{5,1},{6,4},{7,3},{8,10},{9,13},{10,... | collective-permute-start | bytes 1327112 | tf_op jit(solution)/shard_map/ppermute | solution.py:682
  28.4 7.8 %collective-permute-start.8 = (bf16[24,3072]{1,0:T(8,128)(2,1)S(1)}, bf16[24,3072]{1,0:T(8,128)(2,1)S(1)}, u32[]{:S(2)}, u32[]{:S(2)}) collective-permute-start(bf16[24,3072]{1,0:T(8,128)(2,1)S(1)} %copy-done.19), channel_id=1, source_target_pairs={{0,16},{1,17},{2,18},{3,19},{4,20},{5,21},{6,22},{7,23},{8,24},{9,... | collective-permute-start | bytes 442376 | tf_op jit(solution)/shard_map/ppermute | solution.py:682
  36.4 21.5 %copy-start.20 = (bf16[96,768]{1,0:T(8,128)(2,1)S(1)}, bf16[96,768]{1,0:T(8,128)(2,1)}, u32[]{:S(2)}) copy-start(bf16[96,768]{1,0:T(8,128)(2,1)} %param.34) | copy-start | bytes 442372
  36.5 21.9 %copy-start.10 = (bf16[4,2,72,768]{3,2,1,0:T(8,128)(2,1)}, bf16[4,2,72,768]{3,2,1,0:T(8,128)(2,1)S(1)}, u32[]{:S(2)}) copy-start(bf16[4,2,72,768]{3,2,1,0:T(8,128)(2,1)S(1)} %broadcast_select_fusion.2.refs_2_) | copy-start | bytes 2654212
  36.5 6.8 %collective-permute-start.12 = (bf16[2,2,24,768]{3,2,1,0:T(8,128)(2,1)S(1)}, bf16[2,2,24,768]{3,2,1,0:T(8,128)(2,1)S(1)}, u32[]{:S(2)}, u32[]{:S(2)}) collective-permute-start(bf16[2,2,24,768]{3,2,1,0:T(8,128)(2,1)S(1)} %broadcast_select_fusion.12), channel_id=1, source_target_pairs={{0,2},{1,5},{2,0},{3,7},{4,6},{5,1},{6,4},{7,3},{8,10},{9,13},{10,... | collective-permute-start | bytes 442376 | tf_op jit(solution)/shard_map/ppermute | solution.py:682
  38.1 6.7 %collective-permute-start.13 = (bf16[2,24,3072]{2,1,0:T(8,128)(2,1)S(1)}, bf16[2,24,3072]{2,1,0:T(8,128)(2,1)S(1)}, u32[]{:S(2)}, u32[]{:S(2)}) collective-permute-start(bf16[2,24,3072]{2,1,0:T(8,128)(2,1)S(1)} %broadcast_select_fusion.9), channel_id=1, source_target_pairs={{0,8},{1,9},{2,10},{3,11},{4,12},{5,13},{6,14},{7,15},{8,0},{9,1},... | collective-permute-start | bytes 884744 | tf_op jit(solution)/shard_map/ppermute | solution.py:682
  38.1 3.8 %collective-permute-start.11 = (bf16[16,768]{1,0:T(8,128)(2,1)S(1)}, bf16[16,768]{1,0:T(8,128)(2,1)S(1)}, u32[]{:S(2)}, u32[]{:S(2)}) collective-permute-start(bf16[16,768]{1,0:T(8,128)(2,1)S(1)} %add.699), channel_id=1, source_target_pairs={{0,4},{1,3},{2,6},{3,1},{4,0},{5,7},{6,2},{7,5},{8,12},{9,11},{10,... | collective-permute-start | bytes 73736 | tf_op jit(solution)/shard_map/ppermute | solution.py:682
  39.6 13.0 %collective-permute-start.9 = (bf16[4,2,72,768]{3,2,1,0:T(8,128)(2,1)S(1)}, bf16[4,2,72,768]{3,2,1,0:T(8,128)(2,1)S(1)}, u32[]{:S(2)}, u32[]{:S(2)}) collective-permute-start(bf16[4,2,72,768]{3,2,1,0:T(8,128)(2,1)S(1)} %broadcast_select_fusion.2.refs_2_), channel_id=1, source_target_pairs={{0,4},{1,3},{2,6},{3,1},{4,0},{5,7},{6,2},{7,5},{8,12},{9,11},{10,... | collective-permute-start | bytes 2654216 | tf_op jit(solution)/shard_map/ppermute | solution.py:682
  40.1 12.5 %collective-permute-start.10 = (bf16[4,2,72,768]{3,2,1,0:T(8,128)(2,1)S(1)}, bf16[4,2,72,768]{3,2,1,0:T(8,128)(2,1)S(1)}, u32[]{:S(2)}, u32[]{:S(2)}) collective-permute-start(bf16[4,2,72,768]{3,2,1,0:T(8,128)(2,1)S(1)} %broadcast_select_fusion.2.refs_2_), channel_id=1, source_target_pairs={{0,1},{1,0},{2,3},{3,2},{4,5},{5,4},{6,7},{7,6},{8,9},{9,8},{10,11... | collective-permute-start | bytes 2654216 | tf_op jit(solution)/shard_map/ppermute | solution.py:682
  43.5 26.2 %copy-start.14 = (bf16[4,2,24,768]{3,2,1,0:T(8,128)(2,1)}, bf16[4,2,24,768]{3,2,1,0:T(8,128)(2,1)S(1)}, u32[]{:S(2)}) copy-start(bf16[4,2,24,768]{3,2,1,0:T(8,128)(2,1)S(1)} %broadcast_select_fusion.8.refs_3_) | copy-start | bytes 884740
  52.7 3.1 collective-permute-start.14
  52.8 2.4 collective-permute-start.15
  55.8 12.4 %collective-permute-start.17 = (bf16[2,2,24,3072]{3,2,1,0:T(8,128)(2,1)S(1)}, bf16[2,2,24,3072]{3,2,1,0:T(8,128)(2,1)S(1)}, u32[]{:S(2)}, u32[]{:S(2)}) collective-permute-start(bf16[2,2,24,3072]{3,2,1,0:T(8,128)(2,1)S(1)} %broadcast_select_fusion.4), channel_id=1, source_target_pairs={{0,2},{1,5},{2,0},{3,7},{4,6},{5,1},{6,4},{7,3},{8,10},{9,13},{10,... | collective-permute-start | bytes 1769480 | tf_op jit(solution)/shard_map/ppermute | solution.py:682
  57.3 11.1 %collective-permute-start.16 = (bf16[4,2,24,768]{3,2,1,0:T(8,128)(2,1)S(1)}, bf16[4,2,24,768]{3,2,1,0:T(8,128)(2,1)S(1)}, u32[]{:S(2)}, u32[]{:S(2)}) collective-permute-start(bf16[4,2,24,768]{3,2,1,0:T(8,128)(2,1)S(1)} %broadcast_select_fusion.8.refs_3_), channel_id=1, source_target_pairs={{0,4},{1,3},{2,6},{3,1},{4,0},{5,7},{6,2},{7,5},{8,12},{9,11},{10,... | collective-permute-start | bytes 884744 | tf_op jit(solution)/shard_map/ppermute | solution.py:682
  57.8 9.5 %collective-permute-start.18 = (bf16[96,768]{1,0:T(8,128)(2,1)S(1)}, bf16[96,768]{1,0:T(8,128)(2,1)S(1)}, u32[]{:S(2)}, u32[]{:S(2)}) collective-permute-start(bf16[96,768]{1,0:T(8,128)(2,1)S(1)} %copy-done.20), channel_id=1, source_target_pairs={{0,16},{1,17},{2,18},{3,19},{4,20},{5,21},{6,22},{7,23},{8,24},{9,... | collective-permute-start | bytes 442376 | tf_op jit(solution)/shard_map/ppermute | solution.py:682
  68.4 16.4 %copy-start.5 = (bf16[4,2,24,3072]{3,2,1,0:T(8,128)(2,1)}, bf16[4,2,24,3072]{3,2,1,0:T(8,128)(2,1)S(1)}, u32[]{:S(2)}) copy-start(bf16[4,2,24,3072]{3,2,1,0:T(8,128)(2,1)S(1)} %broadcast_select_fusion.1.refs_2_) | copy-start | bytes 3538948
  68.4 14.1 %copy-start.29 = (bf16[4,2,24,768]{3,2,1,0:T(8,128)(2,1)}, bf16[4,2,24,768]{3,2,1,0:T(8,128)(2,1)S(1)}, u32[]{:S(2)}) copy-start(bf16[4,2,24,768]{3,2,1,0:T(8,128)(2,1)S(1)} %collective-permute-done.16.refs_4_) | copy-start | bytes 884740
  68.5 16.4 %collective-permute-start.19 = (bf16[4,2,24,3072]{3,2,1,0:T(8,128)(2,1)S(1)}, bf16[4,2,24,3072]{3,2,1,0:T(8,128)(2,1)}, u32[]{:S(2)}, u32[]{:S(2)}) collective-permute-start(bf16[4,2,24,3072]{3,2,1,0:T(8,128)(2,1)S(1)} %broadcast_select_fusion.1.refs_2_), channel_id=1, source_target_pairs={{0,4},{1,3},{2,6},{3,1},{4,0},{5,7},{6,2},{7,5},{8,12},{9,11},{10,... | collective-permute-start | bytes 3538952 | tf_op jit(solution)/shard_map/ppermute | solution.py:682
  69.6 13.1 %collective-permute-start.21 = (bf16[4,2,24,768]{3,2,1,0:T(8,128)(2,1)S(1)}, bf16[4,2,24,768]{3,2,1,0:T(8,128)(2,1)S(1)}, u32[]{:S(2)}, u32[]{:S(2)}) collective-permute-start(bf16[4,2,24,768]{3,2,1,0:T(8,128)(2,1)S(1)} %broadcast_select_fusion.8.refs_3_), channel_id=1, source_target_pairs={{0,1},{1,0},{2,3},{3,2},{4,5},{5,4},{6,7},{7,6},{8,9},{9,8},{10,11... | collective-permute-start | bytes 884744 | tf_op jit(solution)/shard_map/ppermute | solution.py:682
  69.6 12.9 %collective-permute-start.20 = (bf16[2,96,768]{2,1,0:T(8,128)(2,1)S(1)}, bf16[2,96,768]{2,1,0:T(8,128)(2,1)S(1)}, u32[]{:S(2)}, u32[]{:S(2)}) collective-permute-start(bf16[2,96,768]{2,1,0:T(8,128)(2,1)S(1)} %broadcast_select_fusion.7), channel_id=1, source_target_pairs={{0,8},{1,9},{2,10},{3,11},{4,12},{5,13},{6,14},{7,15},{8,0},{9,1},... | collective-permute-start | bytes 884744 | tf_op jit(solution)/shard_map/ppermute | solution.py:682
  71.7 11.1 %collective-permute-start.22 = (bf16[4,2,24,768]{3,2,1,0:T(8,128)(2,1)S(1)}, bf16[4,2,24,768]{3,2,1,0:T(8,128)(2,1)S(1)}, u32[]{:S(2)}, u32[]{:S(2)}) collective-permute-start(bf16[4,2,24,768]{3,2,1,0:T(8,128)(2,1)S(1)} %collective-permute-done.16.refs_4_), channel_id=1, source_target_pairs={{0,1},{1,0},{2,3},{3,2},{4,5},{5,4},{6,7},{7,6},{8,9},{9,8},{10,11... | collective-permute-start | bytes 884744 | tf_op jit(solution)/shard_map/ppermute | solution.py:682
  84.8 10.6 %collective-permute-start.23 = (bf16[4,2,24,3072]{3,2,1,0:T(8,128)(2,1)S(1)}, bf16[4,2,24,3072]{3,2,1,0:T(8,128)(2,1)}, u32[]{:S(2)}, u32[]{:S(2)}) collective-permute-start(bf16[4,2,24,3072]{3,2,1,0:T(8,128)(2,1)S(1)} %broadcast_select_fusion.1.refs_2_), channel_id=1, source_target_pairs={{0,1},{1,0},{2,3},{3,2},{4,5},{5,4},{6,7},{7,6},{8,9},{9,8},{10,11... | collective-permute-start | bytes 3538952 | tf_op jit(solution)/shard_map/ppermute | solution.py:682
  84.8 10.6 %collective-permute-start.24 = (bf16[4,2,24,3072]{3,2,1,0:T(8,128)(2,1)}, bf16[4,2,24,3072]{3,2,1,0:T(8,128)(2,1)}, u32[]{:S(2)}, u32[]{:S(2)}) collective-permute-start(bf16[4,2,24,3072]{3,2,1,0:T(8,128)(2,1)} %collective-permute-done.19.refs_3_), channel_id=1, source_target_pairs={{0,1},{1,0},{2,3},{3,2},{4,5},{5,4},{6,7},{7,6},{8,9},{9,8},{10,11... | collective-permute-start | bytes 3538952 | tf_op jit(solution)/shard_map/ppermute | solution.py:682
  85.4 9.9 %collective-permute-start.25 = (bf16[2,2,96,768]{3,2,1,0:T(8,128)(2,1)S(1)}, bf16[2,2,96,768]{3,2,1,0:T(8,128)(2,1)S(1)}, u32[]{:S(2)}, u32[]{:S(2)}) collective-permute-start(bf16[2,2,96,768]{3,2,1,0:T(8,128)(2,1)S(1)} %broadcast_select_fusion.3), channel_id=1, source_target_pairs={{0,2},{1,5},{2,0},{3,7},{4,6},{5,1},{6,4},{7,3},{8,10},{9,13},{10,... | collective-permute-start | bytes 1769480 | tf_op jit(solution)/shard_map/ppermute | solution.py:682
  95.4 23.2 %copy-start.6 = (bf16[4,2,96,768]{3,2,1,0:T(8,128)(2,1)}, bf16[4,2,96,768]{3,2,1,0:T(8,128)(2,1)S(1)}, u32[]{:S(2)}) copy-start(bf16[4,2,96,768]{3,2,1,0:T(8,128)(2,1)S(1)} %broadcast_select_fusion.refs_3_) | copy-start | bytes 3538948
  95.4 23.2 %collective-permute-start.26 = (bf16[4,2,96,768]{3,2,1,0:T(8,128)(2,1)S(1)}, bf16[4,2,96,768]{3,2,1,0:T(8,128)(2,1)S(1)}, u32[]{:S(2)}, u32[]{:S(2)}) collective-permute-start(bf16[4,2,96,768]{3,2,1,0:T(8,128)(2,1)S(1)} %broadcast_select_fusion.refs_3_), channel_id=1, source_target_pairs={{0,4},{1,3},{2,6},{3,1},{4,0},{5,7},{6,2},{7,5},{8,12},{9,11},{10,... | collective-permute-start | bytes 3538952 | tf_op jit(solution)/shard_map/ppermute | solution.py:682
  96.6 22.0 %collective-permute-start.27 = (bf16[4,2,96,768]{3,2,1,0:T(8,128)(2,1)S(1)}, bf16[4,2,96,768]{3,2,1,0:T(8,128)(2,1)}, u32[]{:S(2)}, u32[]{:S(2)}) collective-permute-start(bf16[4,2,96,768]{3,2,1,0:T(8,128)(2,1)S(1)} %broadcast_select_fusion.refs_3_), channel_id=1, source_target_pairs={{0,1},{1,0},{2,3},{3,2},{4,5},{5,4},{6,7},{7,6},{8,9},{9,8},{10,11... | collective-permute-start | bytes 3538952 | tf_op jit(solution)/shard_map/ppermute | solution.py:682
  118.6 3.0 collective-permute-start.28
  136.2 4.7 %collective-permute-start.29 = (bf16[8,1536]{1,0:T(8,128)(2,1)S(1)}, bf16[8,1536]{1,0:T(8,128)(2,1)S(1)}, u32[]{:S(2)}, u32[]{:S(2)}) collective-permute-start(bf16[8,1536]{1,0:T(8,128)(2,1)S(1)} %convert_element_type.383), channel_id=1, source_target_pairs={{0,16},{1,17},{2,18},{3,19},{4,20},{5,21},{6,22},{7,23},{8,24},{9,... | collective-permute-start | bytes 73736 | tf_op jit(solution)/shard_map/ppermute | solution.py:682
  141.0 4.1 %collective-permute-start.30 = (bf16[2,8,1536]{2,1,0:T(8,128)(2,1)S(1)}, bf16[2,8,1536]{2,1,0:T(8,128)(2,1)S(1)}, u32[]{:S(2)}, u32[]{:S(2)}) collective-permute-start(bf16[2,8,1536]{2,1,0:T(8,128)(2,1)S(1)} %broadcast_select_fusion.15), channel_id=1, source_target_pairs={{0,8},{1,9},{2,10},{3,11},{4,12},{5,13},{6,14},{7,15},{8,0},{9,1},... | collective-permute-start | bytes 147464 | tf_op jit(solution)/shard_map/ppermute | solution.py:682
  145.2 4.7 %collective-permute-start.31 = (bf16[2,2,8,1536]{3,2,1,0:T(8,128)(2,1)S(1)}, bf16[2,2,8,1536]{3,2,1,0:T(8,128)(2,1)S(1)}, u32[]{:S(2)}, u32[]{:S(2)}) collective-permute-start(bf16[2,2,8,1536]{3,2,1,0:T(8,128)(2,1)S(1)} %broadcast_select_fusion.13), channel_id=1, source_target_pairs={{0,2},{1,5},{2,0},{3,7},{4,6},{5,1},{6,4},{7,3},{8,10},{9,13},{10,... | collective-permute-start | bytes 294920 | tf_op jit(solution)/shard_map/ppermute | solution.py:682
  150.1 5.7 %collective-permute-start.32 = (bf16[2,2,2,8,1536]{4,3,2,1,0:T(8,128)(2,1)S(1)}, bf16[2,2,2,8,1536]{4,3,2,1,0:T(8,128)(2,1)S(1)}, u32[]{:S(2)}, u32[]{:S(2)}) collective-permute-start(bf16[2,2,2,8,1536]{4,3,2,1,0:T(8,128)(2,1)S(1)} %broadcast_select_fusion.11), channel_id=1, source_target_pairs={{0,4},{1,3},{2,6},{3,1},{4,0},{5,7},{6,2},{7,5},{8,12},{9,11},{10,... | collective-permute-start | bytes 589832 | tf_op jit(solution)/shard_map/ppermute | solution.py:682
  155.9 1.8 collective-permute-start.33
  176.0 15.8 %collective-permute-start.34 = (bf16[4,2,2,96,768]{4,3,2,1,0:T(8,128)(2,1)}, bf16[4,2,2,96,768]{4,3,2,1,0:T(8,128)(2,1)}, u32[]{:S(2)}, u32[]{:S(2)}) collective-permute-start(bf16[4,2,2,96,768]{4,3,2,1,0:T(8,128)(2,1)} %get-tuple-element.193), channel_id=1, source_target_pairs={{0,1},{1,0},{2,3},{3,2},{4,5},{5,4},{6,7},{7,6},{8,9},{9,8},{10,11... | collective-permute-start | bytes 7077896 | tf_op jit(solution)/shard_map/ppermute | solution.py:682
  176.1 15.7 %copy-start.3 = (bf16[4,2,2,96,768]{4,3,2,1,0:T(8,128)(2,1)S(1)}, bf16[4,2,2,96,768]{4,3,2,1,0:T(8,128)(2,1)}, u32[]{:S(2)}) copy-start(bf16[4,2,2,96,768]{4,3,2,1,0:T(8,128)(2,1)} %get-tuple-element.192) | copy-start | bytes 7077892
  193.4 21.7 %collective-permute-start.36 = (bf16[4,2,2,24,3072]{4,3,2,1,0:T(8,128)(2,1)}, bf16[4,2,2,24,3072]{4,3,2,1,0:T(8,128)(2,1)}, u32[]{:S(2)}, u32[]{:S(2)}) collective-permute-start(bf16[4,2,2,24,3072]{4,3,2,1,0:T(8,128)(2,1)} %get-tuple-element.204), channel_id=1, source_target_pairs={{0,1},{1,0},{2,3},{3,2},{4,5},{5,4},{6,7},{7,6},{8,9},{9,8},{10,11... | collective-permute-start | bytes 7077896 | tf_op jit(solution)/shard_map/ppermute | solution.py:682
  194.0 18.6 %collective-permute-start.35 = (bf16[2,2,2,96,768]{4,3,0,2,1:T(8,128)(2,1)S(1)}, bf16[2,2,2,96,768]{4,3,0,2,1:T(8,128)(2,1)}, u32[]{:S(2)}, u32[]{:S(2)}) collective-permute-start(bf16[2,2,2,96,768]{4,3,0,2,1:T(8,128)(2,1)S(1)} %copy.47), channel_id=1, source_target_pairs={{0,2},{1,5},{2,0},{3,7},{4,6},{5,1},{6,4},{7,3},{8,10},{9,13},{10,... | collective-permute-start | bytes 3538952 | tf_op jit(solution)/shard_map/ppermute | solution.py:682
  217.9 28.8 %collective-permute-start.37 = (bf16[2,2,96,768]{3,2,1,0:T(8,128)(2,1)}, bf16[2,2,96,768]{3,2,1,0:T(8,128)(2,1)}, u32[]{:S(2)}, u32[]{:S(2)}) collective-permute-start(bf16[2,2,96,768]{3,2,1,0:T(8,128)(2,1)} %fusion.5), channel_id=1, source_target_pairs={{0,4},{1,3},{2,6},{3,1},{4,0},{5,7},{6,2},{7,5},{8,12},{9,11},{10,... | collective-permute-start | bytes 1769480 | tf_op jit(solution)/shard_map/ppermute | solution.py:682
  218.9 27.8 %collective-permute-start.38 = (bf16[2,2,2,24,3072]{4,3,2,1,0:T(8,128)(2,1)}, bf16[2,2,2,24,3072]{4,3,2,1,0:T(8,128)(2,1)S(1)}, u32[]{:S(2)}, u32[]{:S(2)}) collective-permute-start(bf16[2,2,2,24,3072]{4,3,2,1,0:T(8,128)(2,1)} %fusion.1), channel_id=1, source_target_pairs={{0,8},{1,9},{2,10},{3,11},{4,12},{5,13},{6,14},{7,15},{8,0},{9,1},... | collective-permute-start | bytes 3538952 | tf_op jit(solution)/shard_map/ppermute | solution.py:682
  246.7 23.7 %copy-start.9 = (bf16[2,2,2,24,3072]{4,3,2,1,0:T(8,128)(2,1)}, bf16[2,2,2,24,3072]{4,3,2,1,0:T(8,128)(2,1)S(1)}, u32[]{:S(2)}) copy-start(bf16[2,2,2,24,3072]{4,3,2,1,0:T(8,128)(2,1)S(1)} %collective-permute-done.38) | copy-start | bytes 3538948
  246.7 6.1 %collective-permute-start.39 = (bf16[4,2,2,12,24,256]{5,4,3,2,1,0:T(8,128)(2,1)}, bf16[4,2,2,12,24,256]{5,4,3,2,1,0:T(8,128)(2,1)}, u32[]{:S(2)}, u32[]{:S(2)}) collective-permute-start(bf16[4,2,2,12,24,256]{5,4,3,2,1,0:T(8,128)(2,1)} %get-tuple-element.221), channel_id=1, source_target_pairs={{0,1},{1,0},{2,3},{3,2},{4,5},{5,4},{6,7},{7,6},{8,9},{9,8},{10,11... | collective-permute-start | bytes 7077896 | tf_op jit(solution)/shard_map/ppermute | solution.py:682
  247.8 4.9 %collective-permute-start.42 = (bf16[3,24,256]{2,1,0:T(8,128)(2,1)S(1)}, bf16[3,24,256]{2,1,0:T(8,128)(2,1)S(1)}, u32[]{:S(2)}, u32[]{:S(2)}) collective-permute-start(bf16[3,24,256]{2,1,0:T(8,128)(2,1)S(1)} %convert_element_type.431), channel_id=1, source_target_pairs={{0,1},{1,0},{2,3},{3,2},{4,5},{5,4},{6,7},{7,6},{8,9},{9,8},{10,11... | collective-permute-start | bytes 110600 | tf_op jit(solution)/shard_map/ppermute | solution.py:682
  255.0 15.4 %collective-permute-start.41 = (bf16[2,2,24,3072]{3,2,1,0:T(8,128)(2,1)}, bf16[2,2,24,3072]{3,2,1,0:T(8,128)(2,1)}, u32[]{:S(2)}, u32[]{:S(2)}) collective-permute-start(bf16[2,2,24,3072]{3,2,1,0:T(8,128)(2,1)} %fusion.4), channel_id=1, source_target_pairs={{0,2},{1,5},{2,0},{3,7},{4,6},{5,1},{6,4},{7,3},{8,10},{9,13},{10,... | collective-permute-start | bytes 1769480 | tf_op jit(solution)/shard_map/ppermute | solution.py:682
  257.7 20.5 %collective-permute-start.43 = (bf16[99,24,256]{2,1,0:T(8,128)(2,1)}, bf16[99,24,256]{2,1,0:T(8,128)(2,1)}, u32[]{:S(2)}, u32[]{:S(2)}) collective-permute-start(bf16[99,24,256]{2,1,0:T(8,128)(2,1)} %pad_maximum_fusion), channel_id=1, source_target_pairs={{0,2},{1,5},{2,0},{3,7},{4,6},{5,1},{6,4},{7,3},{8,10},{9,13},{10,... | collective-permute-start | bytes 3649544 | tf_op jit(solution)/shard_map/ppermute | solution.py:682
  258.2 10.2 %collective-permute-start.40 = (bf16[2,96,768]{2,1,0:T(8,128)(2,1)}, bf16[2,96,768]{2,1,0:T(8,128)(2,1)S(1)}, u32[]{:S(2)}, u32[]{:S(2)}) collective-permute-start(bf16[2,96,768]{2,1,0:T(8,128)(2,1)} %fusion.10), channel_id=1, source_target_pairs={{0,8},{1,9},{2,10},{3,11},{4,12},{5,13},{6,14},{7,15},{8,0},{9,1},... | collective-permute-start | bytes 884744 | tf_op jit(solution)/shard_map/ppermute | solution.py:682
  268.4 11.2 %copy-start.15 = (bf16[2,96,768]{2,1,0:T(8,128)(2,1)}, bf16[2,96,768]{2,1,0:T(8,128)(2,1)S(1)}, u32[]{:S(2)}) copy-start(bf16[2,96,768]{2,1,0:T(8,128)(2,1)S(1)} %collective-permute-done.40) | copy-start | bytes 884740
  281.1 6.8 %collective-permute-start.45 = (bf16[2,24,3072]{2,1,0:T(8,128)(2,1)S(1)}, bf16[2,24,3072]{2,1,0:T(8,128)(2,1)S(1)}, u32[]{:S(2)}, u32[]{:S(2)}) collective-permute-start(bf16[2,24,3072]{2,1,0:T(8,128)(2,1)S(1)} %fusion.9), channel_id=1, source_target_pairs={{0,4},{1,3},{2,6},{3,1},{4,0},{5,7},{6,2},{7,5},{8,12},{9,11},{10,... | collective-permute-start | bytes 884744 | tf_op jit(solution)/shard_map/ppermute | solution.py:682
  283.1 13.0 %copy-start.7 = (f32[3,24,256]{2,1,0:T(8,128)}, f32[3,24,256]{2,1,0:T(8,128)S(1)}, u32[]{:S(2)}) copy-start(f32[3,24,256]{2,1,0:T(8,128)S(1)} %get-tuple-element.233) | copy-start | bytes 221188
  283.2 11.5 %collective-permute-start.44 = (bf16[51,24,256]{2,1,0:T(8,128)(2,1)S(1)}, bf16[51,24,256]{2,1,0:T(8,128)(2,1)S(1)}, u32[]{:S(2)}, u32[]{:S(2)}) collective-permute-start(bf16[51,24,256]{2,1,0:T(8,128)(2,1)S(1)} %pad_maximum_fusion.2), channel_id=1, source_target_pairs={{0,4},{1,3},{2,6},{3,1},{4,0},{5,7},{6,2},{7,5},{8,12},{9,11},{10,... | collective-permute-start | bytes 1880072 | tf_op jit(solution)/shard_map/ppermute | solution.py:682
  284.2 14.6 %collective-permute-start.49 = (bf16[96,768]{1,0:T(8,128)(2,1)}, bf16[96,768]{1,0:T(8,128)(2,1)}, u32[]{:S(2)}, u32[]{:S(2)}) collective-permute-start(bf16[96,768]{1,0:T(8,128)(2,1)} %fusion.16), channel_id=1, source_target_pairs={{0,16},{1,17},{2,18},{3,19},{4,20},{5,21},{6,22},{7,23},{8,24},{9,... | collective-permute-start | bytes 442376 | tf_op jit(solution)/shard_map/ppermute | solution.py:682
  296.2 10.7 %collective-permute-start.46 = (bf16[27,24,256]{2,1,0:T(8,128)(2,1)S(1)}, bf16[27,24,256]{2,1,0:T(8,128)(2,1)S(1)}, u32[]{:S(2)}, u32[]{:S(2)}) collective-permute-start(bf16[27,24,256]{2,1,0:T(8,128)(2,1)S(1)} %pad_maximum_fusion.3), channel_id=1, source_target_pairs={{0,8},{1,9},{2,10},{3,11},{4,12},{5,13},{6,14},{7,15},{8,0},{9,1},... | collective-permute-start | bytes 995336 | tf_op jit(solution)/shard_map/ppermute | solution.py:682
  298.7 12.7 %copy-start.18 = (bf16[2,24,3072]{2,1,0:T(8,128)(2,1)S(1)}, bf16[2,24,3072]{2,1,0:T(8,128)(2,1)}, u32[]{:S(2)}) copy-start(bf16[2,24,3072]{2,1,0:T(8,128)(2,1)} %copy-done.17) | copy-start | bytes 884740
  300.8 10.7 %collective-permute-start.48 = (bf16[24,3072]{1,0:T(8,128)(2,1)}, bf16[24,3072]{1,0:T(8,128)(2,1)S(1)}, u32[]{:S(2)}, u32[]{:S(2)}) collective-permute-start(bf16[24,3072]{1,0:T(8,128)(2,1)} %fusion.15), channel_id=1, source_target_pairs={{0,16},{1,17},{2,18},{3,19},{4,20},{5,21},{6,22},{7,23},{8,24},{9,... | collective-permute-start | bytes 442376 | tf_op jit(solution)/shard_map/ppermute | solution.py:682
  308.8 8.2 %collective-permute-start.47 = (bf16[15,24,256]{2,1,0:T(8,128)(2,1)S(1)}, bf16[15,24,256]{2,1,0:T(8,128)(2,1)S(1)}, u32[]{:S(2)}, u32[]{:S(2)}) collective-permute-start(bf16[15,24,256]{2,1,0:T(8,128)(2,1)S(1)} %pad_maximum_fusion.4), channel_id=1, source_target_pairs={{0,16},{1,17},{2,18},{3,19},{4,20},{5,21},{6,22},{7,23},{8,24},{9,... | collective-permute-start | bytes 552968 | tf_op jit(solution)/shard_map/ppermute | solution.py:682
  311.5 11.2 %copy-start.1 = (bf16[96]{0:T(256)(128)(2,1)S(1)}, bf16[96]{0:T(256)(128)(2,1)}, u32[]{:S(2)}) copy-start(bf16[96]{0:T(256)(128)(2,1)} %param.33) | copy-start | bytes 580
  (18 other events, 77.7 us)

commit v4 on v3

--- a/solution.py
+++ b/solution.py
@@ -16,6 +16,7 @@
 ROWS = 256
 BLOCK = 768
 AXIS = "fsdp"
+CUBE = 32
 norm_eps = 1e-12
 pool_eps = 1e-06
 sim_scale = 50.0
@@ -236,15 +237,20 @@
     )(lengths, q, k, v, *before)
 
 
+def halves(ref):
+    return [slice(i * ROWS, (i + 1) * ROWS) for i in range(ref.shape[0] // ROWS)]
+
+
 def close_body(cube, x_ref, c_ref, vec_ref, *refs):
     parts, (hat_ref, inv_ref, n_ref, full_ref, w_ref, sems, out_sem) = refs[:-7], refs[-7:]
     onward = assemble(cube, parts, w_ref, full_ref, sems, out_sem)
-    w = w_ref.reshape(D, D) if cube else w_ref
-    branch = nn(c_ref[...], w[...]) + vec_ref[B_OUTPUT : B_OUTPUT + 1].astype(f32)
-    hat, inv = layer_norm(x_ref[...].astype(f32) + branch)
-    hat_ref[...] = hat
-    inv_ref[...] = inv
-    n_ref[...] = (hat * vec_ref[G_ATTN : G_ATTN + 1].astype(f32) + vec_ref[S_ATTN : S_ATTN + 1].astype(f32)).astype(low)
+    w = (w_ref.reshape(D, D) if cube else w_ref)[...]
+    branches = [nn(c_ref[r, :], w) + vec_ref[B_OUTPUT : B_OUTPUT + 1].astype(f32) for r in halves(x_ref)]
+    for r, branch in zip(halves(x_ref), branches):
+        hat, inv = layer_norm(x_ref[r, :].astype(f32) + branch)
+        hat_ref[r, :] = hat
+        inv_ref[r, :] = inv
+        n_ref[r, :] = (hat * vec_ref[G_ATTN : G_ATTN + 1].astype(f32) + vec_ref[S_ATTN : S_ATTN + 1].astype(f32)).astype(low)
 
     @pl.when(pl.program_id(0) == pl.num_programs(0) - 1)
     def _():
@@ -256,9 +262,9 @@
     shape = (4, 2, 2, 2, 24, D) if cube else (D, D)
     hat, inv, n, full = pl.pallas_call(
         lambda *refs: close_body(cube, *refs),
-        grid=(t // ROWS,),
-        in_specs=[row_block(D), row_block(D), whole(vec.shape)] + [ANY] * len(parts),
-        out_specs=[row_block(D), row_block(1), row_block(D), ANY],
+        grid=(t // (2 * ROWS),),
+        in_specs=[row_block(D, 2 * ROWS), row_block(D, 2 * ROWS), whole(vec.shape)] + [ANY] * len(parts),
+        out_specs=[row_block(D, 2 * ROWS), row_block(1, 2 * ROWS), row_block(D, 2 * ROWS), ANY],
         out_shape=[S((t, D), f32), S((t, 1), f32), S((t, D), low), S(shape, low)],
         scratch_shapes=scratch_for(shape),
         name="close",
@@ -268,47 +274,55 @@
 
 
 def open_back_body(dres_ref, dh_ref, wi_ref, hat_ref, inv_ref, wo_ref, vec_ref, before_ref, dr_ref, da_ref, dc_ref, sums_ref):
-    hat = hat_ref[...]
-    dn = dres_ref[...] + nt(dh_ref[...], wi_ref[...])
-    dres = layer_norm_back(dn, vec_ref[G_ATTN : G_ATTN + 1].astype(f32), hat, inv_ref[...])
-    dr_ref[...] = dres
-    dao = dres.astype(low)
-    da_ref[...] = dao
-    dc_ref[...] = nt(dao, wo_ref[0]).astype(low)
-
     @pl.when(pl.program_id(0) == 0)
     def _():
         sums_ref[...] = before_ref[...]
 
-    sums_ref[B_OUTPUT : B_OUTPUT + 1] += jnp.sum(dao.astype(f32), axis=0, keepdims=True)
-    sums_ref[G_ATTN : G_ATTN + 1] += jnp.sum(dn * hat, axis=0, keepdims=True)
-    sums_ref[S_ATTN : S_ATTN + 1] += jnp.sum(dn, axis=0, keepdims=True)
+    grads = [dres_ref[r, :] + nt(dh_ref[r, :], wi_ref[...]) for r in halves(dres_ref)]
+    for r, dn in zip(halves(dres_ref), grads):
+        hat = hat_ref[r, :]
+        dres = layer_norm_back(dn, vec_ref[G_ATTN : G_ATTN + 1].astype(f32), hat, inv_ref[r, :])
+        dr_ref[r, :] = dres
+        dao = dres.astype(low)
+        da_ref[r, :] = dao
+        dc_ref[r, :] = nt(dao, wo_ref[0]).astype(low)
+        sums_ref[B_OUTPUT : B_OUTPUT + 1] += jnp.sum(dao.astype(f32), axis=0, keepdims=True)
+        sums_ref[G_ATTN : G_ATTN + 1] += jnp.sum(dn * hat, axis=0, keepdims=True)
+        sums_ref[S_ATTN : S_ATTN + 1] += jnp.sum(dn, axis=0, keepdims=True)
 
 
 def open_back(dres, dh, wi, hat, inv, full, vec, sums):
     t = dres.shape[0]
     return pl.pallas_call(
         open_back_body,
-        grid=(t // ROWS,),
-        in_specs=[row_block(D), row_block(FF), whole(wi.shape), row_block(D), row_block(1), mat_of(0), whole(vec.shape), whole((16, D))],
-        out_specs=[row_block(D)] * 3 + [whole((16, D))],
+        grid=(t // (2 * ROWS),),
+        in_specs=[row_block(D, 2 * ROWS), row_block(FF, 2 * ROWS), whole(wi.shape), row_block(D, 2 * ROWS), row_block(1, 2 * ROWS), mat_of(0), whole(vec.shape), whole((16, D))],
+        out_specs=[row_block(D, 2 * ROWS)] * 3 + [whole((16, D))],
         out_shape=[S((t, D), f32), S((t, D), low), S((t, D), low), S((16, D), f32)],
         name="open_back",
         **params(10 * t * D * D, 20 * t * D + 10 * D * D, room=60),
     )(dres, dh, wi, hat, inv, full, vec, sums)
 
 
-def heads_back_body(cube, q_ref, k_ref, v_ref, dc_ref, p_ref, x_ref, before_ref, c_hbm, da_hbm, *refs):
-    dq_ref, dk_ref, dv_ref, sums_ref = refs[:4]
-    shares, (c_ref, da_ref, sems) = refs[4:-3], refs[-3:]
+def device_rows(table):
+    rows = 8 * CUBE
+    row, lane = (lax.broadcasted_iota(jnp.int32, (rows, D), axis) for axis in range(2))
+    out = []
+    for values, r in (
+        (jnp.concatenate([table[:8]] * CUBE, axis=0), D // CUBE),
+        (jnp.concatenate([jnp.broadcast_to(table[B_INNER + j : B_INNER + j + 1], (rows * D // FF, D)) for j in range(FF // D)], axis=0), FF // CUBE),
+    ):
+        own = jnp.where(lane // r == (row // 8) % (D // r), values, 0.0).astype(low)
+        at, to = (lax.broadcasted_iota(jnp.int32, (D, WIDE // 2), axis) for axis in range(2))
+        out.append(nn(own, jnp.where(at % r == to, 1.0, 0.0).astype(low)))
+    return jnp.concatenate(out, axis=1)
+
+
+def heads_back_body(cube, q_ref, k_ref, v_ref, dc_ref, p_ref, x_ref, before_ref, c_ref, da_ref, *refs):
+    dq_ref, dk_ref, dv_ref, *shares = refs[:-1]
+    table_ref = refs[-1]
     step = pl.program_id(0)
-    copies = [pltpu.make_async_copy(c_hbm, c_ref, sems.at[0]), pltpu.make_async_copy(da_hbm, da_ref, sems.at[1])]
     masks, masks32 = head_masks(low), head_masks(f32)
-
-    @pl.when(step == 0)
-    def _():
-        for copy in copies:
-            copy.start()
 
     def sentence(s):
         rows = pl.ds(pl.multiple_of(s * LEN, LEN), LEN)
@@ -320,57 +334,63 @@
         dk_ref[rows, :] = (nn(ds, stacked(q, masks)) * HEAD_DIM ** (-0.5)).astype(low)
         dq_ref[rows, :] = (unstacked(tn(ds, k), masks32) * HEAD_DIM ** (-0.5)).astype(low)
 
-    @pl.when(step < GROUPS)
-    def _():
-        pl.loop(0, q_ref.shape[0] // LEN, unroll=BACK_UNROLL)(sentence)
-        sums_ref[...] = jnp.zeros_like(sums_ref)
-        sums_ref[0, :16, :] = before_ref[...]
-        sums_ref[0, B_QUERY : B_QUERY + 1] = jnp.sum(dq_ref[...].astype(f32), axis=0, keepdims=True)
-        sums_ref[0, B_VALUE : B_VALUE + 1] = jnp.sum(dv_ref[...].astype(f32), axis=0, keepdims=True)
-        for m, grad in enumerate((dq_ref, dk_ref, dv_ref)):
-            put_shares(cube, tn(x_ref[...], grad[...]), shares, m)
-
-    @pl.when(step == GROUPS)
-    def _():
-        for copy in copies:
-            copy.wait()
-        for m in range(GROUPS):
-            put_shares(cube, tn(c_ref[...], da_ref[:, m * WIDE : (m + 1) * WIDE]), shares, m)
+    @pl.when(step == 0)
+    def _():
+        table_ref[...] = before_ref[...]
+
+    pl.loop(0, q_ref.shape[0] // LEN, unroll=BACK_UNROLL)(sentence)
+    cols = pl.ds(pl.multiple_of(step * WIDE, WIDE), WIDE)
+    table_ref[B_QUERY : B_QUERY + 1, cols] = jnp.sum(dq_ref[...].astype(f32), axis=0, keepdims=True)
+    table_ref[B_VALUE : B_VALUE + 1, cols] = jnp.sum(dv_ref[...].astype(f32), axis=0, keepdims=True)
+    for m, (rows, grad) in enumerate(((x_ref, dq_ref), (x_ref, dk_ref), (x_ref, dv_ref), (c_ref, da_ref))):
+        full = tn(rows[...], grad[...])
+        if cube:
+            full = full.reshape(4, 2, 2, 2, 24, WIDE)
+
+            def put(ref, p, q, value, m=m):
+                ref[:, p, q, 24 * m : 24 * (m + 1)] = value.astype(ref.dtype)
+
+            write_shares(lambda y, x, c: full[:, y, x, c], *shares, put)
+        else:
+            shares[1][m] = full
+    if cube:
+
+        def put_rows(ref, p, q, value):
+            ref[:, p, q, 96:] = value.astype(ref.dtype)
+
+        @pl.when(step < GROUPS - 1)
+        def _():
+            write_shares(lambda y, x, c: jnp.zeros((4, 8, WIDE), f32), *shares, put_rows)
+
+        @pl.when(step == GROUPS - 1)
+        def _():
+            values = device_rows(table_ref[...]).reshape(4, 2, 2, 2, 8, WIDE)
+            write_shares(lambda y, x, c: values[:, y, x, c], *shares, put_rows)
+    else:
+        shares[0][...] = table_ref[...]
 
 
 BACK_UNROLL = 16
-
-
-def put_shares(cube, full, refs, m):
-    if cube:
-        full = full.reshape(4, 2, 2, 2, 24, WIDE)
-
-        def put(ref, p, q, value):
-            ref[:, p, q, m] = value.astype(ref.dtype)
-
-        write_shares(lambda y, x, c: full[:, y, x, c], *refs, put)
-    else:
-        refs[0][m] = full
 
 
 def heads_back(q, k, v, dc, p, x, sums, c, da, cube):
     t = q.shape[0]
-    col = pl.BlockSpec((t, WIDE), lambda i: (0, jnp.minimum(i, GROUPS - 1)))
+    col = pl.BlockSpec((t, WIDE), lambda i: (0, i))
     if cube:
-        spec = pl.BlockSpec((4, 2, 2, 3, 24, WIDE), lambda i: (0, 0, 0, i, 0, 0))
-        shape = (4, 2, 2, 3 * GROUPS + 3, 24, WIDE)
+        spec = pl.BlockSpec((4, 2, 2, 104, WIDE), lambda i: (0, 0, 0, 0, i))
+        shape = (4, 2, 2, 104, D)
         specs, shapes = [spec] * 2, [S(shape, KEEP), S(shape, low)]
     else:
-        specs, shapes = [pl.BlockSpec((3, D, WIDE), lambda i: (i, 0, 0))], [S((3 * GROUPS + 3, D, WIDE), f32)]
+        specs = [whole((16, D)), pl.BlockSpec((4, D, WIDE), lambda i: (0, 0, i))]
+        shapes = [S((16, D), f32), S((4, D, D), f32)]
     return pl.pallas_call(
         lambda *refs: heads_back_body(cube, *refs),
-        grid=(GROUPS + 1,),
+        grid=(GROUPS,),
         in_specs=[col] * 4
-        + [pl.BlockSpec((1, t, WIDE), lambda i: (jnp.minimum(i, GROUPS - 1), 0, 0)), whole((t, D))]
-        + [pl.BlockSpec((16, WIDE), lambda i: (0, jnp.minimum(i, GROUPS - 1))), ANY, ANY],
-        out_specs=[col] * 3 + [pl.BlockSpec((1, 24, WIDE), lambda i: (jnp.minimum(i, GROUPS - 1), 0, 0))] + specs,
-        out_shape=[S((t, D), low)] * 3 + [S((GROUPS, 24, WIDE), f32)] + shapes,
-        scratch_shapes=[pltpu.VMEM((t, D), low), pltpu.VMEM((t, D), low), pltpu.SemaphoreType.DMA((2,))],
+        + [pl.BlockSpec((1, t, WIDE), lambda i: (i, 0, 0)), whole((t, D)), whole((16, D)), whole((t, D)), col],
+        out_specs=[col] * 3 + specs,
+        out_shape=[S((t, D), low)] * 3 + shapes,
+        scratch_shapes=[pltpu.VMEM((16, D), f32)],
         name="heads_back",
         **params(t * D * 24000, t * D * 20, room=60),
     )(q, k, v, dc, p, x, sums, c, da)
@@ -440,10 +460,13 @@
             cols = pl.ds(side * D, D)
             cls = rows[LEN * (2 * s + side) : LEN * (2 * s + side) + 1]
             cls_ref[at, cols] = cls
-            unit_ref[at, cols] = cls * lax.rsqrt(jnp.sum(cls * cls, axis=-1, keepdims=True) + pool_eps)
 
     @pl.when(step == pl.num_programs(0) - 1)
     def _():
+        for side in range(2):
+            cls = cls_ref[:, side * D : (side + 1) * D]
+            unit = cls * lax.rsqrt(jnp.sum(cls * cls, axis=-1, keepdims=True) + pool_eps)
+            unit_ref[:, side * D : (side + 1) * D] = unit.astype(low)
         onward.wait()
 
 
@@ -457,7 +480,7 @@
         grid=(t // ROWS,),
         in_specs=[row_block(FF), row_block(D), whole(vec.shape)] + [ANY] * len(parts),
         out_specs=[row_block(D), row_block(D), row_block(1), once, once, ANY],
-        out_shape=[S((t, D), low), S((t, D), f32), S((t, 1), f32), S((pairs, 2 * D), f32), S((pairs, 2 * D), f32), S(shape, low)],
+        out_shape=[S((t, D), low), S((t, D), f32), S((t, 1), f32), S((pairs, 2 * D), f32), S((pairs, 2 * D), low), S(shape, low)],
         scratch_shapes=[pltpu.VMEM(shape, low), pltpu.SemaphoreType.DMA((4,)), pltpu.SemaphoreType.DMA],
         name="outer",
         **params(2 * t * D * FF, 10 * t * D + 2 * t * FF + 4 * D * FF, room=60),
@@ -486,8 +509,20 @@
 def outer_back_body(cube, cot_ref, dc_ref, hat2_ref, inv2_ref, a_ref, vec_ref, dres_ref, dbr_ref, sums_ref, *refs):
     j = pl.program_id(0)
 
+    def write(dw):
+        if cube:
+            dw = dw.reshape(2, 2, 2, 96, D)
+
+            def put(ref, p, q, value):
+                ref[0, p, q] = value.astype(ref.dtype)
+
+            write_shares(lambda y, x, c: dw[y, x, c], *refs, put)
+        else:
+            refs[0][...] = dw
+
     @pl.when(j == 0)
     def _():
+        dw = jnp.zeros((BLOCK, D), f32)
         dgain = jnp.zeros((1, D), f32)
         dshift = jnp.zeros((1, D), f32)
         dbias = jnp.zeros((1, D), f32)
@@ -507,21 +542,16 @@
             dbr = dres.astype(low)
             dbr_ref[rows, :] = dbr
             dbias += jnp.sum(dbr.astype(f32), axis=0, keepdims=True)
+            dw += tn(a_ref[rows, :], dbr)
+        write(dw)
         sums_ref[...] = jnp.zeros_like(sums_ref)
         sums_ref[B_OUTER : B_OUTER + 1] = dbias
         sums_ref[G_FFN : G_FFN + 1] = dgain
         sums_ref[S_FFN : S_FFN + 1] = dshift
 
-    dw = tn(a_ref[...], dbr_ref[...])
-    if cube:
-        dw = dw.reshape(2, 2, 2, 96, D)
-
-        def put(ref, p, q, value):
-            ref[0, p, q] = value.astype(ref.dtype)
-
-        write_shares(lambda y, x, c: dw[y, x, c], *refs, put)
-    else:
-        refs[0][...] = dw
+    @pl.when(j > 0)
+    def _():
+        write(tn(a_ref[...], dbr_ref[...]))
 
 
 def outer_back(cot, dc, hat2, inv2, a, vec, cube):
@@ -649,7 +679,6 @@
     return loss[0, 0], dc
 
 
-CUBE = 32
 CORE = [(i, i ^ 1) for i in range(CUBE)]
 FAR_Z = [(i, i ^ 16) for i in range(CUBE)]
 NEAR_Z = [(i, i ^ 8) for i in range(CUBE)]
@@ -666,6 +695,7 @@
         self.near_z, self.far_z = (self.me >> 3) & 1, (self.me >> 4) & 1
         self.first = jnp.where(self.core == 0, x, y)
         self.second = jnp.where(self.core == 0, y, x)
+        self.bits = [b.reshape(1) for b in (self.first, self.second, self.near_z, self.far_z)]
 
 
 def join(own, other, axis, bit):
@@ -708,45 +738,26 @@
         self.left = [(2, place.first), (2, place.second), (1, place.near_z), (0, place.far_z)]
         if early_z:
             self.left = [(1, place.near_z), (1, place.first), (1, place.second), (0, place.far_z)]
-        self.came = self.along = None
+        self.came = None
+
+    def start(self, route):
+        self.came, self.away = send(self.away, route), None
+
+    def settle(self):
+        self.terms.append(self.came.reshape(self.terms[0].shape))
+        axis, bit = self.left.pop(0)
+        self.away = sum(pick(term, axis, 1 - bit).astype(f32) for term in self.terms).astype(low)
+        self.terms = [pick(term, axis, bit) for term in self.terms]
 
     def total(self):
-        self.settle()
-        return sum(term.astype(f32) for term in self.terms)
-
-    def take_along(self, along):
-        self.along = along
-
-    def start(self, route):
-        away = self.away
-        if self.along is not None:
-            away = jnp.concatenate([away.reshape(-1, *self.along.shape[1:]), self.along.astype(low)], axis=0)
-        self.came, self.away = send(away, route), None
-
-    def settle(self):
-        if self.came is not None:
-            came, self.came = self.came, None
-            if self.along is not None:
-                count = self.along.shape[0]
-                self.along = self.along + came[-count:].astype(f32)
-                came = came[:-count]
-            self.terms.append(came.reshape(self.terms[0].shape))
-            if self.left:
-                axis, bit = self.left.pop(0)
-                self.away = sum(pick(term, axis, 1 - bit).astype(f32) for term in self.terms).astype(low)
-                self.terms = [pick(term, axis, bit) for term in self.terms]
-
-
-def windows(sums, *values):
-    for s in sums:
-        s.settle()
-    aways = [s.away for s in sums if s.away is not None]
-    done = together(*values, *aways)
-    values, aways = done[: len(values)], list(done[len(values) :])
-    for s in sums:
-        if s.away is not None:
-            s.away = aways.pop(0)
-    return values
+        return sum(term.astype(f32) for term in (*self.terms, self.came))
+
+
+def arrive(sums, *values):
+    done = together(*values, *[s.came for s in sums])
+    for s, came in zip(sums, done[len(values) :]):
+        s.came = came
+    return done[: len(values)]
 
 
 def spread_rows(rows, at, count):
@@ -770,13 +781,6 @@
     table.append(jnp.where(lane == place.me, copies, 0.0))
     table.append(jnp.zeros((2, D), f32))
     return jnp.concatenate(table, axis=0).astype(low)
-
-
-def own_vectors(total, place):
-    r, fold = D // CUBE, FF // CUBE
-    mine = lax.dynamic_slice(total, (0, place.me * r), (B_INNER, r))
-    inner = lax.dynamic_slice(total, (B_INNER + place.me // (D // fold), (place.me % (D // fold)) * fold), (1, fold))
-    return [mine[i] for i in range(B_INNER)] + [inner[0]]
 
 
 def pack_body(*refs):
@@ -898,51 +902,61 @@
         act, out_far, other = together(act, out_far, other)
         out_parts = (out, out_far, other, send(out_far, CORE))
         block_out, hat2, inv2, cls, unit, outer_mat = outer(act, hat1, vec, out_parts, cube)
-        loss, d_cls = pair_loss(gather_blocks(unit.astype(low), place), vec, cls)
+        loss, d_cls = pair_loss(gather_blocks(unit, place), vec, cls)
         dres, dbr, sums, *shares = outer_back(
             out_cotangent.reshape(count * LEN, D), d_cls, hat2, inv2, act, vec, cube
         )
         o = Reduction(shares, place)
-        (dbr,) = windows([o], dbr)
+        dbr, o.away = together(dbr, o.away)
         o.start(CORE)
         dh, sums, *shares = inner_back(dbr, normed, slope, outer_mat, sums, cube)
         i = Reduction(shares, place, early_z=True)
-        (dh,) = windows([o, i], dh)
+        dh, i.away = arrive([o], dh, i.away)
+        i.start(CORE)
+        o.settle()
         o.start(FIRST)
-        i.start(CORE)
+        dh, dres = together(dh, dres)
         d_resid, d_attn, d_context, sums = open_back(dres, dh, inner_mat, hat1, inv1, output_mat, vec, sums)
-        (d_context,) = windows([o, i], d_context)
+        (d_context,) = arrive([o, i], d_context)
+        o.settle()
         o.start(SECOND)
+        i.settle()
         i.start(NEAR_Z)
-        d_queries, d_keys, d_values, sums, *shares = heads_back(
+        d_queries, d_keys, d_values, *shares = heads_back(
             queries, keys, values, d_context, probs, x, sums, context, d_attn, cube
         )
         a = Reduction(shares, place)
-        d_queries, sums, *came = together(d_queries, sums, a.away, o.came, i.came)
-        a.away, o.came, i.came = came
+        d_queries, a.away = arrive([o, i], d_queries, a.away)
         a.start(CORE)
-        sums = sums + send(sums.astype(low), CORE).astype(f32)
+        o.settle()
+        i.settle()
+        o.away, i.away = arrive([a], o.away, i.away)
         a.settle()
-        a.take_along(sums)
-        windows([o, i, a])
         a.start(FIRST)
         o.start(NEAR_Z)
         i.start(FIRST)
         grad_rows = token_grad(d_resid, d_queries, d_keys, d_values, full)
-        (grad_rows,) = windows([o, i, a], grad_rows)
+        (grad_rows,) = arrive([o, i, a], grad_rows)
+        a.settle()
         a.start(SECOND)
+        o.settle()
+        o.start(FAR_Z)
+        i.settle()
         i.start(SECOND)
-        o.start(FAR_Z)
-        windows([i, a])
+        arrive([i, a])
+        a.settle()
         a.start(NEAR_Z)
+        i.settle()
         i.start(FAR_Z)
-        windows([a])
+        grad_w_outer = o.total()
+        (grad_w_outer,) = arrive([a], grad_w_outer)
+        a.settle()
         a.start(FAR_Z)
-        grad_w_outer, grad_w_inner, g_a = o.total(), i.total(), a.total()
-        g_mats = [jnp.concatenate([g_a[n], g_a[3 + n], g_a[6 + n]], axis=1) for n in range(3)]
-        g_mats.append(jnp.concatenate([g_a[9], g_a[10], g_a[11]], axis=1))
-        sums = jnp.concatenate([a.along[g] for g in range(GROUPS)], axis=1)
-        grads = own_vectors(sums, place)
+        grad_w_inner = i.total()
+        g_attn = a.total()
+        g_mats = [g_attn[24 * n : 24 * (n + 1)] for n in range(4)]
+        small, inner_part = g_attn[96:, D - WIDE :], g_attn[96, D - WIDE // 2 :]
+        grads = [small[n, : D // CUBE] for n in range(B_INNER)] + [inner_part[: FF // CUBE]]
     else:
         rows = [every(v).reshape(-1, D) for v in vectors]
         vec = jnp.concatenate(rows + [jnp.zeros((4, D), low)], axis=0)
@@ -952,21 +966,18 @@
         hat1, inv1, normed, output_mat = close(x, context, vec, (every(w_output),), cube)
         act, slope, inner_mat = inner(normed, vec, (every(w_inner),), cube)
         block_out, hat2, inv2, cls, unit, outer_mat = outer(act, hat1, vec, (every(w_outer),), cube)
-        loss, d_cls = plain_loss(every(unit.astype(low)), every(partners), cls)
+        loss, d_cls = plain_loss(every(unit), every(partners), cls)
         dres, dbr, sums, d_outer = outer_back(
             out_cotangent.reshape(count * LEN, D), d_cls, hat2, inv2, act, vec, cube
         )
         dh, sums, d_inner = inner_back(dbr, normed, slope, outer_mat, sums, cube)
         d_resid, d_attn, d_context, sums = open_back(dres, dh, inner_mat, hat1, inv1, output_mat, vec, sums)
-        d_queries, d_keys, d_values, sums, d_a = heads_back(
+        d_queries, d_keys, d_values, sums, d_mats = heads_back(
             queries, keys, values, d_context, probs, x, sums, context, d_attn, cube
         )
-        sums = jnp.concatenate([sums[g] for g in range(GROUPS)], axis=1)
         grad_rows = token_grad(d_resid, d_queries, d_keys, d_values, full)
         grad_w_outer, grad_w_inner = scatter(d_outer), scatter(d_inner)
-        d_mats = [jnp.concatenate([d_a[n], d_a[3 + n], d_a[6 + n]], axis=1) for n in range(3)]
-        d_mats.append(jnp.concatenate([d_a[9], d_a[10], d_a[11]], axis=1))
-        g_mats = [scatter(d) for d in d_mats]
+        g_mats = [scatter(d_mats[n]) for n in range(4)]
         grads = [scatter(sums[n]) for n in range(B_INNER)] + [scatter(sums[B_INNER:CODES].reshape(-1))]
     (
         grad_b_query,

time: 324 us -> 321 us (level)
  waiting for transfers between devices: 79 us -> 85.8 us
  other arithmetic: 40.7 us -> 34 us
    ppermute x50 -> x49, waiting for transfers between devices: 79 us -> 85.8 us  [send(): return lax.ppermute(field, AXIS, route)]
    concatenate x9 -> x0, other arithmetic: 3.85 us -> none  [the longest x3 1.91 us: local(): jnp.concatenate([g_a[n], g_a[3 + n], g_a[6 + n]], axis=1)]
    convert_element_type x6 -> x0, other arithmetic: 3.38 us -> none  [the longest x4 1.59 us: start(): self.along.astype(low)]
    ppermute x50 -> x49, starting transfers between devices: 46.2 us -> 44.8 us  [send(): return lax.ppermute(field, AXIS, route)]
  transfers between devices with their start and end apart: 50 -> 49, of which waited for: 26 -> 26; matrix products, arithmetic and copies ran while one was open for 9% -> 8% of each run, Pallas kernels for 36% -> 37%
where the time goes in v4:
time: 321 us; the launch traced here: 320 us
  Pallas kernels  147 us (46%)
  waiting for transfers between devices  85.8 us (27%)
  starting transfers between devices  44.8 us (14%)
  other arithmetic  34 us (11%)
  local copies, waits for them, and re-layouts  6.58 us (2%)
    ppermute x49, waiting for transfers between devices, send(): return lax.ppermute(field, AXIS, route)  85.8 us
    ppermute x49, starting transfers between devices, send(): return lax.ppermute(field, AXIS, route)  44.8 us
    pallas_call x1, Pallas kernels, heads_back(): pl.pallas_call(lambda *refs: heads_back_body(cube, *refs), grid=(GROUPS,)...  29.9 us
    convert_element_type x12, other arithmetic, settle(): sum((pick(term, axis, 1 - bit).astype(f32) for term in self.terms))  22.8 us
    pallas_call x1, Pallas kernels, inner(): pl.pallas_call(lambda *refs: inner_body(cube, *refs), grid=(t // ROWS,),...  22 us
    pallas_call x1, Pallas kernels, inner_back(): pl.pallas_call(lambda *refs: inner_back_body(cube, *refs), grid=(FF // BL...  15.7 us
    pallas_call x1, Pallas kernels, open_back(): pl.pallas_call(open_back_body, grid=(t // (2 * ROWS),), in_specs=[row_blo...  14 us
    pallas_call x1, Pallas kernels, outer_back(): pl.pallas_call(lambda *refs: outer_back_body(cube, *refs), grid=(FF // BL...  13.7 us
  transfers between devices with their start and end apart: 49, of which 26 were waited for; matrix products, arithmetic and copies ran while one was open for 8% of the time, Pallas kernels for 37%

profile of v4, /device:TPU:0, one launch (start us, length us, event | category | flops | bytes accessed | tf_op | source)
XLA Modules:
  0.0 320.1 jit_solution(16441317060205173177)
XLA Ops:
  0.7 1.5 pack.1
  2.2 4.0 %collective-permute-start = (bf16[72,768]{1,0:T(8,128)(2,1)}, bf16[72,768]{1,0:T(8,128)(2,1)S(1)}, u32[]{:S(2)}, u32[]{:S(2)}) collective-permute-start(bf16[72,768]{1,0:T(8,128)(2,1)} %pack.1), channel_id=1, source_target_pairs={{0,16},{1,17},{2,18},{3,19},{4,20},{5,21},{6,22},{7,23},{8,24},{9,... | collective-permute-start | bytes 331784 | tf_op jit(solution)/shard_map/ppermute | solution.py:712
  8.5 4.7 %collective-permute-done.1 = bf16[16,768]{1,0:T(8,128)(2,1)S(1)} collective-permute-done((bf16[16,768]{1,0:T(8,128)(2,1)S(1)}, bf16[16,768]{1,0:T(8,128)(2,1)S(1)}, u32[]{:S(2)}, u32[]{:S(2)}) %collective-permute-start.1) | collective-permute-done | bytes 24608 | tf_op jit(solution)/shard_map/ppermute | solution.py:712
  14.3 1.6 collective-permute-start.3
  15.9 2.2 collective-permute-start.4
  18.3 3.1 collective-permute-done.4
  21.5 3.9 %collective-permute-done.2 = bf16[2,72,768]{2,1,0:T(8,128)(2,1)S(1)} collective-permute-done((bf16[2,72,768]{2,1,0:T(8,128)(2,1)S(1)}, bf16[2,72,768]{2,1,0:T(8,128)(2,1)S(1)}, u32[]{:S(2)}, u32[]{:S(2)}) %collective-permute-start.2) | collective-permute-done | bytes 221216 | tf_op jit(solution)/shard_map/ppermute | solution.py:712
  25.5 1.6 collective-permute-start.6
  29.4 2.7 collective-permute-done.7
  32.1 4.1 %collective-permute-done.8 = bf16[24,3072]{1,0:T(8,128)(2,1)S(1)} collective-permute-done((bf16[24,3072]{1,0:T(8,128)(2,1)S(1)}, bf16[24,3072]{1,0:T(8,128)(2,1)S(1)}, u32[]{:S(2)}, u32[]{:S(2)}) %collective-permute-start.8) | collective-permute-done | bytes 147488 | tf_op jit(solution)/shard_map/ppermute | solution.py:712
  36.5 1.6 collective-permute-start.12
  38.1 1.5 collective-permute-start.11
  40.1 1.8 collective-permute-done.11
  41.9 1.4 collective-permute-done.12
  43.5 1.3 collective-permute-done.13
  44.9 7.7 %collective-permute-done.9.refs_3_ = bf16[4,2,72,768]{3,2,1,0:T(8,128)(2,1)S(1)} collective-permute-done((bf16[4,2,72,768]{3,2,1,0:T(8,128)(2,1)S(1)}, bf16[4,2,72,768]{3,2,1,0:T(8,128)(2,1)S(1)}, u32[]{:S(2)}, u32[]{:S(2)}) %collective-permute-start.9) | collective-permute-done | bytes 884768 | tf_op jit(solution)/shard_map/ppermute | solution.py:712
  53.2 1.9 collective-permute-done.15
  55.8 1.5 collective-permute-start.17
  58.4 9.0 %project.1 = (bf16[1024,768]{1,0:T(8,128)(2,1)}, bf16[1024,768]{1,0:T(8,128)(2,1)}, bf16[1024,768]{1,0:T(8,128)(2,1)}, bf16[3,4,2,2,2,24,768]{6,5,4,3,2,1,0:T(8,128)(2,1)}) custom-call(bf16[1024,768]{1,0:T(8,128)(2,1)} %bitcast.220, bf16[16,768]{1,0:T(8,128)(2,1)} %add.653.refs_1_.refs_2_.codes_ref.refs_5_.vec_ref, bf16[4,2,72,768]{3,2,1,0:T(8,128)(2,1)} %copy-done.8, ...), custom_call_target="tpu_custom_call" | custom-call | flops 3623878656 | bytes 13369344 | tf_op jit(solution)/shard_map/project/pallas_call | solution.py:128
  69.6 2.0 collective-permute-start.20
  71.9 10.7 %attend.1 = (f32[3,1024,256]{2,1,0:T(8,128)}, bf16[1024,768]{1,0:T(8,128)(2,1)}) custom-call(s32[16]{0:T(128)} %refs_0_.3, bf16[1024,768]{1,0:T(8,128)(2,1)} %get-tuple-element.152.refs_1_.refs_0_, bf16[1024,768]{1,0:T(8,128)(2,1)} %get-tuple-element.153.refs_2_.refs_1_, bf16[1024,768]{1,0:T(8,128)(2,1)} %get-tuple-element.154.refs_3_.refs_2_), custom_call_target="tpu_custom_call" | custom-call | flops 6039797760 | bytes 15728640 | tf_op jit(solution)/shard_map/attend/pallas_call | solution.py:225
  82.8 2.1 collective-permute-done.19.refs_3_
  85.4 1.5 collective-permute-start.25
  86.8 6.6 %close.1 = (f32[1024,768]{1,0:T(8,128)}, f32[1024,1]{1,0:T(8,128)}, bf16[1024,768]{1,0:T(8,128)(2,1)}, bf16[4,2,2,2,24,768]{5,4,3,2,1,0:T(8,128)(2,1)}) custom-call(bf16[1024,768]{1,0:T(8,128)(2,1)} %bitcast.221, bf16[1024,768]{1,0:T(8,128)(2,1)} %get-tuple-element.159.refs_1_.refs_7_, bf16[16,768]{1,0:T(8,128)(2,1)} %add.653.refs_1_.refs_2_.codes_ref.refs_5_.vec_ref, ...), custom_call_target="tpu_custom_call" | custom-call | flops 1207959552 | bytes 10223616 | tf_op jit(solution)/shard_map/close/pallas_call | solution.py:263
  93.5 1.8 collective-permute-done.25
  96.6 22.0 %inner.1 = (bf16[1024,3072]{1,0:T(8,128)(2,1)}, bf16[1024,3072]{1,0:T(8,128)(2,1)}, bf16[4,2,2,2,24,3072]{5,4,3,2,1,0:T(8,128)(2,1)}) custom-call(bf16[1024,768]{1,0:T(8,128)(2,1)} %get-tuple-element.168.refs_0_.refs_1_, bf16[16,768]{1,0:T(8,128)(2,1)} %add.653.refs_1_.refs_2_.codes_ref.refs_5_.vec_ref, bf16[4,2,24,3072]{3,2,1,0:T(8,128)(2,1)} %copy-done.5, ...), custom_call_target="tpu_custom_call" | custom-call | flops 14495514624 | bytes 23592960 | tf_op jit(solution)/shard_map/inner/pallas_call | solution.py:430
  119.2 2.5 collective-permute-done.28.refs_6_
  122.8 12.5 %outer.1 = (bf16[1024,768]{1,0:T(8,128)(2,1)}, f32[1024,768]{1,0:T(8,128)}, f32[1024,1]{1,0:T(8,128)}, f32[8,1536]{1,0:T(8,128)}, bf16[8,1536]{1,0:T(8,128)(2,1)}, /*index=5*/bf16[4,2,2,2,96,768]{5,4,3,2,1,0:T(8,128)(2,1)}) custom-call(bf16[1024,3072]{1,0:T(8,128)(2,1)} %get-tuple-element.175.refs_0_.refs_4_, ...), custom_call_target="tpu_custom_call" | custom-call | flops 4831838208 | bytes 23592960 | tf_op jit(solution)/shard_map/outer/pallas_call | solution.py:478
  135.2 2.1 collective-permute-start.29
  137.3 2.9 collective-permute-done.29
  141.1 2.0 collective-permute-start.30
  143.1 2.1 collective-permute-done.30
  145.3 1.7 collective-permute-start.31
  146.9 3.1 collective-permute-done.31
  151.1 4.8 %collective-permute-done.32 = bf16[2,2,2,8,1536]{4,3,2,1,0:T(8,128)(2,1)S(1)} collective-permute-done((bf16[2,2,2,8,1536]{4,3,2,1,0:T(8,128)(2,1)S(1)}, bf16[2,2,2,8,1536]{4,3,2,1,0:T(8,128)(2,1)S(1)}, u32[]{:S(2)}, u32[]{:S(2)}) %collective-permute-start.32) | collective-permute-done | bytes 196640 | tf_op jit(solution)/shard_map/ppermute | solution.py:712
  156.0 1.7 collective-permute-done.33
  158.9 2.9 pair_loss.1
  161.7 13.7 %outer_back.1 = (f32[1024,768]{1,0:T(8,128)}, bf16[1024,768]{1,0:T(8,128)(2,1)}, f32[16,768]{1,0:T(8,128)}, bf16[4,2,2,96,768]{4,3,2,1,0:T(8,128)(2,1)}, bf16[4,2,2,96,768]{4,3,2,1,0:T(8,128)(2,1)}) custom-call(bf16[1024,768]{1,0:T(8,128)(2,1)} %bitcast.219, f32[8,1536]{1,0:T(8,128)} %get-tuple-element.183.refs_1_, f32[1024,768]{1,0:T(8,128)} %get-tuple-element.184.refs_2_, ...), custom_call_target="tpu_custom_call" | custom-call | flops 9663676416 | bytes 36175872 | tf_op jit(solution)/shard_map/outer_back/pallas_call | solution.py:564
  175.5 15.7 %inner_back.1 = (bf16[1024,3072]{1,0:T(8,128)(2,1)}, f32[16,768]{1,0:T(8,128)}, bf16[4,2,2,24,3072]{4,3,2,1,0:T(8,128)(2,1)}, bf16[4,2,2,24,3072]{4,3,2,1,0:T(8,128)(2,1)}) custom-call(bf16[1024,768]{1,0:T(8,128)(2,1)} %get-tuple-element.188.refs_0_, bf16[1024,768]{1,0:T(8,128)(2,1)} %get-tuple-element.168.refs_0_.refs_1_, ...), custom_call_target="tpu_custom_call" | custom-call | flops 9663676416 | bytes 34603008 | tf_op jit(solution)/shard_map/inner_back/pallas_call | solution.py:604
  191.7 2.6 fusion.2
  194.2 2.1 collective-permute-start.35
  196.4 14.0 %open_back.1 = (f32[1024,768]{1,0:T(8,128)}, bf16[1024,768]{1,0:T(8,128)(2,1)}, bf16[1024,768]{1,0:T(8,128)(2,1)}, f32[16,768]{1,0:T(8,128)}) custom-call(f32[1024,768]{1,0:T(8,128)} %get-tuple-element.197.dres_ref, bf16[1024,3072]{1,0:T(8,128)(2,1)} %get-tuple-element.198.dh_ref, bf16[768,3072]{1,0:T(8,128)(2,1)} %bitcast.223, ...), custom_call_target="tpu_custom_call" | custom-call | flops 6039797760 | bytes 21626880 | tf_op jit(solution)/shard_map/open_back/pallas_call | solution.py:296
  210.8 2.7 fusion.5
  214.4 1.6 fusion.3
  216.0 2.1 collective-permute-start.38
  218.1 29.9 %heads_back.1 = (bf16[1024,768]{1,0:T(8,128)(2,1)}, bf16[1024,768]{1,0:T(8,128)(2,1)}, bf16[1024,768]{1,0:T(8,128)(2,1)}, bf16[4,2,2,104,768]{4,3,2,1,0:T(8,128)(2,1)}, bf16[4,2,2,104,768]{4,3,2,1,0:T(8,128)(2,1)}) custom-call(bf16[1024,768]{1,0:T(8,128)(2,1)} %get-tuple-element.152.refs_1_.refs_0_, bf16[1024,768]{1,0:T(8,128)(2,1)} %get-tuple-element.153.refs_2_.refs_1_, ...), custom_call_target="tpu_custom_call" | custom-call | flops 18874368000 | bytes 15728640 | tf_op jit(solution)/shard_map/heads_back/pallas_call | solution.py:386
  248.9 1.5 fusion.10
  250.4 2.5 fusion.4
  253.3 2.7 fusion
  256.5 1.5 collective-permute-start.41
  258.1 8.9 %token_grad.1 = f32[1024,768]{1,0:T(8,128)} custom-call(f32[1024,768]{1,0:T(8,128)} %get-tuple-element.203.dr_ref, bf16[1024,768]{1,0:T(8,128)(2,1)} %get-tuple-element.217.dq_ref, bf16[1024,768]{1,0:T(8,128)(2,1)} %get-tuple-element.218.dk_ref, bf16[1024,768]{1,0:T(8,128)(2,1)} %get-tuple-element.219.dv_ref, bf16[3,768,768]{2,1,0:T(8,128)(2,1)} %bitcast.183, ...), custom_call_target="tpu_custom_call" | custom-call | flops 3623878656 | bytes 14548992 | tf_op jit(solution)/shard_map/token_grad/pallas_call | solution.py:627
  266.9 12.8 %collective-permute-done.41 = bf16[2,2,24,3072]{3,2,1,0:T(8,128)(2,1)S(1)} collective-permute-done((bf16[2,2,24,3072]{3,2,1,0:T(8,128)(2,1)}, bf16[2,2,24,3072]{3,2,1,0:T(8,128)(2,1)S(1)}, u32[]{:S(2)}, u32[]{:S(2)}) %collective-permute-start.41) | collective-permute-done | bytes 589856 | tf_op jit(solution)/shard_map/ppermute | solution.py:712
  280.6 2.4 fusion.1
  284.1 2.1 fusion.9
  287.1 1.3 slice.56
  288.3 1.2 fusion.15
  290.3 6.5 %collective-permute-done.43 = bf16[2,24,3072]{2,1,0:T(8,128)(2,1)} collective-permute-done((bf16[2,24,3072]{2,1,0:T(8,128)(2,1)}, bf16[2,24,3072]{2,1,0:T(8,128)(2,1)}, u32[]{:S(2)}, u32[]{:S(2)}) %collective-permute-start.43) | collective-permute-done | bytes 294944 | tf_op jit(solution)/shard_map/ppermute | solution.py:712
  296.8 1.2 fusion.8
  298.2 1.2 fusion.13
  299.4 1.6 collective-permute-start.48
  301.0 2.0 fusion.16
  303.0 6.2 %collective-permute-done.46 = bf16[2,104,768]{2,1,0:T(8,128)(2,1)S(1)} collective-permute-done((bf16[2,104,768]{2,1,0:T(8,128)(2,1)S(1)}, bf16[2,104,768]{2,1,0:T(8,128)(2,1)S(1)}, u32[]{:S(2)}, u32[]{:S(2)}) %collective-permute-start.46) | collective-permute-done | bytes 319520 | tf_op jit(solution)/shard_map/ppermute | solution.py:712
  310.4 2.0 fusion.14
  312.4 4.8 %collective-permute-done.47 = bf16[104,768]{1,0:T(8,128)(2,1)S(1)} collective-permute-done((bf16[104,768]{1,0:T(8,128)(2,1)S(1)}, bf16[104,768]{1,0:T(8,128)(2,1)S(1)}, u32[]{:S(2)}, u32[]{:S(2)}) %collective-permute-start.47) | collective-permute-done | bytes 159776 | tf_op jit(solution)/shard_map/ppermute | solution.py:712
  (159 shorter events, 30.0 us)
Async XLA Ops:
  0.7 6.5 %copy-start = (bf16[96]{0:T(256)(128)(2,1)S(1)}, bf16[96]{0:T(256)(128)(2,1)}, u32[]{:S(2)}) copy-start(bf16[96]{0:T(256)(128)(2,1)} %param.33) | copy-start | bytes 580
  0.7 20.7 %copy-start.15 = (bf16[24,768]{1,0:T(8,128)(2,1)S(1)}, bf16[24,768]{1,0:T(8,128)(2,1)}, u32[]{:S(2)}) copy-start(bf16[24,768]{1,0:T(8,128)(2,1)} %param.26) | copy-start | bytes 110596
  0.7 27.8 %copy-start.13 = (bf16[24,3072]{1,0:T(8,128)(2,1)S(1)}, bf16[24,3072]{1,0:T(8,128)(2,1)}, u32[]{:S(2)}) copy-start(bf16[24,3072]{1,0:T(8,128)(2,1)} %param.32) | copy-start | bytes 442372
  2.2 11.1 %collective-permute-start = (bf16[72,768]{1,0:T(8,128)(2,1)}, bf16[72,768]{1,0:T(8,128)(2,1)S(1)}, u32[]{:S(2)}, u32[]{:S(2)}) collective-permute-start(bf16[72,768]{1,0:T(8,128)(2,1)} %pack.1), channel_id=1, source_target_pairs={{0,16},{1,17},{2,18},{3,19},{4,20},{5,21},{6,22},{7,23},{8,24},{9,... | collective-permute-start | bytes 331784 | tf_op jit(solution)/shard_map/ppermute | solution.py:712
  8.5 4.7 %collective-permute-start.1 = (bf16[16,768]{1,0:T(8,128)(2,1)S(1)}, bf16[16,768]{1,0:T(8,128)(2,1)S(1)}, u32[]{:S(2)}, u32[]{:S(2)}) collective-permute-start(bf16[16,768]{1,0:T(8,128)(2,1)S(1)} %maximum_maximum_fusion), channel_id=1, source_target_pairs={{0,16},{1,17},{2,18},{3,19},{4,20},{5,21},{6,22},{7,23},{8,24},{9,... | collective-permute-start | bytes 73736 | tf_op jit(solution)/shard_map/ppermute | solution.py:712
  14.3 4.0 %collective-permute-start.3 = (bf16[16,768]{1,0:T(8,128)(2,1)S(1)}, bf16[16,768]{1,0:T(8,128)(2,1)S(1)}, u32[]{:S(2)}, u32[]{:S(2)}) collective-permute-start(bf16[16,768]{1,0:T(8,128)(2,1)S(1)} %fusion.62), channel_id=1, source_target_pairs={{0,8},{1,9},{2,10},{3,11},{4,12},{5,13},{6,14},{7,15},{8,0},{9,1},... | collective-permute-start | bytes 73736 | tf_op jit(solution)/shard_map/ppermute | solution.py:712
  15.9 5.5 %collective-permute-start.4 = (bf16[24,768]{1,0:T(8,128)(2,1)}, bf16[24,768]{1,0:T(8,128)(2,1)S(1)}, u32[]{:S(2)}, u32[]{:S(2)}) collective-permute-start(bf16[24,768]{1,0:T(8,128)(2,1)} %param.26), channel_id=1, source_target_pairs={{0,16},{1,17},{2,18},{3,19},{4,20},{5,21},{6,22},{7,23},{8,24},{9,... | collective-permute-start | bytes 110600 | tf_op jit(solution)/shard_map/ppermute | solution.py:712
  18.2 7.2 %collective-permute-start.2 = (bf16[2,72,768]{2,1,0:T(8,128)(2,1)S(1)}, bf16[2,72,768]{2,1,0:T(8,128)(2,1)S(1)}, u32[]{:S(2)}, u32[]{:S(2)}) collective-permute-start(bf16[2,72,768]{2,1,0:T(8,128)(2,1)S(1)} %broadcast_select_fusion.10), channel_id=1, source_target_pairs={{0,8},{1,9},{2,10},{3,11},{4,12},{5,13},{6,14},{7,15},{8,0},{9,1},... | collective-permute-start | bytes 663560 | tf_op jit(solution)/shard_map/ppermute | solution.py:712
  25.5 3.9 %collective-permute-start.6 = (bf16[16,768]{1,0:T(8,128)(2,1)S(1)}, bf16[16,768]{1,0:T(8,128)(2,1)S(1)}, u32[]{:S(2)}, u32[]{:S(2)}) collective-permute-start(bf16[16,768]{1,0:T(8,128)(2,1)S(1)} %add.650), channel_id=1, source_target_pairs={{0,2},{1,5},{2,0},{3,7},{4,6},{5,1},{6,4},{7,3},{8,10},{9,13},{10,... | collective-permute-start | bytes 73736 | tf_op jit(solution)/shard_map/ppermute | solution.py:712
  27.0 5.0 %collective-permute-start.7 = (bf16[2,24,768]{2,1,0:T(8,128)(2,1)S(1)}, bf16[2,24,768]{2,1,0:T(8,128)(2,1)S(1)}, u32[]{:S(2)}, u32[]{:S(2)}) collective-permute-start(bf16[2,24,768]{2,1,0:T(8,128)(2,1)S(1)} %broadcast_select_fusion.14), channel_id=1, source_target_pairs={{0,8},{1,9},{2,10},{3,11},{4,12},{5,13},{6,14},{7,15},{8,0},{9,1},... | collective-permute-start | bytes 221192 | tf_op jit(solution)/shard_map/ppermute | solution.py:712
  27.9 8.5 %collective-permute-start.5 = (bf16[2,2,72,768]{3,2,1,0:T(8,128)(2,1)S(1)}, bf16[2,2,72,768]{3,2,1,0:T(8,128)(2,1)S(1)}, u32[]{:S(2)}, u32[]{:S(2)}) collective-permute-start(bf16[2,2,72,768]{3,2,1,0:T(8,128)(2,1)S(1)} %broadcast_select_fusion.5), channel_id=1, source_target_pairs={{0,2},{1,5},{2,0},{3,7},{4,6},{5,1},{6,4},{7,3},{8,10},{9,13},{10,... | collective-permute-start | bytes 1327112 | tf_op jit(solution)/shard_map/ppermute | solution.py:712
  28.4 7.8 %collective-permute-start.8 = (bf16[24,3072]{1,0:T(8,128)(2,1)S(1)}, bf16[24,3072]{1,0:T(8,128)(2,1)S(1)}, u32[]{:S(2)}, u32[]{:S(2)}) collective-permute-start(bf16[24,3072]{1,0:T(8,128)(2,1)S(1)} %copy-done.13), channel_id=1, source_target_pairs={{0,16},{1,17},{2,18},{3,19},{4,20},{5,21},{6,22},{7,23},{8,24},{9,... | collective-permute-start | bytes 442376 | tf_op jit(solution)/shard_map/ppermute | solution.py:712
  36.4 21.5 %copy-start.14 = (bf16[96,768]{1,0:T(8,128)(2,1)S(1)}, bf16[96,768]{1,0:T(8,128)(2,1)}, u32[]{:S(2)}) copy-start(bf16[96,768]{1,0:T(8,128)(2,1)} %param.34) | copy-start | bytes 442372
  36.5 21.9 %copy-start.8 = (bf16[4,2,72,768]{3,2,1,0:T(8,128)(2,1)}, bf16[4,2,72,768]{3,2,1,0:T(8,128)(2,1)S(1)}, u32[]{:S(2)}) copy-start(bf16[4,2,72,768]{3,2,1,0:T(8,128)(2,1)S(1)} %broadcast_select_fusion.2.refs_2_) | copy-start | bytes 2654212
  36.5 6.8 %collective-permute-start.12 = (bf16[2,2,24,768]{3,2,1,0:T(8,128)(2,1)S(1)}, bf16[2,2,24,768]{3,2,1,0:T(8,128)(2,1)S(1)}, u32[]{:S(2)}, u32[]{:S(2)}) collective-permute-start(bf16[2,2,24,768]{3,2,1,0:T(8,128)(2,1)S(1)} %broadcast_select_fusion.12), channel_id=1, source_target_pairs={{0,2},{1,5},{2,0},{3,7},{4,6},{5,1},{6,4},{7,3},{8,10},{9,13},{10,... | collective-permute-start | bytes 442376 | tf_op jit(solution)/shard_map/ppermute | solution.py:712
  38.1 6.7 %collective-permute-start.13 = (bf16[2,24,3072]{2,1,0:T(8,128)(2,1)S(1)}, bf16[2,24,3072]{2,1,0:T(8,128)(2,1)S(1)}, u32[]{:S(2)}, u32[]{:S(2)}) collective-permute-start(bf16[2,24,3072]{2,1,0:T(8,128)(2,1)S(1)} %broadcast_select_fusion.9), channel_id=1, source_target_pairs={{0,8},{1,9},{2,10},{3,11},{4,12},{5,13},{6,14},{7,15},{8,0},{9,1},... | collective-permute-start | bytes 884744 | tf_op jit(solution)/shard_map/ppermute | solution.py:712
  38.1 3.8 %collective-permute-start.11 = (bf16[16,768]{1,0:T(8,128)(2,1)S(1)}, bf16[16,768]{1,0:T(8,128)(2,1)S(1)}, u32[]{:S(2)}, u32[]{:S(2)}) collective-permute-start(bf16[16,768]{1,0:T(8,128)(2,1)S(1)} %add.651), channel_id=1, source_target_pairs={{0,4},{1,3},{2,6},{3,1},{4,0},{5,7},{6,2},{7,5},{8,12},{9,11},{10,... | collective-permute-start | bytes 73736 | tf_op jit(solution)/shard_map/ppermute | solution.py:712
  39.6 13.0 %collective-permute-start.9 = (bf16[4,2,72,768]{3,2,1,0:T(8,128)(2,1)S(1)}, bf16[4,2,72,768]{3,2,1,0:T(8,128)(2,1)S(1)}, u32[]{:S(2)}, u32[]{:S(2)}) collective-permute-start(bf16[4,2,72,768]{3,2,1,0:T(8,128)(2,1)S(1)} %broadcast_select_fusion.2.refs_2_), channel_id=1, source_target_pairs={{0,4},{1,3},{2,6},{3,1},{4,0},{5,7},{6,2},{7,5},{8,12},{9,11},{10,... | collective-permute-start | bytes 2654216 | tf_op jit(solution)/shard_map/ppermute | solution.py:712
  40.1 12.5 %collective-permute-start.10 = (bf16[4,2,72,768]{3,2,1,0:T(8,128)(2,1)S(1)}, bf16[4,2,72,768]{3,2,1,0:T(8,128)(2,1)S(1)}, u32[]{:S(2)}, u32[]{:S(2)}) collective-permute-start(bf16[4,2,72,768]{3,2,1,0:T(8,128)(2,1)S(1)} %broadcast_select_fusion.2.refs_2_), channel_id=1, source_target_pairs={{0,1},{1,0},{2,3},{3,2},{4,5},{5,4},{6,7},{7,6},{8,9},{9,8},{10,11... | collective-permute-start | bytes 2654216 | tf_op jit(solution)/shard_map/ppermute | solution.py:712
  43.5 26.2 %copy-start.12 = (bf16[4,2,24,768]{3,2,1,0:T(8,128)(2,1)}, bf16[4,2,24,768]{3,2,1,0:T(8,128)(2,1)S(1)}, u32[]{:S(2)}) copy-start(bf16[4,2,24,768]{3,2,1,0:T(8,128)(2,1)S(1)} %broadcast_select_fusion.8.refs_3_) | copy-start | bytes 884740
  52.7 4.7 %copy-start.18 = (bf16[4,2,72,768]{3,2,1,0:T(8,128)(2,1)}, bf16[4,2,72,768]{3,2,1,0:T(8,128)(2,1)S(1)}, u32[]{:S(2)}) copy-start(bf16[4,2,72,768]{3,2,1,0:T(8,128)(2,1)S(1)} %collective-permute-done.9.refs_3_) | copy-start | bytes 2654212
  52.7 5.2 %copy-start.19 = (bf16[4,2,72,768]{3,2,1,0:T(8,128)(2,1)}, bf16[4,2,72,768]{3,2,1,0:T(8,128)(2,1)S(1)}, u32[]{:S(2)}) copy-start(bf16[4,2,72,768]{3,2,1,0:T(8,128)(2,1)S(1)} %collective-permute-done.10.refs_4_) | copy-start | bytes 2654212
  52.7 3.1 collective-permute-start.14
  52.8 2.4 collective-permute-start.15
  55.8 12.4 %collective-permute-start.17 = (bf16[2,2,24,3072]{3,2,1,0:T(8,128)(2,1)S(1)}, bf16[2,2,24,3072]{3,2,1,0:T(8,128)(2,1)S(1)}, u32[]{:S(2)}, u32[]{:S(2)}) collective-permute-start(bf16[2,2,24,3072]{3,2,1,0:T(8,128)(2,1)S(1)} %broadcast_select_fusion.4), channel_id=1, source_target_pairs={{0,2},{1,5},{2,0},{3,7},{4,6},{5,1},{6,4},{7,3},{8,10},{9,13},{10,... | collective-permute-start | bytes 1769480 | tf_op jit(solution)/shard_map/ppermute | solution.py:712
  57.3 11.1 %collective-permute-start.16 = (bf16[4,2,24,768]{3,2,1,0:T(8,128)(2,1)S(1)}, bf16[4,2,24,768]{3,2,1,0:T(8,128)(2,1)S(1)}, u32[]{:S(2)}, u32[]{:S(2)}) collective-permute-start(bf16[4,2,24,768]{3,2,1,0:T(8,128)(2,1)S(1)} %broadcast_select_fusion.8.refs_3_), channel_id=1, source_target_pairs={{0,4},{1,3},{2,6},{3,1},{4,0},{5,7},{6,2},{7,5},{8,12},{9,11},{10,... | collective-permute-start | bytes 884744 | tf_op jit(solution)/shard_map/ppermute | solution.py:712
  57.8 9.5 %collective-permute-start.18 = (bf16[96,768]{1,0:T(8,128)(2,1)S(1)}, bf16[96,768]{1,0:T(8,128)(2,1)S(1)}, u32[]{:S(2)}, u32[]{:S(2)}) collective-permute-start(bf16[96,768]{1,0:T(8,128)(2,1)S(1)} %copy-done.14), channel_id=1, source_target_pairs={{0,16},{1,17},{2,18},{3,19},{4,20},{5,21},{6,22},{7,23},{8,24},{9,... | collective-permute-start | bytes 442376 | tf_op jit(solution)/shard_map/ppermute | solution.py:712
  68.4 16.4 %copy-start.5 = (bf16[4,2,24,3072]{3,2,1,0:T(8,128)(2,1)}, bf16[4,2,24,3072]{3,2,1,0:T(8,128)(2,1)S(1)}, u32[]{:S(2)}) copy-start(bf16[4,2,24,3072]{3,2,1,0:T(8,128)(2,1)S(1)} %broadcast_select_fusion.1.refs_2_) | copy-start | bytes 3538948
  68.4 14.1 %copy-start.21 = (bf16[4,2,24,768]{3,2,1,0:T(8,128)(2,1)}, bf16[4,2,24,768]{3,2,1,0:T(8,128)(2,1)S(1)}, u32[]{:S(2)}) copy-start(bf16[4,2,24,768]{3,2,1,0:T(8,128)(2,1)S(1)} %collective-permute-done.16.refs_4_) | copy-start | bytes 884740
  68.5 16.4 %collective-permute-start.19 = (bf16[4,2,24,3072]{3,2,1,0:T(8,128)(2,1)S(1)}, bf16[4,2,24,3072]{3,2,1,0:T(8,128)(2,1)}, u32[]{:S(2)}, u32[]{:S(2)}) collective-permute-start(bf16[4,2,24,3072]{3,2,1,0:T(8,128)(2,1)S(1)} %broadcast_select_fusion.1.refs_2_), channel_id=1, source_target_pairs={{0,4},{1,3},{2,6},{3,1},{4,0},{5,7},{6,2},{7,5},{8,12},{9,11},{10,... | collective-permute-start | bytes 3538952 | tf_op jit(solution)/shard_map/ppermute | solution.py:712
  69.6 13.1 %collective-permute-start.21 = (bf16[4,2,24,768]{3,2,1,0:T(8,128)(2,1)S(1)}, bf16[4,2,24,768]{3,2,1,0:T(8,128)(2,1)S(1)}, u32[]{:S(2)}, u32[]{:S(2)}) collective-permute-start(bf16[4,2,24,768]{3,2,1,0:T(8,128)(2,1)S(1)} %broadcast_select_fusion.8.refs_3_), channel_id=1, source_target_pairs={{0,1},{1,0},{2,3},{3,2},{4,5},{5,4},{6,7},{7,6},{8,9},{9,8},{10,11... | collective-permute-start | bytes 884744 | tf_op jit(solution)/shard_map/ppermute | solution.py:712
  69.6 12.9 %collective-permute-start.20 = (bf16[2,96,768]{2,1,0:T(8,128)(2,1)S(1)}, bf16[2,96,768]{2,1,0:T(8,128)(2,1)S(1)}, u32[]{:S(2)}, u32[]{:S(2)}) collective-permute-start(bf16[2,96,768]{2,1,0:T(8,128)(2,1)S(1)} %broadcast_select_fusion.7), channel_id=1, source_target_pairs={{0,8},{1,9},{2,10},{3,11},{4,12},{5,13},{6,14},{7,15},{8,0},{9,1},... | collective-permute-start | bytes 884744 | tf_op jit(solution)/shard_map/ppermute | solution.py:712
  71.7 11.1 %collective-permute-start.22 = (bf16[4,2,24,768]{3,2,1,0:T(8,128)(2,1)S(1)}, bf16[4,2,24,768]{3,2,1,0:T(8,128)(2,1)S(1)}, u32[]{:S(2)}, u32[]{:S(2)}) collective-permute-start(bf16[4,2,24,768]{3,2,1,0:T(8,128)(2,1)S(1)} %collective-permute-done.16.refs_4_), channel_id=1, source_target_pairs={{0,1},{1,0},{2,3},{3,2},{4,5},{5,4},{6,7},{7,6},{8,9},{9,8},{10,11... | collective-permute-start | bytes 884744 | tf_op jit(solution)/shard_map/ppermute | solution.py:712
  84.8 10.6 %collective-permute-start.23 = (bf16[4,2,24,3072]{3,2,1,0:T(8,128)(2,1)S(1)}, bf16[4,2,24,3072]{3,2,1,0:T(8,128)(2,1)}, u32[]{:S(2)}, u32[]{:S(2)}) collective-permute-start(bf16[4,2,24,3072]{3,2,1,0:T(8,128)(2,1)S(1)} %broadcast_select_fusion.1.refs_2_), channel_id=1, source_target_pairs={{0,1},{1,0},{2,3},{3,2},{4,5},{5,4},{6,7},{7,6},{8,9},{9,8},{10,11... | collective-permute-start | bytes 3538952 | tf_op jit(solution)/shard_map/ppermute | solution.py:712
  84.8 10.6 %collective-permute-start.24 = (bf16[4,2,24,3072]{3,2,1,0:T(8,128)(2,1)}, bf16[4,2,24,3072]{3,2,1,0:T(8,128)(2,1)}, u32[]{:S(2)}, u32[]{:S(2)}) collective-permute-start(bf16[4,2,24,3072]{3,2,1,0:T(8,128)(2,1)} %collective-permute-done.19.refs_3_), channel_id=1, source_target_pairs={{0,1},{1,0},{2,3},{3,2},{4,5},{5,4},{6,7},{7,6},{8,9},{9,8},{10,11... | collective-permute-start | bytes 3538952 | tf_op jit(solution)/shard_map/ppermute | solution.py:712
  85.4 9.9 %collective-permute-start.25 = (bf16[2,2,96,768]{3,2,1,0:T(8,128)(2,1)S(1)}, bf16[2,2,96,768]{3,2,1,0:T(8,128)(2,1)S(1)}, u32[]{:S(2)}, u32[]{:S(2)}) collective-permute-start(bf16[2,2,96,768]{3,2,1,0:T(8,128)(2,1)S(1)} %broadcast_select_fusion.3), channel_id=1, source_target_pairs={{0,2},{1,5},{2,0},{3,7},{4,6},{5,1},{6,4},{7,3},{8,10},{9,13},{10,... | collective-permute-start | bytes 1769480 | tf_op jit(solution)/shard_map/ppermute | solution.py:712
  95.4 23.2 %copy-start.6 = (bf16[4,2,96,768]{3,2,1,0:T(8,128)(2,1)}, bf16[4,2,96,768]{3,2,1,0:T(8,128)(2,1)S(1)}, u32[]{:S(2)}) copy-start(bf16[4,2,96,768]{3,2,1,0:T(8,128)(2,1)S(1)} %broadcast_select_fusion.refs_3_) | copy-start | bytes 3538948
  95.4 23.2 %collective-permute-start.26 = (bf16[4,2,96,768]{3,2,1,0:T(8,128)(2,1)S(1)}, bf16[4,2,96,768]{3,2,1,0:T(8,128)(2,1)S(1)}, u32[]{:S(2)}, u32[]{:S(2)}) collective-permute-start(bf16[4,2,96,768]{3,2,1,0:T(8,128)(2,1)S(1)} %broadcast_select_fusion.refs_3_), channel_id=1, source_target_pairs={{0,4},{1,3},{2,6},{3,1},{4,0},{5,7},{6,2},{7,5},{8,12},{9,11},{10,... | collective-permute-start | bytes 3538952 | tf_op jit(solution)/shard_map/ppermute | solution.py:712
  96.6 22.1 %collective-permute-start.27 = (bf16[4,2,96,768]{3,2,1,0:T(8,128)(2,1)S(1)}, bf16[4,2,96,768]{3,2,1,0:T(8,128)(2,1)}, u32[]{:S(2)}, u32[]{:S(2)}) collective-permute-start(bf16[4,2,96,768]{3,2,1,0:T(8,128)(2,1)S(1)} %broadcast_select_fusion.refs_3_), channel_id=1, source_target_pairs={{0,1},{1,0},{2,3},{3,2},{4,5},{5,4},{6,7},{7,6},{8,9},{9,8},{10,11... | collective-permute-start | bytes 3538952 | tf_op jit(solution)/shard_map/ppermute | solution.py:712
  118.7 3.0 collective-permute-start.28
  135.2 5.0 %collective-permute-start.29 = (bf16[8,1536]{1,0:T(8,128)(2,1)}, bf16[8,1536]{1,0:T(8,128)(2,1)S(1)}, u32[]{:S(2)}, u32[]{:S(2)}) collective-permute-start(bf16[8,1536]{1,0:T(8,128)(2,1)} %get-tuple-element.179), channel_id=1, source_target_pairs={{0,16},{1,17},{2,18},{3,19},{4,20},{5,21},{6,22},{7,23},{8,24},{9,... | collective-permute-start | bytes 73736 | tf_op jit(solution)/shard_map/ppermute | solution.py:712
  141.1 4.1 %collective-permute-start.30 = (bf16[2,8,1536]{2,1,0:T(8,128)(2,1)S(1)}, bf16[2,8,1536]{2,1,0:T(8,128)(2,1)S(1)}, u32[]{:S(2)}, u32[]{:S(2)}) collective-permute-start(bf16[2,8,1536]{2,1,0:T(8,128)(2,1)S(1)} %broadcast_select_fusion.15), channel_id=1, source_target_pairs={{0,8},{1,9},{2,10},{3,11},{4,12},{5,13},{6,14},{7,15},{8,0},{9,1},... | collective-permute-start | bytes 147464 | tf_op jit(solution)/shard_map/ppermute | solution.py:712
  145.3 4.7 %collective-permute-start.31 = (bf16[2,2,8,1536]{3,2,1,0:T(8,128)(2,1)S(1)}, bf16[2,2,8,1536]{3,2,1,0:T(8,128)(2,1)S(1)}, u32[]{:S(2)}, u32[]{:S(2)}) collective-permute-start(bf16[2,2,8,1536]{3,2,1,0:T(8,128)(2,1)S(1)} %broadcast_select_fusion.13), channel_id=1, source_target_pairs={{0,2},{1,5},{2,0},{3,7},{4,6},{5,1},{6,4},{7,3},{8,10},{9,13},{10,... | collective-permute-start | bytes 294920 | tf_op jit(solution)/shard_map/ppermute | solution.py:712
  150.1 5.7 %collective-permute-start.32 = (bf16[2,2,2,8,1536]{4,3,2,1,0:T(8,128)(2,1)S(1)}, bf16[2,2,2,8,1536]{4,3,2,1,0:T(8,128)(2,1)S(1)}, u32[]{:S(2)}, u32[]{:S(2)}) collective-permute-start(bf16[2,2,2,8,1536]{4,3,2,1,0:T(8,128)(2,1)S(1)} %broadcast_select_fusion.11), channel_id=1, source_target_pairs={{0,4},{1,3},{2,6},{3,1},{4,0},{5,7},{6,2},{7,5},{8,12},{9,11},{10,... | collective-permute-start | bytes 589832 | tf_op jit(solution)/shard_map/ppermute | solution.py:712
  155.9 1.8 collective-permute-start.33
  175.4 15.8 %collective-permute-start.34 = (bf16[4,2,2,96,768]{4,3,2,1,0:T(8,128)(2,1)}, bf16[4,2,2,96,768]{4,3,2,1,0:T(8,128)(2,1)}, u32[]{:S(2)}, u32[]{:S(2)}) collective-permute-start(bf16[4,2,2,96,768]{4,3,2,1,0:T(8,128)(2,1)} %get-tuple-element.194), channel_id=1, source_target_pairs={{0,1},{1,0},{2,3},{3,2},{4,5},{5,4},{6,7},{7,6},{8,9},{9,8},{10,11... | collective-permute-start | bytes 7077896 | tf_op jit(solution)/shard_map/ppermute | solution.py:712
  175.5 16.2 %copy-start.4 = (bf16[4,2,2,96,768]{4,3,2,1,0:T(8,128)(2,1)S(1)}, bf16[4,2,2,96,768]{4,3,2,1,0:T(8,128)(2,1)}, u32[]{:S(2)}) copy-start(bf16[4,2,2,96,768]{4,3,2,1,0:T(8,128)(2,1)} %get-tuple-element.205) | copy-start | bytes 7077892
  191.2 19.5 %collective-permute-start.36 = (bf16[4,2,2,24,3072]{4,3,2,1,0:T(8,128)(2,1)}, bf16[4,2,2,24,3072]{4,3,2,1,0:T(8,128)(2,1)}, u32[]{:S(2)}, u32[]{:S(2)}) collective-permute-start(bf16[4,2,2,24,3072]{4,3,2,1,0:T(8,128)(2,1)} %get-tuple-element.207), channel_id=1, source_target_pairs={{0,1},{1,0},{2,3},{3,2},{4,5},{5,4},{6,7},{7,6},{8,9},{9,8},{10,11... | collective-permute-start | bytes 7077896 | tf_op jit(solution)/shard_map/ppermute | solution.py:712
  194.2 16.5 %collective-permute-start.35 = (bf16[2,2,2,96,768]{4,3,2,1,0:T(8,128)(2,1)}, bf16[2,2,2,96,768]{4,3,2,1,0:T(8,128)(2,1)S(1)}, u32[]{:S(2)}, u32[]{:S(2)}) collective-permute-start(bf16[2,2,2,96,768]{4,3,2,1,0:T(8,128)(2,1)} %fusion.2), channel_id=1, source_target_pairs={{0,2},{1,5},{2,0},{3,7},{4,6},{5,1},{6,4},{7,3},{8,10},{9,13},{10,... | collective-permute-start | bytes 3538952 | tf_op jit(solution)/shard_map/ppermute | solution.py:712
  210.7 5.2 %copy-start.7 = (bf16[2,2,2,96,768]{4,3,2,1,0:T(8,128)(2,1)}, bf16[2,2,2,96,768]{4,3,2,1,0:T(8,128)(2,1)S(1)}, u32[]{:S(2)}) copy-start(bf16[2,2,2,96,768]{4,3,2,1,0:T(8,128)(2,1)S(1)} %collective-permute-done.35) | copy-start | bytes 3538948
  213.5 34.6 %collective-permute-start.37 = (bf16[2,2,96,768]{3,2,1,0:T(8,128)(2,1)}, bf16[2,2,96,768]{3,2,1,0:T(8,128)(2,1)S(1)}, u32[]{:S(2)}, u32[]{:S(2)}) collective-permute-start(bf16[2,2,96,768]{3,2,1,0:T(8,128)(2,1)} %fusion.5), channel_id=1, source_target_pairs={{0,4},{1,3},{2,6},{3,1},{4,0},{5,7},{6,2},{7,5},{8,12},{9,11},{10,... | collective-permute-start | bytes 1769480 | tf_op jit(solution)/shard_map/ppermute | solution.py:712
  216.0 32.1 %collective-permute-start.38 = (bf16[2,2,2,24,3072]{4,3,2,1,0:T(8,128)(2,1)S(1)}, bf16[2,2,2,24,3072]{4,3,2,1,0:T(8,128)(2,1)}, u32[]{:S(2)}, u32[]{:S(2)}) collective-permute-start(bf16[2,2,2,24,3072]{4,3,2,1,0:T(8,128)(2,1)S(1)} %fusion.3), channel_id=1, source_target_pairs={{0,8},{1,9},{2,10},{3,11},{4,12},{5,13},{6,14},{7,15},{8,0},{9,1},... | collective-permute-start | bytes 3538952 | tf_op jit(solution)/shard_map/ppermute | solution.py:712
  248.1 5.2 %collective-permute-start.39 = (bf16[4,2,2,104,768]{4,3,2,1,0:T(8,128)(2,1)}, bf16[4,2,2,104,768]{4,3,2,1,0:T(8,128)(2,1)}, u32[]{:S(2)}, u32[]{:S(2)}) collective-permute-start(bf16[4,2,2,104,768]{4,3,2,1,0:T(8,128)(2,1)} %get-tuple-element.223), channel_id=1, source_target_pairs={{0,1},{1,0},{2,3},{3,2},{4,5},{5,4},{6,7},{7,6},{8,9},{9,8},{10,11... | collective-permute-start | bytes 7667720 | tf_op jit(solution)/shard_map/ppermute | solution.py:712
  256.0 23.8 %collective-permute-start.42 = (bf16[2,2,2,104,768]{4,3,2,1,0:T(8,128)(2,1)}, bf16[2,2,2,104,768]{4,3,2,1,0:T(8,128)(2,1)}, u32[]{:S(2)}, u32[]{:S(2)}) collective-permute-start(bf16[2,2,2,104,768]{4,3,2,1,0:T(8,128)(2,1)} %fusion), channel_id=1, source_target_pairs={{0,2},{1,5},{2,0},{3,7},{4,6},{5,1},{6,4},{7,3},{8,10},{9,13},{10,... | collective-permute-start | bytes 3833864 | tf_op jit(solution)/shard_map/ppermute | solution.py:712
  256.5 23.3 %collective-permute-start.41 = (bf16[2,2,24,3072]{3,2,1,0:T(8,128)(2,1)}, bf16[2,2,24,3072]{3,2,1,0:T(8,128)(2,1)S(1)}, u32[]{:S(2)}, u32[]{:S(2)}) collective-permute-start(bf16[2,2,24,3072]{3,2,1,0:T(8,128)(2,1)} %fusion.4), channel_id=1, source_target_pairs={{0,2},{1,5},{2,0},{3,7},{4,6},{5,1},{6,4},{7,3},{8,10},{9,13},{10,... | collective-permute-start | bytes 1769480 | tf_op jit(solution)/shard_map/ppermute | solution.py:712
  258.0 8.9 %collective-permute-start.40 = (bf16[2,96,768]{2,1,0:T(8,128)(2,1)S(1)}, bf16[2,96,768]{2,1,0:T(8,128)(2,1)S(1)}, u32[]{:S(2)}, u32[]{:S(2)}) collective-permute-start(bf16[2,96,768]{2,1,0:T(8,128)(2,1)S(1)} %fusion.10), channel_id=1, source_target_pairs={{0,8},{1,9},{2,10},{3,11},{4,12},{5,13},{6,14},{7,15},{8,0},{9,1},... | collective-permute-start | bytes 884744 | tf_op jit(solution)/shard_map/ppermute | solution.py:712
  283.0 13.9 %collective-permute-start.44 = (bf16[2,2,104,768]{3,2,1,0:T(8,128)(2,1)}, bf16[2,2,104,768]{3,2,1,0:T(8,128)(2,1)S(1)}, u32[]{:S(2)}, u32[]{:S(2)}) collective-permute-start(bf16[2,2,104,768]{3,2,1,0:T(8,128)(2,1)} %fusion.1), channel_id=1, source_target_pairs={{0,4},{1,3},{2,6},{3,1},{4,0},{5,7},{6,2},{7,5},{8,12},{9,11},{10,... | collective-permute-start | bytes 1916936 | tf_op jit(solution)/shard_map/ppermute | solution.py:712
  286.2 10.7 %collective-permute-start.43 = (bf16[2,24,3072]{2,1,0:T(8,128)(2,1)}, bf16[2,24,3072]{2,1,0:T(8,128)(2,1)}, u32[]{:S(2)}, u32[]{:S(2)}) collective-permute-start(bf16[2,24,3072]{2,1,0:T(8,128)(2,1)} %fusion.9), channel_id=1, source_target_pairs={{0,4},{1,3},{2,6},{3,1},{4,0},{5,7},{6,2},{7,5},{8,12},{9,11},{10,... | collective-permute-start | bytes 884744 | tf_op jit(solution)/shard_map/ppermute | solution.py:712
  287.1 11.1 %copy-start.11 = (bf16[2,2,24,3072]{3,2,1,0:T(8,128)(2,1)S(1)}, bf16[2,2,24,3072]{3,2,1,0:T(8,128)(2,1)}, u32[]{:S(2)}) copy-start(bf16[2,2,24,3072]{3,2,1,0:T(8,128)(2,1)} %copy-done.10) | copy-start | bytes 1769476
  289.6 11.5 %collective-permute-start.45 = (bf16[96,768]{1,0:T(8,128)(2,1)S(1)}, bf16[96,768]{1,0:T(8,128)(2,1)S(1)}, u32[]{:S(2)}, u32[]{:S(2)}) collective-permute-start(bf16[96,768]{1,0:T(8,128)(2,1)S(1)} %fusion.15), channel_id=1, source_target_pairs={{0,16},{1,17},{2,18},{3,19},{4,20},{5,21},{6,22},{7,23},{8,24},{9,... | collective-permute-start | bytes 442376 | tf_op jit(solution)/shard_map/ppermute | solution.py:712
  298.1 11.1 %collective-permute-start.46 = (bf16[2,104,768]{2,1,0:T(8,128)(2,1)S(1)}, bf16[2,104,768]{2,1,0:T(8,128)(2,1)S(1)}, u32[]{:S(2)}, u32[]{:S(2)}) collective-permute-start(bf16[2,104,768]{2,1,0:T(8,128)(2,1)S(1)} %fusion.8), channel_id=1, source_target_pairs={{0,8},{1,9},{2,10},{3,11},{4,12},{5,13},{6,14},{7,15},{8,0},{9,1},... | collective-permute-start | bytes 958472 | tf_op jit(solution)/shard_map/ppermute | solution.py:712
  299.4 11.0 %collective-permute-start.48 = (bf16[24,3072]{1,0:T(8,128)(2,1)S(1)}, bf16[24,3072]{1,0:T(8,128)(2,1)S(1)}, u32[]{:S(2)}, u32[]{:S(2)}) collective-permute-start(bf16[24,3072]{1,0:T(8,128)(2,1)S(1)} %fusion.13), channel_id=1, source_target_pairs={{0,16},{1,17},{2,18},{3,19},{4,20},{5,21},{6,22},{7,23},{8,24},{9,... | collective-permute-start | bytes 442376 | tf_op jit(solution)/shard_map/ppermute | solution.py:712
  309.2 11.0 %copy-start.1 = (bf16[96]{0:T(256)(128)(2,1)S(1)}, bf16[96]{0:T(256)(128)(2,1)}, u32[]{:S(2)}) copy-start(bf16[96]{0:T(256)(128)(2,1)} %param.33) | copy-start | bytes 580
  310.3 6.9 %collective-permute-start.47 = (bf16[104,768]{1,0:T(8,128)(2,1)S(1)}, bf16[104,768]{1,0:T(8,128)(2,1)S(1)}, u32[]{:S(2)}, u32[]{:S(2)}) collective-permute-start(bf16[104,768]{1,0:T(8,128)(2,1)S(1)} %fusion.11), channel_id=1, source_target_pairs={{0,16},{1,17},{2,18},{3,19},{4,20},{5,21},{6,22},{7,23},{8,24},{9,... | collective-permute-start | bytes 479240 | tf_op jit(solution)/shard_map/ppermute | solution.py:712
  (9 other events, 23.0 us)

commit v5 on v4

--- a/solution.py
+++ b/solution.py
@@ -86,8 +86,9 @@
     return ref
 
 
-def project_body(cube, x_ref, vec_ref, *refs):
-    parts, (q_ref, k_ref, v_ref, full_ref, w_ref, sems, out_sem) = refs[:-7], refs[-7:]
+def project_body(cube, count, biases, x_ref, vec_ref, *refs):
+    outs = len(biases)
+    parts, out_refs, (full_ref, w_ref, sems, out_sem) = refs[: -outs - 4], refs[-outs - 4 : -4], refs[-4:]
     step = pl.program_id(0)
     onward = pltpu.make_async_copy(w_ref, full_ref, out_sem)
 
@@ -98,9 +99,9 @@
             def cut(m):
                 return lambda ref: ref.at[:, :, pl.ds(m * 24, 24), :]
 
-            for m in range(3):
+            for m in range(count):
                 part_copies(parts, w_ref.at[m], sems.at[m], cut(m))
-            for m in range(3):
+            for m in range(count):
                 part_waits(parts, w_ref.at[m], sems.at[m], cut(m))
         else:
             copy = pltpu.make_async_copy(parts[0], w_ref, sems.at[0, 0])
@@ -109,33 +110,32 @@
         onward.start()
 
     x = x_ref[...]
-
-    def mat(m):
-        return w_ref.at[m].reshape(D, D)[...] if cube else w_ref[m]
-
-    q_ref[...] = (nn(x, mat(0)) + vec_ref[B_QUERY : B_QUERY + 1].astype(f32)).astype(low)
-    k_ref[...] = nn(x, mat(1)).astype(low)
-    v_ref[...] = (nn(x, mat(2)) + vec_ref[B_VALUE : B_VALUE + 1].astype(f32)).astype(low)
+    for m, (bias, out) in enumerate(zip(biases, out_refs)):
+        product = nn(x, w_ref.at[m].reshape(D, D)[...] if cube else w_ref[m])
+        if bias is not None:
+            product += vec_ref[bias : bias + 1].astype(f32)
+        out[...] = product.astype(low)
 
     @pl.when(step == pl.num_programs(0) - 1)
     def _():
         onward.wait()
 
 
-def project(x, vec, parts, cube):
+def project(x, vec, parts, count, biases, cube):
     t = x.shape[0]
-    shape = (3, 4, 2, 2, 2, 24, D) if cube else (3, D, D)
-    q, k, v, full = pl.pallas_call(
-        lambda *refs: project_body(cube, *refs),
-        grid=(t // ROWS,),
-        in_specs=[row_block(D), whole(vec.shape)] + [ANY] * len(parts),
-        out_specs=[row_block(D)] * 3 + [ANY],
-        out_shape=[S((t, D), low)] * 3 + [S(shape, low)],
-        scratch_shapes=[pltpu.VMEM(shape, low), pltpu.SemaphoreType.DMA((3, 4)), pltpu.SemaphoreType.DMA],
+    shape = (count, 4, 2, 2, 2, 24, D) if cube else (count, D, D)
+    outs = len(biases)
+    *products, full = pl.pallas_call(
+        lambda *refs: project_body(cube, count, biases, *refs),
+        grid=(t // (2 * ROWS),),
+        in_specs=[row_block(D, 2 * ROWS), whole(vec.shape)] + [ANY] * len(parts),
+        out_specs=[row_block(D, 2 * ROWS)] * outs + [ANY],
+        out_shape=[S((t, D), low)] * outs + [S(shape, low)],
+        scratch_shapes=[pltpu.VMEM(shape, low), pltpu.SemaphoreType.DMA((count, 4)), pltpu.SemaphoreType.DMA],
         name="project",
-        **params(6 * t * D * D, 8 * t * D + 12 * D * D, room=60),
+        **params(2 * outs * t * D * D, 2 * (outs + 1) * t * D + 4 * count * D * D, room=60),
     )(x, vec, *parts)
-    return q, k, v, full.reshape(3, D, D)
+    return *products, full.reshape(count, D, D)
 
 
 def assemble(cube, parts, w_ref, full_ref, sems, out_sem):
@@ -185,11 +185,10 @@
     return (grad - mean - hat * along) * inv
 
 
-def attend_body(start, len_ref, q_ref, k_ref, v_ref, *refs):
-    p_ref, c_ref = refs[-2:]
+def attend_body(len_ref, q_ref, k_ref, v_ref, p_ref, c_ref):
     masks, masks32 = head_masks(low), head_masks(f32)
-    per = ROWS // LEN
-    first = (start + pl.program_id(0)) * per
+    per = q_ref.shape[0] // LEN
+    first = pl.program_id(0) * per
     key_at = lax.broadcasted_iota(jnp.int32, (LEN, WIDE), 0)
 
     def sentence(s):
@@ -208,43 +207,36 @@
     pl.loop(0, per, unroll=UNROLL)(sentence)
 
 
-UNROLL = 4
-
-
-def some_rows(start):
-    return lambda width, rows=ROWS: pl.BlockSpec((rows, width), lambda i, *_: (start + i, 0))
+UNROLL = 8
 
 
 def mat_of(m):
     return pl.BlockSpec((1, D, D), lambda *_: (m, 0, 0), pipeline_mode=pl.Buffered(1))
 
 
-def attend(lengths, q, k, v, start, count, before=()):
+def attend(lengths, q, k, v):
     t = q.shape[0]
-    rows = some_rows(start)
+    rows = row_block(D, 2 * ROWS)
     return pl.pallas_call(
-        lambda *refs: attend_body(start, *refs),
+        attend_body,
         grid_spec=pltpu.PrefetchScalarGridSpec(
             num_scalar_prefetch=1,
-            grid=(count,),
-            in_specs=[rows(D)] * 3 + [ANY] * len(before),
-            out_specs=[pl.BlockSpec((GROUPS, ROWS, WIDE), lambda i, *_: (0, start + i, 0)), rows(D)],
+            grid=(t // (2 * ROWS),),
+            in_specs=[rows] * 3,
+            out_specs=[pl.BlockSpec((GROUPS, 2 * ROWS, WIDE), lambda i, *_: (0, i, 0)), rows],
         ),
         out_shape=[S((GROUPS, t, WIDE), f32), S((t, D), low)],
-        input_output_aliases={4 + i: i for i in range(len(before))},
         name="attend",
-        **params(10 * count * ROWS * D * D, 20 * count * ROWS * D, count * ROWS * D, room=60),
-    )(lengths, q, k, v, *before)
+        **params(10 * t * D * D, 20 * t * D, t * D, room=60),
+    )(lengths, q, k, v)
 
 
 def halves(ref):
     return [slice(i * ROWS, (i + 1) * ROWS) for i in range(ref.shape[0] // ROWS)]
 
 
-def close_body(cube, x_ref, c_ref, vec_ref, *refs):
-    parts, (hat_ref, inv_ref, n_ref, full_ref, w_ref, sems, out_sem) = refs[:-7], refs[-7:]
-    onward = assemble(cube, parts, w_ref, full_ref, sems, out_sem)
-    w = (w_ref.reshape(D, D) if cube else w_ref)[...]
+def close_body(x_ref, c_ref, w_ref, vec_ref, hat_ref, inv_ref, n_ref):
+    w = w_ref[0]
     branches = [nn(c_ref[r, :], w) + vec_ref[B_OUTPUT : B_OUTPUT + 1].astype(f32) for r in halves(x_ref)]
     for r, branch in zip(halves(x_ref), branches):
         hat, inv = layer_norm(x_ref[r, :].astype(f32) + branch)
@@ -252,25 +244,19 @@
         inv_ref[r, :] = inv
         n_ref[r, :] = (hat * vec_ref[G_ATTN : G_ATTN + 1].astype(f32) + vec_ref[S_ATTN : S_ATTN + 1].astype(f32)).astype(low)
 
-    @pl.when(pl.program_id(0) == pl.num_programs(0) - 1)
-    def _():
-        onward.wait()
-
-
-def close(x, c, vec, parts, cube):
+
+def close(x, c, full, vec):
     t = x.shape[0]
-    shape = (4, 2, 2, 2, 24, D) if cube else (D, D)
-    hat, inv, n, full = pl.pallas_call(
-        lambda *refs: close_body(cube, *refs),
+    rows = row_block(D, 2 * ROWS)
+    return pl.pallas_call(
+        close_body,
         grid=(t // (2 * ROWS),),
-        in_specs=[row_block(D, 2 * ROWS), row_block(D, 2 * ROWS), whole(vec.shape)] + [ANY] * len(parts),
-        out_specs=[row_block(D, 2 * ROWS), row_block(1, 2 * ROWS), row_block(D, 2 * ROWS), ANY],
-        out_shape=[S((t, D), f32), S((t, 1), f32), S((t, D), low), S(shape, low)],
-        scratch_shapes=scratch_for(shape),
+        in_specs=[rows, rows, mat_of(1), whole(vec.shape)],
+        out_specs=[rows, row_block(1, 2 * ROWS), rows],
+        out_shape=[S((t, D), f32), S((t, 1), f32), S((t, D), low)],
         name="close",
-        **params(2 * t * D * D, 10 * t * D + 4 * D * D, room=60),
-    )(x, c, vec, *parts)
-    return hat, inv, n, full.reshape(1, D, D)
+        **params(2 * t * D * D, 10 * t * D + 2 * D * D, room=60),
+    )(x, c, full, vec)
 
 
 def open_back_body(dres_ref, dh_ref, wi_ref, hat_ref, inv_ref, wo_ref, vec_ref, before_ref, dr_ref, da_ref, dc_ref, sums_ref):
@@ -296,7 +282,7 @@
     return pl.pallas_call(
         open_back_body,
         grid=(t // (2 * ROWS),),
-        in_specs=[row_block(D, 2 * ROWS), row_block(FF, 2 * ROWS), whole(wi.shape), row_block(D, 2 * ROWS), row_block(1, 2 * ROWS), mat_of(0), whole(vec.shape), whole((16, D))],
+        in_specs=[row_block(D, 2 * ROWS), row_block(FF, 2 * ROWS), whole(wi.shape), row_block(D, 2 * ROWS), row_block(1, 2 * ROWS), mat_of(1), whole(vec.shape), whole((16, D))],
         out_specs=[row_block(D, 2 * ROWS)] * 3 + [whole((16, D))],
         out_shape=[S((t, D), f32), S((t, D), low), S((t, D), low), S((16, D), f32)],
         name="open_back",
@@ -621,23 +607,28 @@
     )
 
 
-def token_grad(dr, dq, dk, dv, full):
+def token_grad(dr, dq, dk, dv, qk, vo):
     t = dr.shape[0]
 
     return pl.pallas_call(
         token_grad_body,
         grid=(t // ROWS,),
-        in_specs=[row_block(D)] * 4 + [mat_of(0), mat_of(1), mat_of(2)],
+        in_specs=[row_block(D)] * 4 + [mat_of(0), mat_of(1), mat_of(0)],
         out_specs=row_block(D),
         out_shape=S((t, D), f32),
         name="token_grad",
         **params(6 * t * D * D, 14 * t * D + 6 * D * D, room=60),
-    )(dr, dq, dk, dv, full, full, full)
-
-
-def loss_body(units_ref, codes_ref, cls_ref, loss_ref, dc_ref, table_ref, ds_ref):
-    sources, targets = units_ref[:, :D], units_ref[:, D:]
-    pairs, own = units_ref.shape[0], cls_ref.shape[0]
+    )(dr, dq, dk, dv, qk, qk, vo)
+
+
+def loss_body(near, far, near_other, far_other, codes_ref, cls_ref, loss_ref, dc_ref, table_ref, ds_ref, units_ref, sems):
+    parts = (near, far, near_other, far_other)
+    part_copies(parts, units_ref, sems, everything)
+    part_waits(parts, units_ref, sems, everything)
+    own = cls_ref.shape[0]
+    pairs = CUBE * own
+    units = units_ref.reshape(pairs, 2 * D)
+    sources, targets = units[:, :D], units[:, D:]
     codes = codes_ref[CODES : CODES + 2, :pairs].astype(f32)
     partner = (codes[0:1] + 64.0 * codes[1:2]).astype(jnp.int32)
     matched = lax.broadcasted_iota(jnp.int32, (pairs, pairs), 0) == partner
@@ -664,18 +655,20 @@
         dc_ref[:, cols] = inv * du - cls * (inv * inv * inv * jnp.sum(du * cls, axis=-1, keepdims=True))
 
 
-def pair_loss(units, vec, cls):
-    pairs, own = units.shape[0], cls.shape[0]
+def pair_loss(parts, vec, cls):
+    own = cls.shape[0]
+    pairs = CUBE * own
     loss, dc = pl.pallas_call(
         loss_body,
-        in_specs=[whole(units.shape), whole(vec.shape), whole(cls.shape)],
+        in_specs=[ANY] * 4 + [whole(vec.shape), whole(cls.shape)],
         out_specs=[whole((8, 128)), whole(cls.shape)],
         out_shape=[S((8, 128), f32), S(cls.shape, f32)],
-        scratch_shapes=[pltpu.VMEM((pairs, D), f32), pltpu.VMEM((pairs, D), f32)],
+        scratch_shapes=[pltpu.VMEM((pairs, D), f32), pltpu.VMEM((pairs, D), f32),
+                        pltpu.VMEM((4, 2, 2, 2, own, 2 * D), low), pltpu.SemaphoreType.DMA((4,))],
         grid=(1,),
         name="pair_loss",
         **params(6 * pairs * pairs * D, 4 * pairs * D, 4 * pairs * pairs, room=60),
-    )(units, vec, cls)
+    )(*parts, vec, cls)
     return loss[0, 0], dc
 
 
@@ -716,15 +709,6 @@
     block = join(block, send(block, FAR_Z), 0, place.far_z)
     block = join(block, send(block, NEAR_Z), 1, place.near_z)
     return join(block, send(block, FIRST), 2, place.first)
-
-
-def gather_blocks(block, place):
-    near = spread(block, place)
-    block = join(near, send(near, SECOND), 3, place.second)
-    other = send(block, CORE)
-    zero = jnp.where(place.core == 0, block, other)
-    one = jnp.where(place.core == 0, other, block)
-    return jnp.stack([jnp.swapaxes(zero, 2, 3), one], axis=4).reshape(-1, block.shape[-1])
 
 
 def together(*values):
@@ -855,46 +839,48 @@
     count = tokens.shape[0]
     x = tokens.reshape(count * LEN, D)
     vectors = (b_query, b_value, b_output, gain_attn, shift_attn, b_outer, gain_ffn, shift_ffn, b_inner)
-    blocks = count * LEN // ROWS
-    lower, higher = blocks // 2, blocks - blocks // 2
     if cube:
         place = Place()
-        qkv = pack(w_query, w_key, w_value)
+        qk = pack(w_query, w_key)
+        vo = pack(w_value, w_output)
         vec = vector_table(vectors, partners, place)
-        qkv = join(qkv, send(qkv, FAR_Z), 0, place.far_z)
+        qk = join(qk, send(qk, FAR_Z), 0, place.far_z)
         vec = vec + send(vec, FAR_Z)
-        qkv, vec, w_output = together(qkv, vec, w_output)
-        qkv = join(qkv, send(qkv, NEAR_Z), 1, place.near_z)
+        qk, vec, vo = together(qk, vec, vo)
+        qk = join(qk, send(qk, NEAR_Z), 1, place.near_z)
         vec = vec + send(vec, NEAR_Z)
-        prj = join(w_output, send(w_output, FAR_Z), 0, place.far_z)
-        qkv, vec, prj, w_inner = together(qkv, vec, prj, w_inner)
-        qkv = join(qkv, send(qkv, FIRST), 2, place.first).reshape(4, 2, 72, D)
+        vo = join(vo, send(vo, FAR_Z), 0, place.far_z)
+        qk, vec, vo, w_inner = together(qk, vec, vo, w_inner)
+        qk = join(qk, send(qk, FIRST), 2, place.first).reshape(4, 2, 48, D)
         vec = vec + send(vec, FIRST)
-        prj = join(prj, send(prj, NEAR_Z), 1, place.near_z)
+        vo = join(vo, send(vo, NEAR_Z), 1, place.near_z)
         inn = join(w_inner, send(w_inner, FAR_Z), 0, place.far_z)
-        qkv, vec, prj, inn = together(qkv, vec, prj, inn)
-        far = send(qkv, SECOND)
-        other = send(qkv, CORE)
+        qk, vec, vo, inn = together(qk, vec, vo, inn)
+        far = send(qk, SECOND)
+        other = send(qk, CORE)
         vec = vec + send(vec, SECOND)
-        prj = join(prj, send(prj, FIRST), 2, place.first).reshape(4, 2, 24, D)
+        vo = join(vo, send(vo, FIRST), 2, place.first).reshape(4, 2, 48, D)
         inn = join(inn, send(inn, NEAR_Z), 1, place.near_z)
-        far, other, vec, prj, inn = together(far, other, vec, prj, inn)
-        qkv_parts = (qkv, far, other, send(far, CORE))
+        far, other, vec, vo, inn = together(far, other, vec, vo, inn)
+        qk_parts = (qk, far, other, send(far, CORE))
         vec = vec + send(vec, CORE)
-        qkv_parts, vec, prj, inn, w_outer = together(qkv_parts, vec, prj, inn, w_outer)
+        qk_parts, vec, vo, inn, w_outer = together(qk_parts, vec, vo, inn, w_outer)
+        vo_far = send(vo, SECOND)
+        other = send(vo, CORE)
         inn = join(inn, send(inn, FIRST), 2, place.first).reshape(4, 2, 24, FF)
-        prj_far = send(prj, SECOND)
         out = join(w_outer, send(w_outer, FAR_Z), 0, place.far_z)
-        queries, keys, values, full = project(x, vec, qkv_parts, cube)
-        queries, prj_far, inn, out = together(queries, prj_far, inn, out)
+        queries, keys, qk = project(x, vec, qk_parts, 2, (B_QUERY, None), cube)
+        queries, vo_far, other, inn, out = together(queries, vo_far, other, inn, out)
+        vo_parts = (vo, vo_far, other, send(vo_far, CORE))
         inn_far = send(inn, SECOND)
+        values, vo = project(x, vec, vo_parts, 2, (B_VALUE,), cube)
+        values, out = together(values, out)
         out = join(out, send(out, NEAR_Z), 1, place.near_z)
-        prj_parts = (prj, prj_far, send(prj, CORE), send(prj_far, CORE))
-        probs, context = attend(lengths, queries, keys, values, 0, blocks)
-        context, inn, inn_far, out, prj_parts = together(context, inn, inn_far, out, prj_parts)
+        probs, context = attend(lengths, queries, keys, values)
+        context, inn, inn_far, out = together(context, inn, inn_far, out)
         inn_parts = (inn, inn_far, send(inn, CORE), send(inn_far, CORE))
         out = join(out, send(out, FIRST), 2, place.first).reshape(4, 2, 96, D)
-        hat1, inv1, normed, output_mat = close(x, context, vec, prj_parts, cube)
+        hat1, inv1, normed = close(x, context, vo, vec)
         normed, inn_parts, out = together(normed, inn_parts, out)
         out_far = send(out, SECOND)
         other = send(out, CORE)
@@ -902,7 +888,9 @@
         act, out_far, other = together(act, out_far, other)
         out_parts = (out, out_far, other, send(out_far, CORE))
         block_out, hat2, inv2, cls, unit, outer_mat = outer(act, hat1, vec, out_parts, cube)
-        loss, d_cls = pair_loss(gather_blocks(unit, place), vec, cls)
+        near = spread(unit, place).reshape(4, 2, *unit.shape)
+        far = send(near, SECOND)
+        loss, d_cls = pair_loss((near, far, send(near, CORE), send(far, CORE)), vec, cls)
         dres, dbr, sums, *shares = outer_back(
             out_cotangent.reshape(count * LEN, D), d_cls, hat2, inv2, act, vec, cube
         )
@@ -916,7 +904,7 @@
         o.settle()
         o.start(FIRST)
         dh, dres = together(dh, dres)
-        d_resid, d_attn, d_context, sums = open_back(dres, dh, inner_mat, hat1, inv1, output_mat, vec, sums)
+        d_resid, d_attn, d_context, sums = open_back(dres, dh, inner_mat, hat1, inv1, vo, vec, sums)
         (d_context,) = arrive([o, i], d_context)
         o.settle()
         o.start(SECOND)
@@ -935,7 +923,7 @@
         a.start(FIRST)
         o.start(NEAR_Z)
         i.start(FIRST)
-        grad_rows = token_grad(d_resid, d_queries, d_keys, d_values, full)
+        grad_rows = token_grad(d_resid, d_queries, d_keys, d_values, qk, vo)
         (grad_rows,) = arrive([o, i, a], grad_rows)
         a.settle()
         a.start(SECOND)
@@ -960,10 +948,11 @@
     else:
         rows = [every(v).reshape(-1, D) for v in vectors]
         vec = jnp.concatenate(rows + [jnp.zeros((4, D), low)], axis=0)
-        qkv_parts = (jnp.stack([every(w) for w in (w_query, w_key, w_value)]),)
-        queries, keys, values, full = project(x, vec, qkv_parts, cube)
-        probs, context = attend(lengths, queries, keys, values, 0, blocks)
-        hat1, inv1, normed, output_mat = close(x, context, vec, (every(w_output),), cube)
+        qk_parts, vo_parts = ((jnp.stack([every(w) for w in ws]),) for ws in ((w_query, w_key), (w_value, w_output)))
+        queries, keys, qk = project(x, vec, qk_parts, 2, (B_QUERY, None), cube)
+        values, vo = project(x, vec, vo_parts, 2, (B_VALUE,), cube)
+        probs, context = attend(lengths, queries, keys, values)
+        hat1, inv1, normed = close(x, context, vo, vec)
         act, slope, inner_mat = inner(normed, vec, (every(w_inner),), cube)
         block_out, hat2, inv2, cls, unit, outer_mat = outer(act, hat1, vec, (every(w_outer),), cube)
         loss, d_cls = plain_loss(every(unit), every(partners), cls)
@@ -971,11 +960,11 @@
             out_cotangent.reshape(count * LEN, D), d_cls, hat2, inv2, act, vec, cube
         )
         dh, sums, d_inner = inner_back(dbr, normed, slope, outer_mat, sums, cube)
-        d_resid, d_attn, d_context, sums = open_back(dres, dh, inner_mat, hat1, inv1, output_mat, vec, sums)
+        d_resid, d_attn, d_context, sums = open_back(dres, dh, inner_mat, hat1, inv1, vo, vec, sums)
         d_queries, d_keys, d_values, sums, d_mats = heads_back(
             queries, keys, values, d_context, probs, x, sums, context, d_attn, cube
         )
-        grad_rows = token_grad(d_resid, d_queries, d_keys, d_values, full)
+        grad_rows = token_grad(d_resid, d_queries, d_keys, d_values, qk, vo)
         grad_w_outer, grad_w_inner = scatter(d_outer), scatter(d_inner)
         g_mats = [scatter(d_mats[n]) for n in range(4)]
         grads = [scatter(sums[n]) for n in range(B_INNER)] + [scatter(sums[B_INNER:CODES].reshape(-1))]

time: 321 us -> 322 us (level)
  waiting for transfers between devices: 85.8 us -> 79.8 us
  Pallas kernels: 147 us -> 151 us
    ppermute x49 -> x50, waiting for transfers between devices: 85.8 us -> 79.8 us  [send(): return lax.ppermute(field, AXIS, route)]
    pallas_call x4 -> x5, Pallas kernels: 29.1 us -> 31 us  [the longest x2 12.3 us: project(): pl.pallas_call(lambda *refs: project_body(cube, count, biases, *refs), gr...]
    ppermute x49 -> x50, starting transfers between devices: 44.8 us -> 44.1 us  [send(): return lax.ppermute(field, AXIS, route)]
  transfers between devices with their start and end apart: 49 -> 50, of which waited for: 26 -> 27; matrix products, arithmetic and copies ran while one was open for 8% -> 8% of each run, Pallas kernels for 37% -> 37%
where the time goes in v5:
time: 322 us; the launch traced here: 318 us
  Pallas kernels  151 us (47%)
  waiting for transfers between devices  79.8 us (25%)
  starting transfers between devices  44.1 us (14%)
  other arithmetic  33.5 us (10%)
  local copies, waits for them, and re-layouts  8.09 us (3%)
    ppermute x50, waiting for transfers between devices, send(): return lax.ppermute(field, AXIS, route)  79.8 us
    ppermute x50, starting transfers between devices, send(): return lax.ppermute(field, AXIS, route)  44.1 us
    pallas_call x1, Pallas kernels, heads_back(): pl.pallas_call(lambda *refs: heads_back_body(cube, *refs), grid=(GROUPS,)...  29.6 us
    convert_element_type x12, other arithmetic, settle(): sum((pick(term, axis, 1 - bit).astype(f32) for term in self.terms))  22.6 us
    pallas_call x1, Pallas kernels, inner(): pl.pallas_call(lambda *refs: inner_body(cube, *refs), grid=(t // ROWS,),...  22 us
    pallas_call x1, Pallas kernels, inner_back(): pl.pallas_call(lambda *refs: inner_back_body(cube, *refs), grid=(FF // BL...  15.8 us
    pallas_call x1, Pallas kernels, open_back(): pl.pallas_call(open_back_body, grid=(t // (2 * ROWS),), in_specs=[row_blo...  14.2 us
    pallas_call x1, Pallas kernels, outer_back(): pl.pallas_call(lambda *refs: outer_back_body(cube, *refs), grid=(FF // BL...  13.5 us
  transfers between devices with their start and end apart: 50, of which 27 were waited for; matrix products, arithmetic and copies ran while one was open for 8% of the time, Pallas kernels for 37%

profile of v5, /device:TPU:0, one launch (start us, length us, event | category | flops | bytes accessed | tf_op | source)
XLA Modules:
  0.0 318.3 jit_solution(15728992256041432622)
XLA Ops:
  0.7 1.5 pack.2
  2.1 4.0 %collective-permute-start = (bf16[48,768]{1,0:T(8,128)(2,1)}, bf16[48,768]{1,0:T(8,128)(2,1)S(1)}, u32[]{:S(2)}, u32[]{:S(2)}) collective-permute-start(bf16[48,768]{1,0:T(8,128)(2,1)} %pack.2), channel_id=1, source_target_pairs={{0,16},{1,17},{2,18},{3,19},{4,20},{5,21},{6,22},{7,23},{8,24},{9,... | collective-permute-start | bytes 221192 | tf_op jit(solution)/shard_map/ppermute | solution.py:705
  8.5 1.4 pack.3
  9.9 3.3 %collective-permute-done.1 = bf16[16,768]{1,0:T(8,128)(2,1)S(1)} collective-permute-done((bf16[16,768]{1,0:T(8,128)(2,1)S(1)}, bf16[16,768]{1,0:T(8,128)(2,1)S(1)}, u32[]{:S(2)}, u32[]{:S(2)}) %collective-permute-start.1) | collective-permute-done | bytes 24608 | tf_op jit(solution)/shard_map/ppermute | solution.py:705
  14.2 1.6 collective-permute-start.3
  16.6 1.7 collective-permute-done.3
  18.3 3.8 %collective-permute-done.4 = bf16[48,768]{1,0:T(8,128)(2,1)S(1)} collective-permute-done((bf16[48,768]{1,0:T(8,128)(2,1)}, bf16[48,768]{1,0:T(8,128)(2,1)S(1)}, u32[]{:S(2)}, u32[]{:S(2)}) %collective-permute-start.4) | collective-permute-done | bytes 73760 | tf_op jit(solution)/shard_map/ppermute | solution.py:705
  24.1 1.5 collective-permute-start.6
  28.0 3.1 collective-permute-done.8
  34.0 1.5 collective-permute-start.11
  36.0 1.8 collective-permute-done.11
  37.8 4.6 %collective-permute-done.12 = bf16[2,2,48,768]{3,2,1,0:T(8,128)(2,1)S(1)} collective-permute-done((bf16[2,2,48,768]{3,2,1,0:T(8,128)(2,1)S(1)}, bf16[2,2,48,768]{3,2,1,0:T(8,128)(2,1)S(1)}, u32[]{:S(2)}, u32[]{:S(2)}) %collective-permute-start.12) | collective-permute-done | bytes 294944 | tf_op jit(solution)/shard_map/ppermute | solution.py:705
  42.6 2.7 collective-permute-done.9.refs_3_
  45.9 1.5 collective-permute-done.15
  48.1 1.4 collective-permute-start.18
  50.0 1.9 collective-permute-start.19
  51.9 7.0 %project.2 = (bf16[1024,768]{1,0:T(8,128)(2,1)}, bf16[1024,768]{1,0:T(8,128)(2,1)}, bf16[2,4,2,2,2,24,768]{6,5,4,3,2,1,0:T(8,128)(2,1)}) custom-call(bf16[1024,768]{1,0:T(8,128)(2,1)} %bitcast.204, bf16[16,768]{1,0:T(8,128)(2,1)} %add.653.refs_1_.vec_ref.refs_2_.codes_ref.refs_5_, bf16[4,2,48,768]{3,2,1,0:T(8,128)(2,1)} %copy-done.9, ...), custom_call_target="tpu_custom_call" | custom-call | flops 2415919104 | bytes 9437184 | tf_op jit(solution)/shard_map/project/pallas_call | solution.py:128
  58.9 1.5 collective-permute-done.19
  60.5 3.3 %collective-permute-done.18 = bf16[2,2,24,3072]{3,2,1,0:T(8,128)(2,1)S(1)} collective-permute-done((bf16[2,2,24,3072]{3,2,1,0:T(8,128)(2,1)S(1)}, bf16[2,2,24,3072]{3,2,1,0:T(8,128)(2,1)S(1)}, u32[]{:S(2)}, u32[]{:S(2)}) %collective-permute-start.18) | collective-permute-done | bytes 589856 | tf_op jit(solution)/shard_map/ppermute | solution.py:705
  64.9 1.3 collective-permute-done.20.refs_5_
  67.0 5.4 %project.3 = (bf16[1024,768]{1,0:T(8,128)(2,1)}, bf16[2,4,2,2,2,24,768]{6,5,4,3,2,1,0:T(8,128)(2,1)}) custom-call(bf16[1024,768]{1,0:T(8,128)(2,1)} %bitcast.205, bf16[16,768]{1,0:T(8,128)(2,1)} %add.653.refs_1_.vec_ref.refs_2_.codes_ref.refs_5_, bf16[4,2,48,768]{3,2,1,0:T(8,128)(2,1)} %copy-done.8, bf16[4,2,48,768]{3,2,1,0:T(8,128)(2,1)} %collective-permute-done.16.refs_3_, ...), custom_call_target="tpu_custom_call" | custom-call | flops 1207959552 | bytes 7864320 | tf_op jit(solution)/shard_map/project/pallas_call | solution.py:128
  72.4 1.8 collective-permute-start.22
  74.2 9.3 %attend.1 = (f32[3,1024,256]{2,1,0:T(8,128)}, bf16[1024,768]{1,0:T(8,128)(2,1)}) custom-call(s32[16]{0:T(128)} %len_ref.1, bf16[1024,768]{1,0:T(8,128)(2,1)} %get-tuple-element.151.q_ref.refs_0_, bf16[1024,768]{1,0:T(8,128)(2,1)} %get-tuple-element.152.k_ref.refs_1_, bf16[1024,768]{1,0:T(8,128)(2,1)} %get-tuple-element.157.v_ref.refs_2_), custom_call_target="tpu_custom_call" | custom-call | flops 6039797760 | bytes 15728640 | tf_op jit(solution)/shard_map/attend/pallas_call | solution.py:220
  85.1 5.6 %close.1 = (f32[1024,768]{1,0:T(8,128)}, f32[1024,1]{1,0:T(8,128)}, bf16[1024,768]{1,0:T(8,128)(2,1)}) custom-call(bf16[1024,768]{1,0:T(8,128)(2,1)} %bitcast.206, bf16[1024,768]{1,0:T(8,128)(2,1)} %get-tuple-element.161.c_ref.refs_7_, bf16[2,768,768]{2,1,0:T(8,128)(2,1)} %bitcast.183, bf16[16,768]{1,0:T(8,128)(2,1)} %add.653.refs_1_.vec_ref.refs_2_.codes_ref.refs_5_), custom_call_target="tpu_custom_call" | custom-call | flops 1207959552 | bytes 9043968 | tf_op jit(solution)/shard_map/close/pallas_call | solution.py:251
  90.8 3.4 %collective-permute-done.25 = bf16[2,2,96,768]{3,2,1,0:T(8,128)(2,1)S(1)} collective-permute-done((bf16[2,2,96,768]{3,2,1,0:T(8,128)(2,1)S(1)}, bf16[2,2,96,768]{3,2,1,0:T(8,128)(2,1)S(1)}, u32[]{:S(2)}, u32[]{:S(2)}) %collective-permute-start.25) | collective-permute-done | bytes 589856 | tf_op jit(solution)/shard_map/ppermute | solution.py:705
  95.2 22.0 %inner.1 = (bf16[1024,3072]{1,0:T(8,128)(2,1)}, bf16[1024,3072]{1,0:T(8,128)(2,1)}, bf16[4,2,2,2,24,3072]{5,4,3,2,1,0:T(8,128)(2,1)}) custom-call(bf16[1024,768]{1,0:T(8,128)(2,1)} %get-tuple-element.167.refs_0_.refs_1_, bf16[16,768]{1,0:T(8,128)(2,1)} %add.653.refs_1_.vec_ref.refs_2_.codes_ref.refs_5_, bf16[4,2,24,3072]{3,2,1,0:T(8,128)(2,1)} %copy-done.5, ...), custom_call_target="tpu_custom_call" | custom-call | flops 14495514624 | bytes 23592960 | tf_op jit(solution)/shard_map/inner/pallas_call | solution.py:416
  117.8 2.5 collective-permute-done.28.refs_6_
  121.3 12.7 %outer.1 = (bf16[1024,768]{1,0:T(8,128)(2,1)}, f32[1024,768]{1,0:T(8,128)}, f32[1024,1]{1,0:T(8,128)}, f32[8,1536]{1,0:T(8,128)}, bf16[8,1536]{1,0:T(8,128)(2,1)}, /*index=5*/bf16[4,2,2,2,96,768]{5,4,3,2,1,0:T(8,128)(2,1)}) custom-call(bf16[1024,3072]{1,0:T(8,128)(2,1)} %get-tuple-element.174.refs_0_.refs_4_, ...), custom_call_target="tpu_custom_call" | custom-call | flops 4831838208 | bytes 23592960 | tf_op jit(solution)/shard_map/outer/pallas_call | solution.py:464
  134.0 1.6 collective-permute-start.29
  135.5 3.5 %collective-permute-done.29 = bf16[8,1536]{1,0:T(8,128)(2,1)S(1)} collective-permute-done((bf16[8,1536]{1,0:T(8,128)(2,1)}, bf16[8,1536]{1,0:T(8,128)(2,1)S(1)}, u32[]{:S(2)}, u32[]{:S(2)}) %collective-permute-start.29) | collective-permute-done | bytes 24608 | tf_op jit(solution)/shard_map/ppermute | solution.py:705
  140.1 3.8 %collective-permute-done.30 = bf16[2,8,1536]{2,1,0:T(8,128)(2,1)S(1)} collective-permute-done((bf16[2,8,1536]{2,1,0:T(8,128)(2,1)S(1)}, bf16[2,8,1536]{2,1,0:T(8,128)(2,1)S(1)}, u32[]{:S(2)}, u32[]{:S(2)}) %collective-permute-start.30) | collective-permute-done | bytes 49184 | tf_op jit(solution)/shard_map/ppermute | solution.py:705
  145.4 3.6 %collective-permute-done.31 = bf16[2,2,8,1536]{3,2,1,0:T(8,128)(2,1)S(1)} collective-permute-done((bf16[2,2,8,1536]{3,2,1,0:T(8,128)(2,1)S(1)}, bf16[2,2,8,1536]{3,2,1,0:T(8,128)(2,1)S(1)}, u32[]{:S(2)}, u32[]{:S(2)}) %collective-permute-start.31) | collective-permute-done | bytes 98336 | tf_op jit(solution)/shard_map/ppermute | solution.py:705
  149.1 1.3 collective-permute-start.32
  150.4 4.4 %collective-permute-done.32.far = bf16[4,2,8,1536]{3,2,1,0:T(8,128)(2,1)S(1)} collective-permute-done((bf16[4,2,8,1536]{3,2,1,0:T(8,128)(2,1)S(1)}, bf16[4,2,8,1536]{3,2,1,0:T(8,128)(2,1)S(1)}, u32[]{:S(2)}, u32[]{:S(2)}) %collective-permute-start.32) | collective-permute-done | bytes 196640 | tf_op jit(solution)/shard_map/ppermute | solution.py:705
  154.9 1.4 collective-permute-done.34.far_other
  157.0 3.8 %pair_loss.1 = (f32[8,128]{1,0:T(8,128)}, f32[8,1536]{1,0:T(8,128)}) custom-call(bf16[4,2,8,1536]{3,2,1,0:T(8,128)(2,1)} %copy-done.13, bf16[4,2,8,1536]{3,2,1,0:T(8,128)(2,1)} %copy-done.22, bf16[4,2,8,1536]{3,2,1,0:T(8,128)(2,1)} %copy-done.23, bf16[4,2,8,1536]{3,2,1,0:T(8,128)(2,1)} %copy-done.24, ...), custom_call_target="tpu_custom_call" | custom-call | flops 301989888 | bytes 786432 | tf_op jit(solution)/shard_map/pair_loss/pallas_call | solution.py:661
  160.8 13.5 %outer_back.1 = (f32[1024,768]{1,0:T(8,128)}, bf16[1024,768]{1,0:T(8,128)(2,1)}, f32[16,768]{1,0:T(8,128)}, bf16[4,2,2,96,768]{4,3,2,1,0:T(8,128)(2,1)}, bf16[4,2,2,96,768]{4,3,2,1,0:T(8,128)(2,1)}) custom-call(bf16[1024,768]{1,0:T(8,128)(2,1)} %bitcast.223, f32[8,1536]{1,0:T(8,128)} %get-tuple-element.182.refs_1_, f32[1024,768]{1,0:T(8,128)} %get-tuple-element.183.refs_2_, ...), custom_call_target="tpu_custom_call" | custom-call | flops 9663676416 | bytes 36175872 | tf_op jit(solution)/shard_map/outer_back/pallas_call | solution.py:550
  174.5 15.8 %inner_back.1 = (bf16[1024,3072]{1,0:T(8,128)(2,1)}, f32[16,768]{1,0:T(8,128)}, bf16[4,2,2,24,3072]{4,3,2,1,0:T(8,128)(2,1)}, bf16[4,2,2,24,3072]{4,3,2,1,0:T(8,128)(2,1)}) custom-call(bf16[1024,768]{1,0:T(8,128)(2,1)} %get-tuple-element.187.refs_0_, bf16[1024,768]{1,0:T(8,128)(2,1)} %get-tuple-element.167.refs_0_.refs_1_, ...), custom_call_target="tpu_custom_call" | custom-call | flops 9663676416 | bytes 34603008 | tf_op jit(solution)/shard_map/inner_back/pallas_call | solution.py:590
  190.7 2.6 fusion.2
  194.4 14.2 %open_back.1 = (f32[1024,768]{1,0:T(8,128)}, bf16[1024,768]{1,0:T(8,128)(2,1)}, bf16[1024,768]{1,0:T(8,128)(2,1)}, f32[16,768]{1,0:T(8,128)}) custom-call(f32[1024,768]{1,0:T(8,128)} %get-tuple-element.196.dres_ref, bf16[1024,3072]{1,0:T(8,128)(2,1)} %get-tuple-element.197.dh_ref, bf16[768,3072]{1,0:T(8,128)(2,1)} %bitcast.224, ...), custom_call_target="tpu_custom_call" | custom-call | flops 6039797760 | bytes 21626880 | tf_op jit(solution)/shard_map/open_back/pallas_call | solution.py:282
  209.7 2.5 fusion.5
  212.2 1.2 collective-permute-start.38
  213.5 1.6 fusion.3
  215.4 29.6 %heads_back.1 = (bf16[1024,768]{1,0:T(8,128)(2,1)}, bf16[1024,768]{1,0:T(8,128)(2,1)}, bf16[1024,768]{1,0:T(8,128)(2,1)}, bf16[4,2,2,104,768]{4,3,2,1,0:T(8,128)(2,1)}, bf16[4,2,2,104,768]{4,3,2,1,0:T(8,128)(2,1)}) custom-call(bf16[1024,768]{1,0:T(8,128)(2,1)} %get-tuple-element.151.q_ref.refs_0_, bf16[1024,768]{1,0:T(8,128)(2,1)} %get-tuple-element.152.k_ref.refs_1_, ...), custom_call_target="tpu_custom_call" | custom-call | flops 18874368000 | bytes 15728640 | tf_op jit(solution)/shard_map/heads_back/pallas_call | solution.py:372
  245.8 1.5 fusion.10
  247.4 2.5 fusion.4
  250.2 2.7 fusion
  252.9 1.2 collective-permute-start.43
  254.9 1.8 collective-permute-start.41
  256.7 8.9 %token_grad.1 = f32[1024,768]{1,0:T(8,128)} custom-call(f32[1024,768]{1,0:T(8,128)} %get-tuple-element.201.dr_ref, bf16[1024,768]{1,0:T(8,128)(2,1)} %get-tuple-element.215.dq_ref, bf16[1024,768]{1,0:T(8,128)(2,1)} %get-tuple-element.216.dk_ref, bf16[1024,768]{1,0:T(8,128)(2,1)} %get-tuple-element.217.dv_ref, bf16[2,768,768]{2,1,0:T(8,128)(2,1)} %bitcast.181, ...), custom_call_target="tpu_custom_call" | custom-call | flops 3623878656 | bytes 14548992 | tf_op jit(solution)/shard_map/token_grad/pallas_call | solution.py:613
  265.6 11.1 %collective-permute-done.42 = bf16[2,2,24,3072]{3,2,1,0:T(8,128)(2,1)S(1)} collective-permute-done((bf16[2,2,24,3072]{3,2,1,0:T(8,128)(2,1)}, bf16[2,2,24,3072]{3,2,1,0:T(8,128)(2,1)S(1)}, u32[]{:S(2)}, u32[]{:S(2)}) %collective-permute-start.42) | collective-permute-done | bytes 589856 | tf_op jit(solution)/shard_map/ppermute | solution.py:705
  277.5 2.4 fusion.1
  280.6 2.1 fusion.9
  282.7 1.3 collective-permute-start.44
  284.0 1.3 slice.56
  286.5 2.6 collective-permute-start.46
  289.1 4.7 %collective-permute-done.44 = bf16[2,24,3072]{2,1,0:T(8,128)(2,1)} collective-permute-done((bf16[2,24,3072]{2,1,0:T(8,128)(2,1)}, bf16[2,24,3072]{2,1,0:T(8,128)(2,1)}, u32[]{:S(2)}, u32[]{:S(2)}) %collective-permute-start.44) | collective-permute-done | bytes 294944 | tf_op jit(solution)/shard_map/ppermute | solution.py:705
  295.0 1.8 collective-permute-start.47
  296.8 1.2 fusion.13
  298.1 1.5 collective-permute-start.49
  299.6 2.0 fusion.16
  301.6 4.6 %collective-permute-done.47 = bf16[2,104,768]{2,1,0:T(8,128)(2,1)S(1)} collective-permute-done((bf16[2,104,768]{2,1,0:T(8,128)(2,1)S(1)}, bf16[2,104,768]{2,1,0:T(8,128)(2,1)S(1)}, u32[]{:S(2)}, u32[]{:S(2)}) %collective-permute-start.47) | collective-permute-done | bytes 319520 | tf_op jit(solution)/shard_map/ppermute | solution.py:705
  308.3 2.0 fusion.14
  310.2 4.7 %collective-permute-done.48 = bf16[104,768]{1,0:T(8,128)(2,1)S(1)} collective-permute-done((bf16[104,768]{1,0:T(8,128)(2,1)S(1)}, bf16[104,768]{1,0:T(8,128)(2,1)S(1)}, u32[]{:S(2)}, u32[]{:S(2)}) %collective-permute-start.48) | collective-permute-done | bytes 159776 | tf_op jit(solution)/shard_map/ppermute | solution.py:705
  (164 shorter events, 37.3 us)
Async XLA Ops:
  0.7 6.4 %copy-start = (bf16[96]{0:T(256)(128)(2,1)S(1)}, bf16[96]{0:T(256)(128)(2,1)}, u32[]{:S(2)}) copy-start(bf16[96]{0:T(256)(128)(2,1)} %param.33) | copy-start | bytes 580
  0.7 22.5 %copy-start.14 = (bf16[24,3072]{1,0:T(8,128)(2,1)S(1)}, bf16[24,3072]{1,0:T(8,128)(2,1)}, u32[]{:S(2)}) copy-start(bf16[24,3072]{1,0:T(8,128)(2,1)} %param.32) | copy-start | bytes 442372
  2.1 11.1 %collective-permute-start = (bf16[48,768]{1,0:T(8,128)(2,1)}, bf16[48,768]{1,0:T(8,128)(2,1)S(1)}, u32[]{:S(2)}, u32[]{:S(2)}) collective-permute-start(bf16[48,768]{1,0:T(8,128)(2,1)} %pack.2), channel_id=1, source_target_pairs={{0,16},{1,17},{2,18},{3,19},{4,20},{5,21},{6,22},{7,23},{8,24},{9,... | collective-permute-start | bytes 221192 | tf_op jit(solution)/shard_map/ppermute | solution.py:705
  8.4 4.7 %collective-permute-start.1 = (bf16[16,768]{1,0:T(8,128)(2,1)S(1)}, bf16[16,768]{1,0:T(8,128)(2,1)S(1)}, u32[]{:S(2)}, u32[]{:S(2)}) collective-permute-start(bf16[16,768]{1,0:T(8,128)(2,1)S(1)} %maximum_maximum_fusion), channel_id=1, source_target_pairs={{0,16},{1,17},{2,18},{3,19},{4,20},{5,21},{6,22},{7,23},{8,24},{9,... | collective-permute-start | bytes 73736 | tf_op jit(solution)/shard_map/ppermute | solution.py:705
  14.2 4.0 %collective-permute-start.3 = (bf16[16,768]{1,0:T(8,128)(2,1)S(1)}, bf16[16,768]{1,0:T(8,128)(2,1)S(1)}, u32[]{:S(2)}, u32[]{:S(2)}) collective-permute-start(bf16[16,768]{1,0:T(8,128)(2,1)S(1)} %fusion.62), channel_id=1, source_target_pairs={{0,8},{1,9},{2,10},{3,11},{4,12},{5,13},{6,14},{7,15},{8,0},{9,1},... | collective-permute-start | bytes 73736 | tf_op jit(solution)/shard_map/ppermute | solution.py:705
  15.9 6.2 %collective-permute-start.4 = (bf16[48,768]{1,0:T(8,128)(2,1)}, bf16[48,768]{1,0:T(8,128)(2,1)S(1)}, u32[]{:S(2)}, u32[]{:S(2)}) collective-permute-start(bf16[48,768]{1,0:T(8,128)(2,1)} %pack.3), channel_id=1, source_target_pairs={{0,16},{1,17},{2,18},{3,19},{4,20},{5,21},{6,22},{7,23},{8,24},{9,... | collective-permute-start | bytes 221192 | tf_op jit(solution)/shard_map/ppermute | solution.py:705
  16.5 6.6 %collective-permute-start.2 = (bf16[2,48,768]{2,1,0:T(8,128)(2,1)S(1)}, bf16[2,48,768]{2,1,0:T(8,128)(2,1)S(1)}, u32[]{:S(2)}, u32[]{:S(2)}) collective-permute-start(bf16[2,48,768]{2,1,0:T(8,128)(2,1)S(1)} %broadcast_select_fusion.12), channel_id=1, source_target_pairs={{0,8},{1,9},{2,10},{3,11},{4,12},{5,13},{6,14},{7,15},{8,0},{9,1},... | collective-permute-start | bytes 442376 | tf_op jit(solution)/shard_map/ppermute | solution.py:705
  23.2 7.8 %collective-permute-start.8 = (bf16[24,3072]{1,0:T(8,128)(2,1)S(1)}, bf16[24,3072]{1,0:T(8,128)(2,1)S(1)}, u32[]{:S(2)}, u32[]{:S(2)}) collective-permute-start(bf16[24,3072]{1,0:T(8,128)(2,1)S(1)} %copy-done.14), channel_id=1, source_target_pairs={{0,16},{1,17},{2,18},{3,19},{4,20},{5,21},{6,22},{7,23},{8,24},{9,... | collective-permute-start | bytes 442376 | tf_op jit(solution)/shard_map/ppermute | solution.py:705
  24.1 3.8 %collective-permute-start.6 = (bf16[16,768]{1,0:T(8,128)(2,1)S(1)}, bf16[16,768]{1,0:T(8,128)(2,1)S(1)}, u32[]{:S(2)}, u32[]{:S(2)}) collective-permute-start(bf16[16,768]{1,0:T(8,128)(2,1)S(1)} %add.650), channel_id=1, source_target_pairs={{0,2},{1,5},{2,0},{3,7},{4,6},{5,1},{6,4},{7,3},{8,10},{9,13},{10,... | collective-permute-start | bytes 73736 | tf_op jit(solution)/shard_map/ppermute | solution.py:705
  25.6 6.7 %collective-permute-start.5 = (bf16[2,2,48,768]{3,2,1,0:T(8,128)(2,1)S(1)}, bf16[2,2,48,768]{3,2,1,0:T(8,128)(2,1)S(1)}, u32[]{:S(2)}, u32[]{:S(2)}) collective-permute-start(bf16[2,2,48,768]{3,2,1,0:T(8,128)(2,1)S(1)} %broadcast_select_fusion.9), channel_id=1, source_target_pairs={{0,2},{1,5},{2,0},{3,7},{4,6},{5,1},{6,4},{7,3},{8,10},{9,13},{10,... | collective-permute-start | bytes 884744 | tf_op jit(solution)/shard_map/ppermute | solution.py:705
  26.1 5.7 %collective-permute-start.7 = (bf16[2,48,768]{2,1,0:T(8,128)(2,1)S(1)}, bf16[2,48,768]{2,1,0:T(8,128)(2,1)S(1)}, u32[]{:S(2)}, u32[]{:S(2)}) collective-permute-start(bf16[2,48,768]{2,1,0:T(8,128)(2,1)S(1)} %broadcast_select_fusion.11), channel_id=1, source_target_pairs={{0,8},{1,9},{2,10},{3,11},{4,12},{5,13},{6,14},{7,15},{8,0},{9,1},... | collective-permute-start | bytes 442376 | tf_op jit(solution)/shard_map/ppermute | solution.py:705
  32.3 17.7 %copy-start.15 = (bf16[96,768]{1,0:T(8,128)(2,1)S(1)}, bf16[96,768]{1,0:T(8,128)(2,1)}, u32[]{:S(2)}) copy-start(bf16[96,768]{1,0:T(8,128)(2,1)} %param.34) | copy-start | bytes 442372
  32.5 19.4 %copy-start.9 = (bf16[4,2,48,768]{3,2,1,0:T(8,128)(2,1)}, bf16[4,2,48,768]{3,2,1,0:T(8,128)(2,1)S(1)}, u32[]{:S(2)}) copy-start(bf16[4,2,48,768]{3,2,1,0:T(8,128)(2,1)S(1)} %broadcast_select_fusion.5.refs_2_) | copy-start | bytes 1769476
  32.5 9.9 %collective-permute-start.12 = (bf16[2,2,48,768]{3,2,1,0:T(8,128)(2,1)S(1)}, bf16[2,2,48,768]{3,2,1,0:T(8,128)(2,1)S(1)}, u32[]{:S(2)}, u32[]{:S(2)}) collective-permute-start(bf16[2,2,48,768]{3,2,1,0:T(8,128)(2,1)S(1)} %broadcast_select_fusion.8), channel_id=1, source_target_pairs={{0,2},{1,5},{2,0},{3,7},{4,6},{5,1},{6,4},{7,3},{8,10},{9,13},{10,... | collective-permute-start | bytes 884744 | tf_op jit(solution)/shard_map/ppermute | solution.py:705
  33.7 8.8 %collective-permute-start.13 = (bf16[2,24,3072]{2,1,0:T(8,128)(2,1)S(1)}, bf16[2,24,3072]{2,1,0:T(8,128)(2,1)S(1)}, u32[]{:S(2)}, u32[]{:S(2)}) collective-permute-start(bf16[2,24,3072]{2,1,0:T(8,128)(2,1)S(1)} %broadcast_select_fusion.7), channel_id=1, source_target_pairs={{0,8},{1,9},{2,10},{3,11},{4,12},{5,13},{6,14},{7,15},{8,0},{9,1},... | collective-permute-start | bytes 884744 | tf_op jit(solution)/shard_map/ppermute | solution.py:705
  34.0 3.8 %collective-permute-start.11 = (bf16[16,768]{1,0:T(8,128)(2,1)S(1)}, bf16[16,768]{1,0:T(8,128)(2,1)S(1)}, u32[]{:S(2)}, u32[]{:S(2)}) collective-permute-start(bf16[16,768]{1,0:T(8,128)(2,1)S(1)} %add.651), channel_id=1, source_target_pairs={{0,4},{1,3},{2,6},{3,1},{4,0},{5,7},{6,2},{7,5},{8,12},{9,11},{10,... | collective-permute-start | bytes 73736 | tf_op jit(solution)/shard_map/ppermute | solution.py:705
  35.5 9.9 %collective-permute-start.9 = (bf16[4,2,48,768]{3,2,1,0:T(8,128)(2,1)S(1)}, bf16[4,2,48,768]{3,2,1,0:T(8,128)(2,1)S(1)}, u32[]{:S(2)}, u32[]{:S(2)}) collective-permute-start(bf16[4,2,48,768]{3,2,1,0:T(8,128)(2,1)S(1)} %broadcast_select_fusion.5.refs_2_), channel_id=1, source_target_pairs={{0,4},{1,3},{2,6},{3,1},{4,0},{5,7},{6,2},{7,5},{8,12},{9,11},{10,... | collective-permute-start | bytes 1769480 | tf_op jit(solution)/shard_map/ppermute | solution.py:705
  36.0 9.4 %collective-permute-start.10 = (bf16[4,2,48,768]{3,2,1,0:T(8,128)(2,1)S(1)}, bf16[4,2,48,768]{3,2,1,0:T(8,128)(2,1)S(1)}, u32[]{:S(2)}, u32[]{:S(2)}) collective-permute-start(bf16[4,2,48,768]{3,2,1,0:T(8,128)(2,1)S(1)} %broadcast_select_fusion.5.refs_2_), channel_id=1, source_target_pairs={{0,1},{1,0},{2,3},{3,2},{4,5},{5,4},{6,7},{7,6},{8,9},{9,8},{10,11... | collective-permute-start | bytes 1769480 | tf_op jit(solution)/shard_map/ppermute | solution.py:705
  42.5 16.4 %copy-start.8 = (bf16[4,2,48,768]{3,2,1,0:T(8,128)(2,1)}, bf16[4,2,48,768]{3,2,1,0:T(8,128)(2,1)S(1)}, u32[]{:S(2)}) copy-start(bf16[4,2,48,768]{3,2,1,0:T(8,128)(2,1)S(1)} %broadcast_select_fusion.4.refs_2_) | copy-start | bytes 1769476
  45.4 4.6 %copy-start.19 = (bf16[4,2,48,768]{3,2,1,0:T(8,128)(2,1)}, bf16[4,2,48,768]{3,2,1,0:T(8,128)(2,1)S(1)}, u32[]{:S(2)}) copy-start(bf16[4,2,48,768]{3,2,1,0:T(8,128)(2,1)S(1)} %collective-permute-done.10.refs_4_) | copy-start | bytes 1769476
  45.4 2.7 collective-permute-start.14
  45.4 2.0 collective-permute-start.15
  48.1 15.7 %collective-permute-start.18 = (bf16[2,2,24,3072]{3,2,1,0:T(8,128)(2,1)S(1)}, bf16[2,2,24,3072]{3,2,1,0:T(8,128)(2,1)S(1)}, u32[]{:S(2)}, u32[]{:S(2)}) collective-permute-start(bf16[2,2,24,3072]{3,2,1,0:T(8,128)(2,1)S(1)} %broadcast_select_fusion.3), channel_id=1, source_target_pairs={{0,2},{1,5},{2,0},{3,7},{4,6},{5,1},{6,4},{7,3},{8,10},{9,13},{10,... | collective-permute-start | bytes 1769480 | tf_op jit(solution)/shard_map/ppermute | solution.py:705
  49.5 14.4 %collective-permute-start.16 = (bf16[4,2,48,768]{3,2,1,0:T(8,128)(2,1)S(1)}, bf16[4,2,48,768]{3,2,1,0:T(8,128)(2,1)}, u32[]{:S(2)}, u32[]{:S(2)}) collective-permute-start(bf16[4,2,48,768]{3,2,1,0:T(8,128)(2,1)S(1)} %broadcast_select_fusion.4.refs_2_), channel_id=1, source_target_pairs={{0,4},{1,3},{2,6},{3,1},{4,0},{5,7},{6,2},{7,5},{8,12},{9,11},{10,... | collective-permute-start | bytes 1769480 | tf_op jit(solution)/shard_map/ppermute | solution.py:705
  50.0 13.9 %collective-permute-start.17 = (bf16[4,2,48,768]{3,2,1,0:T(8,128)(2,1)S(1)}, bf16[4,2,48,768]{3,2,1,0:T(8,128)(2,1)}, u32[]{:S(2)}, u32[]{:S(2)}) collective-permute-start(bf16[4,2,48,768]{3,2,1,0:T(8,128)(2,1)S(1)} %broadcast_select_fusion.4.refs_2_), channel_id=1, source_target_pairs={{0,1},{1,0},{2,3},{3,2},{4,5},{5,4},{6,7},{7,6},{8,9},{9,8},{10,11... | collective-permute-start | bytes 1769480 | tf_op jit(solution)/shard_map/ppermute | solution.py:705
  50.0 10.3 %collective-permute-start.19 = (bf16[96,768]{1,0:T(8,128)(2,1)S(1)}, bf16[96,768]{1,0:T(8,128)(2,1)S(1)}, u32[]{:S(2)}, u32[]{:S(2)}) collective-permute-start(bf16[96,768]{1,0:T(8,128)(2,1)S(1)} %copy-done.15), channel_id=1, source_target_pairs={{0,16},{1,17},{2,18},{3,19},{4,20},{5,21},{6,22},{7,23},{8,24},{9,... | collective-permute-start | bytes 442376 | tf_op jit(solution)/shard_map/ppermute | solution.py:705
  63.9 19.7 %copy-start.5 = (bf16[4,2,24,3072]{3,2,1,0:T(8,128)(2,1)}, bf16[4,2,24,3072]{3,2,1,0:T(8,128)(2,1)S(1)}, u32[]{:S(2)}) copy-start(bf16[4,2,24,3072]{3,2,1,0:T(8,128)(2,1)S(1)} %broadcast_select_fusion.1.refs_2_) | copy-start | bytes 3538948
  64.0 2.3 collective-permute-start.20
  64.0 19.6 %collective-permute-start.21 = (bf16[4,2,24,3072]{3,2,1,0:T(8,128)(2,1)S(1)}, bf16[4,2,24,3072]{3,2,1,0:T(8,128)(2,1)}, u32[]{:S(2)}, u32[]{:S(2)}) collective-permute-start(bf16[4,2,24,3072]{3,2,1,0:T(8,128)(2,1)S(1)} %broadcast_select_fusion.1.refs_2_), channel_id=1, source_target_pairs={{0,4},{1,3},{2,6},{3,1},{4,0},{5,7},{6,2},{7,5},{8,12},{9,11},{10,... | collective-permute-start | bytes 3538952 | tf_op jit(solution)/shard_map/ppermute | solution.py:705
  72.4 11.1 %collective-permute-start.22 = (bf16[2,96,768]{2,1,0:T(8,128)(2,1)S(1)}, bf16[2,96,768]{2,1,0:T(8,128)(2,1)S(1)}, u32[]{:S(2)}, u32[]{:S(2)}) collective-permute-start(bf16[2,96,768]{2,1,0:T(8,128)(2,1)S(1)} %broadcast_select_fusion.6), channel_id=1, source_target_pairs={{0,8},{1,9},{2,10},{3,11},{4,12},{5,13},{6,14},{7,15},{8,0},{9,1},... | collective-permute-start | bytes 884744 | tf_op jit(solution)/shard_map/ppermute | solution.py:705
  83.7 10.6 %collective-permute-start.23 = (bf16[4,2,24,3072]{3,2,1,0:T(8,128)(2,1)S(1)}, bf16[4,2,24,3072]{3,2,1,0:T(8,128)(2,1)}, u32[]{:S(2)}, u32[]{:S(2)}) collective-permute-start(bf16[4,2,24,3072]{3,2,1,0:T(8,128)(2,1)S(1)} %broadcast_select_fusion.1.refs_2_), channel_id=1, source_target_pairs={{0,1},{1,0},{2,3},{3,2},{4,5},{5,4},{6,7},{7,6},{8,9},{9,8},{10,11... | collective-permute-start | bytes 3538952 | tf_op jit(solution)/shard_map/ppermute | solution.py:705
  83.8 10.6 %collective-permute-start.24 = (bf16[4,2,24,3072]{3,2,1,0:T(8,128)(2,1)}, bf16[4,2,24,3072]{3,2,1,0:T(8,128)(2,1)}, u32[]{:S(2)}, u32[]{:S(2)}) collective-permute-start(bf16[4,2,24,3072]{3,2,1,0:T(8,128)(2,1)} %collective-permute-done.21.refs_3_), channel_id=1, source_target_pairs={{0,1},{1,0},{2,3},{3,2},{4,5},{5,4},{6,7},{7,6},{8,9},{9,8},{10,11... | collective-permute-start | bytes 3538952 | tf_op jit(solution)/shard_map/ppermute | solution.py:705
  84.3 9.9 %collective-permute-start.25 = (bf16[2,2,96,768]{3,2,1,0:T(8,128)(2,1)S(1)}, bf16[2,2,96,768]{3,2,1,0:T(8,128)(2,1)S(1)}, u32[]{:S(2)}, u32[]{:S(2)}) collective-permute-start(bf16[2,2,96,768]{3,2,1,0:T(8,128)(2,1)S(1)} %broadcast_select_fusion.2), channel_id=1, source_target_pairs={{0,2},{1,5},{2,0},{3,7},{4,6},{5,1},{6,4},{7,3},{8,10},{9,13},{10,... | collective-permute-start | bytes 1769480 | tf_op jit(solution)/shard_map/ppermute | solution.py:705
  94.3 22.9 %copy-start.6 = (bf16[4,2,96,768]{3,2,1,0:T(8,128)(2,1)}, bf16[4,2,96,768]{3,2,1,0:T(8,128)(2,1)S(1)}, u32[]{:S(2)}) copy-start(bf16[4,2,96,768]{3,2,1,0:T(8,128)(2,1)S(1)} %broadcast_select_fusion.refs_3_) | copy-start | bytes 3538948
  94.3 22.9 %collective-permute-start.26 = (bf16[4,2,96,768]{3,2,1,0:T(8,128)(2,1)S(1)}, bf16[4,2,96,768]{3,2,1,0:T(8,128)(2,1)S(1)}, u32[]{:S(2)}, u32[]{:S(2)}) collective-permute-start(bf16[4,2,96,768]{3,2,1,0:T(8,128)(2,1)S(1)} %broadcast_select_fusion.refs_3_), channel_id=1, source_target_pairs={{0,4},{1,3},{2,6},{3,1},{4,0},{5,7},{6,2},{7,5},{8,12},{9,11},{10,... | collective-permute-start | bytes 3538952 | tf_op jit(solution)/shard_map/ppermute | solution.py:705
  95.2 22.1 %collective-permute-start.27 = (bf16[4,2,96,768]{3,2,1,0:T(8,128)(2,1)S(1)}, bf16[4,2,96,768]{3,2,1,0:T(8,128)(2,1)}, u32[]{:S(2)}, u32[]{:S(2)}) collective-permute-start(bf16[4,2,96,768]{3,2,1,0:T(8,128)(2,1)S(1)} %broadcast_select_fusion.refs_3_), channel_id=1, source_target_pairs={{0,1},{1,0},{2,3},{3,2},{4,5},{5,4},{6,7},{7,6},{8,9},{9,8},{10,11... | collective-permute-start | bytes 3538952 | tf_op jit(solution)/shard_map/ppermute | solution.py:705
  117.3 3.0 collective-permute-start.28
  134.0 5.0 %collective-permute-start.29 = (bf16[8,1536]{1,0:T(8,128)(2,1)}, bf16[8,1536]{1,0:T(8,128)(2,1)S(1)}, u32[]{:S(2)}, u32[]{:S(2)}) collective-permute-start(bf16[8,1536]{1,0:T(8,128)(2,1)} %get-tuple-element.178), channel_id=1, source_target_pairs={{0,16},{1,17},{2,18},{3,19},{4,20},{5,21},{6,22},{7,23},{8,24},{9,... | collective-permute-start | bytes 73736 | tf_op jit(solution)/shard_map/ppermute | solution.py:705
  139.8 4.1 %collective-permute-start.30 = (bf16[2,8,1536]{2,1,0:T(8,128)(2,1)S(1)}, bf16[2,8,1536]{2,1,0:T(8,128)(2,1)S(1)}, u32[]{:S(2)}, u32[]{:S(2)}) collective-permute-start(bf16[2,8,1536]{2,1,0:T(8,128)(2,1)S(1)} %broadcast_select_fusion.14), channel_id=1, source_target_pairs={{0,8},{1,9},{2,10},{3,11},{4,12},{5,13},{6,14},{7,15},{8,0},{9,1},... | collective-permute-start | bytes 147464 | tf_op jit(solution)/shard_map/ppermute | solution.py:705
  144.0 5.0 %collective-permute-start.31 = (bf16[2,2,8,1536]{3,2,1,0:T(8,128)(2,1)S(1)}, bf16[2,2,8,1536]{3,2,1,0:T(8,128)(2,1)S(1)}, u32[]{:S(2)}, u32[]{:S(2)}) collective-permute-start(bf16[2,2,8,1536]{3,2,1,0:T(8,128)(2,1)S(1)} %broadcast_select_fusion.13), channel_id=1, source_target_pairs={{0,2},{1,5},{2,0},{3,7},{4,6},{5,1},{6,4},{7,3},{8,10},{9,13},{10,... | collective-permute-start | bytes 294920 | tf_op jit(solution)/shard_map/ppermute | solution.py:705
  149.1 7.2 %copy-start.13 = (bf16[4,2,8,1536]{3,2,1,0:T(8,128)(2,1)}, bf16[4,2,8,1536]{3,2,1,0:T(8,128)(2,1)S(1)}, u32[]{:S(2)}) copy-start(bf16[4,2,8,1536]{3,2,1,0:T(8,128)(2,1)S(1)} %broadcast_select_fusion.10.near) | copy-start | bytes 589828
  149.1 5.7 %collective-permute-start.32 = (bf16[4,2,8,1536]{3,2,1,0:T(8,128)(2,1)S(1)}, bf16[4,2,8,1536]{3,2,1,0:T(8,128)(2,1)S(1)}, u32[]{:S(2)}, u32[]{:S(2)}) collective-permute-start(bf16[4,2,8,1536]{3,2,1,0:T(8,128)(2,1)S(1)} %broadcast_select_fusion.10.near), channel_id=1, source_target_pairs={{0,4},{1,3},{2,6},{3,1},{4,0},{5,7},{6,2},{7,5},{8,12},{9,11},{10,... | collective-permute-start | bytes 589832 | tf_op jit(solution)/shard_map/ppermute | solution.py:705
  150.4 4.4 %collective-permute-start.33 = (bf16[4,2,8,1536]{3,2,1,0:T(8,128)(2,1)S(1)}, bf16[4,2,8,1536]{3,2,1,0:T(8,128)(2,1)S(1)}, u32[]{:S(2)}, u32[]{:S(2)}) collective-permute-start(bf16[4,2,8,1536]{3,2,1,0:T(8,128)(2,1)S(1)} %broadcast_select_fusion.10.near), channel_id=1, source_target_pairs={{0,1},{1,0},{2,3},{3,2},{4,5},{5,4},{6,7},{7,6},{8,9},{9,8},{10,11... | collective-permute-start | bytes 589832 | tf_op jit(solution)/shard_map/ppermute | solution.py:705
  154.9 1.4 collective-permute-start.34
  174.3 15.9 %collective-permute-start.35 = (bf16[4,2,2,96,768]{4,3,2,1,0:T(8,128)(2,1)}, bf16[4,2,2,96,768]{4,3,2,1,0:T(8,128)(2,1)}, u32[]{:S(2)}, u32[]{:S(2)}) collective-permute-start(bf16[4,2,2,96,768]{4,3,2,1,0:T(8,128)(2,1)} %get-tuple-element.193), channel_id=1, source_target_pairs={{0,1},{1,0},{2,3},{3,2},{4,5},{5,4},{6,7},{7,6},{8,9},{9,8},{10,11... | collective-permute-start | bytes 7077896 | tf_op jit(solution)/shard_map/ppermute | solution.py:705
  174.4 16.2 %copy-start.4 = (bf16[4,2,2,96,768]{4,3,2,1,0:T(8,128)(2,1)S(1)}, bf16[4,2,2,96,768]{4,3,2,1,0:T(8,128)(2,1)}, u32[]{:S(2)}) copy-start(bf16[4,2,2,96,768]{4,3,2,1,0:T(8,128)(2,1)} %get-tuple-element.203) | copy-start | bytes 7077892
  190.2 19.4 %collective-permute-start.37 = (bf16[4,2,2,24,3072]{4,3,2,1,0:T(8,128)(2,1)}, bf16[4,2,2,24,3072]{4,3,2,1,0:T(8,128)(2,1)}, u32[]{:S(2)}, u32[]{:S(2)}) collective-permute-start(bf16[4,2,2,24,3072]{4,3,2,1,0:T(8,128)(2,1)} %get-tuple-element.205), channel_id=1, source_target_pairs={{0,1},{1,0},{2,3},{3,2},{4,5},{5,4},{6,7},{7,6},{8,9},{9,8},{10,11... | collective-permute-start | bytes 7077896 | tf_op jit(solution)/shard_map/ppermute | solution.py:705
  193.3 16.4 %collective-permute-start.36 = (bf16[2,2,2,96,768]{4,3,2,1,0:T(8,128)(2,1)}, bf16[2,2,2,96,768]{4,3,2,1,0:T(8,128)(2,1)S(1)}, u32[]{:S(2)}, u32[]{:S(2)}) collective-permute-start(bf16[2,2,2,96,768]{4,3,2,1,0:T(8,128)(2,1)} %fusion.2), channel_id=1, source_target_pairs={{0,2},{1,5},{2,0},{3,7},{4,6},{5,1},{6,4},{7,3},{8,10},{9,13},{10,... | collective-permute-start | bytes 3538952 | tf_op jit(solution)/shard_map/ppermute | solution.py:705
  208.7 4.8 %copy-start.3 = (bf16[4,2,2,24,3072]{4,3,2,1,0:T(8,128)(2,1)S(1)}, bf16[4,2,2,24,3072]{4,3,2,1,0:T(8,128)(2,1)}, u32[]{:S(2)}) copy-start(bf16[4,2,2,24,3072]{4,3,2,1,0:T(8,128)(2,1)} %get-tuple-element.213) | copy-start | bytes 7077892
  209.7 5.4 %copy-start.7 = (bf16[2,2,2,96,768]{4,3,2,1,0:T(8,128)(2,1)}, bf16[2,2,2,96,768]{4,3,2,1,0:T(8,128)(2,1)S(1)}, u32[]{:S(2)}) copy-start(bf16[2,2,2,96,768]{4,3,2,1,0:T(8,128)(2,1)S(1)} %collective-permute-done.36) | copy-start | bytes 3538948
  212.2 32.8 %collective-permute-start.38 = (bf16[2,2,96,768]{3,2,1,0:T(8,128)(2,1)}, bf16[2,2,96,768]{3,2,1,0:T(8,128)(2,1)S(1)}, u32[]{:S(2)}, u32[]{:S(2)}) collective-permute-start(bf16[2,2,96,768]{3,2,1,0:T(8,128)(2,1)} %fusion.5), channel_id=1, source_target_pairs={{0,4},{1,3},{2,6},{3,1},{4,0},{5,7},{6,2},{7,5},{8,12},{9,11},{10,... | collective-permute-start | bytes 1769480 | tf_op jit(solution)/shard_map/ppermute | solution.py:705
  215.1 29.9 %collective-permute-start.39 = (bf16[2,2,2,24,3072]{4,3,2,1,0:T(8,128)(2,1)S(1)}, bf16[2,2,2,24,3072]{4,3,2,1,0:T(8,128)(2,1)}, u32[]{:S(2)}, u32[]{:S(2)}) collective-permute-start(bf16[2,2,2,24,3072]{4,3,2,1,0:T(8,128)(2,1)S(1)} %fusion.3), channel_id=1, source_target_pairs={{0,8},{1,9},{2,10},{3,11},{4,12},{5,13},{6,14},{7,15},{8,0},{9,1},... | collective-permute-start | bytes 3538952 | tf_op jit(solution)/shard_map/ppermute | solution.py:705
  245.0 5.2 %collective-permute-start.40 = (bf16[4,2,2,104,768]{4,3,2,1,0:T(8,128)(2,1)}, bf16[4,2,2,104,768]{4,3,2,1,0:T(8,128)(2,1)}, u32[]{:S(2)}, u32[]{:S(2)}) collective-permute-start(bf16[4,2,2,104,768]{4,3,2,1,0:T(8,128)(2,1)} %get-tuple-element.221), channel_id=1, source_target_pairs={{0,1},{1,0},{2,3},{3,2},{4,5},{5,4},{6,7},{7,6},{8,9},{9,8},{10,11... | collective-permute-start | bytes 7667720 | tf_op jit(solution)/shard_map/ppermute | solution.py:705
  252.9 23.8 %collective-permute-start.43 = (bf16[2,2,2,104,768]{4,3,2,1,0:T(8,128)(2,1)}, bf16[2,2,2,104,768]{4,3,2,1,0:T(8,128)(2,1)}, u32[]{:S(2)}, u32[]{:S(2)}) collective-permute-start(bf16[2,2,2,104,768]{4,3,2,1,0:T(8,128)(2,1)} %fusion), channel_id=1, source_target_pairs={{0,2},{1,5},{2,0},{3,7},{4,6},{5,1},{6,4},{7,3},{8,10},{9,13},{10,... | collective-permute-start | bytes 3833864 | tf_op jit(solution)/shard_map/ppermute | solution.py:705
  254.2 22.5 %collective-permute-start.42 = (bf16[2,2,24,3072]{3,2,1,0:T(8,128)(2,1)}, bf16[2,2,24,3072]{3,2,1,0:T(8,128)(2,1)S(1)}, u32[]{:S(2)}, u32[]{:S(2)}) collective-permute-start(bf16[2,2,24,3072]{3,2,1,0:T(8,128)(2,1)} %fusion.4), channel_id=1, source_target_pairs={{0,2},{1,5},{2,0},{3,7},{4,6},{5,1},{6,4},{7,3},{8,10},{9,13},{10,... | collective-permute-start | bytes 1769480 | tf_op jit(solution)/shard_map/ppermute | solution.py:705
  254.9 10.7 %collective-permute-start.41 = (bf16[2,96,768]{2,1,0:T(8,128)(2,1)S(1)}, bf16[2,96,768]{2,1,0:T(8,128)(2,1)S(1)}, u32[]{:S(2)}, u32[]{:S(2)}) collective-permute-start(bf16[2,96,768]{2,1,0:T(8,128)(2,1)S(1)} %fusion.10), channel_id=1, source_target_pairs={{0,8},{1,9},{2,10},{3,11},{4,12},{5,13},{6,14},{7,15},{8,0},{9,1},... | collective-permute-start | bytes 884744 | tf_op jit(solution)/shard_map/ppermute | solution.py:705
  279.9 13.9 %collective-permute-start.45 = (bf16[2,2,104,768]{3,2,1,0:T(8,128)(2,1)}, bf16[2,2,104,768]{3,2,1,0:T(8,128)(2,1)S(1)}, u32[]{:S(2)}, u32[]{:S(2)}) collective-permute-start(bf16[2,2,104,768]{3,2,1,0:T(8,128)(2,1)} %fusion.1), channel_id=1, source_target_pairs={{0,4},{1,3},{2,6},{3,1},{4,0},{5,7},{6,2},{7,5},{8,12},{9,11},{10,... | collective-permute-start | bytes 1916936 | tf_op jit(solution)/shard_map/ppermute | solution.py:705
  282.7 11.0 %collective-permute-start.44 = (bf16[2,24,3072]{2,1,0:T(8,128)(2,1)}, bf16[2,24,3072]{2,1,0:T(8,128)(2,1)}, u32[]{:S(2)}, u32[]{:S(2)}) collective-permute-start(bf16[2,24,3072]{2,1,0:T(8,128)(2,1)} %fusion.9), channel_id=1, source_target_pairs={{0,4},{1,3},{2,6},{3,1},{4,0},{5,7},{6,2},{7,5},{8,12},{9,11},{10,... | collective-permute-start | bytes 884744 | tf_op jit(solution)/shard_map/ppermute | solution.py:705
  284.0 12.8 %copy-start.12 = (bf16[2,2,24,3072]{3,2,1,0:T(8,128)(2,1)S(1)}, bf16[2,2,24,3072]{3,2,1,0:T(8,128)(2,1)}, u32[]{:S(2)}) copy-start(bf16[2,2,24,3072]{3,2,1,0:T(8,128)(2,1)} %copy-done.11) | copy-start | bytes 1769476
  286.5 13.1 %collective-permute-start.46 = (bf16[96,768]{1,0:T(8,128)(2,1)S(1)}, bf16[96,768]{1,0:T(8,128)(2,1)S(1)}, u32[]{:S(2)}, u32[]{:S(2)}) collective-permute-start(bf16[96,768]{1,0:T(8,128)(2,1)S(1)} %fusion.15), channel_id=1, source_target_pairs={{0,16},{1,17},{2,18},{3,19},{4,20},{5,21},{6,22},{7,23},{8,24},{9,... | collective-permute-start | bytes 442376 | tf_op jit(solution)/shard_map/ppermute | solution.py:705
  295.0 11.1 %collective-permute-start.47 = (bf16[2,104,768]{2,1,0:T(8,128)(2,1)S(1)}, bf16[2,104,768]{2,1,0:T(8,128)(2,1)S(1)}, u32[]{:S(2)}, u32[]{:S(2)}) collective-permute-start(bf16[2,104,768]{2,1,0:T(8,128)(2,1)S(1)} %fusion.8), channel_id=1, source_target_pairs={{0,8},{1,9},{2,10},{3,11},{4,12},{5,13},{6,14},{7,15},{8,0},{9,1},... | collective-permute-start | bytes 958472 | tf_op jit(solution)/shard_map/ppermute | solution.py:705
  298.1 10.2 %collective-permute-start.49 = (bf16[24,3072]{1,0:T(8,128)(2,1)S(1)}, bf16[24,3072]{1,0:T(8,128)(2,1)S(1)}, u32[]{:S(2)}, u32[]{:S(2)}) collective-permute-start(bf16[24,3072]{1,0:T(8,128)(2,1)S(1)} %fusion.13), channel_id=1, source_target_pairs={{0,16},{1,17},{2,18},{3,19},{4,20},{5,21},{6,22},{7,23},{8,24},{9,... | collective-permute-start | bytes 442376 | tf_op jit(solution)/shard_map/ppermute | solution.py:705
  306.1 11.7 %copy-start.1 = (bf16[96]{0:T(256)(128)(2,1)S(1)}, bf16[96]{0:T(256)(128)(2,1)}, u32[]{:S(2)}) copy-start(bf16[96]{0:T(256)(128)(2,1)} %param.33) | copy-start | bytes 580
  307.3 7.7 %collective-permute-start.48 = (bf16[104,768]{1,0:T(8,128)(2,1)S(1)}, bf16[104,768]{1,0:T(8,128)(2,1)S(1)}, u32[]{:S(2)}, u32[]{:S(2)}) collective-permute-start(bf16[104,768]{1,0:T(8,128)(2,1)S(1)} %fusion.11), channel_id=1, source_target_pairs={{0,16},{1,17},{2,18},{3,19},{4,20},{5,21},{6,22},{7,23},{8,24},{9,... | collective-permute-start | bytes 479240 | tf_op jit(solution)/shard_map/ppermute | solution.py:705
  (11 other events, 19.2 us)

commit v6 on v5

--- a/solution.py
+++ b/solution.py
@@ -133,7 +133,7 @@
         out_shape=[S((t, D), low)] * outs + [S(shape, low)],
         scratch_shapes=[pltpu.VMEM(shape, low), pltpu.SemaphoreType.DMA((count, 4)), pltpu.SemaphoreType.DMA],
         name="project",
-        **params(2 * outs * t * D * D, 2 * (outs + 1) * t * D + 4 * count * D * D, room=60),
+        **params(2 * outs * t * D * D, 2 * (outs + 1) * t * D + 4 * count * D * D, room=16),
     )(x, vec, *parts)
     return *products, full.reshape(count, D, D)
 
@@ -394,13 +394,19 @@
 
 
 def inner_body(cube, n_ref, vec_ref, *refs):
-    parts, (a_ref, gp_ref, full_ref, w_ref, sems, out_sem) = refs[:-6], refs[-6:]
+    parts, (a_ref, gp_ref, full_ref, w_ref, sems, out_sem, bias_ref) = refs[:-7], refs[-7:]
     onward = assemble(cube, parts, w_ref, full_ref, sems, out_sem)
-    n = n_ref[...]
+
+    @pl.when(pl.program_id(0) == 0)
+    def _():
+        bias_ref[...] = vec_ref[...].astype(f32)
+
     w = w_ref.reshape(D, FF) if cube else w_ref
-    for j in range(FF // BLOCK):
-        cols = pl.ds(j * BLOCK, BLOCK)
-        h = nn(n, w[:, cols]) + vec_ref[B_INNER + j : B_INNER + j + 1].astype(f32)
+
+    @pl.loop(0, FF // BLOCK)
+    def _(j):
+        cols = pl.ds(pl.multiple_of(j * BLOCK, BLOCK), BLOCK)
+        h = nn(n_ref[...], w[:, cols]) + bias_ref[pl.ds(B_INNER + j, 1), :]
         act, slope = gelu_parts(h)
         a_ref[:, cols] = act.astype(low)
         gp_ref[:, cols] = slope.astype(low)
@@ -419,7 +425,7 @@
         in_specs=[row_block(D), whole(vec.shape)] + [ANY] * len(parts),
         out_specs=[row_block(FF), row_block(FF), ANY],
         out_shape=[S((t, FF), low), S((t, FF), low), S(shape, low)],
-        scratch_shapes=[pltpu.VMEM(shape, low), pltpu.SemaphoreType.DMA((4,)), pltpu.SemaphoreType.DMA],
+        scratch_shapes=[*scratch_for(shape), pltpu.VMEM((16, D), f32)],
         name="inner",
         **params(6 * t * D * FF, 2 * t * D + 4 * t * FF + 4 * D * FF, 2 * t * FF, room=60),
     )(n, vec, *parts)
@@ -667,7 +673,7 @@
                         pltpu.VMEM((4, 2, 2, 2, own, 2 * D), low), pltpu.SemaphoreType.DMA((4,))],
         grid=(1,),
         name="pair_loss",
-        **params(6 * pairs * pairs * D, 4 * pairs * D, 4 * pairs * pairs, room=60),
+        **params(6 * pairs * pairs * D, 4 * pairs * D, 4 * pairs * pairs, room=12),
     )(*parts, vec, cls)
     return loss[0, 0], dc
 

time: 322 us -> 317 us (0.984)
  Pallas kernels: 151 us -> 143 us
  waiting for transfers between devices: 79.8 us -> 83.1 us
    pallas_call x2, Pallas kernels: 12.3 us -> 5.29 us  [project(): pl.pallas_call(lambda *refs: project_body(cube, count, biases, *refs), gr...]
    unnamed x50, local copies, waits for them, and re-layouts: 4.1 us -> 7.96 us
    ppermute x50, waiting for transfers between devices: 79.8 us -> 83.1 us  [send(): return lax.ppermute(field, AXIS, route)]
  transfers between devices with their start and end apart: 50 -> 50, of which waited for: 27 -> 27; matrix products, arithmetic and copies ran while one was open for 8% -> 8% of each run, Pallas kernels for 37% -> 36%
where the time goes in v6:
time: 317 us; the launch traced here: 315 us
  Pallas kernels  143 us (45%)
  waiting for transfers between devices  83.1 us (26%)
  starting transfers between devices  43.9 us (14%)
  other arithmetic  32.9 us (10%)
  local copies, waits for them, and re-layouts  11.2 us (4%)
    ppermute x50, waiting for transfers between devices, send(): return lax.ppermute(field, AXIS, route)  83.1 us
    ppermute x50, starting transfers between devices, send(): return lax.ppermute(field, AXIS, route)  43.9 us
    pallas_call x1, Pallas kernels, heads_back(): pl.pallas_call(lambda *refs: heads_back_body(cube, *refs), grid=(GROUPS,)...  29.9 us
    pallas_call x1, Pallas kernels, inner(): pl.pallas_call(lambda *refs: inner_body(cube, *refs), grid=(t // ROWS,),...  23.4 us
    convert_element_type x12, other arithmetic, settle(): sum((pick(term, axis, 1 - bit).astype(f32) for term in self.terms))  22.6 us
    pallas_call x1, Pallas kernels, inner_back(): pl.pallas_call(lambda *refs: inner_back_body(cube, *refs), grid=(FF // BL...  15.8 us
    pallas_call x1, Pallas kernels, open_back(): pl.pallas_call(open_back_body, grid=(t // (2 * ROWS),), in_specs=[row_blo...  14 us
    pallas_call x1, Pallas kernels, outer_back(): pl.pallas_call(lambda *refs: outer_back_body(cube, *refs), grid=(FF // BL...  13.5 us
  transfers between devices with their start and end apart: 50, of which 27 were waited for; matrix products, arithmetic and copies ran while one was open for 8% of the time, Pallas kernels for 36%

profile of v6, /device:TPU:0, one launch (start us, length us, event | category | flops | bytes accessed | tf_op | source)
XLA Modules:
  0.0 315.5 jit_solution(15637316389286848596)
XLA Ops:
  0.7 1.5 pack.2
  2.1 4.0 %collective-permute-start = (bf16[48,768]{1,0:T(8,128)(2,1)}, bf16[48,768]{1,0:T(8,128)(2,1)S(1)}, u32[]{:S(2)}, u32[]{:S(2)}) collective-permute-start(bf16[48,768]{1,0:T(8,128)(2,1)} %pack.2), channel_id=1, source_target_pairs={{0,16},{1,17},{2,18},{3,19},{4,20},{5,21},{6,22},{7,23},{8,24},{9,... | collective-permute-start | bytes 221192 | tf_op jit(solution)/shard_map/ppermute | solution.py:711
  8.5 1.4 pack.3
  9.9 3.3 %collective-permute-done.1 = bf16[16,768]{1,0:T(8,128)(2,1)S(1)} collective-permute-done((bf16[16,768]{1,0:T(8,128)(2,1)S(1)}, bf16[16,768]{1,0:T(8,128)(2,1)S(1)}, u32[]{:S(2)}, u32[]{:S(2)}) %collective-permute-start.1) | collective-permute-done | bytes 24608 | tf_op jit(solution)/shard_map/ppermute | solution.py:711
  14.2 1.6 collective-permute-start.3
  16.6 1.7 collective-permute-done.3
  18.3 3.8 %collective-permute-done.4 = bf16[48,768]{1,0:T(8,128)(2,1)S(1)} collective-permute-done((bf16[48,768]{1,0:T(8,128)(2,1)}, bf16[48,768]{1,0:T(8,128)(2,1)S(1)}, u32[]{:S(2)}, u32[]{:S(2)}) %collective-permute-start.4) | collective-permute-done | bytes 73760 | tf_op jit(solution)/shard_map/ppermute | solution.py:711
  24.1 1.5 collective-permute-start.6
  28.0 3.1 collective-permute-done.8
  34.0 1.5 collective-permute-start.11
  36.0 1.8 collective-permute-done.11
  37.8 4.6 %collective-permute-done.12 = bf16[2,2,48,768]{3,2,1,0:T(8,128)(2,1)S(1)} collective-permute-done((bf16[2,2,48,768]{3,2,1,0:T(8,128)(2,1)S(1)}, bf16[2,2,48,768]{3,2,1,0:T(8,128)(2,1)S(1)}, u32[]{:S(2)}, u32[]{:S(2)}) %collective-permute-start.12) | collective-permute-done | bytes 294944 | tf_op jit(solution)/shard_map/ppermute | solution.py:711
  42.6 2.7 collective-permute-done.9.refs_3_
  45.9 1.5 collective-permute-done.15
  47.4 1.4 collective-permute-start.18
  49.4 1.8 collective-permute-start.19
  51.2 3.3 %project.2 = (bf16[1024,768]{1,0:T(8,128)(2,1)S(1)}, bf16[1024,768]{1,0:T(8,128)(2,1)S(1)}, bf16[2,4,2,2,2,24,768]{6,5,4,3,2,1,0:T(8,128)(2,1)S(1)}) custom-call(bf16[1024,768]{1,0:T(8,128)(2,1)S(1)} %bitcast.188, bf16[16,768]{1,0:T(8,128)(2,1)S(1)} %add.653.refs_1_.vec_ref.refs_2_.codes_ref.refs_5_, ...), custom_call_target="tpu_custom_call" | custom-call | flops 2415919104 | bytes 9437184 | tf_op jit(solution)/shard_map/project/pallas_call | solution.py:128
  54.4 1.4 copy-done.2
  55.8 3.9 %collective-permute-done.19 = bf16[96,768]{1,0:T(8,128)(2,1)S(1)} collective-permute-done((bf16[96,768]{1,0:T(8,128)(2,1)S(1)}, bf16[96,768]{1,0:T(8,128)(2,1)S(1)}, u32[]{:S(2)}, u32[]{:S(2)}) %collective-permute-start.19) | collective-permute-done | bytes 147488 | tf_op jit(solution)/shard_map/ppermute | solution.py:711
  59.8 3.3 %collective-permute-done.18 = bf16[2,2,24,3072]{3,2,1,0:T(8,128)(2,1)S(1)} collective-permute-done((bf16[2,2,24,3072]{3,2,1,0:T(8,128)(2,1)S(1)}, bf16[2,2,24,3072]{3,2,1,0:T(8,128)(2,1)S(1)}, u32[]{:S(2)}, u32[]{:S(2)}) %collective-permute-start.18) | collective-permute-done | bytes 589856 | tf_op jit(solution)/shard_map/ppermute | solution.py:711
  65.4 2.0 project.3
  67.5 1.4 copy-done.3
  70.0 1.8 collective-permute-start.22
  71.8 9.3 %attend.1 = (f32[3,1024,256]{2,1,0:T(8,128)}, bf16[1024,768]{1,0:T(8,128)(2,1)}) custom-call(s32[16]{0:T(128)} %len_ref.1, bf16[1024,768]{1,0:T(8,128)(2,1)} %copy-done.10, bf16[1024,768]{1,0:T(8,128)(2,1)} %copy-done.11, bf16[1024,768]{1,0:T(8,128)(2,1)} %copy-done.7), custom_call_target="tpu_custom_call" | custom-call | flops 6039797760 | bytes 15728640 | tf_op jit(solution)/shard_map/attend/pallas_call | solution.py:220
  82.7 5.6 %close.1 = (f32[1024,768]{1,0:T(8,128)}, f32[1024,1]{1,0:T(8,128)}, bf16[1024,768]{1,0:T(8,128)(2,1)}) custom-call(bf16[1024,768]{1,0:T(8,128)(2,1)} %bitcast.186, bf16[1024,768]{1,0:T(8,128)(2,1)} %get-tuple-element.161.c_ref.refs_7_, bf16[2,768,768]{2,1,0:T(8,128)(2,1)} %bitcast.183, bf16[16,768]{1,0:T(8,128)(2,1)} %copy-done.5), custom_call_target="tpu_custom_call" | custom-call | flops 1207959552 | bytes 9043968 | tf_op jit(solution)/shard_map/close/pallas_call | solution.py:251
  88.3 3.4 %collective-permute-done.25 = bf16[2,2,96,768]{3,2,1,0:T(8,128)(2,1)S(1)} collective-permute-done((bf16[2,2,96,768]{3,2,1,0:T(8,128)(2,1)S(1)}, bf16[2,2,96,768]{3,2,1,0:T(8,128)(2,1)S(1)}, u32[]{:S(2)}, u32[]{:S(2)}) %collective-permute-start.25) | collective-permute-done | bytes 589856 | tf_op jit(solution)/shard_map/ppermute | solution.py:711
  92.7 23.4 %inner.1 = (bf16[1024,3072]{1,0:T(8,128)(2,1)}, bf16[1024,3072]{1,0:T(8,128)(2,1)}, bf16[4,2,2,2,24,3072]{5,4,3,2,1,0:T(8,128)(2,1)}) custom-call(bf16[1024,768]{1,0:T(8,128)(2,1)} %get-tuple-element.167.refs_0_.refs_1_, bf16[16,768]{1,0:T(8,128)(2,1)} %copy-done.5, bf16[4,2,24,3072]{3,2,1,0:T(8,128)(2,1)} %copy-done.15, ...), custom_call_target="tpu_custom_call" | custom-call | flops 14495514624 | bytes 23592960 | tf_op jit(solution)/shard_map/inner/pallas_call | solution.py:422
  116.7 2.5 collective-permute-done.28.refs_6_
  120.2 12.9 %outer.1 = (bf16[1024,768]{1,0:T(8,128)(2,1)}, f32[1024,768]{1,0:T(8,128)}, f32[1024,1]{1,0:T(8,128)}, f32[8,1536]{1,0:T(8,128)}, bf16[8,1536]{1,0:T(8,128)(2,1)}, /*index=5*/bf16[4,2,2,2,96,768]{5,4,3,2,1,0:T(8,128)(2,1)}) custom-call(bf16[1024,3072]{1,0:T(8,128)(2,1)} %get-tuple-element.174.refs_0_.refs_4_, ...), custom_call_target="tpu_custom_call" | custom-call | flops 4831838208 | bytes 23592960 | tf_op jit(solution)/shard_map/outer/pallas_call | solution.py:470
  133.1 1.6 collective-permute-start.29
  134.7 3.5 %collective-permute-done.29 = bf16[8,1536]{1,0:T(8,128)(2,1)S(1)} collective-permute-done((bf16[8,1536]{1,0:T(8,128)(2,1)}, bf16[8,1536]{1,0:T(8,128)(2,1)S(1)}, u32[]{:S(2)}, u32[]{:S(2)}) %collective-permute-start.29) | collective-permute-done | bytes 24608 | tf_op jit(solution)/shard_map/ppermute | solution.py:711
  139.2 3.8 %collective-permute-done.30 = bf16[2,8,1536]{2,1,0:T(8,128)(2,1)S(1)} collective-permute-done((bf16[2,8,1536]{2,1,0:T(8,128)(2,1)S(1)}, bf16[2,8,1536]{2,1,0:T(8,128)(2,1)S(1)}, u32[]{:S(2)}, u32[]{:S(2)}) %collective-permute-start.30) | collective-permute-done | bytes 49184 | tf_op jit(solution)/shard_map/ppermute | solution.py:711
  143.1 1.2 collective-permute-start.31
  144.6 3.6 %collective-permute-done.31 = bf16[2,2,8,1536]{3,2,1,0:T(8,128)(2,1)S(1)} collective-permute-done((bf16[2,2,8,1536]{3,2,1,0:T(8,128)(2,1)S(1)}, bf16[2,2,8,1536]{3,2,1,0:T(8,128)(2,1)S(1)}, u32[]{:S(2)}, u32[]{:S(2)}) %collective-permute-start.31) | collective-permute-done | bytes 98336 | tf_op jit(solution)/shard_map/ppermute | solution.py:711
  148.3 1.3 collective-permute-start.32
  149.6 4.4 %collective-permute-done.32.far = bf16[4,2,8,1536]{3,2,1,0:T(8,128)(2,1)S(1)} collective-permute-done((bf16[4,2,8,1536]{3,2,1,0:T(8,128)(2,1)S(1)}, bf16[4,2,8,1536]{3,2,1,0:T(8,128)(2,1)S(1)}, u32[]{:S(2)}, u32[]{:S(2)}) %collective-permute-start.32) | collective-permute-done | bytes 196640 | tf_op jit(solution)/shard_map/ppermute | solution.py:711
  154.0 1.4 collective-permute-done.34.far_other
  156.3 1.3 pair_loss.1
  158.2 13.5 %outer_back.1 = (f32[1024,768]{1,0:T(8,128)}, bf16[1024,768]{1,0:T(8,128)(2,1)}, f32[16,768]{1,0:T(8,128)}, bf16[4,2,2,96,768]{4,3,2,1,0:T(8,128)(2,1)}, bf16[4,2,2,96,768]{4,3,2,1,0:T(8,128)(2,1)}) custom-call(bf16[1024,768]{1,0:T(8,128)(2,1)} %bitcast.223, f32[8,1536]{1,0:T(8,128)} %copy-done.9, f32[1024,768]{1,0:T(8,128)} %get-tuple-element.183.refs_2_, ...), custom_call_target="tpu_custom_call" | custom-call | flops 9663676416 | bytes 36175872 | tf_op jit(solution)/shard_map/outer_back/pallas_call | solution.py:556
  171.8 15.8 %inner_back.1 = (bf16[1024,3072]{1,0:T(8,128)(2,1)}, f32[16,768]{1,0:T(8,128)}, bf16[4,2,2,24,3072]{4,3,2,1,0:T(8,128)(2,1)}, bf16[4,2,2,24,3072]{4,3,2,1,0:T(8,128)(2,1)}) custom-call(bf16[1024,768]{1,0:T(8,128)(2,1)} %get-tuple-element.187.refs_0_, bf16[1024,768]{1,0:T(8,128)(2,1)} %get-tuple-element.167.refs_0_.refs_1_, ...), custom_call_target="tpu_custom_call" | custom-call | flops 9663676416 | bytes 34603008 | tf_op jit(solution)/shard_map/inner_back/pallas_call | solution.py:596
  188.0 2.6 fusion.2
  191.8 14.0 %open_back.1 = (f32[1024,768]{1,0:T(8,128)}, bf16[1024,768]{1,0:T(8,128)(2,1)}, bf16[1024,768]{1,0:T(8,128)(2,1)}, f32[16,768]{1,0:T(8,128)}) custom-call(f32[1024,768]{1,0:T(8,128)} %get-tuple-element.196.dres_ref, bf16[1024,3072]{1,0:T(8,128)(2,1)} %get-tuple-element.197.dh_ref, bf16[768,3072]{1,0:T(8,128)(2,1)} %bitcast.224, ...), custom_call_target="tpu_custom_call" | custom-call | flops 6039797760 | bytes 21626880 | tf_op jit(solution)/shard_map/open_back/pallas_call | solution.py:282
  207.1 2.5 fusion.5
  209.6 1.2 collective-permute-start.38
  210.8 1.6 fusion.3
  212.7 29.9 %heads_back.1 = (bf16[1024,768]{1,0:T(8,128)(2,1)}, bf16[1024,768]{1,0:T(8,128)(2,1)}, bf16[1024,768]{1,0:T(8,128)(2,1)}, bf16[4,2,2,104,768]{4,3,2,1,0:T(8,128)(2,1)}, bf16[4,2,2,104,768]{4,3,2,1,0:T(8,128)(2,1)}) custom-call(bf16[1024,768]{1,0:T(8,128)(2,1)} %copy-done.10, bf16[1024,768]{1,0:T(8,128)(2,1)} %copy-done.11, bf16[1024,768]{1,0:T(8,128)(2,1)} %copy-done.7, ...), custom_call_target="tpu_custom_call" | custom-call | flops 18874368000 | bytes 15728640 | tf_op jit(solution)/shard_map/heads_back/pallas_call | solution.py:372
  243.5 1.5 fusion.10
  245.0 2.5 fusion.4
  247.9 2.7 fusion
  250.5 1.3 collective-permute-start.43
  252.6 1.8 collective-permute-start.41
  254.3 8.9 %token_grad.1 = f32[1024,768]{1,0:T(8,128)} custom-call(f32[1024,768]{1,0:T(8,128)} %get-tuple-element.201.dr_ref, bf16[1024,768]{1,0:T(8,128)(2,1)} %get-tuple-element.215.dq_ref, bf16[1024,768]{1,0:T(8,128)(2,1)} %get-tuple-element.216.dk_ref, bf16[1024,768]{1,0:T(8,128)(2,1)} %get-tuple-element.217.dv_ref, bf16[2,768,768]{2,1,0:T(8,128)(2,1)} %bitcast.181, ...), custom_call_target="tpu_custom_call" | custom-call | flops 3623878656 | bytes 14548992 | tf_op jit(solution)/shard_map/token_grad/pallas_call | solution.py:619
  263.2 11.1 %collective-permute-done.42 = bf16[2,2,24,3072]{3,2,1,0:T(8,128)(2,1)S(1)} collective-permute-done((bf16[2,2,24,3072]{3,2,1,0:T(8,128)(2,1)}, bf16[2,2,24,3072]{3,2,1,0:T(8,128)(2,1)S(1)}, u32[]{:S(2)}, u32[]{:S(2)}) %collective-permute-start.42) | collective-permute-done | bytes 589856 | tf_op jit(solution)/shard_map/ppermute | solution.py:711
  275.1 2.4 fusion.1
  278.3 2.1 fusion.9
  280.4 1.2 collective-permute-start.44
  283.3 2.6 collective-permute-start.46
  286.0 5.4 %collective-permute-done.44 = bf16[2,24,3072]{2,1,0:T(8,128)(2,1)} collective-permute-done((bf16[2,24,3072]{2,1,0:T(8,128)(2,1)}, bf16[2,24,3072]{2,1,0:T(8,128)(2,1)}, u32[]{:S(2)}, u32[]{:S(2)}) %collective-permute-start.44) | collective-permute-done | bytes 294944 | tf_op jit(solution)/shard_map/ppermute | solution.py:711
  292.6 1.9 collective-permute-start.47
  295.7 1.4 collective-permute-start.49
  297.1 2.0 fusion.16
  299.1 4.6 %collective-permute-done.47 = bf16[2,104,768]{2,1,0:T(8,128)(2,1)S(1)} collective-permute-done((bf16[2,104,768]{2,1,0:T(8,128)(2,1)S(1)}, bf16[2,104,768]{2,1,0:T(8,128)(2,1)S(1)}, u32[]{:S(2)}, u32[]{:S(2)}) %collective-permute-start.47) | collective-permute-done | bytes 319520 | tf_op jit(solution)/shard_map/ppermute | solution.py:711
  305.9 2.0 fusion.14
  307.9 4.7 %collective-permute-done.48 = bf16[104,768]{1,0:T(8,128)(2,1)S(1)} collective-permute-done((bf16[104,768]{1,0:T(8,128)(2,1)S(1)}, bf16[104,768]{1,0:T(8,128)(2,1)S(1)}, u32[]{:S(2)}, u32[]{:S(2)}) %collective-permute-start.48) | collective-permute-done | bytes 159776 | tf_op jit(solution)/shard_map/ppermute | solution.py:711
  (164 shorter events, 39.6 us)
Async XLA Ops:
  0.7 6.4 %copy-start = (bf16[96]{0:T(256)(128)(2,1)S(1)}, bf16[96]{0:T(256)(128)(2,1)}, u32[]{:S(2)}) copy-start(bf16[96]{0:T(256)(128)(2,1)} %param.33) | copy-start | bytes 580
  0.7 22.5 %copy-start.21 = (bf16[24,3072]{1,0:T(8,128)(2,1)S(1)}, bf16[24,3072]{1,0:T(8,128)(2,1)}, u32[]{:S(2)}) copy-start(bf16[24,3072]{1,0:T(8,128)(2,1)} %param.32) | copy-start | bytes 442372
  2.1 11.1 %collective-permute-start = (bf16[48,768]{1,0:T(8,128)(2,1)}, bf16[48,768]{1,0:T(8,128)(2,1)S(1)}, u32[]{:S(2)}, u32[]{:S(2)}) collective-permute-start(bf16[48,768]{1,0:T(8,128)(2,1)} %pack.2), channel_id=1, source_target_pairs={{0,16},{1,17},{2,18},{3,19},{4,20},{5,21},{6,22},{7,23},{8,24},{9,... | collective-permute-start | bytes 221192 | tf_op jit(solution)/shard_map/ppermute | solution.py:711
  8.4 4.7 %collective-permute-start.1 = (bf16[16,768]{1,0:T(8,128)(2,1)S(1)}, bf16[16,768]{1,0:T(8,128)(2,1)S(1)}, u32[]{:S(2)}, u32[]{:S(2)}) collective-permute-start(bf16[16,768]{1,0:T(8,128)(2,1)S(1)} %maximum_maximum_fusion), channel_id=1, source_target_pairs={{0,16},{1,17},{2,18},{3,19},{4,20},{5,21},{6,22},{7,23},{8,24},{9,... | collective-permute-start | bytes 73736 | tf_op jit(solution)/shard_map/ppermute | solution.py:711
  14.2 4.0 %collective-permute-start.3 = (bf16[16,768]{1,0:T(8,128)(2,1)S(1)}, bf16[16,768]{1,0:T(8,128)(2,1)S(1)}, u32[]{:S(2)}, u32[]{:S(2)}) collective-permute-start(bf16[16,768]{1,0:T(8,128)(2,1)S(1)} %fusion.62), channel_id=1, source_target_pairs={{0,8},{1,9},{2,10},{3,11},{4,12},{5,13},{6,14},{7,15},{8,0},{9,1},... | collective-permute-start | bytes 73736 | tf_op jit(solution)/shard_map/ppermute | solution.py:711
  15.9 6.2 %collective-permute-start.4 = (bf16[48,768]{1,0:T(8,128)(2,1)}, bf16[48,768]{1,0:T(8,128)(2,1)S(1)}, u32[]{:S(2)}, u32[]{:S(2)}) collective-permute-start(bf16[48,768]{1,0:T(8,128)(2,1)} %pack.3), channel_id=1, source_target_pairs={{0,16},{1,17},{2,18},{3,19},{4,20},{5,21},{6,22},{7,23},{8,24},{9,... | collective-permute-start | bytes 221192 | tf_op jit(solution)/shard_map/ppermute | solution.py:711
  16.5 6.6 %collective-permute-start.2 = (bf16[2,48,768]{2,1,0:T(8,128)(2,1)S(1)}, bf16[2,48,768]{2,1,0:T(8,128)(2,1)S(1)}, u32[]{:S(2)}, u32[]{:S(2)}) collective-permute-start(bf16[2,48,768]{2,1,0:T(8,128)(2,1)S(1)} %broadcast_select_fusion.12), channel_id=1, source_target_pairs={{0,8},{1,9},{2,10},{3,11},{4,12},{5,13},{6,14},{7,15},{8,0},{9,1},... | collective-permute-start | bytes 442376 | tf_op jit(solution)/shard_map/ppermute | solution.py:711
  23.2 7.8 %collective-permute-start.8 = (bf16[24,3072]{1,0:T(8,128)(2,1)S(1)}, bf16[24,3072]{1,0:T(8,128)(2,1)S(1)}, u32[]{:S(2)}, u32[]{:S(2)}) collective-permute-start(bf16[24,3072]{1,0:T(8,128)(2,1)S(1)} %copy-done.21), channel_id=1, source_target_pairs={{0,16},{1,17},{2,18},{3,19},{4,20},{5,21},{6,22},{7,23},{8,24},{9,... | collective-permute-start | bytes 442376 | tf_op jit(solution)/shard_map/ppermute | solution.py:711
  24.1 3.8 %collective-permute-start.6 = (bf16[16,768]{1,0:T(8,128)(2,1)S(1)}, bf16[16,768]{1,0:T(8,128)(2,1)S(1)}, u32[]{:S(2)}, u32[]{:S(2)}) collective-permute-start(bf16[16,768]{1,0:T(8,128)(2,1)S(1)} %add.650), channel_id=1, source_target_pairs={{0,2},{1,5},{2,0},{3,7},{4,6},{5,1},{6,4},{7,3},{8,10},{9,13},{10,... | collective-permute-start | bytes 73736 | tf_op jit(solution)/shard_map/ppermute | solution.py:711
  25.6 6.7 %collective-permute-start.5 = (bf16[2,2,48,768]{3,2,1,0:T(8,128)(2,1)S(1)}, bf16[2,2,48,768]{3,2,1,0:T(8,128)(2,1)S(1)}, u32[]{:S(2)}, u32[]{:S(2)}) collective-permute-start(bf16[2,2,48,768]{3,2,1,0:T(8,128)(2,1)S(1)} %broadcast_select_fusion.9), channel_id=1, source_target_pairs={{0,2},{1,5},{2,0},{3,7},{4,6},{5,1},{6,4},{7,3},{8,10},{9,13},{10,... | collective-permute-start | bytes 884744 | tf_op jit(solution)/shard_map/ppermute | solution.py:711
  26.1 5.7 %collective-permute-start.7 = (bf16[2,48,768]{2,1,0:T(8,128)(2,1)S(1)}, bf16[2,48,768]{2,1,0:T(8,128)(2,1)S(1)}, u32[]{:S(2)}, u32[]{:S(2)}) collective-permute-start(bf16[2,48,768]{2,1,0:T(8,128)(2,1)S(1)} %broadcast_select_fusion.11), channel_id=1, source_target_pairs={{0,8},{1,9},{2,10},{3,11},{4,12},{5,13},{6,14},{7,15},{8,0},{9,1},... | collective-permute-start | bytes 442376 | tf_op jit(solution)/shard_map/ppermute | solution.py:711
  32.3 17.0 %copy-start.22 = (bf16[96,768]{1,0:T(8,128)(2,1)S(1)}, bf16[96,768]{1,0:T(8,128)(2,1)}, u32[]{:S(2)}) copy-start(bf16[96,768]{1,0:T(8,128)(2,1)} %param.34) | copy-start | bytes 442372
  32.3 18.8 %copy-start.4 = (bf16[16,64,768]{2,1,0:T(8,128)(2,1)S(1)}, bf16[16,64,768]{2,1,0:T(8,128)(2,1)}, u32[]{:S(2)}) copy-start(bf16[16,64,768]{2,1,0:T(8,128)(2,1)} %param.19) | copy-start | bytes 4718596
  32.5 9.9 %collective-permute-start.12 = (bf16[2,2,48,768]{3,2,1,0:T(8,128)(2,1)S(1)}, bf16[2,2,48,768]{3,2,1,0:T(8,128)(2,1)S(1)}, u32[]{:S(2)}, u32[]{:S(2)}) collective-permute-start(bf16[2,2,48,768]{3,2,1,0:T(8,128)(2,1)S(1)} %broadcast_select_fusion.8), channel_id=1, source_target_pairs={{0,2},{1,5},{2,0},{3,7},{4,6},{5,1},{6,4},{7,3},{8,10},{9,13},{10,... | collective-permute-start | bytes 884744 | tf_op jit(solution)/shard_map/ppermute | solution.py:711
  33.7 8.8 %collective-permute-start.13 = (bf16[2,24,3072]{2,1,0:T(8,128)(2,1)S(1)}, bf16[2,24,3072]{2,1,0:T(8,128)(2,1)S(1)}, u32[]{:S(2)}, u32[]{:S(2)}) collective-permute-start(bf16[2,24,3072]{2,1,0:T(8,128)(2,1)S(1)} %broadcast_select_fusion.7), channel_id=1, source_target_pairs={{0,8},{1,9},{2,10},{3,11},{4,12},{5,13},{6,14},{7,15},{8,0},{9,1},... | collective-permute-start | bytes 884744 | tf_op jit(solution)/shard_map/ppermute | solution.py:711
  34.0 3.8 %collective-permute-start.11 = (bf16[16,768]{1,0:T(8,128)(2,1)S(1)}, bf16[16,768]{1,0:T(8,128)(2,1)S(1)}, u32[]{:S(2)}, u32[]{:S(2)}) collective-permute-start(bf16[16,768]{1,0:T(8,128)(2,1)S(1)} %add.651), channel_id=1, source_target_pairs={{0,4},{1,3},{2,6},{3,1},{4,0},{5,7},{6,2},{7,5},{8,12},{9,11},{10,... | collective-permute-start | bytes 73736 | tf_op jit(solution)/shard_map/ppermute | solution.py:711
  35.5 9.9 %collective-permute-start.9 = (bf16[4,2,48,768]{3,2,1,0:T(8,128)(2,1)S(1)}, bf16[4,2,48,768]{3,2,1,0:T(8,128)(2,1)S(1)}, u32[]{:S(2)}, u32[]{:S(2)}) collective-permute-start(bf16[4,2,48,768]{3,2,1,0:T(8,128)(2,1)S(1)} %broadcast_select_fusion.5.refs_2_), channel_id=1, source_target_pairs={{0,4},{1,3},{2,6},{3,1},{4,0},{5,7},{6,2},{7,5},{8,12},{9,11},{10,... | collective-permute-start | bytes 1769480 | tf_op jit(solution)/shard_map/ppermute | solution.py:711
  36.0 9.4 %collective-permute-start.10 = (bf16[4,2,48,768]{3,2,1,0:T(8,128)(2,1)S(1)}, bf16[4,2,48,768]{3,2,1,0:T(8,128)(2,1)S(1)}, u32[]{:S(2)}, u32[]{:S(2)}) collective-permute-start(bf16[4,2,48,768]{3,2,1,0:T(8,128)(2,1)S(1)} %broadcast_select_fusion.5.refs_2_), channel_id=1, source_target_pairs={{0,1},{1,0},{2,3},{3,2},{4,5},{5,4},{6,7},{7,6},{8,9},{9,8},{10,11... | collective-permute-start | bytes 1769480 | tf_op jit(solution)/shard_map/ppermute | solution.py:711
  45.4 2.1 collective-permute-start.14
  45.4 2.0 collective-permute-start.15
  47.4 18.0 %copy-start.5 = (bf16[16,768]{1,0:T(8,128)(2,1)}, bf16[16,768]{1,0:T(8,128)(2,1)S(1)}, u32[]{:S(2)}) copy-start(bf16[16,768]{1,0:T(8,128)(2,1)S(1)} %add.653.refs_1_.vec_ref.refs_2_.codes_ref.refs_5_) | copy-start | bytes 73732
  47.4 15.7 %collective-permute-start.18 = (bf16[2,2,24,3072]{3,2,1,0:T(8,128)(2,1)S(1)}, bf16[2,2,24,3072]{3,2,1,0:T(8,128)(2,1)S(1)}, u32[]{:S(2)}, u32[]{:S(2)}) collective-permute-start(bf16[2,2,24,3072]{3,2,1,0:T(8,128)(2,1)S(1)} %broadcast_select_fusion.3), channel_id=1, source_target_pairs={{0,2},{1,5},{2,0},{3,7},{4,6},{5,1},{6,4},{7,3},{8,10},{9,13},{10,... | collective-permute-start | bytes 1769480 | tf_op jit(solution)/shard_map/ppermute | solution.py:711
  48.9 14.4 %collective-permute-start.16 = (bf16[4,2,48,768]{3,2,1,0:T(8,128)(2,1)S(1)}, bf16[4,2,48,768]{3,2,1,0:T(8,128)(2,1)S(1)}, u32[]{:S(2)}, u32[]{:S(2)}) collective-permute-start(bf16[4,2,48,768]{3,2,1,0:T(8,128)(2,1)S(1)} %broadcast_select_fusion.4.refs_2_), channel_id=1, source_target_pairs={{0,4},{1,3},{2,6},{3,1},{4,0},{5,7},{6,2},{7,5},{8,12},{9,11},{10,... | collective-permute-start | bytes 1769480 | tf_op jit(solution)/shard_map/ppermute | solution.py:711
  49.4 13.9 %collective-permute-start.17 = (bf16[4,2,48,768]{3,2,1,0:T(8,128)(2,1)S(1)}, bf16[4,2,48,768]{3,2,1,0:T(8,128)(2,1)S(1)}, u32[]{:S(2)}, u32[]{:S(2)}) collective-permute-start(bf16[4,2,48,768]{3,2,1,0:T(8,128)(2,1)S(1)} %broadcast_select_fusion.4.refs_2_), channel_id=1, source_target_pairs={{0,1},{1,0},{2,3},{3,2},{4,5},{5,4},{6,7},{7,6},{8,9},{9,8},{10,11... | collective-permute-start | bytes 1769480 | tf_op jit(solution)/shard_map/ppermute | solution.py:711
  49.4 10.3 %collective-permute-start.19 = (bf16[96,768]{1,0:T(8,128)(2,1)S(1)}, bf16[96,768]{1,0:T(8,128)(2,1)S(1)}, u32[]{:S(2)}, u32[]{:S(2)}) collective-permute-start(bf16[96,768]{1,0:T(8,128)(2,1)S(1)} %copy-done.22), channel_id=1, source_target_pairs={{0,16},{1,17},{2,18},{3,19},{4,20},{5,21},{6,22},{7,23},{8,24},{9,... | collective-permute-start | bytes 442376 | tf_op jit(solution)/shard_map/ppermute | solution.py:711
  55.8 11.6 %copy-start.10 = (bf16[1024,768]{1,0:T(8,128)(2,1)}, bf16[1024,768]{1,0:T(8,128)(2,1)S(1)}, u32[]{:S(2)}) copy-start(bf16[1024,768]{1,0:T(8,128)(2,1)S(1)} %get-tuple-element.151.q_ref.refs_0_) | copy-start | bytes 4718596
  55.8 11.6 %copy-start.11 = (bf16[1024,768]{1,0:T(8,128)(2,1)}, bf16[1024,768]{1,0:T(8,128)(2,1)S(1)}, u32[]{:S(2)}) copy-start(bf16[1024,768]{1,0:T(8,128)(2,1)S(1)} %get-tuple-element.152.k_ref.refs_1_) | copy-start | bytes 4718596
  63.3 17.9 %copy-start.15 = (bf16[4,2,24,3072]{3,2,1,0:T(8,128)(2,1)}, bf16[4,2,24,3072]{3,2,1,0:T(8,128)(2,1)S(1)}, u32[]{:S(2)}) copy-start(bf16[4,2,24,3072]{3,2,1,0:T(8,128)(2,1)S(1)} %broadcast_select_fusion.1.refs_2_) | copy-start | bytes 3538948
  63.3 2.1 collective-permute-start.20
  63.4 17.8 %collective-permute-start.21 = (bf16[4,2,24,3072]{3,2,1,0:T(8,128)(2,1)S(1)}, bf16[4,2,24,3072]{3,2,1,0:T(8,128)(2,1)}, u32[]{:S(2)}, u32[]{:S(2)}) collective-permute-start(bf16[4,2,24,3072]{3,2,1,0:T(8,128)(2,1)S(1)} %broadcast_select_fusion.1.refs_2_), channel_id=1, source_target_pairs={{0,4},{1,3},{2,6},{3,1},{4,0},{5,7},{6,2},{7,5},{8,12},{9,11},{10,... | collective-permute-start | bytes 3538952 | tf_op jit(solution)/shard_map/ppermute | solution.py:711
  70.0 11.0 %collective-permute-start.22 = (bf16[2,96,768]{2,1,0:T(8,128)(2,1)S(1)}, bf16[2,96,768]{2,1,0:T(8,128)(2,1)S(1)}, u32[]{:S(2)}, u32[]{:S(2)}) collective-permute-start(bf16[2,96,768]{2,1,0:T(8,128)(2,1)S(1)} %broadcast_select_fusion.6), channel_id=1, source_target_pairs={{0,8},{1,9},{2,10},{3,11},{4,12},{5,13},{6,14},{7,15},{8,0},{9,1},... | collective-permute-start | bytes 884744 | tf_op jit(solution)/shard_map/ppermute | solution.py:711
  81.2 10.6 %collective-permute-start.23 = (bf16[4,2,24,3072]{3,2,1,0:T(8,128)(2,1)S(1)}, bf16[4,2,24,3072]{3,2,1,0:T(8,128)(2,1)}, u32[]{:S(2)}, u32[]{:S(2)}) collective-permute-start(bf16[4,2,24,3072]{3,2,1,0:T(8,128)(2,1)S(1)} %broadcast_select_fusion.1.refs_2_), channel_id=1, source_target_pairs={{0,1},{1,0},{2,3},{3,2},{4,5},{5,4},{6,7},{7,6},{8,9},{9,8},{10,11... | collective-permute-start | bytes 3538952 | tf_op jit(solution)/shard_map/ppermute | solution.py:711
  81.3 10.6 %collective-permute-start.24 = (bf16[4,2,24,3072]{3,2,1,0:T(8,128)(2,1)}, bf16[4,2,24,3072]{3,2,1,0:T(8,128)(2,1)}, u32[]{:S(2)}, u32[]{:S(2)}) collective-permute-start(bf16[4,2,24,3072]{3,2,1,0:T(8,128)(2,1)} %collective-permute-done.21.refs_3_), channel_id=1, source_target_pairs={{0,1},{1,0},{2,3},{3,2},{4,5},{5,4},{6,7},{7,6},{8,9},{9,8},{10,11... | collective-permute-start | bytes 3538952 | tf_op jit(solution)/shard_map/ppermute | solution.py:711
  81.8 9.9 %collective-permute-start.25 = (bf16[2,2,96,768]{3,2,1,0:T(8,128)(2,1)S(1)}, bf16[2,2,96,768]{3,2,1,0:T(8,128)(2,1)S(1)}, u32[]{:S(2)}, u32[]{:S(2)}) collective-permute-start(bf16[2,2,96,768]{3,2,1,0:T(8,128)(2,1)S(1)} %broadcast_select_fusion.2), channel_id=1, source_target_pairs={{0,2},{1,5},{2,0},{3,7},{4,6},{5,1},{6,4},{7,3},{8,10},{9,13},{10,... | collective-permute-start | bytes 1769480 | tf_op jit(solution)/shard_map/ppermute | solution.py:711
  91.8 24.3 %copy-start.16 = (bf16[4,2,96,768]{3,2,1,0:T(8,128)(2,1)}, bf16[4,2,96,768]{3,2,1,0:T(8,128)(2,1)S(1)}, u32[]{:S(2)}) copy-start(bf16[4,2,96,768]{3,2,1,0:T(8,128)(2,1)S(1)} %broadcast_select_fusion.refs_3_) | copy-start | bytes 3538948
  91.9 24.3 %collective-permute-start.26 = (bf16[4,2,96,768]{3,2,1,0:T(8,128)(2,1)S(1)}, bf16[4,2,96,768]{3,2,1,0:T(8,128)(2,1)S(1)}, u32[]{:S(2)}, u32[]{:S(2)}) collective-permute-start(bf16[4,2,96,768]{3,2,1,0:T(8,128)(2,1)S(1)} %broadcast_select_fusion.refs_3_), channel_id=1, source_target_pairs={{0,4},{1,3},{2,6},{3,1},{4,0},{5,7},{6,2},{7,5},{8,12},{9,11},{10,... | collective-permute-start | bytes 3538952 | tf_op jit(solution)/shard_map/ppermute | solution.py:711
  92.7 23.4 %collective-permute-start.27 = (bf16[4,2,96,768]{3,2,1,0:T(8,128)(2,1)S(1)}, bf16[4,2,96,768]{3,2,1,0:T(8,128)(2,1)}, u32[]{:S(2)}, u32[]{:S(2)}) collective-permute-start(bf16[4,2,96,768]{3,2,1,0:T(8,128)(2,1)S(1)} %broadcast_select_fusion.refs_3_), channel_id=1, source_target_pairs={{0,1},{1,0},{2,3},{3,2},{4,5},{5,4},{6,7},{7,6},{8,9},{9,8},{10,11... | collective-permute-start | bytes 3538952 | tf_op jit(solution)/shard_map/ppermute | solution.py:711
  116.2 3.0 collective-permute-start.28
  120.2 35.3 %copy-start.6 = (bf16[16,768]{1,0:T(8,128)(2,1)S(1)}, bf16[16,768]{1,0:T(8,128)(2,1)}, u32[]{:S(2)}) copy-start(bf16[16,768]{1,0:T(8,128)(2,1)} %copy-done.5) | copy-start | bytes 73732
  133.1 5.0 %collective-permute-start.29 = (bf16[8,1536]{1,0:T(8,128)(2,1)}, bf16[8,1536]{1,0:T(8,128)(2,1)S(1)}, u32[]{:S(2)}, u32[]{:S(2)}) collective-permute-start(bf16[8,1536]{1,0:T(8,128)(2,1)} %get-tuple-element.178), channel_id=1, source_target_pairs={{0,16},{1,17},{2,18},{3,19},{4,20},{5,21},{6,22},{7,23},{8,24},{9,... | collective-permute-start | bytes 73736 | tf_op jit(solution)/shard_map/ppermute | solution.py:711
  139.0 4.1 %collective-permute-start.30 = (bf16[2,8,1536]{2,1,0:T(8,128)(2,1)S(1)}, bf16[2,8,1536]{2,1,0:T(8,128)(2,1)S(1)}, u32[]{:S(2)}, u32[]{:S(2)}) collective-permute-start(bf16[2,8,1536]{2,1,0:T(8,128)(2,1)S(1)} %broadcast_select_fusion.14), channel_id=1, source_target_pairs={{0,8},{1,9},{2,10},{3,11},{4,12},{5,13},{6,14},{7,15},{8,0},{9,1},... | collective-permute-start | bytes 147464 | tf_op jit(solution)/shard_map/ppermute | solution.py:711
  143.1 5.1 %collective-permute-start.31 = (bf16[2,2,8,1536]{3,2,1,0:T(8,128)(2,1)S(1)}, bf16[2,2,8,1536]{3,2,1,0:T(8,128)(2,1)S(1)}, u32[]{:S(2)}, u32[]{:S(2)}) collective-permute-start(bf16[2,2,8,1536]{3,2,1,0:T(8,128)(2,1)S(1)} %broadcast_select_fusion.13), channel_id=1, source_target_pairs={{0,2},{1,5},{2,0},{3,7},{4,6},{5,1},{6,4},{7,3},{8,10},{9,13},{10,... | collective-permute-start | bytes 294920 | tf_op jit(solution)/shard_map/ppermute | solution.py:711
  148.3 5.7 %collective-permute-start.32 = (bf16[4,2,8,1536]{3,2,1,0:T(8,128)(2,1)S(1)}, bf16[4,2,8,1536]{3,2,1,0:T(8,128)(2,1)S(1)}, u32[]{:S(2)}, u32[]{:S(2)}) collective-permute-start(bf16[4,2,8,1536]{3,2,1,0:T(8,128)(2,1)S(1)} %broadcast_select_fusion.10.near), channel_id=1, source_target_pairs={{0,4},{1,3},{2,6},{3,1},{4,0},{5,7},{6,2},{7,5},{8,12},{9,11},{10,... | collective-permute-start | bytes 589832 | tf_op jit(solution)/shard_map/ppermute | solution.py:711
  149.6 4.4 %collective-permute-start.33 = (bf16[4,2,8,1536]{3,2,1,0:T(8,128)(2,1)S(1)}, bf16[4,2,8,1536]{3,2,1,0:T(8,128)(2,1)S(1)}, u32[]{:S(2)}, u32[]{:S(2)}) collective-permute-start(bf16[4,2,8,1536]{3,2,1,0:T(8,128)(2,1)S(1)} %broadcast_select_fusion.10.near), channel_id=1, source_target_pairs={{0,1},{1,0},{2,3},{3,2},{4,5},{5,4},{6,7},{7,6},{8,9},{9,8},{10,11... | collective-permute-start | bytes 589832 | tf_op jit(solution)/shard_map/ppermute | solution.py:711
  154.0 1.4 collective-permute-start.34
  171.7 15.9 %collective-permute-start.35 = (bf16[4,2,2,96,768]{4,3,2,1,0:T(8,128)(2,1)}, bf16[4,2,2,96,768]{4,3,2,1,0:T(8,128)(2,1)}, u32[]{:S(2)}, u32[]{:S(2)}) collective-permute-start(bf16[4,2,2,96,768]{4,3,2,1,0:T(8,128)(2,1)} %get-tuple-element.193), channel_id=1, source_target_pairs={{0,1},{1,0},{2,3},{3,2},{4,5},{5,4},{6,7},{7,6},{8,9},{9,8},{10,11... | collective-permute-start | bytes 7077896 | tf_op jit(solution)/shard_map/ppermute | solution.py:711
  171.8 16.2 %copy-start.14 = (bf16[4,2,2,96,768]{4,3,2,1,0:T(8,128)(2,1)S(1)}, bf16[4,2,2,96,768]{4,3,2,1,0:T(8,128)(2,1)}, u32[]{:S(2)}) copy-start(bf16[4,2,2,96,768]{4,3,2,1,0:T(8,128)(2,1)} %get-tuple-element.203) | copy-start | bytes 7077892
  187.6 19.5 %collective-permute-start.37 = (bf16[4,2,2,24,3072]{4,3,2,1,0:T(8,128)(2,1)}, bf16[4,2,2,24,3072]{4,3,2,1,0:T(8,128)(2,1)}, u32[]{:S(2)}, u32[]{:S(2)}) collective-permute-start(bf16[4,2,2,24,3072]{4,3,2,1,0:T(8,128)(2,1)} %get-tuple-element.205), channel_id=1, source_target_pairs={{0,1},{1,0},{2,3},{3,2},{4,5},{5,4},{6,7},{7,6},{8,9},{9,8},{10,11... | collective-permute-start | bytes 7077896 | tf_op jit(solution)/shard_map/ppermute | solution.py:711
  190.6 16.4 %collective-permute-start.36 = (bf16[2,2,2,96,768]{4,3,2,1,0:T(8,128)(2,1)}, bf16[2,2,2,96,768]{4,3,2,1,0:T(8,128)(2,1)S(1)}, u32[]{:S(2)}, u32[]{:S(2)}) collective-permute-start(bf16[2,2,2,96,768]{4,3,2,1,0:T(8,128)(2,1)} %fusion.2), channel_id=1, source_target_pairs={{0,2},{1,5},{2,0},{3,7},{4,6},{5,1},{6,4},{7,3},{8,10},{9,13},{10,... | collective-permute-start | bytes 3538952 | tf_op jit(solution)/shard_map/ppermute | solution.py:711
  207.1 5.4 %copy-start.17 = (bf16[2,2,2,96,768]{4,3,2,1,0:T(8,128)(2,1)}, bf16[2,2,2,96,768]{4,3,2,1,0:T(8,128)(2,1)S(1)}, u32[]{:S(2)}) copy-start(bf16[2,2,2,96,768]{4,3,2,1,0:T(8,128)(2,1)S(1)} %collective-permute-done.36) | copy-start | bytes 3538948
  209.6 33.0 %collective-permute-start.38 = (bf16[2,2,96,768]{3,2,1,0:T(8,128)(2,1)}, bf16[2,2,96,768]{3,2,1,0:T(8,128)(2,1)S(1)}, u32[]{:S(2)}, u32[]{:S(2)}) collective-permute-start(bf16[2,2,96,768]{3,2,1,0:T(8,128)(2,1)} %fusion.5), channel_id=1, source_target_pairs={{0,4},{1,3},{2,6},{3,1},{4,0},{5,7},{6,2},{7,5},{8,12},{9,11},{10,... | collective-permute-start | bytes 1769480 | tf_op jit(solution)/shard_map/ppermute | solution.py:711
  212.4 30.2 %collective-permute-start.39 = (bf16[2,2,2,24,3072]{4,3,2,1,0:T(8,128)(2,1)S(1)}, bf16[2,2,2,24,3072]{4,3,2,1,0:T(8,128)(2,1)}, u32[]{:S(2)}, u32[]{:S(2)}) collective-permute-start(bf16[2,2,2,24,3072]{4,3,2,1,0:T(8,128)(2,1)S(1)} %fusion.3), channel_id=1, source_target_pairs={{0,8},{1,9},{2,10},{3,11},{4,12},{5,13},{6,14},{7,15},{8,0},{9,1},... | collective-permute-start | bytes 3538952 | tf_op jit(solution)/shard_map/ppermute | solution.py:711
  242.6 5.2 %collective-permute-start.40 = (bf16[4,2,2,104,768]{4,3,2,1,0:T(8,128)(2,1)}, bf16[4,2,2,104,768]{4,3,2,1,0:T(8,128)(2,1)}, u32[]{:S(2)}, u32[]{:S(2)}) collective-permute-start(bf16[4,2,2,104,768]{4,3,2,1,0:T(8,128)(2,1)} %get-tuple-element.221), channel_id=1, source_target_pairs={{0,1},{1,0},{2,3},{3,2},{4,5},{5,4},{6,7},{7,6},{8,9},{9,8},{10,11... | collective-permute-start | bytes 7667720 | tf_op jit(solution)/shard_map/ppermute | solution.py:711
  250.5 23.8 %collective-permute-start.43 = (bf16[2,2,2,104,768]{4,3,2,1,0:T(8,128)(2,1)}, bf16[2,2,2,104,768]{4,3,2,1,0:T(8,128)(2,1)}, u32[]{:S(2)}, u32[]{:S(2)}) collective-permute-start(bf16[2,2,2,104,768]{4,3,2,1,0:T(8,128)(2,1)} %fusion), channel_id=1, source_target_pairs={{0,2},{1,5},{2,0},{3,7},{4,6},{5,1},{6,4},{7,3},{8,10},{9,13},{10,... | collective-permute-start | bytes 3833864 | tf_op jit(solution)/shard_map/ppermute | solution.py:711
  251.8 22.5 %collective-permute-start.42 = (bf16[2,2,24,3072]{3,2,1,0:T(8,128)(2,1)}, bf16[2,2,24,3072]{3,2,1,0:T(8,128)(2,1)S(1)}, u32[]{:S(2)}, u32[]{:S(2)}) collective-permute-start(bf16[2,2,24,3072]{3,2,1,0:T(8,128)(2,1)} %fusion.4), channel_id=1, source_target_pairs={{0,2},{1,5},{2,0},{3,7},{4,6},{5,1},{6,4},{7,3},{8,10},{9,13},{10,... | collective-permute-start | bytes 1769480 | tf_op jit(solution)/shard_map/ppermute | solution.py:711
  252.6 10.7 %collective-permute-start.41 = (bf16[2,96,768]{2,1,0:T(8,128)(2,1)S(1)}, bf16[2,96,768]{2,1,0:T(8,128)(2,1)S(1)}, u32[]{:S(2)}, u32[]{:S(2)}) collective-permute-start(bf16[2,96,768]{2,1,0:T(8,128)(2,1)S(1)} %fusion.10), channel_id=1, source_target_pairs={{0,8},{1,9},{2,10},{3,11},{4,12},{5,13},{6,14},{7,15},{8,0},{9,1},... | collective-permute-start | bytes 884744 | tf_op jit(solution)/shard_map/ppermute | solution.py:711
  277.5 13.9 %collective-permute-start.45 = (bf16[2,2,104,768]{3,2,1,0:T(8,128)(2,1)}, bf16[2,2,104,768]{3,2,1,0:T(8,128)(2,1)S(1)}, u32[]{:S(2)}, u32[]{:S(2)}) collective-permute-start(bf16[2,2,104,768]{3,2,1,0:T(8,128)(2,1)} %fusion.1), channel_id=1, source_target_pairs={{0,4},{1,3},{2,6},{3,1},{4,0},{5,7},{6,2},{7,5},{8,12},{9,11},{10,... | collective-permute-start | bytes 1916936 | tf_op jit(solution)/shard_map/ppermute | solution.py:711
  280.4 11.0 %collective-permute-start.44 = (bf16[2,24,3072]{2,1,0:T(8,128)(2,1)}, bf16[2,24,3072]{2,1,0:T(8,128)(2,1)}, u32[]{:S(2)}, u32[]{:S(2)}) collective-permute-start(bf16[2,24,3072]{2,1,0:T(8,128)(2,1)} %fusion.9), channel_id=1, source_target_pairs={{0,4},{1,3},{2,6},{3,1},{4,0},{5,7},{6,2},{7,5},{8,12},{9,11},{10,... | collective-permute-start | bytes 884744 | tf_op jit(solution)/shard_map/ppermute | solution.py:711
  281.6 12.9 %copy-start.20 = (bf16[2,2,24,3072]{3,2,1,0:T(8,128)(2,1)S(1)}, bf16[2,2,24,3072]{3,2,1,0:T(8,128)(2,1)}, u32[]{:S(2)}) copy-start(bf16[2,2,24,3072]{3,2,1,0:T(8,128)(2,1)} %copy-done.19) | copy-start | bytes 1769476
  283.3 13.8 %collective-permute-start.46 = (bf16[96,768]{1,0:T(8,128)(2,1)S(1)}, bf16[96,768]{1,0:T(8,128)(2,1)S(1)}, u32[]{:S(2)}, u32[]{:S(2)}) collective-permute-start(bf16[96,768]{1,0:T(8,128)(2,1)S(1)} %fusion.15), channel_id=1, source_target_pairs={{0,16},{1,17},{2,18},{3,19},{4,20},{5,21},{6,22},{7,23},{8,24},{9,... | collective-permute-start | bytes 442376 | tf_op jit(solution)/shard_map/ppermute | solution.py:711
  292.6 11.1 %collective-permute-start.47 = (bf16[2,104,768]{2,1,0:T(8,128)(2,1)S(1)}, bf16[2,104,768]{2,1,0:T(8,128)(2,1)S(1)}, u32[]{:S(2)}, u32[]{:S(2)}) collective-permute-start(bf16[2,104,768]{2,1,0:T(8,128)(2,1)S(1)} %fusion.8), channel_id=1, source_target_pairs={{0,8},{1,9},{2,10},{3,11},{4,12},{5,13},{6,14},{7,15},{8,0},{9,1},... | collective-permute-start | bytes 958472 | tf_op jit(solution)/shard_map/ppermute | solution.py:711
  295.7 10.2 %collective-permute-start.49 = (bf16[24,3072]{1,0:T(8,128)(2,1)S(1)}, bf16[24,3072]{1,0:T(8,128)(2,1)S(1)}, u32[]{:S(2)}, u32[]{:S(2)}) collective-permute-start(bf16[24,3072]{1,0:T(8,128)(2,1)S(1)} %fusion.13), channel_id=1, source_target_pairs={{0,16},{1,17},{2,18},{3,19},{4,20},{5,21},{6,22},{7,23},{8,24},{9,... | collective-permute-start | bytes 442376 | tf_op jit(solution)/shard_map/ppermute | solution.py:711
  303.8 11.7 %copy-start.1 = (bf16[96]{0:T(256)(128)(2,1)S(1)}, bf16[96]{0:T(256)(128)(2,1)}, u32[]{:S(2)}) copy-start(bf16[96]{0:T(256)(128)(2,1)} %param.33) | copy-start | bytes 580
  304.9 7.7 %collective-permute-start.48 = (bf16[104,768]{1,0:T(8,128)(2,1)S(1)}, bf16[104,768]{1,0:T(8,128)(2,1)S(1)}, u32[]{:S(2)}, u32[]{:S(2)}) collective-permute-start(bf16[104,768]{1,0:T(8,128)(2,1)S(1)} %fusion.11), channel_id=1, source_target_pairs={{0,16},{1,17},{2,18},{3,19},{4,20},{5,21},{6,22},{7,23},{8,24},{9,... | collective-permute-start | bytes 479240 | tf_op jit(solution)/shard_map/ppermute | solution.py:711
  (11 other events, 20.5 us)

commit v7 on v6

--- a/solution.py
+++ b/solution.py
@@ -879,17 +879,19 @@
         queries, vo_far, other, inn, out = together(queries, vo_far, other, inn, out)
         vo_parts = (vo, vo_far, other, send(vo_far, CORE))
         inn_far = send(inn, SECOND)
+        came = send(out, NEAR_Z)
         values, vo = project(x, vec, vo_parts, 2, (B_VALUE,), cube)
-        values, out = together(values, out)
-        out = join(out, send(out, NEAR_Z), 1, place.near_z)
+        values, came = together(values, came)
+        out = join(out, came, 1, place.near_z)
+        came = send(out, FIRST)
         probs, context = attend(lengths, queries, keys, values)
-        context, inn, inn_far, out = together(context, inn, inn_far, out)
+        context, inn, inn_far, came = together(context, inn, inn_far, came)
         inn_parts = (inn, inn_far, send(inn, CORE), send(inn_far, CORE))
-        out = join(out, send(out, FIRST), 2, place.first).reshape(4, 2, 96, D)
-        hat1, inv1, normed = close(x, context, vo, vec)
-        normed, inn_parts, out = together(normed, inn_parts, out)
+        out = join(out, came, 2, place.first).reshape(4, 2, 96, D)
         out_far = send(out, SECOND)
         other = send(out, CORE)
+        hat1, inv1, normed = close(x, context, vo, vec)
+        normed, inn_parts = together(normed, inn_parts)
         act, slope, inner_mat = inner(normed, vec, inn_parts, cube)
         act, out_far, other = together(act, out_far, other)
         out_parts = (out, out_far, other, send(out_far, CORE))

time: 317 us -> 318 us (level)
  waiting for transfers between devices: 83.1 us -> 88.4 us
  starting transfers between devices: 43.9 us -> 39.8 us
    ppermute x50, waiting for transfers between devices: 83.1 us -> 88.4 us  [send(): return lax.ppermute(field, AXIS, route)]
    ppermute x50, starting transfers between devices: 43.9 us -> 39.8 us  [send(): return lax.ppermute(field, AXIS, route)]
where the time goes in v7:
time: 318 us; the launch traced here: 317 us
  Pallas kernels  143 us (45%)
  waiting for transfers between devices  88.4 us (28%)
  starting transfers between devices  39.8 us (13%)
  other arithmetic  33.1 us (10%)
  local copies, waits for them, and re-layouts  11.2 us (4%)
    ppermute x50, waiting for transfers between devices, send(): return lax.ppermute(field, AXIS, route)  88.4 us
    ppermute x50, starting transfers between devices, send(): return lax.ppermute(field, AXIS, route)  39.8 us
    pallas_call x1, Pallas kernels, heads_back(): pl.pallas_call(lambda *refs: heads_back_body(cube, *refs), grid=(GROUPS,)...  29.9 us
    pallas_call x1, Pallas kernels, inner(): pl.pallas_call(lambda *refs: inner_body(cube, *refs), grid=(t // ROWS,),...  23.4 us
    convert_element_type x12, other arithmetic, settle(): sum((pick(term, axis, 1 - bit).astype(f32) for term in self.terms))  22.6 us
    pallas_call x1, Pallas kernels, inner_back(): pl.pallas_call(lambda *refs: inner_back_body(cube, *refs), grid=(FF // BL...  15.8 us
    pallas_call x1, Pallas kernels, open_back(): pl.pallas_call(open_back_body, grid=(t // (2 * ROWS),), in_specs=[row_blo...  14 us
    pallas_call x1, Pallas kernels, outer_back(): pl.pallas_call(lambda *refs: outer_back_body(cube, *refs), grid=(FF // BL...  13.5 us
  transfers between devices with their start and end apart: 50, of which 27 were waited for; matrix products, arithmetic and copies ran while one was open for 8% of the time, Pallas kernels for 36%

profile of v7, /device:TPU:0, one launch (start us, length us, event | category | flops | bytes accessed | tf_op | source)
XLA Modules:
  0.0 316.8 jit_solution(9734993570495380455)
XLA Ops:
  0.7 1.5 pack.2
  2.1 4.0 %collective-permute-start = (bf16[48,768]{1,0:T(8,128)(2,1)}, bf16[48,768]{1,0:T(8,128)(2,1)S(1)}, u32[]{:S(2)}, u32[]{:S(2)}) collective-permute-start(bf16[48,768]{1,0:T(8,128)(2,1)} %pack.2), channel_id=1, source_target_pairs={{0,16},{1,17},{2,18},{3,19},{4,20},{5,21},{6,22},{7,23},{8,24},{9,... | collective-permute-start | bytes 221192 | tf_op jit(solution)/shard_map/ppermute | solution.py:711
  8.5 1.4 pack.3
  9.9 3.3 %collective-permute-done.1 = bf16[16,768]{1,0:T(8,128)(2,1)S(1)} collective-permute-done((bf16[16,768]{1,0:T(8,128)(2,1)S(1)}, bf16[16,768]{1,0:T(8,128)(2,1)S(1)}, u32[]{:S(2)}, u32[]{:S(2)}) %collective-permute-start.1) | collective-permute-done | bytes 24608 | tf_op jit(solution)/shard_map/ppermute | solution.py:711
  14.2 1.6 collective-permute-start.3
  16.6 1.7 collective-permute-done.3
  18.3 3.8 %collective-permute-done.4 = bf16[48,768]{1,0:T(8,128)(2,1)S(1)} collective-permute-done((bf16[48,768]{1,0:T(8,128)(2,1)}, bf16[48,768]{1,0:T(8,128)(2,1)S(1)}, u32[]{:S(2)}, u32[]{:S(2)}) %collective-permute-start.4) | collective-permute-done | bytes 73760 | tf_op jit(solution)/shard_map/ppermute | solution.py:711
  24.1 1.5 collective-permute-start.6
  28.0 3.1 collective-permute-done.8
  34.0 1.5 collective-permute-start.11
  36.0 1.8 collective-permute-done.11
  37.8 4.6 %collective-permute-done.12 = bf16[2,2,48,768]{3,2,1,0:T(8,128)(2,1)S(1)} collective-permute-done((bf16[2,2,48,768]{3,2,1,0:T(8,128)(2,1)S(1)}, bf16[2,2,48,768]{3,2,1,0:T(8,128)(2,1)S(1)}, u32[]{:S(2)}, u32[]{:S(2)}) %collective-permute-start.12) | collective-permute-done | bytes 294944 | tf_op jit(solution)/shard_map/ppermute | solution.py:711
  42.6 2.7 collective-permute-done.9.refs_3_
  45.9 1.5 collective-permute-done.15
  47.4 1.4 collective-permute-start.18
  49.4 1.8 collective-permute-start.19
  51.2 3.3 %project.2 = (bf16[1024,768]{1,0:T(8,128)(2,1)S(1)}, bf16[1024,768]{1,0:T(8,128)(2,1)S(1)}, bf16[2,4,2,2,2,24,768]{6,5,4,3,2,1,0:T(8,128)(2,1)S(1)}) custom-call(bf16[1024,768]{1,0:T(8,128)(2,1)S(1)} %bitcast.191, bf16[16,768]{1,0:T(8,128)(2,1)S(1)} %add.653.refs_1_.vec_ref.refs_2_.codes_ref.refs_5_, ...), custom_call_target="tpu_custom_call" | custom-call | flops 2415919104 | bytes 9437184 | tf_op jit(solution)/shard_map/project/pallas_call | solution.py:128
  54.4 1.4 copy-done.2
  55.8 3.9 %collective-permute-done.19 = bf16[96,768]{1,0:T(8,128)(2,1)S(1)} collective-permute-done((bf16[96,768]{1,0:T(8,128)(2,1)S(1)}, bf16[96,768]{1,0:T(8,128)(2,1)S(1)}, u32[]{:S(2)}, u32[]{:S(2)}) %collective-permute-start.19) | collective-permute-done | bytes 147488 | tf_op jit(solution)/shard_map/ppermute | solution.py:711
  59.8 3.3 %collective-permute-done.18 = bf16[2,2,24,3072]{3,2,1,0:T(8,128)(2,1)S(1)} collective-permute-done((bf16[2,2,24,3072]{3,2,1,0:T(8,128)(2,1)S(1)}, bf16[2,2,24,3072]{3,2,1,0:T(8,128)(2,1)S(1)}, u32[]{:S(2)}, u32[]{:S(2)}) %collective-permute-start.18) | collective-permute-done | bytes 589856 | tf_op jit(solution)/shard_map/ppermute | solution.py:711
  64.2 1.8 collective-permute-start.21
  66.0 2.0 project.3
  68.1 1.4 copy-done.3
  70.7 3.2 %collective-permute-done.21 = bf16[2,96,768]{2,1,0:T(8,128)(2,1)S(1)} collective-permute-done((bf16[2,96,768]{2,1,0:T(8,128)(2,1)S(1)}, bf16[2,96,768]{2,1,0:T(8,128)(2,1)S(1)}, u32[]{:S(2)}, u32[]{:S(2)}) %collective-permute-start.21) | collective-permute-done | bytes 294944 | tf_op jit(solution)/shard_map/ppermute | solution.py:711
  74.7 9.3 %attend.1 = (f32[3,1024,256]{2,1,0:T(8,128)}, bf16[1024,768]{1,0:T(8,128)(2,1)}) custom-call(s32[16]{0:T(128)} %len_ref.1, bf16[1024,768]{1,0:T(8,128)(2,1)} %copy-done.10, bf16[1024,768]{1,0:T(8,128)(2,1)} %copy-done.11, bf16[1024,768]{1,0:T(8,128)(2,1)} %copy-done.7), custom_call_target="tpu_custom_call" | custom-call | flops 6039797760 | bytes 15728640 | tf_op jit(solution)/shard_map/attend/pallas_call | solution.py:220
  84.0 1.4 collective-permute-done.23
  87.9 5.6 %close.1 = (f32[1024,768]{1,0:T(8,128)}, f32[1024,1]{1,0:T(8,128)}, bf16[1024,768]{1,0:T(8,128)(2,1)}) custom-call(bf16[1024,768]{1,0:T(8,128)(2,1)} %bitcast.189, bf16[1024,768]{1,0:T(8,128)(2,1)} %get-tuple-element.160.c_ref.refs_7_, bf16[2,768,768]{2,1,0:T(8,128)(2,1)} %bitcast.186, bf16[16,768]{1,0:T(8,128)(2,1)} %copy-done.5), custom_call_target="tpu_custom_call" | custom-call | flops 1207959552 | bytes 9043968 | tf_op jit(solution)/shard_map/close/pallas_call | solution.py:251
  93.5 23.4 %inner.1 = (bf16[1024,3072]{1,0:T(8,128)(2,1)}, bf16[1024,3072]{1,0:T(8,128)(2,1)}, bf16[4,2,2,2,24,3072]{5,4,3,2,1,0:T(8,128)(2,1)}) custom-call(bf16[1024,768]{1,0:T(8,128)(2,1)} %get-tuple-element.165.refs_0_.refs_1_, bf16[16,768]{1,0:T(8,128)(2,1)} %copy-done.5, bf16[4,2,24,3072]{3,2,1,0:T(8,128)(2,1)} %copy-done.15, ...), custom_call_target="tpu_custom_call" | custom-call | flops 14495514624 | bytes 23592960 | tf_op jit(solution)/shard_map/inner/pallas_call | solution.py:422
  117.0 2.8 collective-permute-done.28.refs_6_
  120.9 12.9 %outer.1 = (bf16[1024,768]{1,0:T(8,128)(2,1)}, f32[1024,768]{1,0:T(8,128)}, f32[1024,1]{1,0:T(8,128)}, f32[8,1536]{1,0:T(8,128)}, bf16[8,1536]{1,0:T(8,128)(2,1)}, /*index=5*/bf16[4,2,2,2,96,768]{5,4,3,2,1,0:T(8,128)(2,1)}) custom-call(bf16[1024,3072]{1,0:T(8,128)(2,1)} %get-tuple-element.172.refs_0_.refs_4_, ...), custom_call_target="tpu_custom_call" | custom-call | flops 4831838208 | bytes 23592960 | tf_op jit(solution)/shard_map/outer/pallas_call | solution.py:470
  133.8 1.9 collective-permute-start.29
  135.7 3.4 %collective-permute-done.29 = bf16[8,1536]{1,0:T(8,128)(2,1)S(1)} collective-permute-done((bf16[8,1536]{1,0:T(8,128)(2,1)}, bf16[8,1536]{1,0:T(8,128)(2,1)S(1)}, u32[]{:S(2)}, u32[]{:S(2)}) %collective-permute-start.29) | collective-permute-done | bytes 24608 | tf_op jit(solution)/shard_map/ppermute | solution.py:711
  140.9 3.1 collective-permute-done.30
  144.8 4.8 %collective-permute-done.31 = bf16[2,2,8,1536]{3,2,1,0:T(8,128)(2,1)S(1)} collective-permute-done((bf16[2,2,8,1536]{3,2,1,0:T(8,128)(2,1)S(1)}, bf16[2,2,8,1536]{3,2,1,0:T(8,128)(2,1)S(1)}, u32[]{:S(2)}, u32[]{:S(2)}) %collective-permute-start.31) | collective-permute-done | bytes 98336 | tf_op jit(solution)/shard_map/ppermute | solution.py:711
  149.8 5.6 %collective-permute-done.32.far = bf16[4,2,8,1536]{3,2,1,0:T(8,128)(2,1)S(1)} collective-permute-done((bf16[4,2,8,1536]{3,2,1,0:T(8,128)(2,1)S(1)}, bf16[4,2,8,1536]{3,2,1,0:T(8,128)(2,1)S(1)}, u32[]{:S(2)}, u32[]{:S(2)}) %collective-permute-start.32) | collective-permute-done | bytes 196640 | tf_op jit(solution)/shard_map/ppermute | solution.py:711
  155.4 1.4 collective-permute-done.34.far_other
  157.6 1.3 pair_loss.1
  159.5 13.5 %outer_back.1 = (f32[1024,768]{1,0:T(8,128)}, bf16[1024,768]{1,0:T(8,128)(2,1)}, f32[16,768]{1,0:T(8,128)}, bf16[4,2,2,96,768]{4,3,2,1,0:T(8,128)(2,1)}, bf16[4,2,2,96,768]{4,3,2,1,0:T(8,128)(2,1)}) custom-call(bf16[1024,768]{1,0:T(8,128)(2,1)} %bitcast.225, f32[8,1536]{1,0:T(8,128)} %copy-done.9, f32[1024,768]{1,0:T(8,128)} %get-tuple-element.181.refs_2_, ...), custom_call_target="tpu_custom_call" | custom-call | flops 9663676416 | bytes 36175872 | tf_op jit(solution)/shard_map/outer_back/pallas_call | solution.py:556
  173.2 15.8 %inner_back.1 = (bf16[1024,3072]{1,0:T(8,128)(2,1)}, f32[16,768]{1,0:T(8,128)}, bf16[4,2,2,24,3072]{4,3,2,1,0:T(8,128)(2,1)}, bf16[4,2,2,24,3072]{4,3,2,1,0:T(8,128)(2,1)}) custom-call(bf16[1024,768]{1,0:T(8,128)(2,1)} %get-tuple-element.185.refs_0_, bf16[1024,768]{1,0:T(8,128)(2,1)} %get-tuple-element.165.refs_0_.refs_1_, ...), custom_call_target="tpu_custom_call" | custom-call | flops 9663676416 | bytes 34603008 | tf_op jit(solution)/shard_map/inner_back/pallas_call | solution.py:596
  189.4 2.6 fusion.2
  192.2 14.0 %open_back.1 = (f32[1024,768]{1,0:T(8,128)}, bf16[1024,768]{1,0:T(8,128)(2,1)}, bf16[1024,768]{1,0:T(8,128)(2,1)}, f32[16,768]{1,0:T(8,128)}) custom-call(f32[1024,768]{1,0:T(8,128)} %get-tuple-element.194.dres_ref, bf16[1024,3072]{1,0:T(8,128)(2,1)} %get-tuple-element.195.dh_ref, bf16[768,3072]{1,0:T(8,128)(2,1)} %bitcast.226, ...), custom_call_target="tpu_custom_call" | custom-call | flops 6039797760 | bytes 21626880 | tf_op jit(solution)/shard_map/open_back/pallas_call | solution.py:282
  206.2 2.2 collective-permute-done.36
  208.4 2.5 fusion.5
  211.2 1.6 fusion.3
  212.8 1.6 collective-permute-start.39
  214.4 29.9 %heads_back.1 = (bf16[1024,768]{1,0:T(8,128)(2,1)}, bf16[1024,768]{1,0:T(8,128)(2,1)}, bf16[1024,768]{1,0:T(8,128)(2,1)}, bf16[4,2,2,104,768]{4,3,2,1,0:T(8,128)(2,1)}, bf16[4,2,2,104,768]{4,3,2,1,0:T(8,128)(2,1)}) custom-call(bf16[1024,768]{1,0:T(8,128)(2,1)} %copy-done.10, bf16[1024,768]{1,0:T(8,128)(2,1)} %copy-done.11, bf16[1024,768]{1,0:T(8,128)(2,1)} %copy-done.7, ...), custom_call_target="tpu_custom_call" | custom-call | flops 18874368000 | bytes 15728640 | tf_op jit(solution)/shard_map/heads_back/pallas_call | solution.py:372
  245.1 1.5 fusion.10
  246.7 2.5 fusion.4
  249.5 2.7 fusion
  253.0 1.2 collective-permute-start.42
  254.7 8.9 %token_grad.1 = f32[1024,768]{1,0:T(8,128)} custom-call(f32[1024,768]{1,0:T(8,128)} %get-tuple-element.199.dr_ref, bf16[1024,768]{1,0:T(8,128)(2,1)} %get-tuple-element.213.dq_ref, bf16[1024,768]{1,0:T(8,128)(2,1)} %get-tuple-element.214.dk_ref, bf16[1024,768]{1,0:T(8,128)(2,1)} %get-tuple-element.215.dv_ref, bf16[2,768,768]{2,1,0:T(8,128)(2,1)} %bitcast.184, ...), custom_call_target="tpu_custom_call" | custom-call | flops 3623878656 | bytes 14548992 | tf_op jit(solution)/shard_map/token_grad/pallas_call | solution.py:619
  263.6 12.4 %collective-permute-done.42 = bf16[2,2,24,3072]{3,2,1,0:T(8,128)(2,1)S(1)} collective-permute-done((bf16[2,2,24,3072]{3,2,1,0:T(8,128)(2,1)}, bf16[2,2,24,3072]{3,2,1,0:T(8,128)(2,1)S(1)}, u32[]{:S(2)}, u32[]{:S(2)}) %collective-permute-start.42) | collective-permute-done | bytes 589856 | tf_op jit(solution)/shard_map/ppermute | solution.py:711
  276.8 2.4 fusion.1
  279.9 2.1 fusion.9
  282.0 1.3 collective-permute-start.44
  285.0 2.3 collective-permute-start.46
  287.3 5.7 %collective-permute-done.44 = bf16[2,24,3072]{2,1,0:T(8,128)(2,1)} collective-permute-done((bf16[2,24,3072]{2,1,0:T(8,128)(2,1)}, bf16[2,24,3072]{2,1,0:T(8,128)(2,1)}, u32[]{:S(2)}, u32[]{:S(2)}) %collective-permute-start.44) | collective-permute-done | bytes 294944 | tf_op jit(solution)/shard_map/ppermute | solution.py:711
  293.0 1.2 fusion.8
  294.8 1.2 fusion.13
  296.0 1.9 collective-permute-start.49
  297.9 2.0 fusion.16
  299.9 5.5 %collective-permute-done.47 = bf16[2,104,768]{2,1,0:T(8,128)(2,1)S(1)} collective-permute-done((bf16[2,104,768]{2,1,0:T(8,128)(2,1)S(1)}, bf16[2,104,768]{2,1,0:T(8,128)(2,1)S(1)}, u32[]{:S(2)}, u32[]{:S(2)}) %collective-permute-start.47) | collective-permute-done | bytes 319520 | tf_op jit(solution)/shard_map/ppermute | solution.py:711
  307.2 2.0 fusion.14
  309.2 4.7 %collective-permute-done.48 = bf16[104,768]{1,0:T(8,128)(2,1)S(1)} collective-permute-done((bf16[104,768]{1,0:T(8,128)(2,1)S(1)}, bf16[104,768]{1,0:T(8,128)(2,1)S(1)}, u32[]{:S(2)}, u32[]{:S(2)}) %collective-permute-start.48) | collective-permute-done | bytes 159776 | tf_op jit(solution)/shard_map/ppermute | solution.py:711
  (165 shorter events, 36.1 us)
Async XLA Ops:
  0.7 6.4 %copy-start = (bf16[96]{0:T(256)(128)(2,1)S(1)}, bf16[96]{0:T(256)(128)(2,1)}, u32[]{:S(2)}) copy-start(bf16[96]{0:T(256)(128)(2,1)} %param.33) | copy-start | bytes 580
  0.7 22.5 %copy-start.21 = (bf16[24,3072]{1,0:T(8,128)(2,1)S(1)}, bf16[24,3072]{1,0:T(8,128)(2,1)}, u32[]{:S(2)}) copy-start(bf16[24,3072]{1,0:T(8,128)(2,1)} %param.32) | copy-start | bytes 442372
  2.1 11.1 %collective-permute-start = (bf16[48,768]{1,0:T(8,128)(2,1)}, bf16[48,768]{1,0:T(8,128)(2,1)S(1)}, u32[]{:S(2)}, u32[]{:S(2)}) collective-permute-start(bf16[48,768]{1,0:T(8,128)(2,1)} %pack.2), channel_id=1, source_target_pairs={{0,16},{1,17},{2,18},{3,19},{4,20},{5,21},{6,22},{7,23},{8,24},{9,... | collective-permute-start | bytes 221192 | tf_op jit(solution)/shard_map/ppermute | solution.py:711
  8.4 4.7 %collective-permute-start.1 = (bf16[16,768]{1,0:T(8,128)(2,1)S(1)}, bf16[16,768]{1,0:T(8,128)(2,1)S(1)}, u32[]{:S(2)}, u32[]{:S(2)}) collective-permute-start(bf16[16,768]{1,0:T(8,128)(2,1)S(1)} %maximum_maximum_fusion), channel_id=1, source_target_pairs={{0,16},{1,17},{2,18},{3,19},{4,20},{5,21},{6,22},{7,23},{8,24},{9,... | collective-permute-start | bytes 73736 | tf_op jit(solution)/shard_map/ppermute | solution.py:711
  14.2 4.0 %collective-permute-start.3 = (bf16[16,768]{1,0:T(8,128)(2,1)S(1)}, bf16[16,768]{1,0:T(8,128)(2,1)S(1)}, u32[]{:S(2)}, u32[]{:S(2)}) collective-permute-start(bf16[16,768]{1,0:T(8,128)(2,1)S(1)} %fusion.62), channel_id=1, source_target_pairs={{0,8},{1,9},{2,10},{3,11},{4,12},{5,13},{6,14},{7,15},{8,0},{9,1},... | collective-permute-start | bytes 73736 | tf_op jit(solution)/shard_map/ppermute | solution.py:711
  15.9 6.2 %collective-permute-start.4 = (bf16[48,768]{1,0:T(8,128)(2,1)}, bf16[48,768]{1,0:T(8,128)(2,1)S(1)}, u32[]{:S(2)}, u32[]{:S(2)}) collective-permute-start(bf16[48,768]{1,0:T(8,128)(2,1)} %pack.3), channel_id=1, source_target_pairs={{0,16},{1,17},{2,18},{3,19},{4,20},{5,21},{6,22},{7,23},{8,24},{9,... | collective-permute-start | bytes 221192 | tf_op jit(solution)/shard_map/ppermute | solution.py:711
  16.5 6.6 %collective-permute-start.2 = (bf16[2,48,768]{2,1,0:T(8,128)(2,1)S(1)}, bf16[2,48,768]{2,1,0:T(8,128)(2,1)S(1)}, u32[]{:S(2)}, u32[]{:S(2)}) collective-permute-start(bf16[2,48,768]{2,1,0:T(8,128)(2,1)S(1)} %broadcast_select_fusion.12), channel_id=1, source_target_pairs={{0,8},{1,9},{2,10},{3,11},{4,12},{5,13},{6,14},{7,15},{8,0},{9,1},... | collective-permute-start | bytes 442376 | tf_op jit(solution)/shard_map/ppermute | solution.py:711
  23.2 7.8 %collective-permute-start.8 = (bf16[24,3072]{1,0:T(8,128)(2,1)S(1)}, bf16[24,3072]{1,0:T(8,128)(2,1)S(1)}, u32[]{:S(2)}, u32[]{:S(2)}) collective-permute-start(bf16[24,3072]{1,0:T(8,128)(2,1)S(1)} %copy-done.21), channel_id=1, source_target_pairs={{0,16},{1,17},{2,18},{3,19},{4,20},{5,21},{6,22},{7,23},{8,24},{9,... | collective-permute-start | bytes 442376 | tf_op jit(solution)/shard_map/ppermute | solution.py:711
  24.1 3.8 %collective-permute-start.6 = (bf16[16,768]{1,0:T(8,128)(2,1)S(1)}, bf16[16,768]{1,0:T(8,128)(2,1)S(1)}, u32[]{:S(2)}, u32[]{:S(2)}) collective-permute-start(bf16[16,768]{1,0:T(8,128)(2,1)S(1)} %add.650), channel_id=1, source_target_pairs={{0,2},{1,5},{2,0},{3,7},{4,6},{5,1},{6,4},{7,3},{8,10},{9,13},{10,... | collective-permute-start | bytes 73736 | tf_op jit(solution)/shard_map/ppermute | solution.py:711
  25.6 6.7 %collective-permute-start.5 = (bf16[2,2,48,768]{3,2,1,0:T(8,128)(2,1)S(1)}, bf16[2,2,48,768]{3,2,1,0:T(8,128)(2,1)S(1)}, u32[]{:S(2)}, u32[]{:S(2)}) collective-permute-start(bf16[2,2,48,768]{3,2,1,0:T(8,128)(2,1)S(1)} %broadcast_select_fusion.9), channel_id=1, source_target_pairs={{0,2},{1,5},{2,0},{3,7},{4,6},{5,1},{6,4},{7,3},{8,10},{9,13},{10,... | collective-permute-start | bytes 884744 | tf_op jit(solution)/shard_map/ppermute | solution.py:711
  26.1 5.7 %collective-permute-start.7 = (bf16[2,48,768]{2,1,0:T(8,128)(2,1)S(1)}, bf16[2,48,768]{2,1,0:T(8,128)(2,1)S(1)}, u32[]{:S(2)}, u32[]{:S(2)}) collective-permute-start(bf16[2,48,768]{2,1,0:T(8,128)(2,1)S(1)} %broadcast_select_fusion.11), channel_id=1, source_target_pairs={{0,8},{1,9},{2,10},{3,11},{4,12},{5,13},{6,14},{7,15},{8,0},{9,1},... | collective-permute-start | bytes 442376 | tf_op jit(solution)/shard_map/ppermute | solution.py:711
  32.3 17.0 %copy-start.22 = (bf16[96,768]{1,0:T(8,128)(2,1)S(1)}, bf16[96,768]{1,0:T(8,128)(2,1)}, u32[]{:S(2)}) copy-start(bf16[96,768]{1,0:T(8,128)(2,1)} %param.34) | copy-start | bytes 442372
  32.3 18.8 %copy-start.4 = (bf16[16,64,768]{2,1,0:T(8,128)(2,1)S(1)}, bf16[16,64,768]{2,1,0:T(8,128)(2,1)}, u32[]{:S(2)}) copy-start(bf16[16,64,768]{2,1,0:T(8,128)(2,1)} %param.19) | copy-start | bytes 4718596
  32.5 9.9 %collective-permute-start.12 = (bf16[2,2,48,768]{3,2,1,0:T(8,128)(2,1)S(1)}, bf16[2,2,48,768]{3,2,1,0:T(8,128)(2,1)S(1)}, u32[]{:S(2)}, u32[]{:S(2)}) collective-permute-start(bf16[2,2,48,768]{3,2,1,0:T(8,128)(2,1)S(1)} %broadcast_select_fusion.8), channel_id=1, source_target_pairs={{0,2},{1,5},{2,0},{3,7},{4,6},{5,1},{6,4},{7,3},{8,10},{9,13},{10,... | collective-permute-start | bytes 884744 | tf_op jit(solution)/shard_map/ppermute | solution.py:711
  33.7 8.8 %collective-permute-start.13 = (bf16[2,24,3072]{2,1,0:T(8,128)(2,1)S(1)}, bf16[2,24,3072]{2,1,0:T(8,128)(2,1)S(1)}, u32[]{:S(2)}, u32[]{:S(2)}) collective-permute-start(bf16[2,24,3072]{2,1,0:T(8,128)(2,1)S(1)} %broadcast_select_fusion.7), channel_id=1, source_target_pairs={{0,8},{1,9},{2,10},{3,11},{4,12},{5,13},{6,14},{7,15},{8,0},{9,1},... | collective-permute-start | bytes 884744 | tf_op jit(solution)/shard_map/ppermute | solution.py:711
  34.0 3.8 %collective-permute-start.11 = (bf16[16,768]{1,0:T(8,128)(2,1)S(1)}, bf16[16,768]{1,0:T(8,128)(2,1)S(1)}, u32[]{:S(2)}, u32[]{:S(2)}) collective-permute-start(bf16[16,768]{1,0:T(8,128)(2,1)S(1)} %add.651), channel_id=1, source_target_pairs={{0,4},{1,3},{2,6},{3,1},{4,0},{5,7},{6,2},{7,5},{8,12},{9,11},{10,... | collective-permute-start | bytes 73736 | tf_op jit(solution)/shard_map/ppermute | solution.py:711
  35.5 9.9 %collective-permute-start.9 = (bf16[4,2,48,768]{3,2,1,0:T(8,128)(2,1)S(1)}, bf16[4,2,48,768]{3,2,1,0:T(8,128)(2,1)S(1)}, u32[]{:S(2)}, u32[]{:S(2)}) collective-permute-start(bf16[4,2,48,768]{3,2,1,0:T(8,128)(2,1)S(1)} %broadcast_select_fusion.5.refs_2_), channel_id=1, source_target_pairs={{0,4},{1,3},{2,6},{3,1},{4,0},{5,7},{6,2},{7,5},{8,12},{9,11},{10,... | collective-permute-start | bytes 1769480 | tf_op jit(solution)/shard_map/ppermute | solution.py:711
  36.0 9.4 %collective-permute-start.10 = (bf16[4,2,48,768]{3,2,1,0:T(8,128)(2,1)S(1)}, bf16[4,2,48,768]{3,2,1,0:T(8,128)(2,1)S(1)}, u32[]{:S(2)}, u32[]{:S(2)}) collective-permute-start(bf16[4,2,48,768]{3,2,1,0:T(8,128)(2,1)S(1)} %broadcast_select_fusion.5.refs_2_), channel_id=1, source_target_pairs={{0,1},{1,0},{2,3},{3,2},{4,5},{5,4},{6,7},{7,6},{8,9},{9,8},{10,11... | collective-permute-start | bytes 1769480 | tf_op jit(solution)/shard_map/ppermute | solution.py:711
  45.4 2.1 collective-permute-start.14
  45.4 2.0 collective-permute-start.15
  47.4 18.6 %copy-start.5 = (bf16[16,768]{1,0:T(8,128)(2,1)}, bf16[16,768]{1,0:T(8,128)(2,1)S(1)}, u32[]{:S(2)}) copy-start(bf16[16,768]{1,0:T(8,128)(2,1)S(1)} %add.653.refs_1_.vec_ref.refs_2_.codes_ref.refs_5_) | copy-start | bytes 73732
  47.4 15.7 %collective-permute-start.18 = (bf16[2,2,24,3072]{3,2,1,0:T(8,128)(2,1)S(1)}, bf16[2,2,24,3072]{3,2,1,0:T(8,128)(2,1)S(1)}, u32[]{:S(2)}, u32[]{:S(2)}) collective-permute-start(bf16[2,2,24,3072]{3,2,1,0:T(8,128)(2,1)S(1)} %broadcast_select_fusion.3), channel_id=1, source_target_pairs={{0,2},{1,5},{2,0},{3,7},{4,6},{5,1},{6,4},{7,3},{8,10},{9,13},{10,... | collective-permute-start | bytes 1769480 | tf_op jit(solution)/shard_map/ppermute | solution.py:711
  48.9 14.4 %collective-permute-start.16 = (bf16[4,2,48,768]{3,2,1,0:T(8,128)(2,1)S(1)}, bf16[4,2,48,768]{3,2,1,0:T(8,128)(2,1)S(1)}, u32[]{:S(2)}, u32[]{:S(2)}) collective-permute-start(bf16[4,2,48,768]{3,2,1,0:T(8,128)(2,1)S(1)} %broadcast_select_fusion.4.refs_2_), channel_id=1, source_target_pairs={{0,4},{1,3},{2,6},{3,1},{4,0},{5,7},{6,2},{7,5},{8,12},{9,11},{10,... | collective-permute-start | bytes 1769480 | tf_op jit(solution)/shard_map/ppermute | solution.py:711
  49.4 13.9 %collective-permute-start.17 = (bf16[4,2,48,768]{3,2,1,0:T(8,128)(2,1)S(1)}, bf16[4,2,48,768]{3,2,1,0:T(8,128)(2,1)S(1)}, u32[]{:S(2)}, u32[]{:S(2)}) collective-permute-start(bf16[4,2,48,768]{3,2,1,0:T(8,128)(2,1)S(1)} %broadcast_select_fusion.4.refs_2_), channel_id=1, source_target_pairs={{0,1},{1,0},{2,3},{3,2},{4,5},{5,4},{6,7},{7,6},{8,9},{9,8},{10,11... | collective-permute-start | bytes 1769480 | tf_op jit(solution)/shard_map/ppermute | solution.py:711
  49.4 10.3 %collective-permute-start.19 = (bf16[96,768]{1,0:T(8,128)(2,1)S(1)}, bf16[96,768]{1,0:T(8,128)(2,1)S(1)}, u32[]{:S(2)}, u32[]{:S(2)}) collective-permute-start(bf16[96,768]{1,0:T(8,128)(2,1)S(1)} %copy-done.22), channel_id=1, source_target_pairs={{0,16},{1,17},{2,18},{3,19},{4,20},{5,21},{6,22},{7,23},{8,24},{9,... | collective-permute-start | bytes 442376 | tf_op jit(solution)/shard_map/ppermute | solution.py:711
  55.8 12.3 %copy-start.10 = (bf16[1024,768]{1,0:T(8,128)(2,1)}, bf16[1024,768]{1,0:T(8,128)(2,1)S(1)}, u32[]{:S(2)}) copy-start(bf16[1024,768]{1,0:T(8,128)(2,1)S(1)} %get-tuple-element.150.q_ref.refs_0_) | copy-start | bytes 4718596
  55.8 12.3 %copy-start.11 = (bf16[1024,768]{1,0:T(8,128)(2,1)}, bf16[1024,768]{1,0:T(8,128)(2,1)S(1)}, u32[]{:S(2)}) copy-start(bf16[1024,768]{1,0:T(8,128)(2,1)S(1)} %get-tuple-element.151.k_ref.refs_1_) | copy-start | bytes 4718596
  63.3 22.2 %copy-start.15 = (bf16[4,2,24,3072]{3,2,1,0:T(8,128)(2,1)}, bf16[4,2,24,3072]{3,2,1,0:T(8,128)(2,1)S(1)}, u32[]{:S(2)}) copy-start(bf16[4,2,24,3072]{3,2,1,0:T(8,128)(2,1)S(1)} %broadcast_select_fusion.1.refs_2_) | copy-start | bytes 3538948
  63.3 2.7 collective-permute-start.20
  63.4 20.6 %collective-permute-start.22 = (bf16[4,2,24,3072]{3,2,1,0:T(8,128)(2,1)S(1)}, bf16[4,2,24,3072]{3,2,1,0:T(8,128)(2,1)}, u32[]{:S(2)}, u32[]{:S(2)}) collective-permute-start(bf16[4,2,24,3072]{3,2,1,0:T(8,128)(2,1)S(1)} %broadcast_select_fusion.1.refs_2_), channel_id=1, source_target_pairs={{0,4},{1,3},{2,6},{3,1},{4,0},{5,7},{6,2},{7,5},{8,12},{9,11},{10,... | collective-permute-start | bytes 3538952 | tf_op jit(solution)/shard_map/ppermute | solution.py:711
  64.2 9.6 %collective-permute-start.21 = (bf16[2,96,768]{2,1,0:T(8,128)(2,1)S(1)}, bf16[2,96,768]{2,1,0:T(8,128)(2,1)S(1)}, u32[]{:S(2)}, u32[]{:S(2)}) collective-permute-start(bf16[2,96,768]{2,1,0:T(8,128)(2,1)S(1)} %broadcast_select_fusion.6), channel_id=1, source_target_pairs={{0,8},{1,9},{2,10},{3,11},{4,12},{5,13},{6,14},{7,15},{8,0},{9,1},... | collective-permute-start | bytes 884744 | tf_op jit(solution)/shard_map/ppermute | solution.py:711
  74.0 11.5 %collective-permute-start.23 = (bf16[2,2,96,768]{3,2,1,0:T(8,128)(2,1)S(1)}, bf16[2,2,96,768]{3,2,1,0:T(8,128)(2,1)S(1)}, u32[]{:S(2)}, u32[]{:S(2)}) collective-permute-start(bf16[2,2,96,768]{3,2,1,0:T(8,128)(2,1)S(1)} %broadcast_select_fusion.2), channel_id=1, source_target_pairs={{0,2},{1,5},{2,0},{3,7},{4,6},{5,1},{6,4},{7,3},{8,10},{9,13},{10,... | collective-permute-start | bytes 1769480 | tf_op jit(solution)/shard_map/ppermute | solution.py:711
  85.4 8.1 %collective-permute-start.24 = (bf16[4,2,24,3072]{3,2,1,0:T(8,128)(2,1)S(1)}, bf16[4,2,24,3072]{3,2,1,0:T(8,128)(2,1)}, u32[]{:S(2)}, u32[]{:S(2)}) collective-permute-start(bf16[4,2,24,3072]{3,2,1,0:T(8,128)(2,1)S(1)} %broadcast_select_fusion.1.refs_2_), channel_id=1, source_target_pairs={{0,1},{1,0},{2,3},{3,2},{4,5},{5,4},{6,7},{7,6},{8,9},{9,8},{10,11... | collective-permute-start | bytes 3538952 | tf_op jit(solution)/shard_map/ppermute | solution.py:711
  85.8 7.7 %collective-permute-start.25 = (bf16[4,2,24,3072]{3,2,1,0:T(8,128)(2,1)}, bf16[4,2,24,3072]{3,2,1,0:T(8,128)(2,1)}, u32[]{:S(2)}, u32[]{:S(2)}) collective-permute-start(bf16[4,2,24,3072]{3,2,1,0:T(8,128)(2,1)} %collective-permute-done.22.refs_3_), channel_id=1, source_target_pairs={{0,1},{1,0},{2,3},{3,2},{4,5},{5,4},{6,7},{7,6},{8,9},{9,8},{10,11... | collective-permute-start | bytes 3538952 | tf_op jit(solution)/shard_map/ppermute | solution.py:711
  86.4 7.1 %copy-start.16 = (bf16[4,2,96,768]{3,2,1,0:T(8,128)(2,1)}, bf16[4,2,96,768]{3,2,1,0:T(8,128)(2,1)S(1)}, u32[]{:S(2)}) copy-start(bf16[4,2,96,768]{3,2,1,0:T(8,128)(2,1)S(1)} %broadcast_select_fusion.refs_3_) | copy-start | bytes 3538948
  86.4 30.5 %collective-permute-start.26 = (bf16[4,2,96,768]{3,2,1,0:T(8,128)(2,1)S(1)}, bf16[4,2,96,768]{3,2,1,0:T(8,128)(2,1)S(1)}, u32[]{:S(2)}, u32[]{:S(2)}) collective-permute-start(bf16[4,2,96,768]{3,2,1,0:T(8,128)(2,1)S(1)} %broadcast_select_fusion.refs_3_), channel_id=1, source_target_pairs={{0,4},{1,3},{2,6},{3,1},{4,0},{5,7},{6,2},{7,5},{8,12},{9,11},{10,... | collective-permute-start | bytes 3538952 | tf_op jit(solution)/shard_map/ppermute | solution.py:711
  87.2 29.7 %collective-permute-start.27 = (bf16[4,2,96,768]{3,2,1,0:T(8,128)(2,1)S(1)}, bf16[4,2,96,768]{3,2,1,0:T(8,128)(2,1)}, u32[]{:S(2)}, u32[]{:S(2)}) collective-permute-start(bf16[4,2,96,768]{3,2,1,0:T(8,128)(2,1)S(1)} %broadcast_select_fusion.refs_3_), channel_id=1, source_target_pairs={{0,1},{1,0},{2,3},{3,2},{4,5},{5,4},{6,7},{7,6},{8,9},{9,8},{10,11... | collective-permute-start | bytes 3538952 | tf_op jit(solution)/shard_map/ppermute | solution.py:711
  116.9 2.9 collective-permute-start.28
  120.8 36.0 %copy-start.6 = (bf16[16,768]{1,0:T(8,128)(2,1)S(1)}, bf16[16,768]{1,0:T(8,128)(2,1)}, u32[]{:S(2)}) copy-start(bf16[16,768]{1,0:T(8,128)(2,1)} %copy-done.5) | copy-start | bytes 73732
  133.8 5.3 %collective-permute-start.29 = (bf16[8,1536]{1,0:T(8,128)(2,1)}, bf16[8,1536]{1,0:T(8,128)(2,1)S(1)}, u32[]{:S(2)}, u32[]{:S(2)}) collective-permute-start(bf16[8,1536]{1,0:T(8,128)(2,1)} %get-tuple-element.176), channel_id=1, source_target_pairs={{0,16},{1,17},{2,18},{3,19},{4,20},{5,21},{6,22},{7,23},{8,24},{9,... | collective-permute-start | bytes 73736 | tf_op jit(solution)/shard_map/ppermute | solution.py:711
  139.9 4.1 %collective-permute-start.30 = (bf16[2,8,1536]{2,1,0:T(8,128)(2,1)S(1)}, bf16[2,8,1536]{2,1,0:T(8,128)(2,1)S(1)}, u32[]{:S(2)}, u32[]{:S(2)}) collective-permute-start(bf16[2,8,1536]{2,1,0:T(8,128)(2,1)S(1)} %broadcast_select_fusion.14), channel_id=1, source_target_pairs={{0,8},{1,9},{2,10},{3,11},{4,12},{5,13},{6,14},{7,15},{8,0},{9,1},... | collective-permute-start | bytes 147464 | tf_op jit(solution)/shard_map/ppermute | solution.py:711
  144.0 5.5 %collective-permute-start.31 = (bf16[2,2,8,1536]{3,2,1,0:T(8,128)(2,1)S(1)}, bf16[2,2,8,1536]{3,2,1,0:T(8,128)(2,1)S(1)}, u32[]{:S(2)}, u32[]{:S(2)}) collective-permute-start(bf16[2,2,8,1536]{3,2,1,0:T(8,128)(2,1)S(1)} %broadcast_select_fusion.13), channel_id=1, source_target_pairs={{0,2},{1,5},{2,0},{3,7},{4,6},{5,1},{6,4},{7,3},{8,10},{9,13},{10,... | collective-permute-start | bytes 294920 | tf_op jit(solution)/shard_map/ppermute | solution.py:711
  149.6 5.7 %collective-permute-start.32 = (bf16[4,2,8,1536]{3,2,1,0:T(8,128)(2,1)S(1)}, bf16[4,2,8,1536]{3,2,1,0:T(8,128)(2,1)S(1)}, u32[]{:S(2)}, u32[]{:S(2)}) collective-permute-start(bf16[4,2,8,1536]{3,2,1,0:T(8,128)(2,1)S(1)} %broadcast_select_fusion.10.near), channel_id=1, source_target_pairs={{0,4},{1,3},{2,6},{3,1},{4,0},{5,7},{6,2},{7,5},{8,12},{9,11},{10,... | collective-permute-start | bytes 589832 | tf_op jit(solution)/shard_map/ppermute | solution.py:711
  149.8 5.6 %collective-permute-start.33 = (bf16[4,2,8,1536]{3,2,1,0:T(8,128)(2,1)S(1)}, bf16[4,2,8,1536]{3,2,1,0:T(8,128)(2,1)S(1)}, u32[]{:S(2)}, u32[]{:S(2)}) collective-permute-start(bf16[4,2,8,1536]{3,2,1,0:T(8,128)(2,1)S(1)} %broadcast_select_fusion.10.near), channel_id=1, source_target_pairs={{0,1},{1,0},{2,3},{3,2},{4,5},{5,4},{6,7},{7,6},{8,9},{9,8},{10,11... | collective-permute-start | bytes 589832 | tf_op jit(solution)/shard_map/ppermute | solution.py:711
  155.4 1.4 collective-permute-start.34
  173.0 15.9 %collective-permute-start.35 = (bf16[4,2,2,96,768]{4,3,2,1,0:T(8,128)(2,1)}, bf16[4,2,2,96,768]{4,3,2,1,0:T(8,128)(2,1)}, u32[]{:S(2)}, u32[]{:S(2)}) collective-permute-start(bf16[4,2,2,96,768]{4,3,2,1,0:T(8,128)(2,1)} %get-tuple-element.191), channel_id=1, source_target_pairs={{0,1},{1,0},{2,3},{3,2},{4,5},{5,4},{6,7},{7,6},{8,9},{9,8},{10,11... | collective-permute-start | bytes 7077896 | tf_op jit(solution)/shard_map/ppermute | solution.py:711
  173.2 16.2 %copy-start.14 = (bf16[4,2,2,96,768]{4,3,2,1,0:T(8,128)(2,1)S(1)}, bf16[4,2,2,96,768]{4,3,2,1,0:T(8,128)(2,1)}, u32[]{:S(2)}) copy-start(bf16[4,2,2,96,768]{4,3,2,1,0:T(8,128)(2,1)} %get-tuple-element.201) | copy-start | bytes 7077892
  188.9 19.5 %collective-permute-start.37 = (bf16[4,2,2,24,3072]{4,3,2,1,0:T(8,128)(2,1)}, bf16[4,2,2,24,3072]{4,3,2,1,0:T(8,128)(2,1)}, u32[]{:S(2)}, u32[]{:S(2)}) collective-permute-start(bf16[4,2,2,24,3072]{4,3,2,1,0:T(8,128)(2,1)} %get-tuple-element.203), channel_id=1, source_target_pairs={{0,1},{1,0},{2,3},{3,2},{4,5},{5,4},{6,7},{7,6},{8,9},{9,8},{10,11... | collective-permute-start | bytes 7077896 | tf_op jit(solution)/shard_map/ppermute | solution.py:711
  192.0 16.4 %collective-permute-start.36 = (bf16[2,2,2,96,768]{4,3,2,1,0:T(8,128)(2,1)}, bf16[2,2,2,96,768]{4,3,2,1,0:T(8,128)(2,1)S(1)}, u32[]{:S(2)}, u32[]{:S(2)}) collective-permute-start(bf16[2,2,2,96,768]{4,3,2,1,0:T(8,128)(2,1)} %fusion.2), channel_id=1, source_target_pairs={{0,2},{1,5},{2,0},{3,7},{4,6},{5,1},{6,4},{7,3},{8,10},{9,13},{10,... | collective-permute-start | bytes 3538952 | tf_op jit(solution)/shard_map/ppermute | solution.py:711
  206.2 5.0 %copy-start.13 = (bf16[4,2,2,24,3072]{4,3,2,1,0:T(8,128)(2,1)S(1)}, bf16[4,2,2,24,3072]{4,3,2,1,0:T(8,128)(2,1)}, u32[]{:S(2)}) copy-start(bf16[4,2,2,24,3072]{4,3,2,1,0:T(8,128)(2,1)} %get-tuple-element.211) | copy-start | bytes 7077892
  210.9 33.3 %collective-permute-start.38 = (bf16[2,2,96,768]{3,2,1,0:T(8,128)(2,1)}, bf16[2,2,96,768]{3,2,1,0:T(8,128)(2,1)S(1)}, u32[]{:S(2)}, u32[]{:S(2)}) collective-permute-start(bf16[2,2,96,768]{3,2,1,0:T(8,128)(2,1)} %fusion.5), channel_id=1, source_target_pairs={{0,4},{1,3},{2,6},{3,1},{4,0},{5,7},{6,2},{7,5},{8,12},{9,11},{10,... | collective-permute-start | bytes 1769480 | tf_op jit(solution)/shard_map/ppermute | solution.py:711
  212.8 31.5 %collective-permute-start.39 = (bf16[2,2,2,24,3072]{4,3,2,1,0:T(8,128)(2,1)S(1)}, bf16[2,2,2,24,3072]{4,3,2,1,0:T(8,128)(2,1)}, u32[]{:S(2)}, u32[]{:S(2)}) collective-permute-start(bf16[2,2,2,24,3072]{4,3,2,1,0:T(8,128)(2,1)S(1)} %fusion.3), channel_id=1, source_target_pairs={{0,8},{1,9},{2,10},{3,11},{4,12},{5,13},{6,14},{7,15},{8,0},{9,1},... | collective-permute-start | bytes 3538952 | tf_op jit(solution)/shard_map/ppermute | solution.py:711
  244.3 5.2 %collective-permute-start.40 = (bf16[4,2,2,104,768]{4,3,2,1,0:T(8,128)(2,1)}, bf16[4,2,2,104,768]{4,3,2,1,0:T(8,128)(2,1)}, u32[]{:S(2)}, u32[]{:S(2)}) collective-permute-start(bf16[4,2,2,104,768]{4,3,2,1,0:T(8,128)(2,1)} %get-tuple-element.219), channel_id=1, source_target_pairs={{0,1},{1,0},{2,3},{3,2},{4,5},{5,4},{6,7},{7,6},{8,9},{9,8},{10,11... | collective-permute-start | bytes 7667720 | tf_op jit(solution)/shard_map/ppermute | solution.py:711
  252.2 23.8 %collective-permute-start.43 = (bf16[2,2,2,104,768]{4,3,2,1,0:T(8,128)(2,1)}, bf16[2,2,2,104,768]{4,3,2,1,0:T(8,128)(2,1)}, u32[]{:S(2)}, u32[]{:S(2)}) collective-permute-start(bf16[2,2,2,104,768]{4,3,2,1,0:T(8,128)(2,1)} %fusion), channel_id=1, source_target_pairs={{0,2},{1,5},{2,0},{3,7},{4,6},{5,1},{6,4},{7,3},{8,10},{9,13},{10,... | collective-permute-start | bytes 3833864 | tf_op jit(solution)/shard_map/ppermute | solution.py:711
  253.0 23.0 %collective-permute-start.42 = (bf16[2,2,24,3072]{3,2,1,0:T(8,128)(2,1)}, bf16[2,2,24,3072]{3,2,1,0:T(8,128)(2,1)S(1)}, u32[]{:S(2)}, u32[]{:S(2)}) collective-permute-start(bf16[2,2,24,3072]{3,2,1,0:T(8,128)(2,1)} %fusion.4), channel_id=1, source_target_pairs={{0,2},{1,5},{2,0},{3,7},{4,6},{5,1},{6,4},{7,3},{8,10},{9,13},{10,... | collective-permute-start | bytes 1769480 | tf_op jit(solution)/shard_map/ppermute | solution.py:711
  254.2 9.3 %collective-permute-start.41 = (bf16[2,96,768]{2,1,0:T(8,128)(2,1)S(1)}, bf16[2,96,768]{2,1,0:T(8,128)(2,1)S(1)}, u32[]{:S(2)}, u32[]{:S(2)}) collective-permute-start(bf16[2,96,768]{2,1,0:T(8,128)(2,1)S(1)} %fusion.10), channel_id=1, source_target_pairs={{0,8},{1,9},{2,10},{3,11},{4,12},{5,13},{6,14},{7,15},{8,0},{9,1},... | collective-permute-start | bytes 884744 | tf_op jit(solution)/shard_map/ppermute | solution.py:711
  279.2 13.9 %collective-permute-start.45 = (bf16[2,2,104,768]{3,2,1,0:T(8,128)(2,1)}, bf16[2,2,104,768]{3,2,1,0:T(8,128)(2,1)S(1)}, u32[]{:S(2)}, u32[]{:S(2)}) collective-permute-start(bf16[2,2,104,768]{3,2,1,0:T(8,128)(2,1)} %fusion.1), channel_id=1, source_target_pairs={{0,4},{1,3},{2,6},{3,1},{4,0},{5,7},{6,2},{7,5},{8,12},{9,11},{10,... | collective-permute-start | bytes 1916936 | tf_op jit(solution)/shard_map/ppermute | solution.py:711
  282.0 11.1 %collective-permute-start.44 = (bf16[2,24,3072]{2,1,0:T(8,128)(2,1)}, bf16[2,24,3072]{2,1,0:T(8,128)(2,1)}, u32[]{:S(2)}, u32[]{:S(2)}) collective-permute-start(bf16[2,24,3072]{2,1,0:T(8,128)(2,1)} %fusion.9), channel_id=1, source_target_pairs={{0,4},{1,3},{2,6},{3,1},{4,0},{5,7},{6,2},{7,5},{8,12},{9,11},{10,... | collective-permute-start | bytes 884744 | tf_op jit(solution)/shard_map/ppermute | solution.py:711
  283.3 11.5 %copy-start.20 = (bf16[2,2,24,3072]{3,2,1,0:T(8,128)(2,1)S(1)}, bf16[2,2,24,3072]{3,2,1,0:T(8,128)(2,1)}, u32[]{:S(2)}) copy-start(bf16[2,2,24,3072]{3,2,1,0:T(8,128)(2,1)} %copy-done.19) | copy-start | bytes 1769476
  285.0 12.9 %collective-permute-start.46 = (bf16[96,768]{1,0:T(8,128)(2,1)S(1)}, bf16[96,768]{1,0:T(8,128)(2,1)S(1)}, u32[]{:S(2)}, u32[]{:S(2)}) collective-permute-start(bf16[96,768]{1,0:T(8,128)(2,1)S(1)} %fusion.15), channel_id=1, source_target_pairs={{0,16},{1,17},{2,18},{3,19},{4,20},{5,21},{6,22},{7,23},{8,24},{9,... | collective-permute-start | bytes 442376 | tf_op jit(solution)/shard_map/ppermute | solution.py:711
  294.3 11.1 %collective-permute-start.47 = (bf16[2,104,768]{2,1,0:T(8,128)(2,1)S(1)}, bf16[2,104,768]{2,1,0:T(8,128)(2,1)S(1)}, u32[]{:S(2)}, u32[]{:S(2)}) collective-permute-start(bf16[2,104,768]{2,1,0:T(8,128)(2,1)S(1)} %fusion.8), channel_id=1, source_target_pairs={{0,8},{1,9},{2,10},{3,11},{4,12},{5,13},{6,14},{7,15},{8,0},{9,1},... | collective-permute-start | bytes 958472 | tf_op jit(solution)/shard_map/ppermute | solution.py:711
  296.0 11.2 %collective-permute-start.49 = (bf16[24,3072]{1,0:T(8,128)(2,1)S(1)}, bf16[24,3072]{1,0:T(8,128)(2,1)S(1)}, u32[]{:S(2)}, u32[]{:S(2)}) collective-permute-start(bf16[24,3072]{1,0:T(8,128)(2,1)S(1)} %fusion.13), channel_id=1, source_target_pairs={{0,16},{1,17},{2,18},{3,19},{4,20},{5,21},{6,22},{7,23},{8,24},{9,... | collective-permute-start | bytes 442376 | tf_op jit(solution)/shard_map/ppermute | solution.py:711
  305.4 11.4 %copy-start.1 = (bf16[96]{0:T(256)(128)(2,1)S(1)}, bf16[96]{0:T(256)(128)(2,1)}, u32[]{:S(2)}) copy-start(bf16[96]{0:T(256)(128)(2,1)} %param.33) | copy-start | bytes 580
  306.5 7.4 %collective-permute-start.48 = (bf16[104,768]{1,0:T(8,128)(2,1)S(1)}, bf16[104,768]{1,0:T(8,128)(2,1)S(1)}, u32[]{:S(2)}, u32[]{:S(2)}) collective-permute-start(bf16[104,768]{1,0:T(8,128)(2,1)S(1)} %fusion.11), channel_id=1, source_target_pairs={{0,16},{1,17},{2,18},{3,19},{4,20},{5,21},{6,22},{7,23},{8,24},{9,... | collective-permute-start | bytes 479240 | tf_op jit(solution)/shard_map/ppermute | solution.py:711
  (11 other events, 19.7 us)

commit v8 on v6

--- a/solution.py
+++ b/solution.py
@@ -403,7 +403,7 @@
 
     w = w_ref.reshape(D, FF) if cube else w_ref
 
-    @pl.loop(0, FF // BLOCK)
+    @pl.loop(0, FF // BLOCK, unroll=2)
     def _(j):
         cols = pl.ds(pl.multiple_of(j * BLOCK, BLOCK), BLOCK)
         h = nn(n_ref[...], w[:, cols]) + bias_ref[pl.ds(B_INNER + j, 1), :]

time: 317 us -> 316 us (level)
  no operation moved by 1% of the time
where the time goes in v8:
time: 316 us; the launch traced here: 315 us
  Pallas kernels  142 us (45%)
  waiting for transfers between devices  83.1 us (26%)
  starting transfers between devices  43.9 us (14%)
  other arithmetic  32.9 us (10%)
  local copies, waits for them, and re-layouts  11.2 us (4%)
    ppermute x50, waiting for transfers between devices, send(): return lax.ppermute(field, AXIS, route)  83.1 us
    ppermute x50, starting transfers between devices, send(): return lax.ppermute(field, AXIS, route)  43.9 us
    pallas_call x1, Pallas kernels, heads_back(): pl.pallas_call(lambda *refs: heads_back_body(cube, *refs), grid=(GROUPS,)...  29.9 us
    pallas_call x1, Pallas kernels, inner(): pl.pallas_call(lambda *refs: inner_body(cube, *refs), grid=(t // ROWS,),...  22.8 us
    convert_element_type x12, other arithmetic, settle(): sum((pick(term, axis, 1 - bit).astype(f32) for term in self.terms))  22.6 us
    pallas_call x1, Pallas kernels, inner_back(): pl.pallas_call(lambda *refs: inner_back_body(cube, *refs), grid=(FF // BL...  15.8 us
    pallas_call x1, Pallas kernels, open_back(): pl.pallas_call(open_back_body, grid=(t // (2 * ROWS),), in_specs=[row_blo...  14 us
    pallas_call x1, Pallas kernels, outer_back(): pl.pallas_call(lambda *refs: outer_back_body(cube, *refs), grid=(FF // BL...  13.5 us
  transfers between devices with their start and end apart: 50, of which 27 were waited for; matrix products, arithmetic and copies ran while one was open for 8% of the time, Pallas kernels for 36%

profile of v8, /device:TPU:0, one launch (start us, length us, event | category | flops | bytes accessed | tf_op | source)
XLA Modules:
  0.0 314.9 jit_solution(13276317441420051347)
XLA Ops:
  0.7 1.5 pack.2
  2.1 4.0 %collective-permute-start = (bf16[48,768]{1,0:T(8,128)(2,1)}, bf16[48,768]{1,0:T(8,128)(2,1)S(1)}, u32[]{:S(2)}, u32[]{:S(2)}) collective-permute-start(bf16[48,768]{1,0:T(8,128)(2,1)} %pack.2), channel_id=1, source_target_pairs={{0,16},{1,17},{2,18},{3,19},{4,20},{5,21},{6,22},{7,23},{8,24},{9,... | collective-permute-start | bytes 221192 | tf_op jit(solution)/shard_map/ppermute | solution.py:711
  8.5 1.4 pack.3
  9.9 3.3 %collective-permute-done.1 = bf16[16,768]{1,0:T(8,128)(2,1)S(1)} collective-permute-done((bf16[16,768]{1,0:T(8,128)(2,1)S(1)}, bf16[16,768]{1,0:T(8,128)(2,1)S(1)}, u32[]{:S(2)}, u32[]{:S(2)}) %collective-permute-start.1) | collective-permute-done | bytes 24608 | tf_op jit(solution)/shard_map/ppermute | solution.py:711
  14.2 1.6 collective-permute-start.3
  16.6 1.7 collective-permute-done.3
  18.3 3.8 %collective-permute-done.4 = bf16[48,768]{1,0:T(8,128)(2,1)S(1)} collective-permute-done((bf16[48,768]{1,0:T(8,128)(2,1)}, bf16[48,768]{1,0:T(8,128)(2,1)S(1)}, u32[]{:S(2)}, u32[]{:S(2)}) %collective-permute-start.4) | collective-permute-done | bytes 73760 | tf_op jit(solution)/shard_map/ppermute | solution.py:711
  24.1 1.5 collective-permute-start.6
  28.0 3.1 collective-permute-done.8
  34.0 1.5 collective-permute-start.11
  36.0 1.8 collective-permute-done.11
  37.8 4.6 %collective-permute-done.12 = bf16[2,2,48,768]{3,2,1,0:T(8,128)(2,1)S(1)} collective-permute-done((bf16[2,2,48,768]{3,2,1,0:T(8,128)(2,1)S(1)}, bf16[2,2,48,768]{3,2,1,0:T(8,128)(2,1)S(1)}, u32[]{:S(2)}, u32[]{:S(2)}) %collective-permute-start.12) | collective-permute-done | bytes 294944 | tf_op jit(solution)/shard_map/ppermute | solution.py:711
  42.6 2.7 collective-permute-done.9.refs_3_
  45.9 1.5 collective-permute-done.15
  47.4 1.4 collective-permute-start.18
  49.4 1.8 collective-permute-start.19
  51.2 3.3 %project.2 = (bf16[1024,768]{1,0:T(8,128)(2,1)S(1)}, bf16[1024,768]{1,0:T(8,128)(2,1)S(1)}, bf16[2,4,2,2,2,24,768]{6,5,4,3,2,1,0:T(8,128)(2,1)S(1)}) custom-call(bf16[1024,768]{1,0:T(8,128)(2,1)S(1)} %bitcast.188, bf16[16,768]{1,0:T(8,128)(2,1)S(1)} %add.653.refs_1_.vec_ref.refs_2_.codes_ref.refs_5_, ...), custom_call_target="tpu_custom_call" | custom-call | flops 2415919104 | bytes 9437184 | tf_op jit(solution)/shard_map/project/pallas_call | solution.py:128
  54.4 1.4 copy-done.2
  55.8 3.9 %collective-permute-done.19 = bf16[96,768]{1,0:T(8,128)(2,1)S(1)} collective-permute-done((bf16[96,768]{1,0:T(8,128)(2,1)S(1)}, bf16[96,768]{1,0:T(8,128)(2,1)S(1)}, u32[]{:S(2)}, u32[]{:S(2)}) %collective-permute-start.19) | collective-permute-done | bytes 147488 | tf_op jit(solution)/shard_map/ppermute | solution.py:711
  59.8 3.3 %collective-permute-done.18 = bf16[2,2,24,3072]{3,2,1,0:T(8,128)(2,1)S(1)} collective-permute-done((bf16[2,2,24,3072]{3,2,1,0:T(8,128)(2,1)S(1)}, bf16[2,2,24,3072]{3,2,1,0:T(8,128)(2,1)S(1)}, u32[]{:S(2)}, u32[]{:S(2)}) %collective-permute-start.18) | collective-permute-done | bytes 589856 | tf_op jit(solution)/shard_map/ppermute | solution.py:711
  65.4 2.0 project.3
  67.5 1.4 copy-done.3
  70.0 1.8 collective-permute-start.22
  71.8 9.3 %attend.1 = (f32[3,1024,256]{2,1,0:T(8,128)}, bf16[1024,768]{1,0:T(8,128)(2,1)}) custom-call(s32[16]{0:T(128)} %len_ref.1, bf16[1024,768]{1,0:T(8,128)(2,1)} %copy-done.10, bf16[1024,768]{1,0:T(8,128)(2,1)} %copy-done.11, bf16[1024,768]{1,0:T(8,128)(2,1)} %copy-done.7), custom_call_target="tpu_custom_call" | custom-call | flops 6039797760 | bytes 15728640 | tf_op jit(solution)/shard_map/attend/pallas_call | solution.py:220
  82.7 5.6 %close.1 = (f32[1024,768]{1,0:T(8,128)}, f32[1024,1]{1,0:T(8,128)}, bf16[1024,768]{1,0:T(8,128)(2,1)}) custom-call(bf16[1024,768]{1,0:T(8,128)(2,1)} %bitcast.186, bf16[1024,768]{1,0:T(8,128)(2,1)} %get-tuple-element.161.c_ref.refs_7_, bf16[2,768,768]{2,1,0:T(8,128)(2,1)} %bitcast.183, bf16[16,768]{1,0:T(8,128)(2,1)} %copy-done.5), custom_call_target="tpu_custom_call" | custom-call | flops 1207959552 | bytes 9043968 | tf_op jit(solution)/shard_map/close/pallas_call | solution.py:251
  88.3 3.4 %collective-permute-done.25 = bf16[2,2,96,768]{3,2,1,0:T(8,128)(2,1)S(1)} collective-permute-done((bf16[2,2,96,768]{3,2,1,0:T(8,128)(2,1)S(1)}, bf16[2,2,96,768]{3,2,1,0:T(8,128)(2,1)S(1)}, u32[]{:S(2)}, u32[]{:S(2)}) %collective-permute-start.25) | collective-permute-done | bytes 589856 | tf_op jit(solution)/shard_map/ppermute | solution.py:711
  92.7 22.8 %inner.1 = (bf16[1024,3072]{1,0:T(8,128)(2,1)}, bf16[1024,3072]{1,0:T(8,128)(2,1)}, bf16[4,2,2,2,24,3072]{5,4,3,2,1,0:T(8,128)(2,1)}) custom-call(bf16[1024,768]{1,0:T(8,128)(2,1)} %get-tuple-element.167.refs_0_.refs_1_, bf16[16,768]{1,0:T(8,128)(2,1)} %copy-done.5, bf16[4,2,24,3072]{3,2,1,0:T(8,128)(2,1)} %copy-done.15, ...), custom_call_target="tpu_custom_call" | custom-call | flops 14495514624 | bytes 23592960 | tf_op jit(solution)/shard_map/inner/pallas_call | solution.py:422
  116.2 2.5 collective-permute-done.28.refs_6_
  119.6 12.9 %outer.1 = (bf16[1024,768]{1,0:T(8,128)(2,1)}, f32[1024,768]{1,0:T(8,128)}, f32[1024,1]{1,0:T(8,128)}, f32[8,1536]{1,0:T(8,128)}, bf16[8,1536]{1,0:T(8,128)(2,1)}, /*index=5*/bf16[4,2,2,2,96,768]{5,4,3,2,1,0:T(8,128)(2,1)}) custom-call(bf16[1024,3072]{1,0:T(8,128)(2,1)} %get-tuple-element.174.refs_0_.refs_4_, ...), custom_call_target="tpu_custom_call" | custom-call | flops 4831838208 | bytes 23592960 | tf_op jit(solution)/shard_map/outer/pallas_call | solution.py:470
  132.6 1.6 collective-permute-start.29
  134.1 3.5 %collective-permute-done.29 = bf16[8,1536]{1,0:T(8,128)(2,1)S(1)} collective-permute-done((bf16[8,1536]{1,0:T(8,128)(2,1)}, bf16[8,1536]{1,0:T(8,128)(2,1)S(1)}, u32[]{:S(2)}, u32[]{:S(2)}) %collective-permute-start.29) | collective-permute-done | bytes 24608 | tf_op jit(solution)/shard_map/ppermute | solution.py:711
  138.7 3.8 %collective-permute-done.30 = bf16[2,8,1536]{2,1,0:T(8,128)(2,1)S(1)} collective-permute-done((bf16[2,8,1536]{2,1,0:T(8,128)(2,1)S(1)}, bf16[2,8,1536]{2,1,0:T(8,128)(2,1)S(1)}, u32[]{:S(2)}, u32[]{:S(2)}) %collective-permute-start.30) | collective-permute-done | bytes 49184 | tf_op jit(solution)/shard_map/ppermute | solution.py:711
  142.6 1.2 collective-permute-start.31
  144.0 3.6 %collective-permute-done.31 = bf16[2,2,8,1536]{3,2,1,0:T(8,128)(2,1)S(1)} collective-permute-done((bf16[2,2,8,1536]{3,2,1,0:T(8,128)(2,1)S(1)}, bf16[2,2,8,1536]{3,2,1,0:T(8,128)(2,1)S(1)}, u32[]{:S(2)}, u32[]{:S(2)}) %collective-permute-start.31) | collective-permute-done | bytes 98336 | tf_op jit(solution)/shard_map/ppermute | solution.py:711
  147.7 1.3 collective-permute-start.32
  149.0 4.4 %collective-permute-done.32.far = bf16[4,2,8,1536]{3,2,1,0:T(8,128)(2,1)S(1)} collective-permute-done((bf16[4,2,8,1536]{3,2,1,0:T(8,128)(2,1)S(1)}, bf16[4,2,8,1536]{3,2,1,0:T(8,128)(2,1)S(1)}, u32[]{:S(2)}, u32[]{:S(2)}) %collective-permute-start.32) | collective-permute-done | bytes 196640 | tf_op jit(solution)/shard_map/ppermute | solution.py:711
  153.5 1.4 collective-permute-done.34.far_other
  155.7 1.3 pair_loss.1
  157.6 13.5 %outer_back.1 = (f32[1024,768]{1,0:T(8,128)}, bf16[1024,768]{1,0:T(8,128)(2,1)}, f32[16,768]{1,0:T(8,128)}, bf16[4,2,2,96,768]{4,3,2,1,0:T(8,128)(2,1)}, bf16[4,2,2,96,768]{4,3,2,1,0:T(8,128)(2,1)}) custom-call(bf16[1024,768]{1,0:T(8,128)(2,1)} %bitcast.223, f32[8,1536]{1,0:T(8,128)} %copy-done.9, f32[1024,768]{1,0:T(8,128)} %get-tuple-element.183.refs_2_, ...), custom_call_target="tpu_custom_call" | custom-call | flops 9663676416 | bytes 36175872 | tf_op jit(solution)/shard_map/outer_back/pallas_call | solution.py:556
  171.2 15.8 %inner_back.1 = (bf16[1024,3072]{1,0:T(8,128)(2,1)}, f32[16,768]{1,0:T(8,128)}, bf16[4,2,2,24,3072]{4,3,2,1,0:T(8,128)(2,1)}, bf16[4,2,2,24,3072]{4,3,2,1,0:T(8,128)(2,1)}) custom-call(bf16[1024,768]{1,0:T(8,128)(2,1)} %get-tuple-element.187.refs_0_, bf16[1024,768]{1,0:T(8,128)(2,1)} %get-tuple-element.167.refs_0_.refs_1_, ...), custom_call_target="tpu_custom_call" | custom-call | flops 9663676416 | bytes 34603008 | tf_op jit(solution)/shard_map/inner_back/pallas_call | solution.py:596
  187.5 2.6 fusion.2
  191.2 14.0 %open_back.1 = (f32[1024,768]{1,0:T(8,128)}, bf16[1024,768]{1,0:T(8,128)(2,1)}, bf16[1024,768]{1,0:T(8,128)(2,1)}, f32[16,768]{1,0:T(8,128)}) custom-call(f32[1024,768]{1,0:T(8,128)} %get-tuple-element.196.dres_ref, bf16[1024,3072]{1,0:T(8,128)(2,1)} %get-tuple-element.197.dh_ref, bf16[768,3072]{1,0:T(8,128)(2,1)} %bitcast.224, ...), custom_call_target="tpu_custom_call" | custom-call | flops 6039797760 | bytes 21626880 | tf_op jit(solution)/shard_map/open_back/pallas_call | solution.py:282
  206.5 2.5 fusion.5
  209.0 1.2 collective-permute-start.38
  210.3 1.6 fusion.3
  212.2 29.9 %heads_back.1 = (bf16[1024,768]{1,0:T(8,128)(2,1)}, bf16[1024,768]{1,0:T(8,128)(2,1)}, bf16[1024,768]{1,0:T(8,128)(2,1)}, bf16[4,2,2,104,768]{4,3,2,1,0:T(8,128)(2,1)}, bf16[4,2,2,104,768]{4,3,2,1,0:T(8,128)(2,1)}) custom-call(bf16[1024,768]{1,0:T(8,128)(2,1)} %copy-done.10, bf16[1024,768]{1,0:T(8,128)(2,1)} %copy-done.11, bf16[1024,768]{1,0:T(8,128)(2,1)} %copy-done.7, ...), custom_call_target="tpu_custom_call" | custom-call | flops 18874368000 | bytes 15728640 | tf_op jit(solution)/shard_map/heads_back/pallas_call | solution.py:372
  242.9 1.5 fusion.10
  244.4 2.5 fusion.4
  247.3 2.7 fusion
  250.0 1.3 collective-permute-start.43
  252.0 1.8 collective-permute-start.41
  253.8 8.9 %token_grad.1 = f32[1024,768]{1,0:T(8,128)} custom-call(f32[1024,768]{1,0:T(8,128)} %get-tuple-element.201.dr_ref, bf16[1024,768]{1,0:T(8,128)(2,1)} %get-tuple-element.215.dq_ref, bf16[1024,768]{1,0:T(8,128)(2,1)} %get-tuple-element.216.dk_ref, bf16[1024,768]{1,0:T(8,128)(2,1)} %get-tuple-element.217.dv_ref, bf16[2,768,768]{2,1,0:T(8,128)(2,1)} %bitcast.181, ...), custom_call_target="tpu_custom_call" | custom-call | flops 3623878656 | bytes 14548992 | tf_op jit(solution)/shard_map/token_grad/pallas_call | solution.py:619
  262.7 11.1 %collective-permute-done.42 = bf16[2,2,24,3072]{3,2,1,0:T(8,128)(2,1)S(1)} collective-permute-done((bf16[2,2,24,3072]{3,2,1,0:T(8,128)(2,1)}, bf16[2,2,24,3072]{3,2,1,0:T(8,128)(2,1)S(1)}, u32[]{:S(2)}, u32[]{:S(2)}) %collective-permute-start.42) | collective-permute-done | bytes 589856 | tf_op jit(solution)/shard_map/ppermute | solution.py:711
  274.6 2.4 fusion.1
  277.7 2.1 fusion.9
  279.8 1.2 collective-permute-start.44
  282.8 2.6 collective-permute-start.46
  285.4 5.4 %collective-permute-done.44 = bf16[2,24,3072]{2,1,0:T(8,128)(2,1)} collective-permute-done((bf16[2,24,3072]{2,1,0:T(8,128)(2,1)}, bf16[2,24,3072]{2,1,0:T(8,128)(2,1)}, u32[]{:S(2)}, u32[]{:S(2)}) %collective-permute-start.44) | collective-permute-done | bytes 294944 | tf_op jit(solution)/shard_map/ppermute | solution.py:711
  292.0 1.8 collective-permute-start.47
  295.1 1.4 collective-permute-start.49
  296.6 2.0 fusion.16
  298.5 4.6 %collective-permute-done.47 = bf16[2,104,768]{2,1,0:T(8,128)(2,1)S(1)} collective-permute-done((bf16[2,104,768]{2,1,0:T(8,128)(2,1)S(1)}, bf16[2,104,768]{2,1,0:T(8,128)(2,1)S(1)}, u32[]{:S(2)}, u32[]{:S(2)}) %collective-permute-start.47) | collective-permute-done | bytes 319520 | tf_op jit(solution)/shard_map/ppermute | solution.py:711
  305.3 2.0 fusion.14
  307.3 4.7 %collective-permute-done.48 = bf16[104,768]{1,0:T(8,128)(2,1)S(1)} collective-permute-done((bf16[104,768]{1,0:T(8,128)(2,1)S(1)}, bf16[104,768]{1,0:T(8,128)(2,1)S(1)}, u32[]{:S(2)}, u32[]{:S(2)}) %collective-permute-start.48) | collective-permute-done | bytes 159776 | tf_op jit(solution)/shard_map/ppermute | solution.py:711
  (164 shorter events, 39.7 us)
Async XLA Ops:
  0.7 6.4 %copy-start = (bf16[96]{0:T(256)(128)(2,1)S(1)}, bf16[96]{0:T(256)(128)(2,1)}, u32[]{:S(2)}) copy-start(bf16[96]{0:T(256)(128)(2,1)} %param.33) | copy-start | bytes 580
  0.7 22.5 %copy-start.21 = (bf16[24,3072]{1,0:T(8,128)(2,1)S(1)}, bf16[24,3072]{1,0:T(8,128)(2,1)}, u32[]{:S(2)}) copy-start(bf16[24,3072]{1,0:T(8,128)(2,1)} %param.32) | copy-start | bytes 442372
  2.1 11.1 %collective-permute-start = (bf16[48,768]{1,0:T(8,128)(2,1)}, bf16[48,768]{1,0:T(8,128)(2,1)S(1)}, u32[]{:S(2)}, u32[]{:S(2)}) collective-permute-start(bf16[48,768]{1,0:T(8,128)(2,1)} %pack.2), channel_id=1, source_target_pairs={{0,16},{1,17},{2,18},{3,19},{4,20},{5,21},{6,22},{7,23},{8,24},{9,... | collective-permute-start | bytes 221192 | tf_op jit(solution)/shard_map/ppermute | solution.py:711
  8.4 4.7 %collective-permute-start.1 = (bf16[16,768]{1,0:T(8,128)(2,1)S(1)}, bf16[16,768]{1,0:T(8,128)(2,1)S(1)}, u32[]{:S(2)}, u32[]{:S(2)}) collective-permute-start(bf16[16,768]{1,0:T(8,128)(2,1)S(1)} %maximum_maximum_fusion), channel_id=1, source_target_pairs={{0,16},{1,17},{2,18},{3,19},{4,20},{5,21},{6,22},{7,23},{8,24},{9,... | collective-permute-start | bytes 73736 | tf_op jit(solution)/shard_map/ppermute | solution.py:711
  14.2 4.0 %collective-permute-start.3 = (bf16[16,768]{1,0:T(8,128)(2,1)S(1)}, bf16[16,768]{1,0:T(8,128)(2,1)S(1)}, u32[]{:S(2)}, u32[]{:S(2)}) collective-permute-start(bf16[16,768]{1,0:T(8,128)(2,1)S(1)} %fusion.62), channel_id=1, source_target_pairs={{0,8},{1,9},{2,10},{3,11},{4,12},{5,13},{6,14},{7,15},{8,0},{9,1},... | collective-permute-start | bytes 73736 | tf_op jit(solution)/shard_map/ppermute | solution.py:711
  15.9 6.2 %collective-permute-start.4 = (bf16[48,768]{1,0:T(8,128)(2,1)}, bf16[48,768]{1,0:T(8,128)(2,1)S(1)}, u32[]{:S(2)}, u32[]{:S(2)}) collective-permute-start(bf16[48,768]{1,0:T(8,128)(2,1)} %pack.3), channel_id=1, source_target_pairs={{0,16},{1,17},{2,18},{3,19},{4,20},{5,21},{6,22},{7,23},{8,24},{9,... | collective-permute-start | bytes 221192 | tf_op jit(solution)/shard_map/ppermute | solution.py:711
  16.5 6.6 %collective-permute-start.2 = (bf16[2,48,768]{2,1,0:T(8,128)(2,1)S(1)}, bf16[2,48,768]{2,1,0:T(8,128)(2,1)S(1)}, u32[]{:S(2)}, u32[]{:S(2)}) collective-permute-start(bf16[2,48,768]{2,1,0:T(8,128)(2,1)S(1)} %broadcast_select_fusion.12), channel_id=1, source_target_pairs={{0,8},{1,9},{2,10},{3,11},{4,12},{5,13},{6,14},{7,15},{8,0},{9,1},... | collective-permute-start | bytes 442376 | tf_op jit(solution)/shard_map/ppermute | solution.py:711
  23.2 7.8 %collective-permute-start.8 = (bf16[24,3072]{1,0:T(8,128)(2,1)S(1)}, bf16[24,3072]{1,0:T(8,128)(2,1)S(1)}, u32[]{:S(2)}, u32[]{:S(2)}) collective-permute-start(bf16[24,3072]{1,0:T(8,128)(2,1)S(1)} %copy-done.21), channel_id=1, source_target_pairs={{0,16},{1,17},{2,18},{3,19},{4,20},{5,21},{6,22},{7,23},{8,24},{9,... | collective-permute-start | bytes 442376 | tf_op jit(solution)/shard_map/ppermute | solution.py:711
  24.1 3.8 %collective-permute-start.6 = (bf16[16,768]{1,0:T(8,128)(2,1)S(1)}, bf16[16,768]{1,0:T(8,128)(2,1)S(1)}, u32[]{:S(2)}, u32[]{:S(2)}) collective-permute-start(bf16[16,768]{1,0:T(8,128)(2,1)S(1)} %add.650), channel_id=1, source_target_pairs={{0,2},{1,5},{2,0},{3,7},{4,6},{5,1},{6,4},{7,3},{8,10},{9,13},{10,... | collective-permute-start | bytes 73736 | tf_op jit(solution)/shard_map/ppermute | solution.py:711
  25.6 6.7 %collective-permute-start.5 = (bf16[2,2,48,768]{3,2,1,0:T(8,128)(2,1)S(1)}, bf16[2,2,48,768]{3,2,1,0:T(8,128)(2,1)S(1)}, u32[]{:S(2)}, u32[]{:S(2)}) collective-permute-start(bf16[2,2,48,768]{3,2,1,0:T(8,128)(2,1)S(1)} %broadcast_select_fusion.9), channel_id=1, source_target_pairs={{0,2},{1,5},{2,0},{3,7},{4,6},{5,1},{6,4},{7,3},{8,10},{9,13},{10,... | collective-permute-start | bytes 884744 | tf_op jit(solution)/shard_map/ppermute | solution.py:711
  26.1 5.7 %collective-permute-start.7 = (bf16[2,48,768]{2,1,0:T(8,128)(2,1)S(1)}, bf16[2,48,768]{2,1,0:T(8,128)(2,1)S(1)}, u32[]{:S(2)}, u32[]{:S(2)}) collective-permute-start(bf16[2,48,768]{2,1,0:T(8,128)(2,1)S(1)} %broadcast_select_fusion.11), channel_id=1, source_target_pairs={{0,8},{1,9},{2,10},{3,11},{4,12},{5,13},{6,14},{7,15},{8,0},{9,1},... | collective-permute-start | bytes 442376 | tf_op jit(solution)/shard_map/ppermute | solution.py:711
  32.3 17.0 %copy-start.22 = (bf16[96,768]{1,0:T(8,128)(2,1)S(1)}, bf16[96,768]{1,0:T(8,128)(2,1)}, u32[]{:S(2)}) copy-start(bf16[96,768]{1,0:T(8,128)(2,1)} %param.34) | copy-start | bytes 442372
  32.3 18.8 %copy-start.4 = (bf16[16,64,768]{2,1,0:T(8,128)(2,1)S(1)}, bf16[16,64,768]{2,1,0:T(8,128)(2,1)}, u32[]{:S(2)}) copy-start(bf16[16,64,768]{2,1,0:T(8,128)(2,1)} %param.19) | copy-start | bytes 4718596
  32.5 9.9 %collective-permute-start.12 = (bf16[2,2,48,768]{3,2,1,0:T(8,128)(2,1)S(1)}, bf16[2,2,48,768]{3,2,1,0:T(8,128)(2,1)S(1)}, u32[]{:S(2)}, u32[]{:S(2)}) collective-permute-start(bf16[2,2,48,768]{3,2,1,0:T(8,128)(2,1)S(1)} %broadcast_select_fusion.8), channel_id=1, source_target_pairs={{0,2},{1,5},{2,0},{3,7},{4,6},{5,1},{6,4},{7,3},{8,10},{9,13},{10,... | collective-permute-start | bytes 884744 | tf_op jit(solution)/shard_map/ppermute | solution.py:711
  33.7 8.8 %collective-permute-start.13 = (bf16[2,24,3072]{2,1,0:T(8,128)(2,1)S(1)}, bf16[2,24,3072]{2,1,0:T(8,128)(2,1)S(1)}, u32[]{:S(2)}, u32[]{:S(2)}) collective-permute-start(bf16[2,24,3072]{2,1,0:T(8,128)(2,1)S(1)} %broadcast_select_fusion.7), channel_id=1, source_target_pairs={{0,8},{1,9},{2,10},{3,11},{4,12},{5,13},{6,14},{7,15},{8,0},{9,1},... | collective-permute-start | bytes 884744 | tf_op jit(solution)/shard_map/ppermute | solution.py:711
  34.0 3.8 %collective-permute-start.11 = (bf16[16,768]{1,0:T(8,128)(2,1)S(1)}, bf16[16,768]{1,0:T(8,128)(2,1)S(1)}, u32[]{:S(2)}, u32[]{:S(2)}) collective-permute-start(bf16[16,768]{1,0:T(8,128)(2,1)S(1)} %add.651), channel_id=1, source_target_pairs={{0,4},{1,3},{2,6},{3,1},{4,0},{5,7},{6,2},{7,5},{8,12},{9,11},{10,... | collective-permute-start | bytes 73736 | tf_op jit(solution)/shard_map/ppermute | solution.py:711
  35.5 9.9 %collective-permute-start.9 = (bf16[4,2,48,768]{3,2,1,0:T(8,128)(2,1)S(1)}, bf16[4,2,48,768]{3,2,1,0:T(8,128)(2,1)S(1)}, u32[]{:S(2)}, u32[]{:S(2)}) collective-permute-start(bf16[4,2,48,768]{3,2,1,0:T(8,128)(2,1)S(1)} %broadcast_select_fusion.5.refs_2_), channel_id=1, source_target_pairs={{0,4},{1,3},{2,6},{3,1},{4,0},{5,7},{6,2},{7,5},{8,12},{9,11},{10,... | collective-permute-start | bytes 1769480 | tf_op jit(solution)/shard_map/ppermute | solution.py:711
  36.0 9.4 %collective-permute-start.10 = (bf16[4,2,48,768]{3,2,1,0:T(8,128)(2,1)S(1)}, bf16[4,2,48,768]{3,2,1,0:T(8,128)(2,1)S(1)}, u32[]{:S(2)}, u32[]{:S(2)}) collective-permute-start(bf16[4,2,48,768]{3,2,1,0:T(8,128)(2,1)S(1)} %broadcast_select_fusion.5.refs_2_), channel_id=1, source_target_pairs={{0,1},{1,0},{2,3},{3,2},{4,5},{5,4},{6,7},{7,6},{8,9},{9,8},{10,11... | collective-permute-start | bytes 1769480 | tf_op jit(solution)/shard_map/ppermute | solution.py:711
  45.4 2.1 collective-permute-start.14
  45.4 2.0 collective-permute-start.15
  47.4 18.0 %copy-start.5 = (bf16[16,768]{1,0:T(8,128)(2,1)}, bf16[16,768]{1,0:T(8,128)(2,1)S(1)}, u32[]{:S(2)}) copy-start(bf16[16,768]{1,0:T(8,128)(2,1)S(1)} %add.653.refs_1_.vec_ref.refs_2_.codes_ref.refs_5_) | copy-start | bytes 73732
  47.4 15.7 %collective-permute-start.18 = (bf16[2,2,24,3072]{3,2,1,0:T(8,128)(2,1)S(1)}, bf16[2,2,24,3072]{3,2,1,0:T(8,128)(2,1)S(1)}, u32[]{:S(2)}, u32[]{:S(2)}) collective-permute-start(bf16[2,2,24,3072]{3,2,1,0:T(8,128)(2,1)S(1)} %broadcast_select_fusion.3), channel_id=1, source_target_pairs={{0,2},{1,5},{2,0},{3,7},{4,6},{5,1},{6,4},{7,3},{8,10},{9,13},{10,... | collective-permute-start | bytes 1769480 | tf_op jit(solution)/shard_map/ppermute | solution.py:711
  48.9 14.4 %collective-permute-start.16 = (bf16[4,2,48,768]{3,2,1,0:T(8,128)(2,1)S(1)}, bf16[4,2,48,768]{3,2,1,0:T(8,128)(2,1)S(1)}, u32[]{:S(2)}, u32[]{:S(2)}) collective-permute-start(bf16[4,2,48,768]{3,2,1,0:T(8,128)(2,1)S(1)} %broadcast_select_fusion.4.refs_2_), channel_id=1, source_target_pairs={{0,4},{1,3},{2,6},{3,1},{4,0},{5,7},{6,2},{7,5},{8,12},{9,11},{10,... | collective-permute-start | bytes 1769480 | tf_op jit(solution)/shard_map/ppermute | solution.py:711
  49.4 13.9 %collective-permute-start.17 = (bf16[4,2,48,768]{3,2,1,0:T(8,128)(2,1)S(1)}, bf16[4,2,48,768]{3,2,1,0:T(8,128)(2,1)S(1)}, u32[]{:S(2)}, u32[]{:S(2)}) collective-permute-start(bf16[4,2,48,768]{3,2,1,0:T(8,128)(2,1)S(1)} %broadcast_select_fusion.4.refs_2_), channel_id=1, source_target_pairs={{0,1},{1,0},{2,3},{3,2},{4,5},{5,4},{6,7},{7,6},{8,9},{9,8},{10,11... | collective-permute-start | bytes 1769480 | tf_op jit(solution)/shard_map/ppermute | solution.py:711
  49.4 10.3 %collective-permute-start.19 = (bf16[96,768]{1,0:T(8,128)(2,1)S(1)}, bf16[96,768]{1,0:T(8,128)(2,1)S(1)}, u32[]{:S(2)}, u32[]{:S(2)}) collective-permute-start(bf16[96,768]{1,0:T(8,128)(2,1)S(1)} %copy-done.22), channel_id=1, source_target_pairs={{0,16},{1,17},{2,18},{3,19},{4,20},{5,21},{6,22},{7,23},{8,24},{9,... | collective-permute-start | bytes 442376 | tf_op jit(solution)/shard_map/ppermute | solution.py:711
  55.8 11.6 %copy-start.10 = (bf16[1024,768]{1,0:T(8,128)(2,1)}, bf16[1024,768]{1,0:T(8,128)(2,1)S(1)}, u32[]{:S(2)}) copy-start(bf16[1024,768]{1,0:T(8,128)(2,1)S(1)} %get-tuple-element.151.q_ref.refs_0_) | copy-start | bytes 4718596
  55.8 11.6 %copy-start.11 = (bf16[1024,768]{1,0:T(8,128)(2,1)}, bf16[1024,768]{1,0:T(8,128)(2,1)S(1)}, u32[]{:S(2)}) copy-start(bf16[1024,768]{1,0:T(8,128)(2,1)S(1)} %get-tuple-element.152.k_ref.refs_1_) | copy-start | bytes 4718596
  63.3 17.9 %copy-start.15 = (bf16[4,2,24,3072]{3,2,1,0:T(8,128)(2,1)}, bf16[4,2,24,3072]{3,2,1,0:T(8,128)(2,1)S(1)}, u32[]{:S(2)}) copy-start(bf16[4,2,24,3072]{3,2,1,0:T(8,128)(2,1)S(1)} %broadcast_select_fusion.1.refs_2_) | copy-start | bytes 3538948
  63.3 2.1 collective-permute-start.20
  63.4 17.8 %collective-permute-start.21 = (bf16[4,2,24,3072]{3,2,1,0:T(8,128)(2,1)S(1)}, bf16[4,2,24,3072]{3,2,1,0:T(8,128)(2,1)}, u32[]{:S(2)}, u32[]{:S(2)}) collective-permute-start(bf16[4,2,24,3072]{3,2,1,0:T(8,128)(2,1)S(1)} %broadcast_select_fusion.1.refs_2_), channel_id=1, source_target_pairs={{0,4},{1,3},{2,6},{3,1},{4,0},{5,7},{6,2},{7,5},{8,12},{9,11},{10,... | collective-permute-start | bytes 3538952 | tf_op jit(solution)/shard_map/ppermute | solution.py:711
  70.0 11.0 %collective-permute-start.22 = (bf16[2,96,768]{2,1,0:T(8,128)(2,1)S(1)}, bf16[2,96,768]{2,1,0:T(8,128)(2,1)S(1)}, u32[]{:S(2)}, u32[]{:S(2)}) collective-permute-start(bf16[2,96,768]{2,1,0:T(8,128)(2,1)S(1)} %broadcast_select_fusion.6), channel_id=1, source_target_pairs={{0,8},{1,9},{2,10},{3,11},{4,12},{5,13},{6,14},{7,15},{8,0},{9,1},... | collective-permute-start | bytes 884744 | tf_op jit(solution)/shard_map/ppermute | solution.py:711
  81.2 10.6 %collective-permute-start.23 = (bf16[4,2,24,3072]{3,2,1,0:T(8,128)(2,1)S(1)}, bf16[4,2,24,3072]{3,2,1,0:T(8,128)(2,1)}, u32[]{:S(2)}, u32[]{:S(2)}) collective-permute-start(bf16[4,2,24,3072]{3,2,1,0:T(8,128)(2,1)S(1)} %broadcast_select_fusion.1.refs_2_), channel_id=1, source_target_pairs={{0,1},{1,0},{2,3},{3,2},{4,5},{5,4},{6,7},{7,6},{8,9},{9,8},{10,11... | collective-permute-start | bytes 3538952 | tf_op jit(solution)/shard_map/ppermute | solution.py:711
  81.3 10.6 %collective-permute-start.24 = (bf16[4,2,24,3072]{3,2,1,0:T(8,128)(2,1)}, bf16[4,2,24,3072]{3,2,1,0:T(8,128)(2,1)}, u32[]{:S(2)}, u32[]{:S(2)}) collective-permute-start(bf16[4,2,24,3072]{3,2,1,0:T(8,128)(2,1)} %collective-permute-done.21.refs_3_), channel_id=1, source_target_pairs={{0,1},{1,0},{2,3},{3,2},{4,5},{5,4},{6,7},{7,6},{8,9},{9,8},{10,11... | collective-permute-start | bytes 3538952 | tf_op jit(solution)/shard_map/ppermute | solution.py:711
  81.8 9.9 %collective-permute-start.25 = (bf16[2,2,96,768]{3,2,1,0:T(8,128)(2,1)S(1)}, bf16[2,2,96,768]{3,2,1,0:T(8,128)(2,1)S(1)}, u32[]{:S(2)}, u32[]{:S(2)}) collective-permute-start(bf16[2,2,96,768]{3,2,1,0:T(8,128)(2,1)S(1)} %broadcast_select_fusion.2), channel_id=1, source_target_pairs={{0,2},{1,5},{2,0},{3,7},{4,6},{5,1},{6,4},{7,3},{8,10},{9,13},{10,... | collective-permute-start | bytes 1769480 | tf_op jit(solution)/shard_map/ppermute | solution.py:711
  91.8 23.7 %copy-start.16 = (bf16[4,2,96,768]{3,2,1,0:T(8,128)(2,1)}, bf16[4,2,96,768]{3,2,1,0:T(8,128)(2,1)S(1)}, u32[]{:S(2)}) copy-start(bf16[4,2,96,768]{3,2,1,0:T(8,128)(2,1)S(1)} %broadcast_select_fusion.refs_3_) | copy-start | bytes 3538948
  91.9 23.7 %collective-permute-start.26 = (bf16[4,2,96,768]{3,2,1,0:T(8,128)(2,1)S(1)}, bf16[4,2,96,768]{3,2,1,0:T(8,128)(2,1)S(1)}, u32[]{:S(2)}, u32[]{:S(2)}) collective-permute-start(bf16[4,2,96,768]{3,2,1,0:T(8,128)(2,1)S(1)} %broadcast_select_fusion.refs_3_), channel_id=1, source_target_pairs={{0,4},{1,3},{2,6},{3,1},{4,0},{5,7},{6,2},{7,5},{8,12},{9,11},{10,... | collective-permute-start | bytes 3538952 | tf_op jit(solution)/shard_map/ppermute | solution.py:711
  92.7 22.9 %collective-permute-start.27 = (bf16[4,2,96,768]{3,2,1,0:T(8,128)(2,1)S(1)}, bf16[4,2,96,768]{3,2,1,0:T(8,128)(2,1)}, u32[]{:S(2)}, u32[]{:S(2)}) collective-permute-start(bf16[4,2,96,768]{3,2,1,0:T(8,128)(2,1)S(1)} %broadcast_select_fusion.refs_3_), channel_id=1, source_target_pairs={{0,1},{1,0},{2,3},{3,2},{4,5},{5,4},{6,7},{7,6},{8,9},{9,8},{10,11... | collective-permute-start | bytes 3538952 | tf_op jit(solution)/shard_map/ppermute | solution.py:711
  115.6 3.0 collective-permute-start.28
  119.6 35.3 %copy-start.6 = (bf16[16,768]{1,0:T(8,128)(2,1)S(1)}, bf16[16,768]{1,0:T(8,128)(2,1)}, u32[]{:S(2)}) copy-start(bf16[16,768]{1,0:T(8,128)(2,1)} %copy-done.5) | copy-start | bytes 73732
  132.6 5.0 %collective-permute-start.29 = (bf16[8,1536]{1,0:T(8,128)(2,1)}, bf16[8,1536]{1,0:T(8,128)(2,1)S(1)}, u32[]{:S(2)}, u32[]{:S(2)}) collective-permute-start(bf16[8,1536]{1,0:T(8,128)(2,1)} %get-tuple-element.178), channel_id=1, source_target_pairs={{0,16},{1,17},{2,18},{3,19},{4,20},{5,21},{6,22},{7,23},{8,24},{9,... | collective-permute-start | bytes 73736 | tf_op jit(solution)/shard_map/ppermute | solution.py:711
  138.4 4.1 %collective-permute-start.30 = (bf16[2,8,1536]{2,1,0:T(8,128)(2,1)S(1)}, bf16[2,8,1536]{2,1,0:T(8,128)(2,1)S(1)}, u32[]{:S(2)}, u32[]{:S(2)}) collective-permute-start(bf16[2,8,1536]{2,1,0:T(8,128)(2,1)S(1)} %broadcast_select_fusion.14), channel_id=1, source_target_pairs={{0,8},{1,9},{2,10},{3,11},{4,12},{5,13},{6,14},{7,15},{8,0},{9,1},... | collective-permute-start | bytes 147464 | tf_op jit(solution)/shard_map/ppermute | solution.py:711
  142.6 5.1 %collective-permute-start.31 = (bf16[2,2,8,1536]{3,2,1,0:T(8,128)(2,1)S(1)}, bf16[2,2,8,1536]{3,2,1,0:T(8,128)(2,1)S(1)}, u32[]{:S(2)}, u32[]{:S(2)}) collective-permute-start(bf16[2,2,8,1536]{3,2,1,0:T(8,128)(2,1)S(1)} %broadcast_select_fusion.13), channel_id=1, source_target_pairs={{0,2},{1,5},{2,0},{3,7},{4,6},{5,1},{6,4},{7,3},{8,10},{9,13},{10,... | collective-permute-start | bytes 294920 | tf_op jit(solution)/shard_map/ppermute | solution.py:711
  147.7 5.7 %collective-permute-start.32 = (bf16[4,2,8,1536]{3,2,1,0:T(8,128)(2,1)S(1)}, bf16[4,2,8,1536]{3,2,1,0:T(8,128)(2,1)S(1)}, u32[]{:S(2)}, u32[]{:S(2)}) collective-permute-start(bf16[4,2,8,1536]{3,2,1,0:T(8,128)(2,1)S(1)} %broadcast_select_fusion.10.near), channel_id=1, source_target_pairs={{0,4},{1,3},{2,6},{3,1},{4,0},{5,7},{6,2},{7,5},{8,12},{9,11},{10,... | collective-permute-start | bytes 589832 | tf_op jit(solution)/shard_map/ppermute | solution.py:711
  149.0 4.4 %collective-permute-start.33 = (bf16[4,2,8,1536]{3,2,1,0:T(8,128)(2,1)S(1)}, bf16[4,2,8,1536]{3,2,1,0:T(8,128)(2,1)S(1)}, u32[]{:S(2)}, u32[]{:S(2)}) collective-permute-start(bf16[4,2,8,1536]{3,2,1,0:T(8,128)(2,1)S(1)} %broadcast_select_fusion.10.near), channel_id=1, source_target_pairs={{0,1},{1,0},{2,3},{3,2},{4,5},{5,4},{6,7},{7,6},{8,9},{9,8},{10,11... | collective-permute-start | bytes 589832 | tf_op jit(solution)/shard_map/ppermute | solution.py:711
  153.4 1.4 collective-permute-start.34
  171.1 15.9 %collective-permute-start.35 = (bf16[4,2,2,96,768]{4,3,2,1,0:T(8,128)(2,1)}, bf16[4,2,2,96,768]{4,3,2,1,0:T(8,128)(2,1)}, u32[]{:S(2)}, u32[]{:S(2)}) collective-permute-start(bf16[4,2,2,96,768]{4,3,2,1,0:T(8,128)(2,1)} %get-tuple-element.193), channel_id=1, source_target_pairs={{0,1},{1,0},{2,3},{3,2},{4,5},{5,4},{6,7},{7,6},{8,9},{9,8},{10,11... | collective-permute-start | bytes 7077896 | tf_op jit(solution)/shard_map/ppermute | solution.py:711
  171.2 16.2 %copy-start.14 = (bf16[4,2,2,96,768]{4,3,2,1,0:T(8,128)(2,1)S(1)}, bf16[4,2,2,96,768]{4,3,2,1,0:T(8,128)(2,1)}, u32[]{:S(2)}) copy-start(bf16[4,2,2,96,768]{4,3,2,1,0:T(8,128)(2,1)} %get-tuple-element.203) | copy-start | bytes 7077892
  187.0 19.5 %collective-permute-start.37 = (bf16[4,2,2,24,3072]{4,3,2,1,0:T(8,128)(2,1)}, bf16[4,2,2,24,3072]{4,3,2,1,0:T(8,128)(2,1)}, u32[]{:S(2)}, u32[]{:S(2)}) collective-permute-start(bf16[4,2,2,24,3072]{4,3,2,1,0:T(8,128)(2,1)} %get-tuple-element.205), channel_id=1, source_target_pairs={{0,1},{1,0},{2,3},{3,2},{4,5},{5,4},{6,7},{7,6},{8,9},{9,8},{10,11... | collective-permute-start | bytes 7077896 | tf_op jit(solution)/shard_map/ppermute | solution.py:711
  190.1 16.4 %collective-permute-start.36 = (bf16[2,2,2,96,768]{4,3,2,1,0:T(8,128)(2,1)}, bf16[2,2,2,96,768]{4,3,2,1,0:T(8,128)(2,1)S(1)}, u32[]{:S(2)}, u32[]{:S(2)}) collective-permute-start(bf16[2,2,2,96,768]{4,3,2,1,0:T(8,128)(2,1)} %fusion.2), channel_id=1, source_target_pairs={{0,2},{1,5},{2,0},{3,7},{4,6},{5,1},{6,4},{7,3},{8,10},{9,13},{10,... | collective-permute-start | bytes 3538952 | tf_op jit(solution)/shard_map/ppermute | solution.py:711
  206.5 5.4 %copy-start.17 = (bf16[2,2,2,96,768]{4,3,2,1,0:T(8,128)(2,1)}, bf16[2,2,2,96,768]{4,3,2,1,0:T(8,128)(2,1)S(1)}, u32[]{:S(2)}) copy-start(bf16[2,2,2,96,768]{4,3,2,1,0:T(8,128)(2,1)S(1)} %collective-permute-done.36) | copy-start | bytes 3538948
  209.0 33.0 %collective-permute-start.38 = (bf16[2,2,96,768]{3,2,1,0:T(8,128)(2,1)}, bf16[2,2,96,768]{3,2,1,0:T(8,128)(2,1)S(1)}, u32[]{:S(2)}, u32[]{:S(2)}) collective-permute-start(bf16[2,2,96,768]{3,2,1,0:T(8,128)(2,1)} %fusion.5), channel_id=1, source_target_pairs={{0,4},{1,3},{2,6},{3,1},{4,0},{5,7},{6,2},{7,5},{8,12},{9,11},{10,... | collective-permute-start | bytes 1769480 | tf_op jit(solution)/shard_map/ppermute | solution.py:711
  211.9 30.2 %collective-permute-start.39 = (bf16[2,2,2,24,3072]{4,3,2,1,0:T(8,128)(2,1)S(1)}, bf16[2,2,2,24,3072]{4,3,2,1,0:T(8,128)(2,1)}, u32[]{:S(2)}, u32[]{:S(2)}) collective-permute-start(bf16[2,2,2,24,3072]{4,3,2,1,0:T(8,128)(2,1)S(1)} %fusion.3), channel_id=1, source_target_pairs={{0,8},{1,9},{2,10},{3,11},{4,12},{5,13},{6,14},{7,15},{8,0},{9,1},... | collective-permute-start | bytes 3538952 | tf_op jit(solution)/shard_map/ppermute | solution.py:711
  242.1 5.2 %collective-permute-start.40 = (bf16[4,2,2,104,768]{4,3,2,1,0:T(8,128)(2,1)}, bf16[4,2,2,104,768]{4,3,2,1,0:T(8,128)(2,1)}, u32[]{:S(2)}, u32[]{:S(2)}) collective-permute-start(bf16[4,2,2,104,768]{4,3,2,1,0:T(8,128)(2,1)} %get-tuple-element.221), channel_id=1, source_target_pairs={{0,1},{1,0},{2,3},{3,2},{4,5},{5,4},{6,7},{7,6},{8,9},{9,8},{10,11... | collective-permute-start | bytes 7667720 | tf_op jit(solution)/shard_map/ppermute | solution.py:711
  250.0 23.8 %collective-permute-start.43 = (bf16[2,2,2,104,768]{4,3,2,1,0:T(8,128)(2,1)}, bf16[2,2,2,104,768]{4,3,2,1,0:T(8,128)(2,1)}, u32[]{:S(2)}, u32[]{:S(2)}) collective-permute-start(bf16[2,2,2,104,768]{4,3,2,1,0:T(8,128)(2,1)} %fusion), channel_id=1, source_target_pairs={{0,2},{1,5},{2,0},{3,7},{4,6},{5,1},{6,4},{7,3},{8,10},{9,13},{10,... | collective-permute-start | bytes 3833864 | tf_op jit(solution)/shard_map/ppermute | solution.py:711
  251.2 22.5 %collective-permute-start.42 = (bf16[2,2,24,3072]{3,2,1,0:T(8,128)(2,1)}, bf16[2,2,24,3072]{3,2,1,0:T(8,128)(2,1)S(1)}, u32[]{:S(2)}, u32[]{:S(2)}) collective-permute-start(bf16[2,2,24,3072]{3,2,1,0:T(8,128)(2,1)} %fusion.4), channel_id=1, source_target_pairs={{0,2},{1,5},{2,0},{3,7},{4,6},{5,1},{6,4},{7,3},{8,10},{9,13},{10,... | collective-permute-start | bytes 1769480 | tf_op jit(solution)/shard_map/ppermute | solution.py:711
  252.0 10.7 %collective-permute-start.41 = (bf16[2,96,768]{2,1,0:T(8,128)(2,1)S(1)}, bf16[2,96,768]{2,1,0:T(8,128)(2,1)S(1)}, u32[]{:S(2)}, u32[]{:S(2)}) collective-permute-start(bf16[2,96,768]{2,1,0:T(8,128)(2,1)S(1)} %fusion.10), channel_id=1, source_target_pairs={{0,8},{1,9},{2,10},{3,11},{4,12},{5,13},{6,14},{7,15},{8,0},{9,1},... | collective-permute-start | bytes 884744 | tf_op jit(solution)/shard_map/ppermute | solution.py:711
  276.9 13.9 %collective-permute-start.45 = (bf16[2,2,104,768]{3,2,1,0:T(8,128)(2,1)}, bf16[2,2,104,768]{3,2,1,0:T(8,128)(2,1)S(1)}, u32[]{:S(2)}, u32[]{:S(2)}) collective-permute-start(bf16[2,2,104,768]{3,2,1,0:T(8,128)(2,1)} %fusion.1), channel_id=1, source_target_pairs={{0,4},{1,3},{2,6},{3,1},{4,0},{5,7},{6,2},{7,5},{8,12},{9,11},{10,... | collective-permute-start | bytes 1916936 | tf_op jit(solution)/shard_map/ppermute | solution.py:711
  279.8 11.0 %collective-permute-start.44 = (bf16[2,24,3072]{2,1,0:T(8,128)(2,1)}, bf16[2,24,3072]{2,1,0:T(8,128)(2,1)}, u32[]{:S(2)}, u32[]{:S(2)}) collective-permute-start(bf16[2,24,3072]{2,1,0:T(8,128)(2,1)} %fusion.9), channel_id=1, source_target_pairs={{0,4},{1,3},{2,6},{3,1},{4,0},{5,7},{6,2},{7,5},{8,12},{9,11},{10,... | collective-permute-start | bytes 884744 | tf_op jit(solution)/shard_map/ppermute | solution.py:711
  281.0 12.9 %copy-start.20 = (bf16[2,2,24,3072]{3,2,1,0:T(8,128)(2,1)S(1)}, bf16[2,2,24,3072]{3,2,1,0:T(8,128)(2,1)}, u32[]{:S(2)}) copy-start(bf16[2,2,24,3072]{3,2,1,0:T(8,128)(2,1)} %copy-done.19) | copy-start | bytes 1769476
  282.8 13.8 %collective-permute-start.46 = (bf16[96,768]{1,0:T(8,128)(2,1)S(1)}, bf16[96,768]{1,0:T(8,128)(2,1)S(1)}, u32[]{:S(2)}, u32[]{:S(2)}) collective-permute-start(bf16[96,768]{1,0:T(8,128)(2,1)S(1)} %fusion.15), channel_id=1, source_target_pairs={{0,16},{1,17},{2,18},{3,19},{4,20},{5,21},{6,22},{7,23},{8,24},{9,... | collective-permute-start | bytes 442376 | tf_op jit(solution)/shard_map/ppermute | solution.py:711
  292.0 11.1 %collective-permute-start.47 = (bf16[2,104,768]{2,1,0:T(8,128)(2,1)S(1)}, bf16[2,104,768]{2,1,0:T(8,128)(2,1)S(1)}, u32[]{:S(2)}, u32[]{:S(2)}) collective-permute-start(bf16[2,104,768]{2,1,0:T(8,128)(2,1)S(1)} %fusion.8), channel_id=1, source_target_pairs={{0,8},{1,9},{2,10},{3,11},{4,12},{5,13},{6,14},{7,15},{8,0},{9,1},... | collective-permute-start | bytes 958472 | tf_op jit(solution)/shard_map/ppermute | solution.py:711
  295.1 10.2 %collective-permute-start.49 = (bf16[24,3072]{1,0:T(8,128)(2,1)S(1)}, bf16[24,3072]{1,0:T(8,128)(2,1)S(1)}, u32[]{:S(2)}, u32[]{:S(2)}) collective-permute-start(bf16[24,3072]{1,0:T(8,128)(2,1)S(1)} %fusion.13), channel_id=1, source_target_pairs={{0,16},{1,17},{2,18},{3,19},{4,20},{5,21},{6,22},{7,23},{8,24},{9,... | collective-permute-start | bytes 442376 | tf_op jit(solution)/shard_map/ppermute | solution.py:711
  303.2 11.7 %copy-start.1 = (bf16[96]{0:T(256)(128)(2,1)S(1)}, bf16[96]{0:T(256)(128)(2,1)}, u32[]{:S(2)}) copy-start(bf16[96]{0:T(256)(128)(2,1)} %param.33) | copy-start | bytes 580
  304.3 7.7 %collective-permute-start.48 = (bf16[104,768]{1,0:T(8,128)(2,1)S(1)}, bf16[104,768]{1,0:T(8,128)(2,1)S(1)}, u32[]{:S(2)}, u32[]{:S(2)}) collective-permute-start(bf16[104,768]{1,0:T(8,128)(2,1)S(1)} %fusion.11), channel_id=1, source_target_pairs={{0,16},{1,17},{2,18},{3,19},{4,20},{5,21},{6,22},{7,23},{8,24},{9,... | collective-permute-start | bytes 479240 | tf_op jit(solution)/shard_map/ppermute | solution.py:711
  (11 other events, 20.5 us)
